TPU v7x, 32 devices: a whole 2x2x4 slice. The times are simulated.
32 devices in a mesh: dp: 8 (over y, x, core), tensor: 4 (over z).
Axes of the slice: x: 2, y: 2, z: 4, core: 2. Of those that a mesh axis runs over, the one named last changes fastest.
Arguments:
- inputs: bfloat16 [16384, 768], P('dp'), may hold values from -6 to 6
- w_query: bfloat16 [768, 768], P(None, 'tensor'), may hold values from -0.21875 to 0.21875
- b_query: bfloat16 [768], P('tensor'), may hold values from -3 to 3
- w_key: bfloat16 [768, 768], P(None, 'tensor'), may hold values from -0.21875 to 0.21875
- w_value: bfloat16 [768, 768], P(None, 'tensor'), may hold values from -0.21875 to 0.21875
- b_value: bfloat16 [768], P('tensor'), may hold values from -3 to 3
- w_output: bfloat16 [768, 768], P('tensor'), may hold values from -6 to 6
- b_output: bfloat16 [768], replicated, may hold values from -3 to 3
- gain_attn: bfloat16 [768], replicated, may hold values from 0.5 to 1.5
- shift_attn: bfloat16 [768], replicated, may hold values from -3 to 3
- w_inner: bfloat16 [768, 3072], P(None, 'tensor'), may hold values from -0.21875 to 0.21875
- b_inner: bfloat16 [3072], P('tensor'), may hold values from -3 to 3
- w_outer: bfloat16 [3072, 768], P('tensor'), may hold values from -0.109375 to 0.109375
- b_outer: bfloat16 [768], replicated, may hold values from -3 to 3
- gain_ffn: bfloat16 [768], replicated, may hold values from 0.5 to 1.5
- shift_ffn: bfloat16 [768], replicated, may hold values from -3 to 3
- cotangent: bfloat16 [16384, 768], P('dp'), may hold values from -6 to 6
Outputs:
- layer_out: bfloat16 [16384, 768], P('dp')
- grad_inputs: float32 [16384, 768], P('dp')
- grad_w_query: float32 [768, 768], P('dp', 'tensor')
- grad_b_query: float32 [768], P('tensor')
- grad_w_key: float32 [768, 768], P('dp', 'tensor')
- grad_w_value: float32 [768, 768], P('dp', 'tensor')
- grad_b_value: float32 [768], P('tensor')
- grad_w_output: float32 [768, 768], P('tensor', 'dp')
- grad_b_output: float32 [768], replicated
- grad_gain_attn: float32 [768], replicated
- grad_shift_attn: float32 [768], replicated
- grad_w_inner: float32 [768, 3072], P('dp', 'tensor')
- grad_b_inner: float32 [3072], P('tensor')
- grad_w_outer: float32 [3072, 768], P('tensor', 'dp')
- grad_b_outer: float32 [768], replicated
- grad_gain_ffn: float32 [768], replicated
- grad_shift_ffn: float32 [768], replicated
All inputs are finite; a program needn't handle non-finite values.
Results may differ from a plain program's by a relative error of at most 0.014.
Values sent between devices are 32-bit elements; how exact they have to be, the bound alone decides.
No kernel may reach another device: no remote copies, remote signals or barrier semaphores. Data moves between devices by JAX's collectives and lax.ppermute only.
A program may use at most 128 MiB of HBM per device.

v0:
```python
from functools import partial

import jax
import jax.numpy as jnp
from jax import lax
from jax.sharding import PartitionSpec as P

HEAD_DIM = 64
LENGTH = 512


EPSILON = 1e-12


def norm_forward(values, gain, shift):
    center = values - jnp.mean(values, axis=-1, keepdims=True)
    inverse = lax.rsqrt(jnp.mean(center * center, axis=-1, keepdims=True) + EPSILON)
    normed = center * inverse
    return (normed * gain + shift, normed, inverse)


def norm_backward(upstream, gain, normed, inverse):
    scaled = upstream * gain
    first_mean = jnp.mean(scaled, axis=-1, keepdims=True)
    cross_mean = jnp.mean(scaled * normed, axis=-1, keepdims=True)
    grad_values = inverse * (scaled - first_mean - normed * cross_mean)
    return (grad_values, jnp.sum(upstream * normed, axis=0), jnp.sum(upstream, axis=0))


def contract_rows(left, right):
    return lax.dot_general(
        left, right, (((0,), (0,)), ((), ())), preferred_element_type=jnp.float32
    )


def times_transpose(left, right):
    return lax.dot_general(
        left, right, (((1,), (1,)), ((), ())), preferred_element_type=jnp.float32
    )


def column_sums(values):
    return jnp.sum(values.astype(jnp.float32), axis=0)


def attend_forward(query_seq, key_seq, value_seq, block_rows, scale):
    length, heads_here, head_size = query_seq.shape

    def one_block(query_block):
        scores = (
            jnp.einsum("qhd,khd->hqk", query_block, key_seq, preferred_element_type=jnp.float32)
            * scale
        )
        largest = jnp.max(scores, axis=-1, keepdims=True)
        expon = jnp.exp(scores - largest)
        totals = jnp.sum(expon, axis=-1, keepdims=True)
        probs = (expon / totals).astype(jnp.bfloat16)
        context = jnp.einsum("hqk,khd->qhd", probs, value_seq, preferred_element_type=jnp.float32)
        return (context.astype(jnp.bfloat16), largest[..., 0] + jnp.log(totals[..., 0]))

    blocks = query_seq.reshape(length // block_rows, block_rows, heads_here, head_size)
    context, log_totals = lax.map(one_block, blocks)
    return (context.reshape(length, heads_here * head_size), log_totals)


def attend_backward(query_seq, key_seq, value_seq, grad_context, log_totals, block_rows, scale):
    length, heads_here, head_size = query_seq.shape
    block_shape = (length // block_rows, block_rows, heads_here, head_size)

    def step(carry, pieces):
        grad_keys, grad_values = carry
        query_block, grad_block, lse_block = pieces
        scores = (
            jnp.einsum("qhd,khd->hqk", query_block, key_seq, preferred_element_type=jnp.float32)
            * scale
        )
        probs = jnp.exp(scores - lse_block[..., None])
        grad_values = grad_values + jnp.einsum(
            "hqk,qhd->khd",
            probs.astype(jnp.bfloat16),
            grad_block,
            preferred_element_type=jnp.float32,
        )
        grad_probs = jnp.einsum(
            "qhd,khd->hqk", grad_block, value_seq, preferred_element_type=jnp.float32
        )
        row_terms = jnp.sum(probs * grad_probs, axis=-1, keepdims=True)
        grad_scores = (probs * (grad_probs - row_terms)).astype(jnp.bfloat16)
        grad_query = (
            jnp.einsum("hqk,khd->qhd", grad_scores, key_seq, preferred_element_type=jnp.float32)
            * scale
        )
        grad_keys = (
            grad_keys
            + jnp.einsum(
                "hqk,qhd->khd", grad_scores, query_block, preferred_element_type=jnp.float32
            )
            * scale
        )
        return ((grad_keys, grad_values), grad_query.astype(jnp.bfloat16))

    zeros_init = jnp.zeros(key_seq.shape, jnp.float32)
    (grad_keys, grad_values), grad_query = lax.scan(
        step,
        (zeros_init, zeros_init),
        (query_seq.reshape(block_shape), grad_context.reshape(block_shape), log_totals),
    )
    flat = (length, heads_here * head_size)
    return (
        grad_query.reshape(flat),
        grad_keys.astype(jnp.bfloat16).reshape(flat),
        grad_values.astype(jnp.bfloat16).reshape(flat),
    )


def shards(
    inputs,
    w_query,
    b_query,
    w_key,
    w_value,
    b_value,
    w_output,
    b_output,
    gain_attn,
    shift_attn,
    w_inner,
    b_inner,
    w_outer,
    b_outer,
    gain_ffn,
    shift_ffn,
    cotangent,
):
    tok_rows = inputs.shape[0]
    heads_here = w_query.shape[1] // HEAD_DIM
    block_rows = min(512, LENGTH)
    scale = HEAD_DIM ** (-0.5)
    split_shape = (tok_rows // LENGTH, LENGTH, heads_here, HEAD_DIM)
    queries = (
        jnp.dot(inputs, w_query, preferred_element_type=jnp.float32) + b_query.astype(jnp.float32)
    ).astype(jnp.bfloat16)
    key_rows = jnp.dot(inputs, w_key, preferred_element_type=jnp.float32).astype(jnp.bfloat16)
    value_rows = (
        jnp.dot(inputs, w_value, preferred_element_type=jnp.float32) + b_value.astype(jnp.float32)
    ).astype(jnp.bfloat16)
    query_split = queries.reshape(split_shape)
    key_split = key_rows.reshape(split_shape)
    value_split = value_rows.reshape(split_shape)

    def forward_seq(triple):
        return attend_forward(triple[0], triple[1], triple[2], block_rows, scale)

    context, log_totals = lax.map(forward_seq, (query_split, key_split, value_split))
    context = context.reshape(tok_rows, heads_here * HEAD_DIM)
    attn_part = jnp.dot(context, w_output, preferred_element_type=jnp.float32)
    attn_total = lax.psum(attn_part, "tensor") + b_output.astype(jnp.float32)
    gain_one = gain_attn.astype(jnp.float32)
    gain_two = gain_ffn.astype(jnp.float32)
    hidden, normed_attn, inverse_attn = norm_forward(
        inputs.astype(jnp.float32) + attn_total, gain_one, shift_attn.astype(jnp.float32)
    )
    hidden_bf = hidden.astype(jnp.bfloat16)
    inner = jnp.dot(hidden_bf, w_inner, preferred_element_type=jnp.float32) + b_inner.astype(
        jnp.float32
    )
    active, gelu_pull = jax.vjp(partial(jax.nn.gelu, approximate=False), inner)
    active_bf = active.astype(jnp.bfloat16)
    outer_part = jnp.dot(active_bf, w_outer, preferred_element_type=jnp.float32)
    outer_total = lax.psum(outer_part, "tensor") + b_outer.astype(jnp.float32)
    layer_out, normed_ffn, inverse_ffn = norm_forward(
        hidden + outer_total, gain_two, shift_ffn.astype(jnp.float32)
    )
    grad_resid2, grad_gain_ffn, grad_shift_ffn = norm_backward(
        cotangent.astype(jnp.float32), gain_two, normed_ffn, inverse_ffn
    )
    grad_outer = grad_resid2.astype(jnp.bfloat16)
    grad_b_outer = column_sums(grad_outer)
    grad_w_outer = contract_rows(active_bf, grad_outer)
    grad_active = times_transpose(grad_outer, w_outer)
    grad_inner = gelu_pull(grad_active)[0].astype(jnp.bfloat16)
    grad_b_inner = column_sums(grad_inner)
    grad_w_inner = contract_rows(hidden_bf, grad_inner)
    grad_hidden = grad_resid2 + lax.psum(times_transpose(grad_inner, w_inner), "tensor")
    grad_resid1, grad_gain_attn, grad_shift_attn = norm_backward(
        grad_hidden, gain_one, normed_attn, inverse_attn
    )
    grad_attn = grad_resid1.astype(jnp.bfloat16)
    grad_b_output = column_sums(grad_attn)
    grad_w_output = contract_rows(context, grad_attn)
    grad_context = times_transpose(grad_attn, w_output).astype(jnp.bfloat16)

    def backward_seq(pieces):
        return attend_backward(
            pieces[0], pieces[1], pieces[2], pieces[3], pieces[4], block_rows, scale
        )

    grad_query, grad_key, grad_value = lax.map(
        backward_seq,
        (query_split, key_split, value_split, grad_context.reshape(split_shape), log_totals),
    )
    flat_shape = (tok_rows, heads_here * HEAD_DIM)
    grad_query = grad_query.reshape(flat_shape)
    grad_key = grad_key.reshape(flat_shape)
    grad_value = grad_value.reshape(flat_shape)
    grad_b_query = column_sums(grad_query)
    grad_b_value = column_sums(grad_value)
    grad_w_query = contract_rows(inputs, grad_query)
    grad_w_key = contract_rows(inputs, grad_key)
    grad_w_value = contract_rows(inputs, grad_value)
    input_part = (
        times_transpose(grad_query, w_query)
        + times_transpose(grad_key, w_key)
        + times_transpose(grad_value, w_value)
    )
    grad_inputs = grad_resid1 + lax.psum(input_part, "tensor")
    small_sums = lax.psum(
        (
            grad_b_query,
            grad_b_value,
            grad_b_output,
            grad_gain_attn,
            grad_shift_attn,
            grad_b_inner,
            grad_b_outer,
            grad_gain_ffn,
            grad_shift_ffn,
        ),
        "dp",
    )
    weight_shards = (
        lax.psum_scatter(grad_w_query, "dp", scatter_dimension=0, tiled=True),
        lax.psum_scatter(grad_w_key, "dp", scatter_dimension=0, tiled=True),
        lax.psum_scatter(grad_w_value, "dp", scatter_dimension=0, tiled=True),
        lax.psum_scatter(grad_w_output, "dp", scatter_dimension=1, tiled=True),
        lax.psum_scatter(grad_w_inner, "dp", scatter_dimension=0, tiled=True),
        lax.psum_scatter(grad_w_outer, "dp", scatter_dimension=1, tiled=True),
    )
    return (
        layer_out.astype(jnp.bfloat16),
        grad_inputs,
        weight_shards[0],
        small_sums[0],
        weight_shards[1],
        weight_shards[2],
        small_sums[1],
        weight_shards[3],
        small_sums[2],
        small_sums[3],
        small_sums[4],
        weight_shards[4],
        small_sums[5],
        weight_shards[5],
        small_sums[6],
        small_sums[7],
        small_sums[8],
    )


def solution(mesh):
    in_specs = (
        P("dp", None),
        P(None, "tensor"),
        P("tensor"),
        P(None, "tensor"),
        P(None, "tensor"),
        P("tensor"),
        P("tensor", None),
        P(),
        P(),
        P(),
        P(None, "tensor"),
        P("tensor"),
        P("tensor", None),
        P(),
        P(),
        P(),
        P("dp", None),
    )
    out_specs = (
        P("dp", None),
        P("dp", None),
        P("dp", "tensor"),
        P("tensor"),
        P("dp", "tensor"),
        P("dp", "tensor"),
        P("tensor"),
        P("tensor", "dp"),
        P(),
        P(),
        P(),
        P("dp", "tensor"),
        P("tensor"),
        P("tensor", "dp"),
        P(),
        P(),
        P(),
    )
    return jax.shard_map(shards, mesh=mesh, in_specs=in_specs, out_specs=out_specs, check_vma=False)
```

profile of v0, /device:TPU:0, one launch (start us, length us, event | category | flops | bytes accessed | tf_op | source)
XLA Modules:
  0.0 1302.7 jit_solution(1890085184275890445)
XLA Ops:
  8.0 3.1 fusion.59
  11.9 3.1 fusion.60
  15.7 3.1 convolution_convert_fusion.1
  22.4 13.0 while.10
  37.6 4.7 fusion.73
  45.4 222.6 %all-reduce.6.cloned.1.call-done = f32[2048,768]{1,0:T(8,128)} async-done(((f32[2048,768]{1,0:T(8,128)}), f32[2048,768]{1,0:T(8,128)}) %all-reduce.6.cloned.1.call-update) | async-done | bytes 6291472 | tf_op jit(solution)/shard_map/psum | solution.py:157
  268.0 4.6 fusion.72
  275.3 18.3 %multiply_convert_fusion.1 = (bf16[2048,768]{1,0:T(8,128)(2,1)S(1)}, f32[2048,768]{1,0:T(8,128)}, f32[2048,768]{1,0:T(8,128)}) fusion(f32[768]{0:T(1024)S(1)} %copy-done.32, bf16[2048,768]{1,0:T(8,128)(2,1)S(1)} %fusion.58, bf16[768,768]{1,0:T(8,128)(2,1)S(1)} %copy-done), kind=kOutput, calls=%fused_computation.79 | convolution fusion | flops 2519728128 | bytes 20057088 | tf_op jit(solution)/shard_map/dot_general | solution.py:164
  295.4 4.5 fusion.74
  303.9 217.9 %all-reduce.8.cloned.1.call-done = f32[2048,768]{1,0:T(8,128)} async-done(((f32[2048,768]{1,0:T(8,128)}), f32[2048,768]{1,0:T(8,128)}) %all-reduce.8.cloned.1.call-update) | async-done | bytes 6291472 | tf_op jit(solution)/shard_map/psum | solution.py:170
  521.8 5.7 fusion.70
  529.4 3.6 fusion.52
  533.0 4.5 convert_reduce_fusion.1
  537.6 9.5 convert_reduce_fusion.2
  548.7 4.5 fusion.75
  553.6 221.7 %all-reduce.10.cloned.1.call-done = f32[2048,768]{1,0:T(8,128)} async-done(((f32[2048,768]{1,0:T(8,128)}), f32[2048,768]{1,0:T(8,128)}) %all-reduce.10.cloned.1.call-update) | async-done | bytes 6291472 | tf_op jit(solution)/shard_map/psum | solution.py:184
  775.2 8.7 multiply_reduce_fusion.2
  784.0 5.2 convert_reduce_fusion.3
  796.9 25.6 %while.27 = (s32[]{:T(128)}, bf16[4,512,192]{1,2,0:T(8,128)(2,1)S(1)}, bf16[4,512,192]{1,2,0:T(8,128)(2,1)}, bf16[4,512,192]{1,2,0:T(8,128)(2,1)}, bf16[4,512,3,...) while((s32[]{:T(128)}, ...), condition=%wide.region_17.18_spmd, body=%wide.region_15.17_spmd.sunk | while | flops 513243648 | bytes 26788472 | solution.py:198
  822.7 5.3 fusion.76
  831.5 3.9 add_add_fusion
  835.7 8.0 fusion.63
  843.8 7.0 fusion.78
  854.9 3.6 convolution_bitcast_fusion.2
  865.3 25.8 %all-reduce = (f32[192]{0:T(256)}, f32[192]{0:T(256)}, f32[768]{0:T(1024)}, f32[768]{0:T(1024)}, f32[768]{0:T(1024)}, /*index=5*/f32[768]{0:T(1024)}, f32[768]{0:T(1024)}, f32[768]{0:T(1024)}, f32[768]{0:T(1024)}) all-reduce(f32[192]{0:T(256)S(1)} %convert_reduce_fusion.5, ...), channel_id=1, replica_groups=mesh['dp'=8,'tensor'=4] {'dp'}, use_global_device_ids=true, to_apply=%region_21.22 | all-reduce | flops 5760 | bytes 46080 | tf_op jit(solution)/shard_map/psum | solution.py:217
  892.8 194.5 %all-reduce.12.cloned.1.call-done = f32[2048,768]{1,0:T(8,128)} async-done(((f32[2048,768]{1,0:T(8,128)}), f32[2048,768]{1,0:T(8,128)}) %all-reduce.12.cloned.1.call-update) | async-done | bytes 6291472 | tf_op jit(solution)/shard_map/psum | solution.py:216
  1087.3 8.1 add.177
  1095.4 37.2 %reduce-scatter.17.cloned.1.call-done = f32[768,96]{0,1:T(8,128)} async-done(((f32[768,768]{0,1:T(8,128)}), f32[768,96]{0,1:T(8,128)}) %reduce-scatter.17.cloned.1.call-update) | async-done | bytes 294928 | tf_op jit(solution)/shard_map/reduce_scatter | solution.py:237
  1132.5 46.8 %reduce-scatter.15.cloned.1.call-done = f32[96,768]{1,0:T(8,128)} async-done(((f32[768,768]{1,0:T(8,128)}), f32[96,768]{1,0:T(8,128)}) %reduce-scatter.15.cloned.1.call-update) | async-done | bytes 294928 | tf_op jit(solution)/shard_map/reduce_scatter | solution.py:236
  1179.4 38.7 %reduce-scatter.19.cloned.1.call-done = f32[96,192]{1,0:T(8,128)} async-done(((f32[768,192]{1,0:T(8,128)}), f32[96,192]{1,0:T(8,128)}) %reduce-scatter.19.cloned.1.call-update) | async-done | bytes 73744
  1218.1 38.8 %reduce-scatter.21.cloned.1.call-done = f32[96,192]{1,0:T(8,128)} async-done(((f32[768,192]{1,0:T(8,128)}), f32[96,192]{1,0:T(8,128)}) %reduce-scatter.21.cloned.1.call-update) | async-done | bytes 73744
  1256.8 38.6 %reduce-scatter.23.cloned.1.call-done = f32[96,192]{1,0:T(8,128)} async-done(((f32[768,192]{1,0:T(8,128)}), f32[96,192]{1,0:T(8,128)}) %reduce-scatter.23.cloned.1.call-update) | async-done | bytes 73744
  (218 shorter events, 85.7 us)
Async XLA Ops:
  7.2 268.1 %copy-start = (bf16[768,768]{1,0:T(8,128)(2,1)S(1)}, bf16[768,768]{1,0:T(8,128)(2,1)}, u32[]{:S(2)}) copy-start(bf16[768,768]{1,0:T(8,128)(2,1)} %param.31) | copy-start | bytes 3538948
  7.2 260.8 %all-reduce.6.cloned.1.call-start = ((), (), s32[]{:S(2)}) async-start(), calls=%async_computation.6 | async-start | bytes 12582912 | tf_op jit(solution)/shard_map/psum | solution.py:157
  37.5 6.0 copy-start.36
  42.3 479.5 %all-reduce.8.cloned.1.call-start = ((), (), s32[]{:S(2)}) async-start(), calls=%async_computation.7 | async-start | bytes 12582912 | tf_op jit(solution)/shard_map/psum | solution.py:170
  275.3 18.3 %copy-start.16 = (bf16[2048,768]{1,0:T(8,128)(2,1)}, bf16[2048,768]{1,0:T(8,128)(2,1)S(1)}, u32[]{:S(2)}) copy-start(bf16[2048,768]{1,0:T(8,128)(2,1)S(1)} %fusion.58) | copy-start | bytes 9437188
  275.3 20.1 %copy-start.37 = (bf16[768,768]{1,0:T(8,128)(2,1)S(1)}, bf16[768,768]{1,0:T(8,128)(2,1)}, u32[]{:S(2)}) copy-start(bf16[768,768]{1,0:T(8,128)(2,1)} %param.33) | copy-start | bytes 3538948
  299.8 475.4 %all-reduce.10.cloned.1.call-start = ((), (), s32[]{:S(2)}) async-start(), calls=%async_computation.8 | async-start | bytes 12582912 | tf_op jit(solution)/shard_map/psum | solution.py:184
  529.4 8.1 slice-start.2
  537.5 9.5 copy-start.4
  553.3 222.0 %copy-start.21 = (f32[768]{0:T(1024)S(1)}, f32[768]{0:T(1024)}, u32[]{:S(2)}) copy-start(f32[768]{0:T(1024)} %convert_element_type.125) | copy-start | bytes 9220
  553.3 337.8 %reduce-scatter.25.cloned.1.call-start = ((), (), s32[]{:S(2)}) async-start(), calls=%async_computation.15 | async-start | bytes 884736
  822.5 5.5 copy-start.10
  822.6 5.4 copy-start.15
  822.7 5.5 copy-start.18
  828.1 259.2 %all-reduce.12.cloned.1.call-start = ((), (), s32[]{:S(2)}) async-start(), calls=%async_computation.9 | async-start | bytes 12582912 | tf_op jit(solution)/shard_map/psum | solution.py:216
  835.4 297.1 %reduce-scatter.17.cloned.1.call-start = ((), (), s32[]{:S(2)}) async-start(), calls=%async_computation.11 | async-start | bytes 2654208 | tf_op jit(solution)/shard_map/reduce_scatter | solution.py:237
  843.7 7.1 copy-start.7
  843.8 335.6 %reduce-scatter.15.cloned.1.call-start = ((), (), s32[]{:S(2)}) async-start(), calls=%async_computation.10 | async-start | bytes 2654208 | tf_op jit(solution)/shard_map/reduce_scatter | solution.py:236
  850.8 10.1 copy-start.9
  850.8 367.3 %reduce-scatter.19.cloned.1.call-start = ((), (), s32[]{:S(2)}) async-start(), calls=%async_computation.12 | async-start | bytes 884736
  854.9 10.0 copy-start.13
  854.9 10.2 copy-start.11
  854.9 401.9 %reduce-scatter.21.cloned.1.call-start = ((), (), s32[]{:S(2)}) async-start(), calls=%async_computation.13 | async-start | bytes 884736
  858.5 6.7 copy-start.24
  858.5 6.7 copy-start.25
  858.5 6.7 copy-start.26
  858.5 6.7 copy-start.27
  858.6 6.7 copy-start.28
  858.6 6.7 copy-start.29
  858.6 6.7 copy-start.31
  860.9 434.5 %reduce-scatter.23.cloned.1.call-start = ((), (), s32[]{:S(2)}) async-start(), calls=%async_computation.14 | async-start | bytes 884736
  891.1 404.3 %copy-start.1 = (bf16[768,768]{1,0:T(8,128)(2,1)S(1)}, bf16[768,768]{1,0:T(8,128)(2,1)}, u32[]{:S(2)}) copy-start(bf16[768,768]{1,0:T(8,128)(2,1)} %param.31) | copy-start | bytes 3538948
  (24 other events, 71.1 us)
Sparse Core Ops, SparseCore 0:
  42.4 225.5 all-reduce.5
  300.0 221.7 all-reduce.7
  553.4 221.7 all-reduce.9
  828.2 33.9 reduce-scatter.24
  864.4 222.8 all-reduce.11
  1091.0 41.4 reduce-scatter.16
  1136.8 42.4 reduce-scatter.14
  1183.1 34.9 reduce-scatter.18
  1221.8 34.9 reduce-scatter.20
  1260.4 34.9 reduce-scatter.22
where the time goes:
time: 1310 us; the launch traced here: 1300 us
  waiting for transfers between devices  1060 us (81%)
  matrix products  110 us (8%)
  other arithmetic  58.7 us (4%)
  local copies, waits for them, and re-layouts  34.2 us (3%)
  blocking collectives  25.8 us (2%)
  between operations  15.3 us (1%)
    psum x1, waiting for transfers between devices, shards(): attn_total = lax.psum(attn_part, 'tensor') + b_output.astype(jnp.float32)  223 us
    psum x1, waiting for transfers between devices, shards(): lax.psum(times_transpose(grad_inner, w_inner), 'tensor')  222 us
    psum x1, waiting for transfers between devices, shards(): outer_total = lax.psum(outer_part, 'tensor') + b_outer.astype(jnp.float32)  218 us
    psum x1, waiting for transfers between devices, shards(): grad_inputs = grad_resid1 + lax.psum(input_part, 'tensor')  194 us
    unnamed x14, waiting for transfers between devices  116 us
    reduce_scatter x1, waiting for transfers between devices, shards(): lax.psum_scatter(grad_w_inner, 'dp', scatter_dimension=0, tiled=True)  46.8 us
    reduce_scatter x1, waiting for transfers between devices, shards(): lax.psum_scatter(grad_w_outer, 'dp', scatter_dimension=1, tiled=True)  37.2 us
  transfers between devices with their start and end apart: 10, of which 9 were waited for; matrix products, arithmetic and copies ran while one was open for 4% of the time, Pallas kernels for 0%

commit v1 on v0

v1 whole, which is shorter than its diff:
```python
from functools import partial

import jax
import jax.numpy as jnp
from jax import lax
from jax.experimental import pallas as pl
from jax.experimental.pallas import tpu as pltpu
from jax.sharding import PartitionSpec as P

HEAD_DIM = 64
LENGTH = 512
EPSILON = 1e-12
F32 = jnp.float32
BF16 = jnp.bfloat16
LOG2E = 1.4426950408889634
SCALE = HEAD_DIM ** (-0.5)
fence = lax.optimization_barrier


def dot(left, right, dims):
    return lax.dot_general(left, right, (dims, ((), ())), preferred_element_type=F32)


ROWS = ((0,), (0,))
PLAIN = ((1,), (0,))
COLS = ((1,), (1,))


def norm_forward(values, gain, shift):
    center = values - jnp.mean(values, axis=-1, keepdims=True)
    inverse = lax.rsqrt(jnp.mean(center * center, axis=-1, keepdims=True) + EPSILON)
    normed = center * inverse
    return (normed * gain + shift, normed, inverse)


def norm_backward(upstream, gain, normed, inverse):
    scaled = upstream * gain
    first_mean = jnp.mean(scaled, axis=-1, keepdims=True)
    cross_mean = jnp.mean(scaled * normed, axis=-1, keepdims=True)
    grad_values = inverse * (scaled - first_mean - normed * cross_mean)
    return (grad_values, jnp.sum(upstream * normed, axis=0), jnp.sum(upstream, axis=0))


def attend_kernel(x_ref, wq_ref, wk_ref, wv_ref, bq_ref, bv_ref, out_ref):
    x = x_ref[...]
    q = (dot(x, wq_ref[...], PLAIN) + bq_ref[...]).astype(BF16)
    k = dot(x, wk_ref[...], PLAIN).astype(BF16)
    v = (dot(x, wv_ref[...], PLAIN) + bv_ref[...]).astype(BF16)
    for h in range(q.shape[1] // HEAD_DIM):
        cols = slice(h * HEAD_DIM, (h + 1) * HEAD_DIM)
        scores = dot(q[:, cols], k[:, cols], COLS)
        largest = jnp.max(scores, axis=-1, keepdims=True)
        expon = jnp.exp2((scores - largest) * (SCALE * LOG2E))
        totals = jnp.sum(expon, axis=-1, keepdims=True)
        context = dot(expon.astype(BF16), v[:, cols], PLAIN) / totals
        out_ref[:, cols] = context.astype(BF16).astype(F32)


def attend_forward(inputs, wq, bq, wk, wv, bv):
    rows, width = inputs.shape
    cols = wq.shape[1]
    whole = lambda a: pl.BlockSpec(a.shape, lambda i: (0, 0))
    args = (wq, wk, wv, bq, bv)
    flops = rows * (6 * width * cols + 4 * LENGTH * cols)
    return pl.pallas_call(
        attend_kernel,
        grid=(rows // LENGTH,),
        in_specs=[pl.BlockSpec((LENGTH, width), lambda i: (i, 0))] + [whole(a) for a in args],
        out_specs=pl.BlockSpec((LENGTH, cols), lambda i: (i, 0)),
        out_shape=jax.ShapeDtypeStruct((rows, cols), F32),
        cost_estimate=pl.CostEstimate(
            flops=flops, bytes_accessed=rows * (2 * width + 4 * cols), transcendentals=rows * LENGTH * 3
        ),
        compiler_params=pltpu.CompilerParams(vmem_limit_bytes=48 << 20),
        name="attend_forward",
    )(inputs, *args)


def attend_back_kernel(q_ref, k_ref, v_ref, g_ref, gq_ref, gk_ref, gv_ref):
    for h in range(q_ref.shape[1] // HEAD_DIM):
        cols = slice(h * HEAD_DIM, (h + 1) * HEAD_DIM)
        q, k, v, g = q_ref[:, cols], k_ref[:, cols], v_ref[:, cols], g_ref[:, cols]
        scores = dot(k, q, COLS)
        largest = jnp.max(scores, axis=0, keepdims=True)
        expon = jnp.exp2((scores - largest) * (SCALE * LOG2E))
        probs = expon * (1.0 / jnp.sum(expon, axis=0, keepdims=True))
        gv_ref[:, cols] = dot(probs.astype(BF16), g, PLAIN).astype(BF16)
        weighted = probs * dot(v, g, COLS)
        terms = jnp.sum(weighted, axis=0, keepdims=True)
        grad_scores = (weighted - probs * terms).astype(BF16)
        gq_ref[:, cols] = (dot(grad_scores, k, ROWS) * SCALE).astype(BF16)
        gk_ref[:, cols] = (dot(grad_scores, q, PLAIN) * SCALE).astype(BF16)


def attend_backward(q, k, v, g):
    rows, width = q.shape
    spec = pl.BlockSpec((LENGTH, 2 * HEAD_DIM), lambda i, j: (i, j))
    return pl.pallas_call(
        attend_back_kernel,
        grid=(rows // LENGTH, width // (2 * HEAD_DIM)),
        in_specs=[spec] * 4,
        out_specs=[spec] * 3,
        out_shape=[jax.ShapeDtypeStruct((rows, width), BF16)] * 3,
        cost_estimate=pl.CostEstimate(
            flops=rows * 10 * LENGTH * width,
            bytes_accessed=rows * width * 14,
            transcendentals=rows * LENGTH * (width // HEAD_DIM),
        ),
        compiler_params=pltpu.CompilerParams(vmem_limit_bytes=48 << 20),
        name="attend_backward",
    )(q, k, v, g)


def narrow_kernel(x_ref, out_ref):
    out_ref[...] = x_ref[...].reshape(out_ref.shape).astype(BF16)


def narrow(values, block_rows):
    rows, width = values.shape
    spec = pl.BlockSpec((block_rows, width), lambda i: (i, 0))
    return pl.pallas_call(
        narrow_kernel,
        grid=(rows // block_rows,),
        in_specs=[spec],
        out_specs=spec,
        out_shape=jax.ShapeDtypeStruct((rows, width), BF16),
        cost_estimate=pl.CostEstimate(flops=0, bytes_accessed=6 * rows * width, transcendentals=0),
        name="narrow",
    )(values)


def narrow_pieces(pieces):
    dp, tensor, share, width = pieces.shape
    if share % 8:
        whole = pieces.swapaxes(0, 1).reshape(tensor * dp * share, width)
        return narrow(whole, dp * share).reshape(tensor, dp * share, width)
    return pl.pallas_call(
        narrow_kernel,
        grid=(tensor,),
        in_specs=[pl.BlockSpec((dp, None, share, width), lambda i: (0, i, 0, 0))],
        out_specs=pl.BlockSpec((None, dp * share, width), lambda i: (i, 0, 0)),
        out_shape=jax.ShapeDtypeStruct((tensor, dp * share, width), BF16),
        cost_estimate=pl.CostEstimate(flops=0, bytes_accessed=6 * pieces.size, transcendentals=0),
        name="narrow_pieces",
    )(pieces)


def beside_kernel(x_ref, out_ref):
    out_ref[...] = jnp.concatenate([x_ref[i] for i in range(x_ref.shape[0])], axis=1).astype(BF16)


def narrow_beside(values):
    tensor, rows, cols = values.shape
    return pl.pallas_call(
        beside_kernel,
        out_shape=jax.ShapeDtypeStruct((rows, tensor * cols), BF16),
        cost_estimate=pl.CostEstimate(flops=0, bytes_accessed=6 * values.size, transcendentals=0),
        name="narrow_beside",
    )(values)


def gather_weight(local, dp, tensor):
    rows, width = local.shape
    share = rows // dp
    piece = lax.dynamic_slice_in_dim(local, lax.axis_index("dp") * share, share, 0).astype(F32)
    full = lax.all_gather(piece, ("dp", "tensor"), axis=0)
    return narrow_pieces(full.reshape(dp, tensor, share, width))


def scatter_grad(grad, tensor):
    part = lax.psum_scatter(grad, "dp", scatter_dimension=0, tiled=True)
    part = part.reshape(part.shape[0], tensor, -1).swapaxes(0, 1)
    return lax.psum_scatter(part, "tensor", scatter_dimension=0, tiled=False)


def shards(
    dp,
    tensor,
    inputs,
    w_query,
    b_query,
    w_key,
    w_value,
    b_value,
    w_output,
    b_output,
    gain_attn,
    shift_attn,
    w_inner,
    b_inner,
    w_outer,
    b_outer,
    gain_ffn,
    shift_ffn,
    cotangent,
):
    tok_rows, width = inputs.shape
    own_rows = tok_rows // tensor
    heads_cols = w_query.shape[1]
    ff_cols = w_inner.shape[1]
    z = lax.axis_index("tensor")
    own = lambda a: lax.dynamic_slice_in_dim(a, z * own_rows, own_rows, 0)
    row = lambda a: a.astype(F32)[None, :]

    lens = (heads_cols, heads_cols, ff_cols)
    vectors = jnp.concatenate([b_query, b_value, b_inner]).astype(F32)
    vectors = lax.all_gather(vectors, "tensor", axis=0)
    bq_full = vectors[:, :heads_cols].reshape(1, -1)
    bv_full = vectors[:, heads_cols : 2 * heads_cols].reshape(1, -1)
    bi_full = vectors[:, 2 * heads_cols :].reshape(1, -1)

    wo_full = gather_weight(w_output, dp, tensor).reshape(-1, width)
    wi_full = gather_weight(w_inner, dp, tensor)
    wu_full = gather_weight(w_outer, dp, tensor)
    qkv_local = jnp.concatenate([w_query.T, w_key.T, w_value.T], axis=0)
    qkv_full = gather_weight(qkv_local, dp, tensor).reshape(tensor, 3, heads_cols, width)
    wq_t, wk_t, wv_t = (qkv_full[:, i].reshape(-1, width) for i in range(3))

    context = attend_forward(inputs, w_query, row(b_query), w_key, w_value, row(b_value))
    context = context.reshape(tensor, own_rows, heads_cols)
    context = narrow_beside(lax.all_to_all(context, "tensor", 0, 0, tiled=True))


    x = own(inputs)
    gain_one, gain_two = row(gain_attn), row(gain_ffn)
    attn = dot(context, wo_full, PLAIN) + row(b_output)
    hidden, normed_attn, inverse_attn = norm_forward(x.astype(F32) + attn, gain_one, row(shift_attn))
    hidden_bf = hidden.astype(BF16)
    inner = jnp.concatenate([dot(hidden_bf, wi_full[i], PLAIN) for i in range(tensor)], axis=1) + bi_full
    active, gelu_pull = jax.vjp(partial(jax.nn.gelu, approximate=False), inner)
    active_bf = active.astype(BF16)
    outer = dot(active_bf, wu_full.reshape(-1, width), PLAIN) + row(b_outer)
    layer_out, normed_ffn, inverse_ffn = norm_forward(hidden + outer, gain_two, row(shift_ffn))
    layer_out = narrow(lax.all_gather(layer_out, "tensor", axis=0, tiled=True), own_rows)

    upstream = own(cotangent).astype(F32)
    grad_resid2, grad_gain_ffn, grad_shift_ffn = norm_backward(upstream, gain_two, normed_ffn, inverse_ffn)
    grad_outer = grad_resid2.astype(BF16)
    grad_b_outer = jnp.sum(grad_outer.astype(F32), axis=0)
    grad_active = dot(grad_outer, wu_full.reshape(-1, width), COLS)
    grad_inner = gelu_pull(grad_active)[0].astype(BF16)
    grad_b_inner = jnp.sum(grad_inner.astype(F32), axis=0)
    gu = scatter_grad(dot(grad_outer, active_bf, ROWS), tensor)
    gi = scatter_grad(dot(hidden_bf, grad_inner, ROWS), tensor)
    back = sum(dot(grad_inner[:, i * ff_cols : (i + 1) * ff_cols], wi_full[i], COLS) for i in range(tensor))
    grad_hidden = grad_resid2 + back
    grad_resid1, grad_gain_attn, grad_shift_attn = norm_backward(
        grad_hidden, gain_one, normed_attn, inverse_attn
    )
    grad_attn = grad_resid1.astype(BF16)
    grad_b_output = jnp.sum(grad_attn.astype(F32), axis=0)
    go = scatter_grad(dot(grad_attn, context, ROWS), tensor)
    grad_context = dot(grad_attn, wo_full, COLS).astype(BF16)

    queries = (dot(x, wq_t, COLS) + bq_full).astype(BF16)
    key_rows = dot(x, wk_t, COLS).astype(BF16)
    value_rows = (dot(x, wv_t, COLS) + bv_full).astype(BF16)
    grad_q, grad_k, grad_v = attend_backward(queries, key_rows, value_rows, grad_context)
    grad_x = grad_resid1 + dot(grad_q, wq_t, PLAIN) + dot(grad_k, wk_t, PLAIN) + dot(grad_v, wv_t, PLAIN)
    grad_inputs = lax.all_gather(grad_x, "tensor", axis=0, tiled=True)
    gq, gk, gv = (scatter_grad(dot(x, g, ROWS), tensor) for g in (grad_q, grad_k, grad_v))
    sums = lax.psum(
        jnp.concatenate(
            [
                jnp.sum(grad_q.astype(F32), axis=0),
                jnp.sum(grad_v.astype(F32), axis=0),
                grad_b_inner,
                grad_b_output,
                grad_gain_attn,
                grad_shift_attn,
                grad_b_outer,
                grad_gain_ffn,
                grad_shift_ffn,
            ]
        ),
        ("dp", "tensor"),
    )
    mine = lambda a, n: lax.dynamic_slice_in_dim(a, z * n, n, 0)
    edges = [0, width, 2 * width, 2 * width + ff_cols * tensor]
    s_bq, s_bv, s_bi = (sums[edges[i] : edges[i + 1]] for i in range(3))
    rest = sums[edges[3] :].reshape(6, width)
    return (
        layer_out,
        grad_inputs,
        gq,
        mine(s_bq, heads_cols),
        gk,
        gv,
        mine(s_bv, heads_cols),
        go.T,
        rest[0],
        rest[1],
        rest[2],
        gi,
        mine(s_bi, ff_cols),
        gu.T,
        rest[3],
        rest[4],
        rest[5],
    )


def solution(mesh):
    wide, tall, vector = P(None, "tensor"), P("tensor", None), P("tensor")
    tokens, both = P("dp", None), P("dp", "tensor")
    in_specs = (
        tokens, wide, vector, wide, wide, vector, tall, P(), P(), P(), wide, vector, tall, P(), P(), P(), tokens,
    )
    out_specs = (
        tokens, tokens, both, vector, both, both, vector, P("tensor", "dp"), P(), P(), P(), both, vector,
        P("tensor", "dp"), P(), P(), P(),
    )
    body = partial(shards, mesh.shape["dp"], mesh.shape["tensor"])
    return jax.shard_map(body, mesh=mesh, in_specs=in_specs, out_specs=out_specs, check_vma=False)
```

time: 1310 us -> 1070 us (0.82)
  waiting for transfers between devices: 1060 us -> 774 us
  blocking collectives: 25.8 us -> 92.2 us
  Pallas kernels: 0 us -> 54.8 us
  matrix products: 110 us -> 63.3 us
  other arithmetic: 58.7 us -> 25.1 us
    psum x4 -> x0, waiting for transfers between devices: 857 us -> none  [the longest x1 223 us: shards(): attn_total = lax.psum(attn_part, 'tensor') + b_output.astype(jnp.float32)]
    all_gather x0 -> x6, waiting for transfers between devices: none -> 354 us  [the longest x4 179 us: gather_weight(): full = lax.all_gather(piece, ('dp', 'tensor'), axis=0)]
    reduce_scatter x2 -> x12, waiting for transfers between devices: 84 us -> 419 us  [the longest x6 271 us: scatter_grad(): part = lax.psum_scatter(grad, 'dp', scatter_dimension=0, tiled=True)]
    unnamed x14 -> x18, waiting for transfers between devices: 116 us -> 0.96 us
    pallas_call x0 -> x8, Pallas kernels: none -> 54.8 us  [the longest x4 21.4 us: narrow_pieces(): pl.pallas_call(narrow_kernel, grid=(tensor,), in_specs=[pl.BlockSpec((dp,...]
    all_gather x0 -> x1, blocking collectives: none -> 44.4 us  [shards(): vectors = lax.all_gather(vectors, 'tensor', axis=0)]
    dot_general x45 -> x24, matrix products: 108 us -> 63.3 us  [dot(): lax.dot_general(left, right, (dims, ((), ())), preferred_element_type=F32)]
    psum x1, blocking collectives: 25.8 us -> 47.8 us  [shards(): lax.psum(jnp.concatenate([jnp.sum(grad_q.astype(F32), axis=0), jnp.sum(gr...]
  transfers between devices with their start and end apart: 10 -> 19, of which waited for: 9 -> 17; matrix products, arithmetic and copies ran while one was open for 4% -> 10% of each run, Pallas kernels for 0% -> 5%
where the time goes in v1:
time: 1070 us
  waiting for transfers between devices  774 us (72%)
  blocking collectives  92.2 us (9%)
  matrix products  63.3 us (6%)
  Pallas kernels  54.8 us (5%)
  local copies, waits for them, and re-layouts  32.8 us (3%)
  other arithmetic  25.1 us (2%)
  between operations  15.4 us (1%)
    reduce_scatter x6, waiting for transfers between devices, scatter_grad(): part = lax.psum_scatter(grad, 'dp', scatter_dimension=0, tiled=True)  271 us
    all_gather x4, waiting for transfers between devices, gather_weight(): full = lax.all_gather(piece, ('dp', 'tensor'), axis=0)  179 us
    reduce_scatter x6, waiting for transfers between devices, scatter_grad(): return lax.psum_scatter(part, 'tensor', scatter_dimension=0, tiled=False)  148 us
    all_gather x1, waiting for transfers between devices, shards(): grad_inputs = lax.all_gather(grad_x, 'tensor', axis=0, tiled=True)  110 us
    all_gather x1, waiting for transfers between devices, shards(): lax.all_gather(layer_out, 'tensor', axis=0, tiled=True)  64.8 us
    dot_general x24, matrix products, dot(): lax.dot_general(left, right, (dims, ((), ())), preferred_element_type=F32)  63.3 us
    psum x1, blocking collectives, shards(): lax.psum(jnp.concatenate([jnp.sum(grad_q.astype(F32), axis=0), jnp.sum(gr...  47.8 us
    all_gather x1, blocking collectives, shards(): vectors = lax.all_gather(vectors, 'tensor', axis=0)  44.4 us
  transfers between devices with their start and end apart: 19, of which 17 were waited for; matrix products, arithmetic and copies ran while one was open for 10% of the time, Pallas kernels for 5%

profile of v1, /device:TPU:0, one launch (start us, length us, event | category | flops | bytes accessed | tf_op | source)
XLA Modules:
  0.0 1065.0 jit_solution(14183911299415834458)
XLA Ops:
  13.8 10.7 %attend_forward.1 = f32[2048,192]{1,0:T(8,128)S(1)} custom-call(bf16[2048,768]{1,0:T(8,128)(2,1)} %x_ref.1, bf16[768,192]{1,0:T(8,128)(2,1)S(1)} %copy.43.wq_ref, bf16[768,192]{1,0:T(8,128)(2,1)S(1)} %copy.44.wk_ref, bf16[768,192]{1,0:T(8,128)(2,1)S(1)} %copy.45.wv_ref, f32[1,192]{1,0:T(1,128)S(1)} %get-tuple-element.59.bq_ref, ...), custom_call_target="tpu_custom_call" | custom-call | flops 2617245696 | bytes 4718592 | tf_op jit(solution)/shard_map/attend_forward/pallas_call | solution.py:65
  26.2 6.5 all-to-all-start
  33.9 44.4 %all-gather.4 = f32[4,1,1152]{2,1,0:T(1,128)S(1)} all-gather(f32[1,1,1152]{2,1,0:T(1,128)S(1)} %bitcast_convert_fusion), channel_id=1, replica_groups=mesh['dp'=8,'tensor'=4] {'tensor'}, dimensions={0}, use_global_device_ids=true | all-gather | bytes 23040 | tf_op jit(solution)/shard_map/all_gather | solution.py:207
  85.8 3.7 narrow_pieces.4
  92.5 77.6 %all-gather.18.cloned.1.call-done = f32[3072,768]{1,0:T(8,128)} async-done(((f32[96,768]{1,0:T(8,128)}), f32[3072,768]{1,0:T(8,128)}) %all-gather.18.cloned.1.call-update) | async-done | bytes 9437200 | tf_op jit(solution)/shard_map/all_gather | solution.py:166
  170.0 6.2 narrow_pieces.5
  176.2 77.9 %all-gather.20.cloned.1.call-done = f32[3072,768]{1,0:T(8,128)} async-done(((f32[96,768]{1,0:T(8,128)}), f32[3072,768]{1,0:T(8,128)}) %all-gather.20.cloned.1.call-update) | async-done | bytes 9437200 | tf_op jit(solution)/shard_map/all_gather | solution.py:166
  254.1 6.2 narrow_pieces.6
  266.8 14.6 %multiply_convert_fusion = (bf16[512,3072]{1,0:T(8,128)(2,1)S(1)}, f32[512,3072]{1,0:T(8,128)}) fusion(f32[3072]{0:T(1024)S(1)} %add.161, f32[512,768]{1,0:T(8,128)S(1)} %fusion.20, f32[512,768]{1,0:T(8,128)S(1)} %fusion.19, f32[512,768]{1,0:T(8,128)S(1)} %fusion.17, f32[512,768]{1,0:T(8,128)S(1)} %fusion.15), kind=kLoop, calls=%fused_computation.5 | loop fusion | flops 108527616 | bytes 15740928 | tf_op jit(solution)/shard_map/convert_element_type | solution.py:231
  287.2 10.6 convert_reduce_fusion
  307.4 20.7 %all-gather.22.cloned.1.call-done = f32[2304,768]{1,0:T(8,128)} async-done(((f32[72,768]{1,0:T(8,128)}), f32[2304,768]{1,0:T(8,128)}) %all-gather.22.cloned.1.call-update) | async-done | bytes 7077904 | tf_op jit(solution)/shard_map/all_gather | solution.py:166
  328.0 5.5 narrow_pieces.7
  340.5 15.0 %attend_backward.1 = (bf16[512,768]{1,0:T(8,128)(2,1)S(1)}, bf16[512,768]{1,0:T(8,128)(2,1)S(1)}, bf16[512,768]{1,0:T(8,128)(2,1)S(1)}) custom-call(bf16[512,768]{1,0:T(8,128)(2,1)S(1)} %add_convert_fusion.2.q_ref, bf16[512,768]{1,0:T(8,128)(2,1)S(1)} %convolution_convert_fusion.1.k_ref, bf16[512,768]{1,0:T(8,128)(2,1)S(1)} %add_convert_fusion.1.v_ref, ...), custom_call_target="tpu_custom_call" | custom-call | flops 2013265920 | bytes 5505024 | tf_op jit(solution)/shard_map/attend_backward/pallas_call | solution.py:98
  361.2 3.4 fusion.27
  364.7 8.9 fusion.46
  374.7 7.0 fusion.61
  390.9 27.4 %reduce-scatter.21.cloned.1.call-done = f32[96,768]{1,0:T(8,128)} async-done(((f32[768,768]{1,0:T(8,128)}), f32[96,768]{1,0:T(8,128)}) %reduce-scatter.21.cloned.1.call-update) | async-done | bytes 294928 | tf_op jit(solution)/shard_map/reduce_scatter | solution.py:171
  420.5 44.3 %reduce-scatter.13.cloned.1.call-done = f32[96,768]{1,0:T(8,128)} async-done(((f32[768,768]{1,0:T(8,128)}), f32[96,768]{1,0:T(8,128)}) %reduce-scatter.13.cloned.1.call-update) | async-done | bytes 294928 | tf_op jit(solution)/shard_map/reduce_scatter | solution.py:171
  467.0 44.0 %reduce-scatter.17.cloned.1.call-done = f32[96,768]{1,0:T(8,128)} async-done(((f32[768,768]{1,0:T(8,128)}), f32[96,768]{1,0:T(8,128)}) %reduce-scatter.17.cloned.1.call-update) | async-done | bytes 294928 | tf_op jit(solution)/shard_map/reduce_scatter | solution.py:171
  513.2 77.9 %reduce-scatter.33.cloned.1.call-done = f32[96,3072]{1,0:T(8,128)} async-done(((f32[768,3072]{1,0:T(8,128)}), f32[96,3072]{1,0:T(8,128)}) %reduce-scatter.33.cloned.1.call-update) | async-done | bytes 1179664 | tf_op jit(solution)/shard_map/reduce_scatter | solution.py:171
  593.5 77.4 %reduce-scatter.29.cloned.1.call-done = f32[96,3072]{1,0:T(8,128)} async-done(((f32[768,3072]{1,0:T(8,128)}), f32[96,3072]{1,0:T(8,128)}) %reduce-scatter.29.cloned.1.call-update) | async-done | bytes 1179664 | tf_op jit(solution)/shard_map/reduce_scatter | solution.py:171
  673.8 47.8 %psum.7 = f32[9216]{0:T(1024)S(1)} all-reduce(f32[9216]{0:T(1024)S(1)} %constant_dynamic-update-slice_fusion), channel_id=1, replica_groups=mesh['dp'=8,'tensor'=4] {'dp','tensor'}, use_global_device_ids=true, to_apply=%region_19.0 | all-reduce | flops 9216 | bytes 73728 | tf_op jit(solution)/shard_map/psum | solution.py:262
  724.2 64.8 %all-gather.12.cloned.1.call-done.x_ref = f32[2048,768]{1,0:T(8,128)} async-done(((f32[512,768]{1,0:T(8,128)}), f32[2048,768]{1,0:T(8,128)}) %all-gather.12.cloned.1.call-update) | async-done | bytes 6291472 | tf_op jit(solution)/shard_map/all_gather | solution.py:234
  788.9 5.0 narrow.1
  793.9 110.0 %all-gather.14.cloned.1.call-done = f32[2048,768]{1,0:T(8,128)} async-done(((f32[512,768]{1,0:T(8,128)}), f32[2048,768]{1,0:T(8,128)}) %all-gather.14.cloned.1.call-update) | async-done | bytes 6291472 | tf_op jit(solution)/shard_map/all_gather | solution.py:260
  903.9 21.7 %reduce-scatter.27.cloned.1.call-done = f32[1,96,192]{1,2,0:T(8,128)} async-done(((f32[4,96,192]{1,2,0:T(8,128)}), f32[1,96,192]{1,2,0:T(8,128)}) %reduce-scatter.27.cloned.1.call-update) | async-done | bytes 73744 | tf_op jit(solution)/shard_map/reduce_scatter | solution.py:173
  925.6 21.7 %reduce-scatter.23.cloned.1.call-done = f32[1,96,192]{2,1,0:T(8,128)} async-done(((f32[4,96,192]{2,1,0:T(8,128)}), f32[1,96,192]{2,1,0:T(8,128)}) %reduce-scatter.23.cloned.1.call-update) | async-done | bytes 73744 | tf_op jit(solution)/shard_map/reduce_scatter | solution.py:173
  947.3 21.6 %reduce-scatter.15.cloned.1.call-done = f32[1,96,192]{2,1,0:T(8,128)} async-done(((f32[4,96,192]{2,1,0:T(8,128)}), f32[1,96,192]{2,1,0:T(8,128)}) %reduce-scatter.15.cloned.1.call-update) | async-done | bytes 73744 | tf_op jit(solution)/shard_map/reduce_scatter | solution.py:173
  968.8 21.7 %reduce-scatter.19.cloned.1.call-done = f32[1,96,192]{2,1,0:T(8,128)} async-done(((f32[4,96,192]{2,1,0:T(8,128)}), f32[1,96,192]{2,1,0:T(8,128)}) %reduce-scatter.19.cloned.1.call-update) | async-done | bytes 73744 | tf_op jit(solution)/shard_map/reduce_scatter | solution.py:173
  990.5 30.2 %reduce-scatter.35.cloned.1.call-done = f32[1,96,768]{2,1,0:T(8,128)} async-done(((f32[4,96,768]{2,1,0:T(8,128)}), f32[1,96,768]{2,1,0:T(8,128)}) %reduce-scatter.35.cloned.1.call-update) | async-done | bytes 294928 | tf_op jit(solution)/shard_map/reduce_scatter | solution.py:173
  1020.8 31.2 %reduce-scatter.31.cloned.1.call-done = f32[1,96,768]{2,1,0:T(8,128)} async-done(((f32[4,96,768]{2,1,0:T(8,128)}), f32[1,96,768]{2,1,0:T(8,128)}) %reduce-scatter.31.cloned.1.call-update) | async-done | bytes 294928 | tf_op jit(solution)/shard_map/reduce_scatter | solution.py:173
  1052.0 5.9 copy.80
  (213 shorter events, 78.5 us)
Async XLA Ops:
  7.2 78.5 %all-gather.16.cloned.1.call-start = ((), (), s32[]{:S(2)}) async-start(), calls=%async_computation.27 | async-start | bytes 2433024 | tf_op jit(solution)/shard_map/all_gather | solution.py:166
  8.8 161.3 %all-gather.18.cloned.1.call-start = ((), (), s32[]{:S(2)}) async-start(), calls=%async_computation.28 | async-start | bytes 9732096 | tf_op jit(solution)/shard_map/all_gather | solution.py:166
  10.5 243.6 %all-gather.20.cloned.1.call-start = ((), (), s32[]{:S(2)}) async-start(), calls=%async_computation.29 | async-start | bytes 9732096 | tf_op jit(solution)/shard_map/all_gather | solution.py:166
  26.2 7.5 copy-start.31
  26.2 7.5 copy-start.32
  26.2 7.5 copy-start.33
  26.2 7.5 copy-start.34
  26.2 7.5 copy-start.35
  26.2 7.5 copy-start.36
  26.2 52.1 %all-to-all-start = ((f32[4,512,192]{1,2,0:T(8,128)}), f32[4,512,192]{1,2,0:T(8,128)S(1)}, u32[]{:S(2)}, u32[]{:S(2)}) async-start(f32[4,512,192]{1,2,0:T(8,128)} %copy.46), calls=%async_computation | async-start | bytes 3145728 | tf_op jit(solution)/shard_map/all_to_all | solution.py:221
  32.7 295.3 %all-gather.22.cloned.1.call-start = ((), (), s32[]{:S(2)}) async-start(), calls=%async_computation.30 | async-start | bytes 7299072 | tf_op jit(solution)/shard_map/all_gather | solution.py:166
  33.6 355.4 %reduce-scatter.25.cloned.1.call-start = ((), (), s32[]{:S(2)}) async-start(), calls=%async_computation.21 | async-start | bytes 2654208 | tf_op jit(solution)/shard_map/reduce_scatter | solution.py:171
  92.4 173.5 %copy-start.8 = (bf16[512,768]{1,0:T(8,128)(2,1)}, bf16[512,768]{1,0:T(8,128)(2,1)S(1)}, u32[]{:S(2)}) copy-start(bf16[512,768]{1,0:T(8,128)(2,1)S(1)} %fusion.13) | copy-start | bytes 2359300
  265.9 15.4 %copy-start.16 = (f32[512,768]{1,0:T(8,128)}, f32[512,768]{1,0:T(8,128)S(1)}, u32[]{:S(2)}) copy-start(f32[512,768]{1,0:T(8,128)S(1)} %fusion.17) | copy-start | bytes 4718596
  265.9 15.4 %slice-start = ((s8[4718592]{0:T(1024)(128)(4,1)}), s8[4194304]{0:T(1024)(128)(4,1)S(1)}, s32[]{:S(2)}) async-start(s8[4718592]{0:T(1024)(128)(4,1)} %bitcast.106), calls=%async_computation.31 | async-start | bytes 8388608
  266.8 14.6 %copy-start.17 = (f32[512,768]{1,0:T(8,128)}, f32[512,768]{1,0:T(8,128)S(1)}, u32[]{:S(2)}) copy-start(f32[512,768]{1,0:T(8,128)S(1)} %fusion.15) | copy-start | bytes 4718596
  266.8 14.6 %slice-start.1 = ((s8[4718592]{0:T(1024)(128)(4,1)}), s8[524288]{0:T(1024)(128)(4,1)S(1)}, s32[]{:S(2)}) async-start(s8[4718592]{0:T(1024)(128)(4,1)} %bitcast.106), calls=%async_computation.32 | async-start | bytes 1048576
  287.1 14.4 %copy-start = (f32[512,768]{1,0:T(8,128)}, f32[512,768]{1,0:T(8,128)S(1)}, u32[]{:S(2)}) copy-start(f32[512,768]{1,0:T(8,128)S(1)} %get-tuple-element.32) | copy-start | bytes 4718596
  304.8 34.3 %copy-start.1 = (f32[512,768]{1,0:T(8,128)}, f32[512,768]{1,0:T(8,128)S(1)}, u32[]{:S(2)}) copy-start(f32[512,768]{1,0:T(8,128)S(1)} %get-tuple-element.34) | copy-start | bytes 4718596
  307.1 111.3 %reduce-scatter.21.cloned.1.call-start = ((), (), s32[]{:S(2)}) async-start(), calls=%async_computation.19 | async-start | bytes 2654208 | tf_op jit(solution)/shard_map/reduce_scatter | solution.py:171
  357.8 107.1 %reduce-scatter.13.cloned.1.call-start = ((), (), s32[]{:S(2)}) async-start(), calls=%async_computation.15 | async-start | bytes 2654208 | tf_op jit(solution)/shard_map/reduce_scatter | solution.py:171
  361.2 149.8 %reduce-scatter.17.cloned.1.call-start = ((), (), s32[]{:S(2)}) async-start(), calls=%async_computation.17 | async-start | bytes 2654208 | tf_op jit(solution)/shard_map/reduce_scatter | solution.py:171
  364.6 226.4 %reduce-scatter.33.cloned.1.call-start = ((), (), s32[]{:S(2)}) async-start(), calls=%async_computation.25 | async-start | bytes 10616832 | tf_op jit(solution)/shard_map/reduce_scatter | solution.py:171
  373.6 297.3 %reduce-scatter.29.cloned.1.call-start = ((), (), s32[]{:S(2)}) async-start(), calls=%async_computation.23 | async-start | bytes 10616832 | tf_op jit(solution)/shard_map/reduce_scatter | solution.py:171
  381.7 407.2 %all-gather.12.cloned.1.call-start = ((), (), s32[]{:S(2)}) async-start(), calls=%async_computation.13 | async-start | bytes 7864320 | tf_op jit(solution)/shard_map/all_gather | solution.py:234
  382.4 521.4 %all-gather.14.cloned.1.call-start = ((), (), s32[]{:S(2)}) async-start(), calls=%async_computation.14 | async-start | bytes 7864320 | tf_op jit(solution)/shard_map/all_gather | solution.py:260
  388.9 536.6 %reduce-scatter.27.cloned.1.call-start = ((), (), s32[]{:S(2)}) async-start(), calls=%async_computation.22 | async-start | bytes 491520 | tf_op jit(solution)/shard_map/reduce_scatter | solution.py:173
  390.9 556.4 %reduce-scatter.23.cloned.1.call-start = ((), (), s32[]{:S(2)}) async-start(), calls=%async_computation.20 | async-start | bytes 491520 | tf_op jit(solution)/shard_map/reduce_scatter | solution.py:173
  420.5 548.4 %reduce-scatter.15.cloned.1.call-start = ((), (), s32[]{:S(2)}) async-start(), calls=%async_computation.16 | async-start | bytes 491520 | tf_op jit(solution)/shard_map/reduce_scatter | solution.py:173
  466.9 523.6 %reduce-scatter.19.cloned.1.call-start = ((), (), s32[]{:S(2)}) async-start(), calls=%async_computation.18 | async-start | bytes 491520 | tf_op jit(solution)/shard_map/reduce_scatter | solution.py:173
  513.1 507.7 %reduce-scatter.35.cloned.1.call-start = ((), (), s32[]{:S(2)}) async-start(), calls=%async_computation.26 | async-start | bytes 1474560 | tf_op jit(solution)/shard_map/reduce_scatter | solution.py:173
  593.5 458.6 %reduce-scatter.31.cloned.1.call-start = ((), (), s32[]{:S(2)}) async-start(), calls=%async_computation.24 | async-start | bytes 1474560 | tf_op jit(solution)/shard_map/reduce_scatter | solution.py:173
  (29 other events, 107.8 us)
Sparse Core Ops, SparseCore 0:
  11.4 74.2 all-gather.15
  89.1 80.8 all-gather.17
  173.4 80.6 all-gather.19
  256.7 71.2 all-gather.21
  331.2 41.0 reduce-scatter.24
  375.9 42.4 reduce-scatter.20
  422.3 42.4 reduce-scatter.12
  468.5 42.4 reduce-scatter.16
  514.5 76.4 reduce-scatter.32
  594.4 76.4 reduce-scatter.28
  672.5 116.3 all-gather.11
  790.4 113.4 all-gather.13
  906.7 18.7 reduce-scatter.26
  928.4 18.8 reduce-scatter.22
  950.0 18.8 reduce-scatter.14
  971.7 18.8 reduce-scatter.18
  993.3 27.4 reduce-scatter.34
  1024.1 27.8 reduce-scatter.30

commit v2 on v1

v2 whole, which is shorter than its diff:
```python
from functools import partial

import jax
import jax.numpy as jnp
from jax import lax
from jax.experimental import pallas as pl
from jax.experimental.pallas import tpu as pltpu
from jax.sharding import PartitionSpec as P

HEAD_DIM = 64
LENGTH = 512
EPSILON = 1e-12
F32 = jnp.float32
BF16 = jnp.bfloat16
SCALE = HEAD_DIM ** (-0.5)
EXP_SCALE = SCALE * 1.4426950408889634
ROWS = ((0,), (0,))
PLAIN = ((1,), (0,))
COLS = ((1,), (1,))


def dot(left, right, dims):
    return lax.dot_general(left, right, (dims, ((), ())), preferred_element_type=F32)


def norm_forward(values, gain, shift):
    center = values - jnp.mean(values, axis=-1, keepdims=True)
    inverse = lax.rsqrt(jnp.mean(center * center, axis=-1, keepdims=True) + EPSILON)
    normed = center * inverse
    return (normed * gain + shift, normed, inverse)


def norm_backward(upstream, gain, normed, inverse):
    scaled = upstream * gain
    first_mean = jnp.mean(scaled, axis=-1, keepdims=True)
    cross_mean = jnp.mean(scaled * normed, axis=-1, keepdims=True)
    return inverse * (scaled - first_mean - normed * cross_mean)


def row_sums(values):
    return jnp.sum(values, axis=0, keepdims=True)


def call(kernel, name, grid, ins, outs, flops, exps=0, scratch=(), prefetch=None):
    moved = sum(a.size * a.dtype.itemsize for a, _, _ in ins)
    moved += sum(jnp.dtype(t).itemsize * functools_prod(s) for s, t, _, _ in outs)
    return pl.pallas_call(
        kernel,
        grid=grid,
        in_specs=[pl.BlockSpec(b, m) for _, b, m in ins],
        out_specs=[pl.BlockSpec(b, m) for _, _, b, m in outs],
        out_shape=[jax.ShapeDtypeStruct(s, t) for s, t, _, _ in outs],
        scratch_shapes=list(scratch),
        cost_estimate=pl.CostEstimate(flops=flops, bytes_accessed=moved, transcendentals=exps),
        compiler_params=pltpu.CompilerParams(vmem_limit_bytes=56 << 20),
        name=name,
    )(*(a for a, _, _ in ins))


def functools_prod(shape):
    total = 1
    for n in shape:
        total *= n
    return total


def attend_kernel(x_ref, w_ref, bias_ref, bo_ref, gain_ref, shift_ref, qkv_ref, ctx_ref, hid_ref, nrm_ref, inv_ref):
    slot = pl.program_id(1)
    cols = ctx_ref.shape[-1]
    x = x_ref[...]
    qkv = (dot(x, w_ref[: 3 * cols], COLS) + bias_ref[...]).astype(BF16)
    qkv_ref[...] = qkv
    parts = []
    for h in range(cols // HEAD_DIM):
        q, k, v = (qkv[:, i * cols + h * HEAD_DIM : i * cols + (h + 1) * HEAD_DIM] for i in range(3))
        scores = dot(q, k, COLS)
        largest = jnp.max(scores, axis=-1, keepdims=True)
        expon = jnp.exp2((scores - largest) * EXP_SCALE)
        totals = jnp.sum(expon, axis=-1, keepdims=True)
        parts.append((dot(expon.astype(BF16), v, PLAIN) / totals).astype(BF16))
    context = jnp.concatenate(parts, axis=1)
    ctx_ref[...] = context
    attn = dot(context, w_ref[3 * cols :], PLAIN)

    @pl.when(slot == 0)
    def _():
        hid_ref[...] = attn

    @pl.when(slot > 0)
    def _():
        hid_ref[...] += attn

    @pl.when(slot == pl.num_programs(1) - 1)
    def _():
        values = x.astype(F32) + hid_ref[...] + bo_ref[...]
        hidden, normed, inverse = norm_forward(values, gain_ref[...], shift_ref[...])
        hid_ref[...] = hidden
        nrm_ref[...] = normed
        inv_ref[...] = inverse


def attend_forward(x, weights, bias, b_output, gain, shift):
    rows, width = x.shape
    slots = weights.shape[0]
    cols = width // slots
    mine = lambda i, j: (i, 0)
    flat = lambda i, j: (0, 0)
    token = (LENGTH, width)
    vec = (1, width)
    return call(
        attend_kernel,
        "attend_forward",
        (rows // LENGTH, slots),
        [
            (x, token, mine),
            (weights, (None, width, width), lambda i, j: (j, 0, 0)),
            (bias, (None, 1, 3 * cols), lambda i, j: (j, 0, 0)),
            (b_output, vec, flat),
            (gain, vec, flat),
            (shift, vec, flat),
        ],
        [
            ((slots, rows, 3 * cols), BF16, (None, LENGTH, 3 * cols), lambda i, j: (j, i, 0)),
            ((slots, rows, cols), BF16, (None, LENGTH, cols), lambda i, j: (j, i, 0)),
            ((rows, width), F32, token, mine),
            ((rows, width), F32, token, mine),
            ((rows, 1), F32, (LENGTH, 1), mine),
        ],
        flops=rows * width * (8 * width + 4 * LENGTH),
        exps=rows * LENGTH * (width // HEAD_DIM),
    )


def attend_back_kernel(ga_ref, gr_ref, qkv_ref, w_ref, gqkv_ref, gx_ref, sum_ref):
    slot = pl.program_id(1)
    cols = qkv_ref.shape[-1] // 3
    gctx = dot(ga_ref[...], w_ref[3 * cols :], COLS).astype(BF16)
    for h in range(cols // HEAD_DIM):
        at = [slice(i * cols + h * HEAD_DIM, i * cols + (h + 1) * HEAD_DIM) for i in range(3)]
        q, k, v = (qkv_ref[:, s] for s in at)
        g = gctx[:, at[0]]
        scores = dot(k, q, COLS)
        largest = jnp.max(scores, axis=0, keepdims=True)
        expon = jnp.exp2((scores - largest) * EXP_SCALE)
        probs = expon * (1.0 / row_sums(expon))
        gqkv_ref[:, at[2]] = dot(probs.astype(BF16), g, PLAIN).astype(BF16)
        weighted = probs * dot(v, g, COLS)
        grad_scores = (weighted - probs * row_sums(weighted)).astype(BF16)
        gqkv_ref[:, at[0]] = (dot(grad_scores, k, ROWS) * SCALE).astype(BF16)
        gqkv_ref[:, at[1]] = (dot(grad_scores, q, PLAIN) * SCALE).astype(BF16)
    grads = gqkv_ref[...]
    sums = row_sums(grads.astype(F32))
    back = dot(grads, w_ref[: 3 * cols], PLAIN)
    sum_ref[...] = sums

    @pl.when(slot == 0)
    def _():
        gx_ref[...] = gr_ref[...] + back

    @pl.when(slot > 0)
    def _():
        gx_ref[...] += back


def attend_backward(grad_attn, grad_resid, qkv, weights):
    rows, width = grad_attn.shape
    slots = weights.shape[0]
    cols = width // slots
    mine = lambda i, j: (i, 0)
    token = (LENGTH, width)
    heads = (None, LENGTH, 3 * cols)
    return call(
        attend_back_kernel,
        "attend_backward",
        (rows // LENGTH, slots),
        [
            (grad_attn, token, mine),
            (grad_resid, token, mine),
            (qkv, heads, lambda i, j: (j, i, 0)),
            (weights, (None, width, width), lambda i, j: (j, 0, 0)),
        ],
        [
            ((slots, rows, 3 * cols), BF16, heads, lambda i, j: (j, i, 0)),
            ((rows, width), F32, token, mine),
            ((rows // LENGTH, slots, 1, 3 * cols), F32, (None, None, 1, 3 * cols), lambda i, j: (i, j, 0, 0)),
        ],
        flops=rows * width * (8 * width + 10 * LENGTH),
        exps=rows * LENGTH * (width // HEAD_DIM),
    )


def inner_kernel(h_ref, w_ref, b_ref, act_ref, slope_ref):
    inner = dot(h_ref[...].astype(BF16), w_ref[...], PLAIN) + b_ref[...]
    phi = 0.5 + 0.5 * lax.erf(inner * (0.5**0.5))
    bell = jnp.exp2(inner * inner * (-0.5 * 1.4426950408889634)) * 0.3989422804014327
    act_ref[...] = (inner * phi).astype(BF16)
    slope_ref[...] = phi + inner * bell


def inner_forward(hidden, weights, bias):
    rows, width = hidden.shape
    slots, _, units = weights.shape
    slot = lambda i, j: (i, j, 0)
    block = LENGTH // 2
    return call(
        inner_kernel,
        "inner_forward",
        (slots, rows // block),
        [
            (hidden, (block, width), lambda i, j: (j, 0)),
            (weights, (None, width, units), lambda i, j: (i, 0, 0)),
            (bias, (None, 1, units), lambda i, j: (i, 0, 0)),
        ],
        [
            ((slots, rows, units), BF16, (None, block, units), slot),
            ((slots, rows, units), F32, (None, block, units), slot),
        ],
        flops=2 * rows * width * slots * units,
        exps=2 * rows * slots * units,
    )


def outer_kernel(act_ref, w_ref, hid_ref, cot_ref, bo_ref, gain_ref, shift_ref, out_ref, gr_ref, go_ref, sum_ref):
    slot = pl.program_id(1)
    outer = dot(act_ref[...], w_ref[...], PLAIN)

    @pl.when(slot == 0)
    def _():
        out_ref[...] = outer

    @pl.when(slot > 0)
    def _():
        out_ref[...] += outer

    @pl.when(slot == pl.num_programs(1) - 1)
    def _():
        gain = gain_ref[...]
        values = hid_ref[...] + (out_ref[...] + bo_ref[...])
        layer_out, normed, inverse = norm_forward(values, gain, shift_ref[...])
        out_ref[...] = layer_out
        upstream = cot_ref[...].astype(F32)
        grad = norm_backward(upstream, gain, normed, inverse)
        rounded = grad.astype(BF16)
        gr_ref[...] = grad
        go_ref[...] = rounded
        sum_ref[0:1] = row_sums(upstream * normed)
        sum_ref[1:2] = row_sums(upstream)
        sum_ref[2:3] = row_sums(rounded.astype(F32))


def outer_forward(active, weights, hidden, cotangent, b_outer, gain, shift):
    rows, width = hidden.shape
    slots, units, _ = weights.shape
    mine = lambda i, j: (i, 0)
    flat = lambda i, j: (0, 0)
    token = (LENGTH, width)
    vec = (1, width)
    return call(
        outer_kernel,
        "outer_forward",
        (rows // LENGTH, slots),
        [
            (active, (None, LENGTH, units), lambda i, j: (j, i, 0)),
            (weights, (None, units, width), lambda i, j: (j, 0, 0)),
            (hidden, token, mine),
            (cotangent, token, mine),
            (b_outer, vec, flat),
            (gain, vec, flat),
            (shift, vec, flat),
        ],
        [
            ((rows, width), F32, token, mine),
            ((rows, width), F32, token, mine),
            ((rows, width), BF16, token, mine),
            ((rows // LENGTH, 8, width), F32, (None, 8, width), lambda i, j: (i, 0, 0)),
        ],
        flops=2 * rows * width * slots * units,
    )


def inner_back_kernel(go_ref, wu_ref, slope_ref, wi_ref, gr_ref, nrm_ref, inv_ref, gain_ref,
                      gi_ref, g1_ref, ga_ref, bsum_ref, sum_ref):
    slot = pl.program_id(1)
    grad_inner = (dot(go_ref[...], wu_ref[...], COLS) * slope_ref[...]).astype(BF16)
    gi_ref[...] = grad_inner
    bsum_ref[...] = row_sums(grad_inner.astype(F32))
    back = dot(grad_inner, wi_ref[...], COLS)

    @pl.when(slot == 0)
    def _():
        g1_ref[...] = gr_ref[...] + back

    @pl.when(slot > 0)
    def _():
        g1_ref[...] += back

    @pl.when(slot == pl.num_programs(1) - 1)
    def _():
        upstream, normed = g1_ref[...], nrm_ref[...]
        grad = norm_backward(upstream, gain_ref[...], normed, inv_ref[...])
        rounded = grad.astype(BF16)
        g1_ref[...] = grad
        ga_ref[...] = rounded
        sum_ref[0:1] = row_sums(upstream * normed)
        sum_ref[1:2] = row_sums(upstream)
        sum_ref[2:3] = row_sums(rounded.astype(F32))


def inner_backward(grad_outer, w_outer, slope, w_inner, grad_resid2, normed, inverse, gain):
    rows, width = grad_outer.shape
    slots, units, _ = w_outer.shape
    mine = lambda i, j: (i, 0)
    token = (LENGTH, width)
    slot = lambda i, j: (j, i, 0)
    weight = lambda i, j: (j, 0, 0)
    return call(
        inner_back_kernel,
        "inner_backward",
        (rows // LENGTH, slots),
        [
            (grad_outer, token, mine),
            (w_outer, (None, units, width), weight),
            (slope, (None, LENGTH, units), slot),
            (w_inner, (None, width, units), weight),
            (grad_resid2, token, mine),
            (normed, token, mine),
            (inverse, (LENGTH, 1), mine),
            (gain, (1, width), lambda i, j: (0, 0)),
        ],
        [
            ((slots, rows, units), BF16, (None, LENGTH, units), slot),
            ((rows, width), F32, token, mine),
            ((rows, width), BF16, token, mine),
            ((rows // LENGTH, slots, 1, units), F32, (None, None, 1, units), lambda i, j: (i, j, 0, 0)),
            ((rows // LENGTH, 8, width), F32, (None, 8, width), lambda i, j: (i, 0, 0)),
        ],
        flops=4 * rows * width * slots * units,
    )


def narrow_kernel(x_ref, out_ref):
    out_ref[...] = x_ref[...].astype(BF16)


def narrow(values, block_rows):
    rows, width = values.shape
    at = lambda i: (i, 0)
    block = (block_rows, width)
    out = ((rows, width), BF16, block, at)
    return call(narrow_kernel, "narrow", (rows // block_rows,), [(values, block, at)], [out], 0)[0]


def shift_to(values, tensor, k):
    return lax.ppermute(values, "tensor", [(i, (i + k) % tensor) for i in range(tensor)])


def flip(values, bit):
    return lax.ppermute(values, "dp", [(i, i ^ bit) for i in range(8)])


def assemble_kernel(where_ref, local_ref, *refs):
    *pieces, out_ref, hold, sems = refs
    share = pieces[0].shape[1]
    copies = []
    for n, piece in enumerate(pieces):
        start = pl.multiple_of(where_ref[n], 8)
        copies.append(pltpu.make_async_copy(piece, hold.at[:, pl.ds(start, share)], sems.at[n]))
        copies[-1].start()
    out_ref[0] = local_ref[...]
    for copy in copies:
        copy.wait()
    for k in range(hold.shape[0]):
        out_ref[k + 1] = hold[k].astype(BF16)


def assemble(local, where, pieces):
    rows, width = local.shape
    others = pieces[0].shape[0]
    out = (others + 1, rows, width)
    return pl.pallas_call(
        assemble_kernel,
        in_specs=[pl.BlockSpec(memory_space=pltpu.SMEM), pl.BlockSpec(memory_space=pltpu.VMEM)]
        + [pl.BlockSpec(memory_space=pl.ANY)] * len(pieces),
        out_specs=pl.BlockSpec(memory_space=pltpu.VMEM),
        out_shape=jax.ShapeDtypeStruct(out, BF16),
        scratch_shapes=[pltpu.VMEM((others, rows, width), F32), pltpu.SemaphoreType.DMA((len(pieces),))],
        cost_estimate=pl.CostEstimate(flops=0, bytes_accessed=others * rows * width * 6, transcendentals=0),
        compiler_params=pltpu.CompilerParams(vmem_limit_bytes=56 << 20),
        name="assemble",
    )(where, local, *pieces)


def gather_weight(local, dp, tensor):
    rows, width = local.shape
    share = rows // dp
    me = lax.axis_index("dp")
    piece = lax.dynamic_slice_in_dim(local, me * share, share, 0).astype(F32)
    slots = jnp.stack([shift_to(piece, tensor, k) for k in range(1, tensor)])
    if dp != 8 or share % 16:
        full = lax.all_gather(slots, "dp", axis=1).reshape((tensor - 1) * rows, width)
        full = narrow(full, rows).reshape(tensor - 1, rows, width)
        return jnp.concatenate([local[None], full], axis=0)
    half = share // 2
    first = {0: slots[:, :half]}
    second = {0: slots[:, half:]}
    for held, order in ((first, (2, 4)), (second, (4, 2))):
        for bit in order + (1,):
            for rel in list(held):
                held[rel | bit] = flip(held[rel], bit)
    pieces, where = [], []
    for held, offset in ((first, 0), (second, half)):
        for rel, array in held.items():
            pieces.append(array)
            where.append((me ^ rel) * share + offset)
    return assemble(local, jnp.stack(where), pieces)


def slot_sum(part, tensor):
    total = part[0]
    for k in range(1, tensor):
        total = total + shift_to(part[k], tensor, tensor - k)
    return total


def block_order(width):
    me = lax.axis_index("dp")
    share = width // 8
    rel = jnp.array([7, 5, 3, 1, 6, 4, 2, 0])
    position = lax.broadcasted_iota(jnp.int32, (width, width), 1)
    source = (me ^ rel[jnp.arange(width) // share]) * share + jnp.arange(width) % share
    del position
    return (lax.broadcasted_iota(jnp.int32, (width, width), 0) == source[None, :]).astype(BF16)


def scatter_grad(left, rights, order, dp, tensor):
    width = left.shape[1]
    share = width // dp
    right = jnp.concatenate(list(rights), axis=1)
    cols = right.shape[1] // tensor
    if order is None:
        part = lax.psum_scatter(dot(left, right, ROWS), "dp", scatter_dimension=0, tiled=True)
    else:
        left = dot(left, order, PLAIN).astype(BF16)
        send = dot(left[:, : 4 * share], right, ROWS)
        keep = dot(left[:, 4 * share :], right, ROWS)
        held = keep + flip(send, 1)
        mid = right.shape[1] // 2
        a, b = held[:, :mid], held[:, mid:]
        pick = lambda v, i: v[i * share : (i + 1) * share]
        a_send = jnp.concatenate([pick(a, 0), pick(a, 2)], axis=0)
        a_keep = jnp.concatenate([pick(a, 1), pick(a, 3)], axis=0)
        a = a_keep + flip(a_send, 2)
        b = b[2 * share :] + flip(b[: 2 * share], 4)
        a = pick(a, 1) + flip(pick(a, 0), 4)
        b = pick(b, 1) + flip(pick(b, 0), 2)
        part = jnp.concatenate([a, b], axis=1)
    return slot_sum([part[:, k * cols : (k + 1) * cols] for k in range(tensor)], tensor)


def shards(
    dp,
    tensor,
    inputs,
    w_query,
    b_query,
    w_key,
    w_value,
    b_value,
    w_output,
    b_output,
    gain_attn,
    shift_attn,
    w_inner,
    b_inner,
    w_outer,
    b_outer,
    gain_ffn,
    shift_ffn,
    cotangent,
):
    tok_rows, width = inputs.shape
    own_rows = tok_rows // tensor
    cols = w_query.shape[1]
    z = lax.axis_index("tensor")
    own = lambda a: lax.dynamic_slice_in_dim(a, z * own_rows, own_rows, 0)
    row = lambda a: a.astype(F32)[None, :]

    vectors = row(jnp.concatenate([b_query, jnp.zeros_like(b_query), b_value, b_inner]))
    vectors = jnp.stack([vectors] + [shift_to(vectors, tensor, k) for k in range(1, tensor)])
    qkv_bias, inner_bias = vectors[..., : 3 * cols], vectors[..., 3 * cols :]

    attn_local = jnp.concatenate([w_query.T, w_key.T, w_value.T, w_output], axis=0)
    attn_full = gather_weight(attn_local, dp, tensor)
    inner_full = gather_weight(w_inner, dp, tensor)
    outer_full = gather_weight(w_outer, dp, tensor)

    x, gain_one, gain_two = own(inputs), row(gain_attn), row(gain_ffn)
    qkv, context, hidden, normed, inverse = attend_forward(
        x, attn_full, qkv_bias, row(b_output), gain_one, row(shift_attn)
    )
    active, slope = inner_forward(hidden, inner_full, inner_bias)
    layer_out, grad_resid2, grad_outer, sums_two = outer_forward(
        active, outer_full, hidden, own(cotangent), row(b_outer), gain_two, row(shift_ffn)
    )
    layer_out = narrow(lax.all_gather(layer_out, "tensor", axis=0, tiled=True), own_rows)

    order = block_order(width) if dp == 8 and width % 64 == 0 else None
    gu = scatter_grad(grad_outer, active, order, dp, tensor)
    grad_inner, grad_resid1, grad_attn, inner_sums, sums_one = inner_backward(
        grad_outer, outer_full, slope, inner_full, grad_resid2, normed, inverse, gain_one
    )
    gi = scatter_grad(hidden.astype(BF16), grad_inner, order, dp, tensor)
    go = scatter_grad(grad_attn, context, order, dp, tensor)
    grad_qkv, grad_x, qkv_sums = attend_backward(grad_attn, grad_resid1, qkv, attn_full)
    grad_inputs = lax.all_gather(grad_x, "tensor", axis=0, tiled=True)
    gqkv = scatter_grad(x, grad_qkv, order, dp, tensor)

    by_slot = jnp.concatenate([jnp.sum(qkv_sums, axis=0), jnp.sum(inner_sums, axis=0)], axis=-1)
    by_place = by_slot[(z - jnp.arange(tensor)) % tensor].reshape(-1)
    rest = jnp.concatenate([jnp.sum(sums_one, axis=0)[:3], jnp.sum(sums_two, axis=0)[:3]]).reshape(-1)
    sums = lax.psum(jnp.concatenate([by_place, rest]), ("dp", "tensor"))
    span = by_place.shape[0] // tensor
    mine = lax.dynamic_slice_in_dim(sums, z * span, span, 0)
    rest = sums[by_place.shape[0] :].reshape(6, width)
    return (
        layer_out,
        grad_inputs,
        gqkv[:, :cols],
        mine[:cols],
        gqkv[:, cols : 2 * cols],
        gqkv[:, 2 * cols :],
        mine[2 * cols : 3 * cols],
        go.T,
        rest[2],
        rest[0],
        rest[1],
        gi,
        mine[3 * cols :],
        gu.T,
        rest[5],
        rest[3],
        rest[4],
    )


def solution(mesh):
    wide, tall, vector = P(None, "tensor"), P("tensor", None), P("tensor")
    tokens, both = P("dp", None), P("dp", "tensor")
    in_specs = (
        tokens, wide, vector, wide, wide, vector, tall, P(), P(), P(), wide, vector, tall, P(), P(), P(), tokens,
    )
    out_specs = (
        tokens, tokens, both, vector, both, both, vector, P("tensor", "dp"), P(), P(), P(), both, vector,
        P("tensor", "dp"), P(), P(), P(),
    )
    body = partial(shards, mesh.shape["dp"], mesh.shape["tensor"])
    return jax.shard_map(body, mesh=mesh, in_specs=in_specs, out_specs=out_specs, check_vma=False)
```

time: 1070 us -> 613 us (0.57)
  waiting for transfers between devices: 774 us -> 254 us
  starting transfers between devices: 7.42 us -> 109 us
  blocking collectives: 92.2 us -> 44 us
  Pallas kernels: 54.8 us -> 100 us
  matrix products: 63.3 us -> 33.5 us
  other arithmetic: 25.1 us -> 13.8 us
    reduce_scatter x12 -> x0, waiting for transfers between devices: 419 us -> none  [the longest x6 271 us: scatter_grad(): part = lax.psum_scatter(grad, 'dp', scatter_dimension=0, tiled=True)]
    ppermute x0 -> x86, waiting for transfers between devices: none -> 250 us  [the longest x24 138 us: shift_to(): lax.ppermute(values, 'tensor', [(i, (i + k) % tensor) for i in range(tens...]
    all_gather x4 -> x0, waiting for transfers between devices: 179 us -> none  [gather_weight(): full = lax.all_gather(piece, ('dp', 'tensor'), axis=0)]
    all_gather x1, waiting for transfers between devices: 110 us -> 0.01 us  [shards(): grad_inputs = lax.all_gather(grad_x, 'tensor', axis=0, tiled=True)]
    ppermute x0 -> x86, starting transfers between devices: none -> 109 us  [the longest x24 65.7 us: shift_to(): lax.ppermute(values, 'tensor', [(i, (i + k) % tensor) for i in range(tens...]
    all_gather x1, waiting for transfers between devices: 64.8 us -> 3.69 us  [shards(): lax.all_gather(layer_out, 'tensor', axis=0, tiled=True)]
    pallas_call x8 -> x9, Pallas kernels: 54.8 us -> 100 us  [the longest x6 79.6 us: call(): pl.pallas_call(kernel, grid=grid, in_specs=[pl.BlockSpec(b, m) for _, b,...]
    all_gather x1 -> x0, blocking collectives: 44.4 us -> none  [shards(): vectors = lax.all_gather(vectors, 'tensor', axis=0)]
  transfers between devices with their start and end apart: 19 -> 88, of which waited for: 17 -> 28; matrix products, arithmetic and copies ran while one was open for 10% -> 11% of each run, Pallas kernels for 5% -> 7%
where the time goes in v2:
time: 613 us; the launch traced here: 606 us
  waiting for transfers between devices  254 us (41%)
  starting transfers between devices  109 us (18%)
  Pallas kernels  100 us (16%)
  blocking collectives  44 us (7%)
  local copies, waits for them, and re-layouts  34.9 us (6%)
  matrix products  33.5 us (5%)
  between operations  16.2 us (3%)
  other arithmetic  13.8 us (2%)
    ppermute x24, waiting for transfers between devices, shift_to(): lax.ppermute(values, 'tensor', [(i, (i + k) % tensor) for i in range(tens...  138 us
    ppermute x62, waiting for transfers between devices, flip(): return lax.ppermute(values, 'dp', [(i, i ^ bit) for i in range(8)])  112 us
    pallas_call x6, Pallas kernels, call(): pl.pallas_call(kernel, grid=grid, in_specs=[pl.BlockSpec(b, m) for _, b,...  79.6 us
    ppermute x24, starting transfers between devices, shift_to(): lax.ppermute(values, 'tensor', [(i, (i + k) % tensor) for i in range(tens...  65.7 us
    psum x1, blocking collectives, shards(): sums = lax.psum(jnp.concatenate([by_place, rest]), ('dp', 'tensor'))  44 us
    ppermute x62, starting transfers between devices, flip(): return lax.ppermute(values, 'dp', [(i, i ^ bit) for i in range(8)])  43.6 us
    dot_general x12, matrix products, dot(): lax.dot_general(left, right, (dims, ((), ())), preferred_element_type=F32)  33.5 us
    pallas_call x3, Pallas kernels, assemble(): pl.pallas_call(assemble_kernel, in_specs=[pl.BlockSpec(memory_space=pltpu...  20.7 us
  transfers between devices with their start and end apart: 88, of which 28 were waited for; matrix products, arithmetic and copies ran while one was open for 11% of the time, Pallas kernels for 7%

profile of v2, /device:TPU:0, one launch (start us, length us, event | category | flops | bytes accessed | tf_op | source)
XLA Modules:
  0.0 606.0 jit_solution(13038943014012787403)
XLA Ops:
  23.0 11.5 %collective-permute-done.19 = f32[1,1344]{1,0:T(1,128)S(1)} collective-permute-done((f32[1,1344]{1,0:T(1,128)S(1)}, f32[1,1344]{1,0:T(1,128)S(1)}, u32[]{:S(2)}, u32[]{:S(2)}) %collective-permute-start.19) | collective-permute-done | bytes 5408 | tf_op jit(solution)/shard_map/ppermute | solution.py:354
  34.5 5.8 collective-permute-start.18
  44.2 9.9 %collective-permute-start.37 = (f32[96,768]{1,0:T(8,128)S(1)}, f32[96,768]{1,0:T(8,128)S(1)}, u32[]{:S(2)}, u32[]{:S(2)}) collective-permute-start(f32[96,768]{1,0:T(8,128)S(1)} %dynamic-slice_convert_fusion), channel_id=1, source_target_pairs={{0,1},{1,2},{2,3},{3,0},{4,5},{5,6},{6,7},{7,4},{8,9},{9,10},{10,1... | collective-permute-start | bytes 884744 | tf_op jit(solution)/shard_map/ppermute | solution.py:354
  62.2 16.8 %collective-permute-done.38 = f32[96,768]{1,0:T(8,128)S(1)} collective-permute-done((f32[96,768]{1,0:T(8,128)S(1)}, f32[96,768]{1,0:T(8,128)S(1)}, u32[]{:S(2)}, u32[]{:S(2)}) %collective-permute-start.38) | collective-permute-done | bytes 294944 | tf_op jit(solution)/shard_map/ppermute | solution.py:354
  82.3 8.3 %collective-permute-done.1 = f32[96,768]{1,0:T(8,128)S(1)} collective-permute-done((f32[96,768]{1,0:T(8,128)S(1)}, f32[96,768]{1,0:T(8,128)S(1)}, u32[]{:S(2)}, u32[]{:S(2)}) %collective-permute-start.1) | collective-permute-done | bytes 294944 | tf_op jit(solution)/shard_map/ppermute | solution.py:354
  95.6 8.2 %collective-permute-done.24.refs_2_ = f32[3,48,768]{2,1,0:T(8,128)S(1)} collective-permute-done((f32[3,48,768]{2,1,0:T(8,128)S(1)}, f32[3,48,768]{2,1,0:T(8,128)S(1)}, u32[]{:S(2)}, u32[]{:S(2)}) %collective-permute-start.24) | collective-permute-done | bytes 442400 | tf_op jit(solution)/shard_map/ppermute | solution.py:358
  107.1 7.9 %collective-permute-done.48.refs_10_ = f32[3,48,768]{2,1,0:T(8,128)S(1)} collective-permute-done((f32[3,48,768]{2,1,0:T(8,128)S(1)}, f32[3,48,768]{2,1,0:T(8,128)S(1)}, u32[]{:S(2)}, u32[]{:S(2)}) %collective-permute-start.48) | collective-permute-done | bytes 442400 | tf_op jit(solution)/shard_map/ppermute | solution.py:358
  115.6 8.9 %collective-permute-done.40.refs_1_ = f32[3,48,768]{2,1,0:T(8,128)S(1)} collective-permute-done((f32[3,48,768]{2,1,0:T(8,128)S(1)}, f32[3,48,768]{2,1,0:T(8,128)S(1)}, u32[]{:S(2)}, u32[]{:S(2)}) %collective-permute-start.40) | collective-permute-done | bytes 442400 | tf_op jit(solution)/shard_map/ppermute | solution.py:358
  126.5 7.5 %collective-permute-done.11.refs_10_ = f32[3,48,768]{2,1,0:T(8,128)S(1)} collective-permute-done((f32[3,48,768]{2,1,0:T(8,128)S(1)}, f32[3,48,768]{2,1,0:T(8,128)S(1)}, u32[]{:S(2)}, u32[]{:S(2)}) %collective-permute-start.11) | collective-permute-done | bytes 442400 | tf_op jit(solution)/shard_map/ppermute | solution.py:358
  136.0 7.5 %collective-permute-done.3.refs_1_ = f32[3,48,768]{2,1,0:T(8,128)} collective-permute-done((f32[3,48,768]{2,1,0:T(8,128)S(1)}, f32[3,48,768]{2,1,0:T(8,128)}, u32[]{:S(2)}, u32[]{:S(2)}) %collective-permute-start.3) | collective-permute-done | bytes 442400 | tf_op jit(solution)/shard_map/ppermute | solution.py:358
  144.4 7.8 %collective-permute-done.32.refs_11_ = f32[3,48,768]{2,1,0:T(8,128)} collective-permute-done((f32[3,48,768]{2,1,0:T(8,128)S(1)}, f32[3,48,768]{2,1,0:T(8,128)}, u32[]{:S(2)}, u32[]{:S(2)}) %collective-permute-start.32) | collective-permute-done | bytes 442400 | tf_op jit(solution)/shard_map/ppermute | solution.py:358
  157.4 7.6 %collective-permute-done.12.refs_11_ = f32[3,48,768]{2,1,0:T(8,128)} collective-permute-done((f32[3,48,768]{2,1,0:T(8,128)S(1)}, f32[3,48,768]{2,1,0:T(8,128)}, u32[]{:S(2)}, u32[]{:S(2)}) %collective-permute-start.12) | collective-permute-done | bytes 442400 | tf_op jit(solution)/shard_map/ppermute | solution.py:358
  181.3 6.9 %assemble.4.w_ref.wi_ref = bf16[4,768,768]{2,1,0:T(8,128)(2,1)} custom-call(s32[16]{0:T(128)} %stack.149.where_ref, bf16[768,768]{1,0:T(8,128)(2,1)} %local_ref.2, f32[3,48,768]{2,1,0:T(8,128)} %copy-done.9, f32[3,48,768]{2,1,0:T(8,128)} %copy-done.45, f32[3,48,768]{2,1,0:T(8,128)} %copy-done.44, f32[3,48,768]{2,1,0:T(8,128)} %collective-permute-done.25.refs_3_, ...), custom_call_target="tpu_custom_call" | custom-call | bytes 10616832 | tf_op jit(solution)/shard_map/assemble/pallas_call | solution.py:380
  188.2 7.0 %assemble.3.w_ref = bf16[4,768,768]{2,1,0:T(8,128)(2,1)} custom-call(s32[16]{0:T(128)} %stack.149.where_ref, bf16[768,768]{1,0:T(8,128)(2,1)} %copy-done.4, f32[3,48,768]{2,1,0:T(8,128)} %copy-done.11, f32[3,48,768]{2,1,0:T(8,128)} %collective-permute-done.3.refs_1_, f32[3,48,768]{2,1,0:T(8,128)} %copy-done.50, ...), custom_call_target="tpu_custom_call" | custom-call | bytes 10616832 | tf_op jit(solution)/shard_map/assemble/pallas_call | solution.py:380
  196.5 15.0 %attend_forward.1 = (bf16[4,512,576]{2,1,0:T(8,128)(2,1)}, bf16[4,512,192]{2,1,0:T(8,128)(2,1)}, f32[512,768]{1,0:T(8,128)}, f32[512,768]{1,0:T(8,128)}, f32[512,1]{1,0:T(8,128)}) custom-call(bf16[512,768]{1,0:T(8,128)(2,1)} %constant_dynamic-slice_fusion.1.x_ref, bf16[4,768,768]{2,1,0:T(8,128)(2,1)} %assemble.3.w_ref, ...), custom_call_target="tpu_custom_call" | custom-call | flops 3221225472 | bytes 11816960 | tf_op jit(solution)/shard_map/attend_forward/pallas_call | solution.py:47
  211.5 12.8 %inner_forward.1 = (bf16[4,512,768]{2,1,0:T(8,128)(2,1)}, f32[4,512,768]{2,1,0:T(8,128)}) custom-call(f32[512,768]{1,0:T(8,128)} %get-tuple-element.36.h_ref.hid_ref, bf16[4,768,768]{2,1,0:T(8,128)(2,1)} %assemble.4.w_ref.wi_ref, f32[4,1,768]{2,1,0:T(1,128)} %pad_maximum_fusion.18.b_ref), custom_call_target="tpu_custom_call" | custom-call | flops 2415919104 | bytes 15740928 | tf_op jit(solution)/shard_map/inner_forward/pallas_call | solution.py:47
  226.3 6.8 %assemble.5.w_ref.wu_ref = bf16[4,768,768]{2,1,0:T(8,128)(2,1)} custom-call(s32[16]{0:T(128)} %stack.149.where_ref, bf16[768,768]{1,0:T(8,128)(2,1)} %local_ref.3, f32[3,48,768]{2,1,0:T(8,128)} %copy-done.7, f32[3,48,768]{2,1,0:T(8,128)} %copy-done.38, f32[3,48,768]{2,1,0:T(8,128)} %copy-done.59, f32[3,48,768]{2,1,0:T(8,128)} %copy-done.62, ...), custom_call_target="tpu_custom_call" | custom-call | bytes 10616832 | tf_op jit(solution)/shard_map/assemble/pallas_call | solution.py:380
  233.2 10.1 %outer_forward.1 = (f32[512,768]{1,0:T(8,128)}, f32[512,768]{1,0:T(8,128)}, bf16[512,768]{1,0:T(8,128)(2,1)}, f32[1,8,768]{2,1,0:T(8,128)}) custom-call(bf16[4,512,768]{2,1,0:T(8,128)(2,1)} %get-tuple-element.37.act_ref, bf16[4,768,768]{2,1,0:T(8,128)(2,1)} %assemble.5.w_ref.wu_ref, f32[512,768]{1,0:T(8,128)} %get-tuple-element.36.h_ref.hid_ref, ...), custom_call_target="tpu_custom_call" | custom-call | flops 2415919104 | bytes 14189568 | tf_op jit(solution)/shard_map/outer_forward/pallas_call | solution.py:47
  243.3 14.1 %inner_backward.1 = (bf16[4,512,768]{2,1,0:T(8,128)(2,1)}, f32[512,768]{1,0:T(8,128)}, bf16[512,768]{1,0:T(8,128)(2,1)}, f32[1,4,1,768]{3,2,1,0:T(1,128)}, f32[1,8,768]{2,1,0:T(8,128)}) custom-call(bf16[512,768]{1,0:T(8,128)(2,1)} %get-tuple-element.39.go_ref, bf16[4,768,768]{2,1,0:T(8,128)(2,1)} %assemble.5.w_ref.wu_ref, ...), custom_call_target="tpu_custom_call" | custom-call | flops 4831838208 | bytes 25207808 | tf_op jit(solution)/shard_map/inner_backward/pallas_call | solution.py:47
  257.5 22.7 %attend_backward.1 = (bf16[4,512,576]{2,1,0:T(8,128)(2,1)}, f32[512,768]{1,0:T(8,128)}, f32[1,4,1,576]{3,2,1,0:T(1,128)}) custom-call(bf16[512,768]{1,0:T(8,128)(2,1)} %get-tuple-element.44.ga_ref, f32[512,768]{1,0:T(8,128)} %get-tuple-element.45.gr_ref, bf16[4,512,576]{2,1,0:T(8,128)(2,1)} %get-tuple-element.46.qkv_ref, bf16[4,768,768]{2,1,0:T(8,128)(2,1)} %assemble.3.w_ref), custom_call_target="tpu_custom_call" | custom-call | flops 4429185024 | bytes 13378560 | tf_op jit(solution)/shard_map/attend_backward/pallas_call | solution.py:47
  311.2 44.0 %psum.7 = f32[9984]{0:T(1024)S(1)} all-reduce(f32[9984]{0:T(1024)S(1)} %pad_maximum_fusion.15), channel_id=1, replica_groups=mesh['dp'=8,'tensor'=4] {'dp','tensor'}, use_global_device_ids=true, to_apply=%region_0.1 | all-reduce | flops 9984 | bytes 79872 | tf_op jit(solution)/shard_map/psum | solution.py:521
  361.4 5.1 collective-permute-done.66
  381.6 7.0 %collective-permute-done.68 = f32[96,192]{1,0:T(8,128)S(1)} collective-permute-done((f32[96,192]{1,0:T(8,128)S(1)}, f32[96,192]{1,0:T(8,128)S(1)}, u32[]{:S(2)}, u32[]{:S(2)}) %collective-permute-start.68) | collective-permute-done | bytes 73760 | tf_op jit(solution)/shard_map/ppermute | solution.py:354
  400.5 8.6 %collective-permute-done.55 = f32[192,1152]{1,0:T(8,128)S(1)} collective-permute-done((f32[192,1152]{1,0:T(8,128)}, f32[192,1152]{1,0:T(8,128)S(1)}, u32[]{:S(2)}, u32[]{:S(2)}) %collective-permute-start.55) | collective-permute-done | bytes 884768 | tf_op jit(solution)/shard_map/ppermute | solution.py:358
  425.4 6.4 %collective-permute-start.60 = (f32[96,576]{1,0:T(8,128)S(1)}, f32[96,576]{1,0:T(8,128)S(1)}, u32[]{:S(2)}, u32[]{:S(2)}) collective-permute-start(f32[96,576]{1,0:T(8,128)S(1)} %get-tuple-element.131), channel_id=1, source_target_pairs={{0,2},{1,3},{2,0},{3,1},{4,6},{5,7},{6,4},{7,5},{8,10},{9,11},{10,... | collective-permute-start | bytes 663560 | tf_op jit(solution)/shard_map/ppermute | solution.py:354
  436.0 18.8 %collective-permute-done.60 = f32[96,576]{1,0:T(8,128)S(1)} collective-permute-done((f32[96,576]{1,0:T(8,128)S(1)}, f32[96,576]{1,0:T(8,128)S(1)}, u32[]{:S(2)}, u32[]{:S(2)}) %collective-permute-start.60) | collective-permute-done | bytes 221216 | tf_op jit(solution)/shard_map/ppermute | solution.py:354
  463.5 20.2 %collective-permute-done.74 = f32[192,1536]{1,0:T(8,128)S(1)} collective-permute-done((f32[192,1536]{1,0:T(8,128)S(1)}, f32[192,1536]{1,0:T(8,128)S(1)}, u32[]{:S(2)}, u32[]{:S(2)}) %collective-permute-start.74) | collective-permute-done | bytes 1179680 | tf_op jit(solution)/shard_map/ppermute | solution.py:358
  486.9 10.7 %collective-permute-done.83 = f32[96,1536]{1,0:T(8,128)S(1)} collective-permute-done((f32[96,1536]{1,0:T(8,128)S(1)}, f32[96,1536]{1,0:T(8,128)S(1)}, u32[]{:S(2)}, u32[]{:S(2)}) %collective-permute-start.83) | collective-permute-done | bytes 589856 | tf_op jit(solution)/shard_map/ppermute | solution.py:358
  497.7 14.0 %collective-permute-start.84 = (f32[96,768]{1,0:T(8,128)S(1)}, f32[96,768]{1,0:T(8,128)S(1)}, u32[]{:S(2)}, u32[]{:S(2)}) collective-permute-start(f32[96,768]{1,0:T(8,128)S(1)} %get-tuple-element.127), channel_id=1, source_target_pairs={{0,2},{1,3},{2,0},{3,1},{4,6},{5,7},{6,4},{7,5},{8,10},{9,11},{10,... | collective-permute-start | bytes 884744 | tf_op jit(solution)/shard_map/ppermute | solution.py:354
  518.1 27.3 %collective-permute-done.84 = f32[96,768]{1,0:T(8,128)S(1)} collective-permute-done((f32[96,768]{1,0:T(8,128)S(1)}, f32[96,768]{1,0:T(8,128)S(1)}, u32[]{:S(2)}, u32[]{:S(2)}) %collective-permute-start.84) | collective-permute-done | bytes 294944 | tf_op jit(solution)/shard_map/ppermute | solution.py:354
  551.4 31.8 %collective-permute-done.76 = f32[96,768]{1,0:T(8,128)S(1)} collective-permute-done((f32[96,768]{1,0:T(8,128)S(1)}, f32[96,768]{1,0:T(8,128)S(1)}, u32[]{:S(2)}, u32[]{:S(2)}) %collective-permute-start.76) | collective-permute-done | bytes 294944 | tf_op jit(solution)/shard_map/ppermute | solution.py:354
  592.6 6.0 copy.41
  (453 shorter events, 186.8 us)
Async XLA Ops:
  7.2 576.8 %all-gather.5.cloned.1.call-start = ((), (), s32[]{:S(2)}) async-start(), calls=%async_computation.1 | async-start | bytes 7864320 | tf_op jit(solution)/shard_map/all_gather | solution.py:515
  9.1 31.2 %collective-permute-start.22 = (f32[96,768]{1,0:T(8,128)}, f32[96,768]{1,0:T(8,128)S(1)}, u32[]{:S(2)}, u32[]{:S(2)}) collective-permute-start(f32[96,768]{1,0:T(8,128)} %dynamic-slice_convert_fusion.1), channel_id=1, source_target_pairs={{0,3},{1,0},{2,1},{3,2},{4,7},{5,4},{6,5},{7,6},{8,11},{9,8},{10,9... | collective-permute-start | bytes 884744 | tf_op jit(solution)/shard_map/ppermute | solution.py:354
  14.1 30.1 %collective-permute-start.20 = (f32[96,768]{1,0:T(8,128)}, f32[96,768]{1,0:T(8,128)}, u32[]{:S(2)}, u32[]{:S(2)}) collective-permute-start(f32[96,768]{1,0:T(8,128)} %dynamic-slice_convert_fusion.1), channel_id=1, source_target_pairs={{0,1},{1,2},{2,3},{3,0},{4,5},{5,6},{6,7},{7,4},{8,9},{9,10},{10,1... | collective-permute-start | bytes 884744 | tf_op jit(solution)/shard_map/ppermute | solution.py:354
  21.0 39.0 %collective-permute-start.39 = (f32[96,768]{1,0:T(8,128)S(1)}, f32[96,768]{1,0:T(8,128)S(1)}, u32[]{:S(2)}, u32[]{:S(2)}) collective-permute-start(f32[96,768]{1,0:T(8,128)S(1)} %dynamic-slice_convert_fusion), channel_id=1, source_target_pairs={{0,3},{1,0},{2,1},{3,2},{4,7},{5,4},{6,5},{7,6},{8,11},{9,8},{10,9... | collective-permute-start | bytes 884744 | tf_op jit(solution)/shard_map/ppermute | solution.py:354
  41.3 37.7 %collective-permute-start.38 = (f32[96,768]{1,0:T(8,128)S(1)}, f32[96,768]{1,0:T(8,128)S(1)}, u32[]{:S(2)}, u32[]{:S(2)}) collective-permute-start(f32[96,768]{1,0:T(8,128)S(1)} %dynamic-slice_convert_fusion), channel_id=1, source_target_pairs={{0,2},{1,3},{2,0},{3,1},{4,6},{5,7},{6,4},{7,5},{8,10},{9,11},{10,... | collective-permute-start | bytes 884744 | tf_op jit(solution)/shard_map/ppermute | solution.py:354
  44.2 34.8 %collective-permute-start.37 = (f32[96,768]{1,0:T(8,128)S(1)}, f32[96,768]{1,0:T(8,128)S(1)}, u32[]{:S(2)}, u32[]{:S(2)}) collective-permute-start(f32[96,768]{1,0:T(8,128)S(1)} %dynamic-slice_convert_fusion), channel_id=1, source_target_pairs={{0,1},{1,2},{2,3},{3,0},{4,5},{5,6},{6,7},{7,4},{8,9},{9,10},{10,1... | collective-permute-start | bytes 884744 | tf_op jit(solution)/shard_map/ppermute | solution.py:354
  60.1 30.5 %collective-permute-start.1 = (f32[96,768]{1,0:T(8,128)S(1)}, f32[96,768]{1,0:T(8,128)S(1)}, u32[]{:S(2)}, u32[]{:S(2)}) collective-permute-start(f32[96,768]{1,0:T(8,128)S(1)} %dynamic-slice_convert_fusion.2), channel_id=1, source_target_pairs={{0,2},{1,3},{2,0},{3,1},{4,6},{5,7},{6,4},{7,5},{8,10},{9,11},{10,... | collective-permute-start | bytes 884744 | tf_op jit(solution)/shard_map/ppermute | solution.py:354
  60.1 30.6 %collective-permute-start = (f32[96,768]{1,0:T(8,128)S(1)}, f32[96,768]{1,0:T(8,128)S(1)}, u32[]{:S(2)}, u32[]{:S(2)}) collective-permute-start(f32[96,768]{1,0:T(8,128)S(1)} %dynamic-slice_convert_fusion.2), channel_id=1, source_target_pairs={{0,1},{1,2},{2,3},{3,0},{4,5},{5,6},{6,7},{7,4},{8,9},{9,10},{10,1... | collective-permute-start | bytes 884744 | tf_op jit(solution)/shard_map/ppermute | solution.py:354
  195.3 29.1 %collective-permute-start.51 = (f32[3,48,768]{2,1,0:T(8,128)S(1)}, f32[3,48,768]{2,1,0:T(8,128)S(1)}, u32[]{:S(2)}, u32[]{:S(2)}) collective-permute-start(f32[3,48,768]{2,1,0:T(8,128)S(1)} %copy-done.37), channel_id=1, source_target_pairs={{0,4},{4,0},{8,12},{12,8},{16,20},{20,16},{24,28},{28,24},{1,5},{5... | collective-permute-start | bytes 1327112 | tf_op jit(solution)/shard_map/ppermute | solution.py:358
  195.4 29.0 %collective-permute-start.44 = (f32[3,48,768]{2,1,0:T(8,128)S(1)}, f32[3,48,768]{2,1,0:T(8,128)S(1)}, u32[]{:S(2)}, u32[]{:S(2)}) collective-permute-start(f32[3,48,768]{2,1,0:T(8,128)S(1)} %copy-done.39), channel_id=1, source_target_pairs={{0,4},{4,0},{8,12},{12,8},{16,20},{20,16},{24,28},{28,24},{1,5},{5... | collective-permute-start | bytes 1327112 | tf_op jit(solution)/shard_map/ppermute | solution.py:358
  195.9 28.5 %collective-permute-start.45 = (f32[3,48,768]{2,1,0:T(8,128)S(1)}, f32[3,48,768]{2,1,0:T(8,128)S(1)}, u32[]{:S(2)}, u32[]{:S(2)}) collective-permute-start(f32[3,48,768]{2,1,0:T(8,128)S(1)} %collective-permute-done.41.refs_2_), channel_id=1, source_target_pairs={{0,4},{4,0},{8,12},{12,8},{16,20},{20,16},{24,28},{28,24},{1,5},{5... | collective-permute-start | bytes 1327112 | tf_op jit(solution)/shard_map/ppermute | solution.py:358
  280.2 307.5 %all-gather.3.cloned.1.call-start = ((), (), s32[]{:S(2)}) async-start(), calls=%async_computation | async-start | bytes 7864320 | tf_op jit(solution)/shard_map/all_gather | solution.py:505
  285.1 70.2 %collective-permute-start.62 = (f32[384,768]{1,0:T(8,128)}, f32[384,768]{1,0:T(8,128)}, u32[]{:S(2)}, u32[]{:S(2)}) collective-permute-start(f32[384,768]{1,0:T(8,128)} %fusion.19), channel_id=1, source_target_pairs={{0,4},{4,0},{8,12},{12,8},{16,20},{20,16},{24,28},{28,24},{1,5},{5... | collective-permute-start | bytes 3538952 | tf_op jit(solution)/shard_map/ppermute | solution.py:358
  295.2 80.4 %collective-permute-start.54 = (f32[384,2304]{1,0:T(8,128)}, f32[384,2304]{1,0:T(8,128)}, u32[]{:S(2)}, u32[]{:S(2)}) collective-permute-start(f32[384,2304]{1,0:T(8,128)} %fusion.22), channel_id=1, source_target_pairs={{0,4},{4,0},{8,12},{12,8},{16,20},{20,16},{24,28},{28,24},{1,5},{5... | collective-permute-start | bytes 10616840 | tf_op jit(solution)/shard_map/ppermute | solution.py:358
  304.3 107.8 %collective-permute-start.78 = (f32[384,3072]{1,0:T(8,128)}, f32[384,3072]{1,0:T(8,128)}, u32[]{:S(2)}, u32[]{:S(2)}) collective-permute-start(f32[384,3072]{1,0:T(8,128)} %fusion.13), channel_id=1, source_target_pairs={{0,4},{4,0},{8,12},{12,8},{16,20},{20,16},{24,28},{28,24},{1,5},{5... | collective-permute-start | bytes 14155784 | tf_op jit(solution)/shard_map/ppermute | solution.py:358
  311.0 108.2 %collective-permute-start.70 = (f32[384,3072]{1,0:T(8,128)}, f32[384,3072]{1,0:T(8,128)}, u32[]{:S(2)}, u32[]{:S(2)}) collective-permute-start(f32[384,3072]{1,0:T(8,128)} %fusion.14), channel_id=1, source_target_pairs={{0,4},{4,0},{8,12},{12,8},{16,20},{20,16},{24,28},{28,24},{1,5},{5... | collective-permute-start | bytes 14155784 | tf_op jit(solution)/shard_map/ppermute | solution.py:358
  416.9 44.2 %collective-permute-start.82 = (f32[192,1536]{1,0:T(8,128)S(1)}, f32[192,1536]{1,0:T(8,128)S(1)}, u32[]{:S(2)}, u32[]{:S(2)}) collective-permute-start(f32[192,1536]{1,0:T(8,128)S(1)} %slice.479), channel_id=1, source_target_pairs={{0,16},{4,20},{8,24},{12,28},{16,0},{20,4},{24,8},{28,12},{1,17},{... | collective-permute-start | bytes 3538952 | tf_op jit(solution)/shard_map/ppermute | solution.py:358
  418.7 43.7 %collective-permute-start.79 = (f32[192,1536]{1,0:T(8,128)S(1)}, f32[192,1536]{1,0:T(8,128)S(1)}, u32[]{:S(2)}, u32[]{:S(2)}) collective-permute-start(f32[192,1536]{1,0:T(8,128)S(1)} %pad_maximum_fusion.4), channel_id=1, source_target_pairs={{0,8},{4,12},{8,0},{12,4},{16,24},{20,28},{24,16},{28,20},{1,9},{5... | collective-permute-start | bytes 3538952 | tf_op jit(solution)/shard_map/ppermute | solution.py:358
  425.4 29.4 %collective-permute-start.60 = (f32[96,576]{1,0:T(8,128)S(1)}, f32[96,576]{1,0:T(8,128)S(1)}, u32[]{:S(2)}, u32[]{:S(2)}) collective-permute-start(f32[96,576]{1,0:T(8,128)S(1)} %get-tuple-element.131), channel_id=1, source_target_pairs={{0,2},{1,3},{2,0},{3,1},{4,6},{5,7},{6,4},{7,5},{8,10},{9,11},{10,... | collective-permute-start | bytes 663560 | tf_op jit(solution)/shard_map/ppermute | solution.py:354
  432.1 29.0 %collective-permute-start.57 = (f32[96,576]{1,0:T(8,128)S(1)}, f32[96,576]{1,0:T(8,128)S(1)}, u32[]{:S(2)}, u32[]{:S(2)}) collective-permute-start(f32[96,576]{1,0:T(8,128)S(1)} %slice.423), channel_id=1, source_target_pairs={{0,3},{1,0},{2,1},{3,2},{4,7},{5,4},{6,5},{7,6},{8,11},{9,8},{10,9... | collective-permute-start | bytes 663560 | tf_op jit(solution)/shard_map/ppermute | solution.py:354
  454.8 28.9 %collective-permute-start.74 = (f32[192,1536]{1,0:T(8,128)S(1)}, f32[192,1536]{1,0:T(8,128)S(1)}, u32[]{:S(2)}, u32[]{:S(2)}) collective-permute-start(f32[192,1536]{1,0:T(8,128)S(1)} %slice.463), channel_id=1, source_target_pairs={{0,16},{4,20},{8,24},{12,28},{16,0},{20,4},{24,8},{28,12},{1,17},{... | collective-permute-start | bytes 3538952 | tf_op jit(solution)/shard_map/ppermute | solution.py:358
  456.0 29.2 %collective-permute-start.71 = (f32[192,1536]{1,0:T(8,128)S(1)}, f32[192,1536]{1,0:T(8,128)S(1)}, u32[]{:S(2)}, u32[]{:S(2)}) collective-permute-start(f32[192,1536]{1,0:T(8,128)S(1)} %pad_maximum_fusion.3), channel_id=1, source_target_pairs={{0,8},{4,12},{8,0},{12,4},{16,24},{20,28},{24,16},{28,20},{1,9},{5... | collective-permute-start | bytes 3538952 | tf_op jit(solution)/shard_map/ppermute | solution.py:358
  461.3 36.3 %collective-permute-start.83 = (f32[96,1536]{1,0:T(8,128)S(1)}, f32[96,1536]{1,0:T(8,128)S(1)}, u32[]{:S(2)}, u32[]{:S(2)}) collective-permute-start(f32[96,1536]{1,0:T(8,128)S(1)} %slice.481), channel_id=1, source_target_pairs={{0,8},{4,12},{8,0},{12,4},{16,24},{20,28},{24,16},{28,20},{1,9},{5... | collective-permute-start | bytes 1769480 | tf_op jit(solution)/shard_map/ppermute | solution.py:358
  462.6 49.1 %collective-permute-start.80 = (f32[96,1536]{1,0:T(8,128)S(1)}, f32[96,1536]{1,0:T(8,128)S(1)}, u32[]{:S(2)}, u32[]{:S(2)}) collective-permute-start(f32[96,1536]{1,0:T(8,128)S(1)} %slice.475), channel_id=1, source_target_pairs={{0,16},{4,20},{8,24},{12,28},{16,0},{20,4},{24,8},{28,12},{1,17},{... | collective-permute-start | bytes 1769480 | tf_op jit(solution)/shard_map/ppermute | solution.py:358
  483.9 31.7 %collective-permute-start.75 = (f32[96,1536]{1,0:T(8,128)S(1)}, f32[96,1536]{1,0:T(8,128)S(1)}, u32[]{:S(2)}, u32[]{:S(2)}) collective-permute-start(f32[96,1536]{1,0:T(8,128)S(1)} %slice.465), channel_id=1, source_target_pairs={{0,8},{4,12},{8,0},{12,4},{16,24},{20,28},{24,16},{28,20},{1,9},{5... | collective-permute-start | bytes 1769480 | tf_op jit(solution)/shard_map/ppermute | solution.py:358
  485.4 32.6 %collective-permute-start.72 = (f32[96,1536]{1,0:T(8,128)S(1)}, f32[96,1536]{1,0:T(8,128)S(1)}, u32[]{:S(2)}, u32[]{:S(2)}) collective-permute-start(f32[96,1536]{1,0:T(8,128)S(1)} %slice.459), channel_id=1, source_target_pairs={{0,16},{4,20},{8,24},{12,28},{16,0},{20,4},{24,8},{28,12},{1,17},{... | collective-permute-start | bytes 1769480 | tf_op jit(solution)/shard_map/ppermute | solution.py:358
  497.7 47.7 %collective-permute-start.84 = (f32[96,768]{1,0:T(8,128)S(1)}, f32[96,768]{1,0:T(8,128)S(1)}, u32[]{:S(2)}, u32[]{:S(2)}) collective-permute-start(f32[96,768]{1,0:T(8,128)S(1)} %get-tuple-element.127), channel_id=1, source_target_pairs={{0,2},{1,3},{2,0},{3,1},{4,6},{5,7},{6,4},{7,5},{8,10},{9,11},{10,... | collective-permute-start | bytes 884744 | tf_op jit(solution)/shard_map/ppermute | solution.py:354
  511.6 34.5 %collective-permute-start.85 = (f32[96,768]{1,0:T(8,128)S(1)}, f32[96,768]{1,0:T(8,128)S(1)}, u32[]{:S(2)}, u32[]{:S(2)}) collective-permute-start(f32[96,768]{1,0:T(8,128)S(1)} %get-tuple-element.128), channel_id=1, source_target_pairs={{0,1},{1,2},{2,3},{3,0},{4,5},{5,6},{6,7},{7,4},{8,9},{9,10},{10,1... | collective-permute-start | bytes 884744 | tf_op jit(solution)/shard_map/ppermute | solution.py:354
  511.7 38.8 %collective-permute-start.81 = (f32[96,768]{1,0:T(8,128)S(1)}, f32[96,768]{1,0:T(8,128)S(1)}, u32[]{:S(2)}, u32[]{:S(2)}) collective-permute-start(f32[96,768]{1,0:T(8,128)S(1)} %slice.477), channel_id=1, source_target_pairs={{0,3},{1,0},{2,1},{3,2},{4,7},{5,4},{6,5},{7,6},{8,11},{9,8},{10,9... | collective-permute-start | bytes 884744 | tf_op jit(solution)/shard_map/ppermute | solution.py:354
  515.7 67.4 %collective-permute-start.76 = (f32[96,768]{1,0:T(8,128)S(1)}, f32[96,768]{1,0:T(8,128)S(1)}, u32[]{:S(2)}, u32[]{:S(2)}) collective-permute-start(f32[96,768]{1,0:T(8,128)S(1)} %get-tuple-element.129), channel_id=1, source_target_pairs={{0,2},{1,3},{2,0},{3,1},{4,6},{5,7},{6,4},{7,5},{8,10},{9,11},{10,... | collective-permute-start | bytes 884744 | tf_op jit(solution)/shard_map/ppermute | solution.py:354
  517.9 65.2 %collective-permute-start.77 = (f32[96,768]{1,0:T(8,128)S(1)}, f32[96,768]{1,0:T(8,128)S(1)}, u32[]{:S(2)}, u32[]{:S(2)}) collective-permute-start(f32[96,768]{1,0:T(8,128)S(1)} %get-tuple-element.130), channel_id=1, source_target_pairs={{0,1},{1,2},{2,3},{3,0},{4,5},{5,6},{6,7},{7,4},{8,9},{9,10},{10,1... | collective-permute-start | bytes 884744 | tf_op jit(solution)/shard_map/ppermute | solution.py:354
  545.3 37.9 %collective-permute-start.73 = (f32[96,768]{1,0:T(8,128)S(1)}, f32[96,768]{1,0:T(8,128)S(1)}, u32[]{:S(2)}, u32[]{:S(2)}) collective-permute-start(f32[96,768]{1,0:T(8,128)S(1)} %slice.461), channel_id=1, source_target_pairs={{0,3},{1,0},{2,1},{3,2},{4,7},{5,4},{6,5},{7,6},{8,11},{9,8},{10,9... | collective-permute-start | bytes 884744 | tf_op jit(solution)/shard_map/ppermute | solution.py:354
  (146 other events, 2897.2 us)
Sparse Core Ops, SparseCore 0:
  280.3 123.0 all-gather.4
  405.0 182.6 all-gather.2

commit v3 on v2

v3 whole, which is shorter than its diff:
```python
import math
from functools import partial

import jax
import jax.numpy as jnp
from jax import lax
from jax.experimental import pallas as pl
from jax.experimental.pallas import tpu as pltpu
from jax.sharding import PartitionSpec as P

HEAD_DIM = 64
LENGTH = 512
EPSILON = 1e-12
F32 = jnp.float32
BF16 = jnp.bfloat16
SCALE = HEAD_DIM ** (-0.5)
EXP_SCALE = SCALE * 1.4426950408889634
ROWS = ((0,), (0,))
PLAIN = ((1,), (0,))
COLS = ((1,), (1,))


def dot(left, right, dims):
    return lax.dot_general(left, right, (dims, ((), ())), preferred_element_type=F32)


def norm_forward(values, gain, shift):
    center = values - jnp.mean(values, axis=-1, keepdims=True)
    inverse = lax.rsqrt(jnp.mean(center * center, axis=-1, keepdims=True) + EPSILON)
    normed = center * inverse
    return (normed * gain + shift, normed, inverse)


def norm_backward(upstream, gain, normed, inverse):
    scaled = upstream * gain
    first_mean = jnp.mean(scaled, axis=-1, keepdims=True)
    cross_mean = jnp.mean(scaled * normed, axis=-1, keepdims=True)
    return inverse * (scaled - first_mean - normed * cross_mean)


def row_sums(values):
    return jnp.sum(values, axis=0, keepdims=True)


def size_of(shape, dtype):
    return math.prod(shape) * jnp.dtype(dtype).itemsize


def call(kernel, name, grid, ins, outs, flops, exps=0, scratch=(), prefetch=None, moved=None):
    if moved is None:
        moved = sum(size_of(a.shape, a.dtype) for a, _, _ in ins) + sum(size_of(s, t) for s, t, _, _ in outs)
    lead = () if prefetch is None else (prefetch,)
    return pl.pallas_call(
        kernel,
        grid_spec=pltpu.PrefetchScalarGridSpec(
            num_scalar_prefetch=len(lead),
            grid=grid,
            in_specs=[pl.BlockSpec(b, m) for _, b, m in ins],
            out_specs=[pl.BlockSpec(b, m) for _, _, b, m in outs],
            scratch_shapes=list(scratch),
        ),
        out_shape=[jax.ShapeDtypeStruct(s, t) for s, t, _, _ in outs],
        cost_estimate=pl.CostEstimate(flops=flops, bytes_accessed=moved, transcendentals=exps),
        compiler_params=pltpu.CompilerParams(vmem_limit_bytes=56 << 20),
        name=name,
    )(*lead, *(a for a, _, _ in ins))


def attend_kernel(x_ref, w_ref, bias_ref, ctx_ref):
    cols = w_ref.shape[0] // 3
    parts = []
    qkv = (dot(x_ref[...], w_ref[...], COLS) + bias_ref[...]).astype(BF16)
    for h in range(cols // HEAD_DIM):
        q, k, v = (qkv[:, i * cols + h * HEAD_DIM : i * cols + (h + 1) * HEAD_DIM] for i in range(3))
        scores = dot(q, k, COLS)
        largest = jnp.max(scores, axis=-1, keepdims=True)
        expon = jnp.exp2((scores - largest) * EXP_SCALE)
        totals = jnp.sum(expon, axis=-1, keepdims=True)
        parts.append((dot(expon.astype(BF16), v, PLAIN) / totals).astype(BF16).astype(F32))
    context = jnp.concatenate(parts, axis=1)
    step = ctx_ref.shape[0]
    folds = [context[i * step : (i + 1) * step] for i in range(LENGTH // step)]
    ctx_ref[...] = jnp.concatenate(folds, axis=1)


def fold_of(cols):
    return 1 if cols % 128 == 0 else 2


def attend_forward(inputs, weights, bias):
    rows, width = inputs.shape
    cols = weights.shape[0] // 3
    fold = fold_of(cols)
    flat = lambda i: (0, 0)
    return call(
        attend_kernel,
        "attend_forward",
        (rows // LENGTH,),
        [
            (inputs, (LENGTH, width), lambda i: (i, 0)),
            (weights, weights.shape, flat),
            (bias, bias.shape, flat),
        ],
        [((rows // fold, fold * cols), F32, (LENGTH // fold, fold * cols), lambda i: (i, 0))],
        flops=rows * cols * (6 * width + 4 * LENGTH),
        exps=rows * LENGTH * (cols // HEAD_DIM),
    )[0]


def output_kernel(slot_ref, x_ref, ctx_ref, w_ref, vec_ref, low_ref, hid_ref, hbf_ref, nrm_ref, inv_ref):
    del slot_ref
    slot = pl.program_id(1)
    cols = low_ref.shape[-1]
    folds = [ctx_ref[:, i : i + cols] for i in range(0, ctx_ref.shape[-1], cols)]
    context = jnp.concatenate(folds, axis=0).astype(BF16)
    low_ref[...] = context
    attn = dot(context, w_ref[...], PLAIN)

    @pl.when(slot == 0)
    def _():
        hid_ref[...] = attn

    @pl.when(slot > 0)
    def _():
        hid_ref[...] += attn

    @pl.when(slot == pl.num_programs(1) - 1)
    def _():
        values = x_ref[...].astype(F32) + hid_ref[...] + vec_ref[0:1]
        hidden, normed, inverse = norm_forward(values, vec_ref[1:2], vec_ref[2:3])
        hid_ref[...] = hidden
        hbf_ref[...] = hidden.astype(BF16)
        nrm_ref[...] = normed
        inv_ref[...] = inverse


def output_forward(slots_at, x, context, weights, vectors):
    rows, width = x.shape
    slots, cols, _ = weights.shape
    mine = lambda i, j, at: (i, 0)
    flat = lambda i, j, at: (0, 0)
    token = (LENGTH, width)
    heads = (None, LENGTH, cols)
    return call(
        output_kernel,
        "output_forward",
        (rows // LENGTH, slots),
        [
            (x, token, mine),
            (context, (None, LENGTH // fold_of(cols), fold_of(cols) * cols), lambda i, j, at: (at[j], i, 0)),
            (weights, (None, cols, width), lambda i, j, at: (j, 0, 0)),
            (vectors, vectors.shape, flat),
        ],
        [
            ((slots, rows, cols), BF16, heads, lambda i, j, at: (j, i, 0)),
            ((rows, width), F32, token, mine),
            ((rows, width), BF16, token, mine),
            ((rows, width), F32, token, mine),
            ((rows, 1), F32, (LENGTH, 1), mine),
        ],
        flops=2 * rows * width * width,
        prefetch=slots_at,
    )


def attend_back_kernel(x_ref, ga_ref, gr_ref, w_ref, wo_ref, bias_ref, gqkv_ref, gx_ref, sum_ref):
    slot = pl.program_id(1)
    cols = wo_ref.shape[0]
    gctx = dot(ga_ref[...], wo_ref[...], COLS).astype(BF16)
    qkv = (dot(x_ref[...], w_ref[...], COLS) + bias_ref[...]).astype(BF16)
    for h in range(cols // HEAD_DIM):
        at = [slice(i * cols + h * HEAD_DIM, i * cols + (h + 1) * HEAD_DIM) for i in range(3)]
        q, k, v = (qkv[:, s] for s in at)
        g = gctx[:, at[0]]
        scores = dot(k, q, COLS)
        largest = jnp.max(scores, axis=0, keepdims=True)
        expon = jnp.exp2((scores - largest) * EXP_SCALE)
        probs = expon * (1.0 / row_sums(expon))
        gqkv_ref[:, at[2]] = dot(probs.astype(BF16), g, PLAIN).astype(BF16)
        weighted = probs * dot(v, g, COLS)
        grad_scores = (weighted - probs * row_sums(weighted)).astype(BF16)
        gqkv_ref[:, at[0]] = (dot(grad_scores, k, ROWS) * SCALE).astype(BF16)
        gqkv_ref[:, at[1]] = (dot(grad_scores, q, PLAIN) * SCALE).astype(BF16)
    grads = gqkv_ref[...]
    sum_ref[...] = row_sums(grads.astype(F32))
    back = dot(grads, w_ref[...], PLAIN)

    @pl.when(slot == 0)
    def _():
        gx_ref[...] = gr_ref[...] + back

    @pl.when(slot > 0)
    def _():
        gx_ref[...] += back


def attend_backward(x, grad_attn, grad_resid, weights, w_output, bias):
    rows, width = grad_attn.shape
    slots, cols, _ = w_output.shape
    mine = lambda i, j: (i, 0)
    token = (LENGTH, width)
    heads = (None, LENGTH, 3 * cols)
    weight = lambda i, j: (j, 0, 0)
    return call(
        attend_back_kernel,
        "attend_backward",
        (rows // LENGTH, slots),
        [
            (x, token, mine),
            (grad_attn, token, mine),
            (grad_resid, token, mine),
            (weights, (None, 3 * cols, width), weight),
            (w_output, (None, cols, width), weight),
            (bias, (None, 1, 3 * cols), weight),
        ],
        [
            ((slots, rows, 3 * cols), BF16, heads, lambda i, j: (j, i, 0)),
            ((rows, width), F32, token, mine),
            ((rows // LENGTH, slots, 1, 3 * cols), F32, (None, None, 1, 3 * cols), lambda i, j: (i, j, 0, 0)),
        ],
        flops=0,
        moved=0,
    )


def inner_kernel(h_ref, w_ref, b_ref, act_ref, slope_ref):
    inner = dot(h_ref[...], w_ref[...], PLAIN) + b_ref[...]
    phi = 0.5 + 0.5 * lax.erf(inner * (0.5**0.5))
    bell = jnp.exp2(inner * inner * (-0.5 * 1.4426950408889634)) * 0.3989422804014327
    act_ref[...] = (inner * phi).astype(BF16)
    slope_ref[...] = phi + inner * bell


def inner_forward(hidden, weights, bias):
    rows, width = hidden.shape
    slots, _, units = weights.shape
    slot = lambda i, j: (i, j, 0)
    block = LENGTH // 2
    return call(
        inner_kernel,
        "inner_forward",
        (slots, rows // block),
        [
            (hidden, (block, width), lambda i, j: (j, 0)),
            (weights, (None, width, units), lambda i, j: (i, 0, 0)),
            (bias, (None, 1, units), lambda i, j: (i, 0, 0)),
        ],
        [
            ((slots, rows, units), BF16, (None, block, units), slot),
            ((slots, rows, units), F32, (None, block, units), slot),
        ],
        flops=2 * rows * width * slots * units,
        exps=2 * rows * slots * units,
    )


def outer_kernel(act_ref, w_ref, hid_ref, cot_ref, vec_ref, out_ref, gr_ref, go_ref, sum_ref):
    slot = pl.program_id(1)
    outer = dot(act_ref[...], w_ref[...], PLAIN)

    @pl.when(slot == 0)
    def _():
        out_ref[...] = outer

    @pl.when(slot > 0)
    def _():
        out_ref[...] += outer

    @pl.when(slot == pl.num_programs(1) - 1)
    def _():
        gain = vec_ref[4:5]
        values = hid_ref[...] + (out_ref[...] + vec_ref[3:4])
        layer_out, normed, inverse = norm_forward(values, gain, vec_ref[5:6])
        out_ref[...] = layer_out
        upstream = cot_ref[...].astype(F32)
        grad = norm_backward(upstream, gain, normed, inverse)
        rounded = grad.astype(BF16)
        gr_ref[...] = grad
        go_ref[...] = rounded
        sum_ref[0:1] = row_sums(upstream * normed)
        sum_ref[1:2] = row_sums(upstream)
        sum_ref[2:3] = row_sums(rounded.astype(F32))


def outer_forward(active, weights, hidden, cotangent, vectors):
    rows, width = hidden.shape
    slots, units, _ = weights.shape
    mine = lambda i, j: (i, 0)
    flat = lambda i, j: (0, 0)
    token = (LENGTH, width)
    return call(
        outer_kernel,
        "outer_forward",
        (rows // LENGTH, slots),
        [
            (active, (None, LENGTH, units), lambda i, j: (j, i, 0)),
            (weights, (None, units, width), lambda i, j: (j, 0, 0)),
            (hidden, token, mine),
            (cotangent, token, mine),
            (vectors, vectors.shape, flat),
        ],
        [
            ((rows, width), F32, token, mine),
            ((rows, width), F32, token, mine),
            ((rows, width), BF16, token, mine),
            ((rows // LENGTH, 8, width), F32, (None, 8, width), lambda i, j: (i, 0, 0)),
        ],
        flops=2 * rows * width * slots * units,
    )


def inner_back_kernel(go_ref, wu_ref, slope_ref, wi_ref, gr_ref, nrm_ref, inv_ref, vec_ref,
                      gi_ref, g1_ref, ga_ref, bsum_ref, sum_ref):
    slot = pl.program_id(1)
    grad_inner = (dot(go_ref[...], wu_ref[...], COLS) * slope_ref[...]).astype(BF16)
    gi_ref[...] = grad_inner
    bsum_ref[...] = row_sums(grad_inner.astype(F32))
    back = dot(grad_inner, wi_ref[...], COLS)

    @pl.when(slot == 0)
    def _():
        g1_ref[...] = gr_ref[...] + back

    @pl.when(slot > 0)
    def _():
        g1_ref[...] += back

    @pl.when(slot == pl.num_programs(1) - 1)
    def _():
        upstream, normed = g1_ref[...], nrm_ref[...]
        grad = norm_backward(upstream, vec_ref[1:2], normed, inv_ref[...])
        rounded = grad.astype(BF16)
        g1_ref[...] = grad
        ga_ref[...] = rounded
        sum_ref[0:1] = row_sums(upstream * normed)
        sum_ref[1:2] = row_sums(upstream)
        sum_ref[2:3] = row_sums(rounded.astype(F32))


def inner_backward(grad_outer, w_outer, slope, w_inner, grad_resid2, normed, inverse, vectors):
    rows, width = grad_outer.shape
    slots, units, _ = w_outer.shape
    mine = lambda i, j: (i, 0)
    token = (LENGTH, width)
    slot = lambda i, j: (j, i, 0)
    weight = lambda i, j: (j, 0, 0)
    return call(
        inner_back_kernel,
        "inner_backward",
        (rows // LENGTH, slots),
        [
            (grad_outer, token, mine),
            (w_outer, (None, units, width), weight),
            (slope, (None, LENGTH, units), slot),
            (w_inner, (None, width, units), weight),
            (grad_resid2, token, mine),
            (normed, token, mine),
            (inverse, (LENGTH, 1), mine),
            (vectors, vectors.shape, lambda i, j: (0, 0)),
        ],
        [
            ((slots, rows, units), BF16, (None, LENGTH, units), slot),
            ((rows, width), F32, token, mine),
            ((rows, width), BF16, token, mine),
            ((rows // LENGTH, slots, 1, units), F32, (None, None, 1, units), lambda i, j: (i, j, 0, 0)),
            ((rows // LENGTH, 8, width), F32, (None, 8, width), lambda i, j: (i, 0, 0)),
        ],
        flops=0,
        moved=0,
    )


def narrow_kernel(x_ref, out_ref):
    out_ref[...] = x_ref[...].astype(BF16)


def narrow(values, block_rows):
    rows, width = values.shape
    at = lambda i: (i, 0)
    block = (block_rows, width)
    out = ((rows, width), BF16, block, at)
    return call(narrow_kernel, "narrow", (rows // block_rows,), [(values, block, at)], [out], 0)[0]


def shift_to(values, tensor, k):
    return lax.ppermute(values, "tensor", [(i, (i + k) % tensor) for i in range(tensor)])


def flip(values, bit):
    return lax.ppermute(values, "dp", [(i, i ^ bit) for i in range(8)])


def stage(*values):
    return lax.optimization_barrier(values)


def slots_kernel(slot_ref, local_ref, x_ref, out_ref):
    del slot_ref
    first = pl.program_id(0) == 0

    @pl.when(first)
    def _():
        out_ref[...] = local_ref[...]

    @pl.when(jnp.logical_not(first))
    def _():
        out_ref[...] = x_ref[...].reshape(out_ref.shape).astype(BF16)


def gather_plain(local, dp, tensor):
    rows, width = local.shape
    share = rows // dp
    piece = lax.dynamic_slice_in_dim(local, lax.axis_index("dp") * share, share, 0).astype(F32)
    full = lax.all_gather(piece, ("dp", "tensor"), axis=0).reshape(dp, tensor, share, width)
    order = (lax.axis_index("tensor") - jnp.arange(tensor, dtype=jnp.int32)) % tensor
    if share % 8:
        full = full.swapaxes(0, 1).reshape(1, tensor, rows, width)
    lead, _, part, _ = full.shape
    return pl.pallas_call(
        slots_kernel,
        grid_spec=pltpu.PrefetchScalarGridSpec(
            num_scalar_prefetch=1,
            grid=(tensor,),
            in_specs=[
                pl.BlockSpec((rows, width), lambda i, slot: (0, 0)),
                pl.BlockSpec((lead, None, part, width), lambda i, slot: (0, slot[i], 0, 0)),
            ],
            out_specs=pl.BlockSpec((None, rows, width), lambda i, slot: (i, 0, 0)),
        ),
        out_shape=jax.ShapeDtypeStruct((tensor, rows, width), BF16),
        cost_estimate=pl.CostEstimate(flops=0, bytes_accessed=6 * full.size, transcendentals=0),
        compiler_params=pltpu.CompilerParams(vmem_limit_bytes=48 << 20),
        name="slots",
    )(order, local, full)


def assemble_kernel(plan, *refs):
    where_ref, refs = refs[0], refs[1:]
    count = len(plan)
    targets = (len(refs) - count - 1) // 3
    locals_, pieces, outs, holds, sems = (
        refs[:targets],
        refs[targets : targets + count],
        refs[targets + count : 2 * targets + count],
        refs[2 * targets + count : -1],
        refs[-1],
    )
    copies = []
    for piece, spans in zip(pieces, plan):
        for i, source, rows, target in spans:
            start = pl.multiple_of(where_ref[len(copies)], 8)
            copies.append(
                pltpu.make_async_copy(
                    piece.at[i, :, pl.ds(source, rows)],
                    holds[target].at[:, pl.ds(start, rows)],
                    sems.at[len(copies)],
                )
            )
            copies[-1].start()
    for local, out in zip(locals_, outs):
        out[0] = local[...]
    for copy in copies:
        copy.wait()
    for hold, out in zip(holds, outs):
        for k in range(hold.shape[0]):
            out[k + 1] = hold[k].astype(BF16)


def assemble(locals_, pieces):
    width = locals_[0].shape[1]
    others = pieces[0][0].shape[1]
    where, plan = [], []
    for _, parts in pieces:
        plan.append([])
        for entry, sender, base, spans in parts:
            for row, rows, target, offset in spans:
                plan[-1].append((entry, base + row, rows, target))
                where.append(sender * (locals_[target].shape[0] // 8) + offset)
    total = sum(w.shape[0] for w in locals_)
    space = pl.BlockSpec(memory_space=pltpu.VMEM)
    return pl.pallas_call(
        partial(assemble_kernel, plan),
        in_specs=[pl.BlockSpec(memory_space=pltpu.SMEM)]
        + [space] * len(locals_)
        + [pl.BlockSpec(memory_space=pl.ANY)] * len(pieces),
        out_specs=[space] * len(locals_),
        out_shape=[jax.ShapeDtypeStruct((others + 1,) + w.shape, BF16) for w in locals_],
        scratch_shapes=[pltpu.VMEM((others,) + w.shape, F32) for w in locals_]
        + [pltpu.SemaphoreType.DMA((len(where),))],
        cost_estimate=pl.CostEstimate(flops=0, bytes_accessed=others * total * width * 6, transcendentals=0),
        compiler_params=pltpu.CompilerParams(vmem_limit_bytes=48 << 20),
        name="assemble",
    )(jnp.stack(where), *locals_, *(array for array, _ in pieces))


def shares(weights, dp=8):
    me = lax.axis_index("dp")
    cut = [lax.dynamic_slice_in_dim(w, me * (w.shape[0] // dp), w.shape[0] // dp, 0) for w in weights]
    return jnp.concatenate(cut, axis=0).astype(F32)


def across(values, tensor):
    return [shift_to(values, tensor, k) for k in range(1, tensor)]


def wide(v, w):
    return jnp.concatenate([v, w], axis=0)


def other_core(*values):
    return tuple(flip(v, 1) for v in values)


def halves(arrived, rows):
    return jnp.stack([v[:rows] for v in arrived])[None], jnp.stack([v[rows:] for v in arrived])[None]


def full_weights(locals_, a, b, ay, bx, c, d):
    me = lax.axis_index("dp")
    cut_at, end = a.shape[2], a.shape[2] + b.shape[2]
    ends = [0]
    for w in locals_:
        ends.append(ends[-1] + w.shape[0] // 8)

    def spans(first, last):
        found = []
        for target in range(len(locals_)):
            low, high = max(first, ends[target]), min(last, ends[target + 1])
            if low < high:
                found.append((low - first, high - low, target, low - ends[target]))
        return found

    upper = lambda rels: [(i, me ^ r, 0, spans(0, cut_at)) for i, r in enumerate(rels)]
    lower = lambda rels: [(i, me ^ r, 0, spans(cut_at, end)) for i, r in enumerate(rels)]
    pieces = [
        (a, upper((0, 2))),
        (b, lower((0, 4))),
        (ay, upper((4, 6))),
        (bx, lower((2, 6))),
        (c[0], upper((1, 3))),
        (c[1], lower((1, 5))),
        (d[0], upper((5, 7))),
        (d[1], lower((3, 7))),
    ]
    return assemble(locals_, pieces)


def block_order(width):
    me = lax.axis_index("dp")
    share = width // 8
    rel = jnp.array([7, 5, 3, 1, 6, 4, 2, 0])
    source = (me ^ rel[jnp.arange(width) // share]) * share + jnp.arange(width) % share
    return (lax.broadcasted_iota(jnp.int32, (width, width), 0) == source[None, :]).astype(BF16)


def grad_kernel(count, *refs):
    order_ref, refs = refs[0], refs[1:]
    lefts, rights, (send_ref, keep_ref), holds = (
        refs[:count], refs[count : 2 * count], refs[2 * count : 2 * count + 2], refs[2 * count + 2 :],
    )

    @pl.when(pl.program_id(0) == 0)
    def _():
        for left, hold in zip(lefts, holds):
            hold[...] = dot(left[...], order_ref[...], PLAIN).astype(BF16)

    half = send_ref.shape[0]
    start = 0
    for hold, right in zip(holds, rights):
        span = slice(start, start + right.shape[-1])
        value = dot(hold[...], right[...], ROWS)
        send_ref[:, span] = value[:half]
        keep_ref[:, span] = value[half:]
        start = span.stop


def grad_rows(order, pairs):
    rows, width = pairs[0][0].shape
    slots = pairs[0][1].shape[0]
    cols = sum(r.shape[-1] for _, r in pairs)
    flat = lambda j: (0, 0)
    ins = [(order, order.shape, flat)]
    ins += [(left, left.shape, flat) for left, _ in pairs]
    ins += [(right, (None,) + right.shape[1:], lambda j: (j, 0, 0)) for _, right in pairs]
    out = ((width // 2, slots * cols), F32, (width // 2, cols), lambda j: (0, j))
    scratch = [pltpu.VMEM((rows, width), BF16)] * len(pairs)
    return call(
        partial(grad_kernel, len(pairs)), "grad_rows", (slots,), ins, [out, out], 0, 0, scratch, moved=0
    )


def full_kernel(left_ref, right_ref, out_ref):
    out_ref[...] = dot(left_ref[...], right_ref[...], ROWS)


def grad_full(left, right):
    rows, width = left.shape
    slots, _, cols = right.shape
    return call(
        full_kernel,
        "grad_full",
        (slots,),
        [(left, left.shape, lambda j: (0, 0)), (right, (None, rows, cols), lambda j: (j, 0, 0))],
        [((width, slots * cols), F32, (width, cols), lambda j: (0, j))],
        flops=0,
        moved=0,
    )[0]


def split_paths(held, share):
    mid = held.shape[1] // 2
    pick = lambda i, cols: held[i * share : (i + 1) * share, cols]
    a, b = slice(None, mid), slice(mid, None)
    join = lambda i, j, cols: jnp.concatenate([pick(i, cols), pick(j, cols)], axis=0)
    return (join(0, 2, a), join(1, 3, a)), (join(0, 1, b), join(2, 3, b))


def columns_by_slot(left, right, tensor):
    part = jnp.concatenate([left, right], axis=1)
    cols = part.shape[1] // tensor
    return [part[:, k * cols : (k + 1) * cols] for k in range(tensor)]


def up(values, tensor, step):
    return lax.ppermute(values, "tensor", [(i, i + 1) for i in range(step)])


def down(values, tensor, step):
    return lax.ppermute(values, "tensor", [(i, i - 1) for i in range(tensor - step, tensor)])


def swap(values, tensor, bit):
    return lax.ppermute(values, "tensor", [(i, i ^ bit) for i in range(tensor)])


def scatter_plain(left, right, dp, tensor):
    grad = jnp.concatenate([dot(left, right[k], ROWS) for k in range(tensor)], axis=1)
    part = lax.psum_scatter(grad, "dp", scatter_dimension=0, tiled=True)
    cols = part.shape[1] // tensor
    part = [part[:, k * cols : (k + 1) * cols] for k in range(tensor)]
    return sum((shift_to(part[k], tensor, tensor - k) for k in range(1, tensor)), part[0])


def shards(
    dp,
    tensor,
    inputs,
    w_query,
    b_query,
    w_key,
    w_value,
    b_value,
    w_output,
    b_output,
    gain_attn,
    shift_attn,
    w_inner,
    b_inner,
    w_outer,
    b_outer,
    gain_ffn,
    shift_ffn,
    cotangent,
):
    tok_rows, width = inputs.shape
    own_rows = tok_rows // tensor
    cols = w_query.shape[1]
    z = lax.axis_index("tensor")
    own = lambda a: lax.dynamic_slice_in_dim(a, z * own_rows, own_rows, 0)
    row = lambda a: a.astype(F32)[None, :]

    vectors = row(jnp.concatenate([b_query, jnp.zeros_like(b_query), b_value, b_inner]))
    qkv_local = jnp.concatenate([w_query.T, w_key.T, w_value.T], axis=0)
    x, cot = own(inputs), own(cotangent)
    rows_of = (b_output, gain_attn, shift_attn, b_outer, gain_ffn, shift_ffn, b_outer, b_outer)
    wide_vectors = jnp.stack(rows_of).astype(F32)
    slots_at = (z - jnp.arange(tensor, dtype=jnp.int32)) % tensor
    staged = (
        dp == 8 and tensor == 4 and own_rows == LENGTH and width % 128 == 0
        and w_inner.shape == w_outer.shape == (width, width) and cols % 64 == 0
    )

    def rest_of_attention(context, weights):
        return output_forward(slots_at, x, context, weights, wide_vectors)

    def outer_half(active, weights, hidden):
        return outer_forward(active, weights, hidden, cot, wide_vectors)

    def small_sums(qkv_sums, inner_sums, sums_one, sums_two):
        by_slot = jnp.concatenate([jnp.sum(qkv_sums, axis=0), jnp.sum(inner_sums, axis=0)], axis=-1)
        by_place = by_slot[slots_at].reshape(-1)
        rest = jnp.concatenate([jnp.sum(sums_one, axis=0)[:3], jnp.sum(sums_two, axis=0)[:3]]).reshape(-1)
        return jnp.concatenate([by_place, rest])

    local_bias = vectors[:, : 3 * cols]
    context = attend_forward(inputs, qkv_local, local_bias)
    context = context.reshape(tensor, -1, context.shape[1])
    if not staged:
        vectors = jnp.stack([vectors] + across(vectors, tensor))
        qkv_bias, inner_bias = vectors[..., : 3 * cols], vectors[..., 3 * cols :]
        inner_full, output_full, outer_full, qkv_full = (
            gather_plain(w, dp, tensor) for w in (w_inner, w_output, w_outer, qkv_local)
        )
        context = lax.all_to_all(context, "tensor", 0, 0, tiled=True)
        context, hidden, hidden_bf, normed, inverse = rest_of_attention(context, output_full)
        active, slope = inner_forward(hidden_bf, inner_full, inner_bias)
        layer_out, grad_resid2, grad_outer, sums_two = outer_half(active, outer_full, hidden)
        layer_out = lax.all_gather(layer_out, "tensor", axis=0, tiled=True)
        grad_inner, grad_resid1, grad_attn, inner_sums, sums_one = inner_backward(
            grad_outer, outer_full, slope, inner_full, grad_resid2, normed, inverse, wide_vectors
        )
        grad_qkv, grad_x, qkv_sums = attend_backward(x, grad_attn, grad_resid1, qkv_full, output_full, qkv_bias)
        grad_inputs = lax.all_gather(grad_x, "tensor", axis=0, tiled=True)
        gu = scatter_plain(grad_outer, active, dp, tensor)
        gi = scatter_plain(hidden_bf, grad_inner, dp, tensor)
        go = scatter_plain(grad_attn, context, dp, tensor)
        gqkv = scatter_plain(x, grad_qkv, dp, tensor)
        sums = lax.psum(small_sums(qkv_sums, inner_sums, sums_one, sums_two), ("dp", "tensor"))
    else:
        order = block_order(width)
        share = width // 8
        p1, p2, p3 = shares([w_inner, w_output]), shares([w_outer]), shares([qkv_local])
        n1, n2, n3 = (-(-p.shape[0] // 16) * 8 for p in (p1, p2, p3))

        z1, arrived = across(p1, tensor), across(vectors, tensor)
        vectors = jnp.stack([vectors] + arrived)
        a1, b1 = halves(z1, n1)
        a1, b1, p2, context, vectors = stage(a1, b1, p2, context, vectors)
        qkv_bias, inner_bias = vectors[..., : 3 * cols], vectors[..., 3 * cols :]

        ax, by, z2 = flip(a1, 2), flip(b1, 4), across(p2, tensor)
        a1, b1, (a2, b2) = wide(a1, ax), wide(b1, by), halves(z2, n2)
        a1, b1, a2, b2, context, x, order = stage(a1, b1, a2, b2, context, x, order)

        c1 = other_core(a1, b1)
        context, *c1 = stage(context, *c1)
        context = lax.all_to_all(context, "tensor", 0, 0, tiled=True)
        ay1, bx1, ax, by = flip(a1, 4), flip(b1, 2), flip(a2, 2), flip(b2, 4)
        a2, b2 = wide(a2, ax), wide(b2, by)
        ay1, bx1, a2, b2, context, p3 = stage(ay1, bx1, a2, b2, context, p3)

        d1, ay2, bx2 = other_core(ay1, bx1), flip(a2, 4), flip(b2, 2)
        inner_full, output_full = full_weights([w_inner, w_output], a1, b1, ay1, bx1, c1, d1)
        context, hidden, hidden_bf, normed, inverse = rest_of_attention(context, output_full)
        ay2, bx2, p3, hidden_bf = stage(ay2, bx2, p3, hidden_bf)

        c2, d2, z3 = other_core(a2, b2), other_core(ay2, bx2), across(p3, tensor)
        active, slope = inner_forward(hidden_bf, inner_full, inner_bias)
        *c2, dx, dy, active = stage(*c2, *d2, active)
        (outer_full,) = full_weights([w_outer], a2, b2, ay2, bx2, c2, (dx, dy))
        layer_out, grad_resid2, grad_outer, sums_two = outer_half(active, outer_full, hidden)
        a3, b3 = halves(z3, n3)
        a3, b3, layer_out, grad_outer = stage(a3, b3, layer_out, grad_outer)

        layer_out = lax.all_gather(layer_out, "tensor", axis=0, tiled=True)
        ax, by = flip(a3, 2), flip(b3, 4)
        part1 = grad_full(grad_outer, active)
        a3, b3 = wide(a3, ax), wide(b3, by)
        a3, b3, part1, grad_outer = stage(a3, b3, part1, grad_outer)

        part1 = lax.psum_scatter(part1, "dp", scatter_dimension=0, tiled=True)
        ay3, bx3, c3 = flip(a3, 4), flip(b3, 2), other_core(a3, b3)
        grad_inner, grad_resid1, grad_attn, inner_sums, sums_one = inner_backward(
            grad_outer, outer_full, slope, inner_full, grad_resid2, normed, inverse, wide_vectors
        )
        ay3, bx3, grad_inner, grad_attn = stage(ay3, bx3, grad_inner, grad_attn)

        d3 = other_core(ay3, bx3)
        part2 = grad_full(hidden_bf, grad_inner)
        *d3, part2, grad_attn = stage(*d3, part2, grad_attn)

        part2 = lax.psum_scatter(part2, "dp", scatter_dimension=0, tiled=True)
        (qkv_full,) = full_weights([qkv_local], a3, b3, ay3, bx3, c3, d3)
        grad_qkv, grad_x, qkv_sums = attend_backward(x, grad_attn, grad_resid1, qkv_full, output_full, qkv_bias)
        grad_qkv, grad_x = stage(grad_qkv, grad_x)

        grad_inputs = lax.all_gather(grad_x, "tensor", axis=0, tiled=True)
        send, keep = grad_rows(order, [(x, grad_qkv), (grad_attn, context)])
        extra = small_sums(qkv_sums, inner_sums, sums_one, sums_two)
        extra = jnp.pad(extra, (0, -extra.shape[0] % (8 * width))).reshape(-1, width)
        send, extra = stage(send, extra)

        got = flip(send, 1)
        extra = extra + flip(extra, 1)
        (a, ak), (b, bk) = split_paths(keep + got, share)
        a, b, extra, layer_out = stage(a, b, extra, layer_out)

        ax, by = flip(a, 2), flip(b, 4)
        extra = extra + flip(extra, 2)
        a, b = ak + ax, bk + by
        a_send, b_send, extra = stage(a[:share], b[:share], extra)

        ay, bx = flip(a_send, 4), flip(b_send, 2)
        extra = extra + flip(extra, 4)
        part3 = jnp.concatenate([a[share:] + ay, b[share:] + bx], axis=1)
        parts = wide(wide(part1, part2), part3)
        parts = [parts[:, k * width : (k + 1) * width] for k in range(tensor)]
        u, d, extra = stage(parts[1], parts[3], extra)

        u, d = up(u, tensor, 1), down(d, tensor, 1)
        extra = extra + swap(extra, tensor, 1)
        u, d, extra = stage(parts[2] + u, parts[2] + d, extra)

        u, d = up(u, tensor, 2), down(d, tensor, 2)
        extra = extra + swap(extra, tensor, 2)
        u, d = stage(parts[3] + u, parts[1] + d)

        parts = parts[0] + up(u, tensor, 3) + down(d, tensor, 3)
        gu, gi, gqkv = parts[:share], parts[share : 2 * share], parts[2 * share :]
        gqkv, go = gqkv[:, : 3 * cols], gqkv[:, 3 * cols :]
        sums = extra.reshape(-1)

    layer_out = narrow(layer_out, own_rows)
    span = 3 * cols + w_inner.shape[1]
    mine = lax.dynamic_slice_in_dim(sums, z * span, span, 0)
    rest = sums[span * tensor :][: 6 * width].reshape(6, width)
    return (
        layer_out,
        grad_inputs,
        gqkv[:, :cols],
        mine[:cols],
        gqkv[:, cols : 2 * cols],
        gqkv[:, 2 * cols :],
        mine[2 * cols : 3 * cols],
        go.T,
        rest[2],
        rest[0],
        rest[1],
        gi,
        mine[3 * cols :],
        gu.T,
        rest[5],
        rest[3],
        rest[4],
    )


def solution(mesh):
    wide, tall, vector = P(None, "tensor"), P("tensor", None), P("tensor")
    tokens, both = P("dp", None), P("dp", "tensor")
    in_specs = (
        tokens, wide, vector, wide, wide, vector, tall, P(), P(), P(), wide, vector, tall, P(), P(), P(), tokens,
    )
    out_specs = (
        tokens, tokens, both, vector, both, both, vector, P("tensor", "dp"), P(), P(), P(), both, vector,
        P("tensor", "dp"), P(), P(), P(),
    )
    body = partial(shards, mesh.shape["dp"], mesh.shape["tensor"])
    return jax.shard_map(body, mesh=mesh, in_specs=in_specs, out_specs=out_specs, check_vma=False)
```

time: 613 us -> 516 us (0.84)
  blocking collectives: 44 us -> 0 us
  starting transfers between devices: 109 us -> 69.8 us
  matrix products: 33.5 us -> 0 us
  Pallas kernels: 100 us -> 132 us
  waiting for transfers between devices: 254 us -> 231 us
  other arithmetic: 13.8 us -> 29.7 us
    ppermute x24 -> x12, waiting for transfers between devices: 138 us -> 25.9 us  [shift_to(): lax.ppermute(values, 'tensor', [(i, (i + k) % tensor) for i in range(tens...]
    ppermute x0 -> x8, waiting for transfers between devices: none -> 73.1 us  [the longest x2 55.2 us: swap(): return lax.ppermute(values, 'tensor', [(i, i ^ bit) for i in range(tensor)])]
    ppermute x24 -> x12, starting transfers between devices: 65.7 us -> 20.9 us  [shift_to(): lax.ppermute(values, 'tensor', [(i, (i + k) % tensor) for i in range(tens...]
    psum x1 -> x0, blocking collectives: 44 us -> none  [shards(): sums = lax.psum(jnp.concatenate([by_place, rest]), ('dp', 'tensor'))]
    dot_general x12 -> x0, matrix products: 33.5 us -> none  [dot(): lax.dot_general(left, right, (dims, ((), ())), preferred_element_type=F32)]
    pallas_call x9 -> x13, Pallas kernels: 100 us -> 132 us  [the longest x10 114 us: call(): pl.pallas_call(kernel, grid_spec=pltpu.PrefetchScalarGridSpec(num_scalar_...]
    ppermute x62 -> x32, starting transfers between devices: 43.6 us -> 23.3 us  [flip(): return lax.ppermute(values, 'dp', [(i, i ^ bit) for i in range(8)])]
    ppermute x0 -> x8, starting transfers between devices: none -> 17 us  [the longest x3 12.1 us: up(): return lax.ppermute(values, 'tensor', [(i, i + 1) for i in range(step)])]
  transfers between devices with their start and end apart: 88 -> 57, of which waited for: 28 -> 20; matrix products, arithmetic and copies ran while one was open for 11% -> 8% of each run, Pallas kernels for 7% -> 23%
where the time goes in v3:
time: 516 us; the launch traced here: 514 us
  waiting for transfers between devices  231 us (45%)
  Pallas kernels  132 us (26%)
  starting transfers between devices  69.8 us (14%)
  local copies, waits for them, and re-layouts  35.5 us (7%)
  other arithmetic  29.7 us (6%)
  between operations  16.4 us (3%)
    ppermute x32, waiting for transfers between devices, flip(): return lax.ppermute(values, 'dp', [(i, i ^ bit) for i in range(8)])  125 us
    pallas_call x10, Pallas kernels, call(): pl.pallas_call(kernel, grid_spec=pltpu.PrefetchScalarGridSpec(num_scalar_...  114 us
    ppermute x2, waiting for transfers between devices, swap(): return lax.ppermute(values, 'tensor', [(i, i ^ bit) for i in range(tensor)])  55.2 us
    ppermute x12, waiting for transfers between devices, shift_to(): lax.ppermute(values, 'tensor', [(i, (i + k) % tensor) for i in range(tens...  25.9 us
    ppermute x32, starting transfers between devices, flip(): return lax.ppermute(values, 'dp', [(i, i ^ bit) for i in range(8)])  23.3 us
    ppermute x12, starting transfers between devices, shift_to(): lax.ppermute(values, 'tensor', [(i, (i + k) % tensor) for i in range(tens...  20.9 us
    ppermute x3, waiting for transfers between devices, up(): return lax.ppermute(values, 'tensor', [(i, i + 1) for i in range(step)])  17.9 us
    pallas_call x3, Pallas kernels, assemble(): pl.pallas_call(partial(assemble_kernel, plan), in_specs=[pl.BlockSpec(mem...  17.8 us
  transfers between devices with their start and end apart: 57, of which 20 were waited for; matrix products, arithmetic and copies ran while one was open for 8% of the time, Pallas kernels for 23%

profile of v3, /device:TPU:0, one launch (start us, length us, event | category | flops | bytes accessed | tf_op | source)
XLA Modules:
  0.0 514.3 jit_solution(12899460194261907092)
XLA Ops:
  10.7 5.0 collective-permute-start.2
  26.5 11.6 %attend_forward.1 = f32[1024,384]{1,0:T(8,128)} custom-call(bf16[2048,768]{1,0:T(8,128)(2,1)} %x_ref.1, bf16[576,768]{1,0:T(8,128)(2,1)} %pad_maximum_fusion.3.w_ref.refs_1_, f32[1,576]{1,0:T(1,128)} %slice.250.bias_ref), custom_call_target="tpu_custom_call" | custom-call | flops 2617245696 | bytes 5605632 | tf_op jit(solution)/shard_map/attend_forward/pallas_call | solution.py:53
  42.6 8.4 %collective-permute-done = f32[120,768]{1,0:T(8,128)S(1)} collective-permute-done((f32[120,768]{1,0:T(8,128)}, f32[120,768]{1,0:T(8,128)S(1)}, u32[]{:S(2)}, u32[]{:S(2)}) %collective-permute-start) | collective-permute-done | bytes 368672 | tf_op jit(solution)/shard_map/ppermute | solution.py:386
  64.0 9.1 %collective-permute-done.9 = f32[96,768]{1,0:T(8,128)S(1)} collective-permute-done((f32[96,768]{1,0:T(8,128)S(1)}, f32[96,768]{1,0:T(8,128)S(1)}, u32[]{:S(2)}, u32[]{:S(2)}) %collective-permute-start.9) | collective-permute-done | bytes 294944 | tf_op jit(solution)/shard_map/ppermute | solution.py:386
  75.5 3.5 collective-permute-done.16.refs_8_
  80.1 8.2 %all-to-all-start = ((f32[4,256,384]{2,1,0:T(8,128)}), f32[4,256,384]{2,1,0:T(8,128)}, u32[]{:S(2)}, u32[]{:S(2)}) async-start(f32[4,256,384]{2,1,0:T(8,128)} %bitcast.119), calls=%async_computation | async-start | bytes 3145728 | tf_op jit(solution)/shard_map/all_to_all | solution.py:737
  94.0 31.8 %collective-permute-done.14 = f32[1,3,48,768]{3,2,1,0:T(8,128)} collective-permute-done((f32[1,3,48,768]{3,2,1,0:T(8,128)}, f32[1,3,48,768]{3,2,1,0:T(8,128)}, u32[]{:S(2)}, u32[]{:S(2)}) %collective-permute-start.14) | collective-permute-done | bytes 442400 | tf_op jit(solution)/shard_map/ppermute | solution.py:390
  138.5 7.1 %assemble.3 = (bf16[4,768,768]{2,1,0:T(8,128)(2,1)}, bf16[4,192,768]{2,1,0:T(8,128)(2,1)S(1)}) custom-call(s32[24]{0:T(128)S(1)} %stack.312.refs_0_, bf16[768,768]{1,0:T(8,128)(2,1)} %refs_1_.2, bf16[192,768]{1,0:T(8,128)(2,1)S(1)} %copy-done.16, f32[2,3,64,768]{3,2,1,0:T(8,128)} %copy-done.19, f32[2,3,56,768]{3,2,1,0:T(8,128)S(1)} %copy-done.4, ...), custom_call_target="tpu_custom_call" | custom-call | bytes 13271040 | tf_op jit(solution)/shard_map/assemble/pallas_call | solution.py:481
  146.6 7.8 %output_forward.1 = (bf16[4,512,192]{2,1,0:T(8,128)(2,1)}, f32[512,768]{1,0:T(8,128)}, bf16[512,768]{1,0:T(8,128)(2,1)}, f32[512,768]{1,0:T(8,128)}, f32[512,1]{1,0:T(8,128)}) custom-call(s32[4]{0:T(128)} %and_select_fusion.2.slot_ref, bf16[512,768]{1,0:T(8,128)(2,1)} %constant_dynamic-slice_fusion.1.x_ref.refs_1_, f32[4,256,384]{2,1,0:T(8,128)} %all-to-all-done.ctx_ref, ...), custom_call_target="tpu_custom_call" | custom-call | flops 603979776 | bytes 8284160 | tf_op jit(solution)/shard_map/output_forward/pallas_call | solution.py:53
  154.4 3.6 collective-permute-start.23
  159.2 12.2 %inner_forward.1 = (bf16[4,512,768]{2,1,0:T(8,128)(2,1)}, f32[4,512,768]{2,1,0:T(8,128)}) custom-call(bf16[512,768]{1,0:T(8,128)(2,1)} %get-tuple-element.130.h_ref.left_ref, bf16[4,768,768]{2,1,0:T(8,128)(2,1)} %get-tuple-element.131.w_ref.wi_ref, f32[4,1,768]{2,1,0:T(1,128)} %slice.200.b_ref), custom_call_target="tpu_custom_call" | custom-call | flops 2415919104 | bytes 14954496 | tf_op jit(solution)/shard_map/inner_forward/pallas_call | solution.py:53
  171.5 7.1 %collective-permute-done.22 = f32[72,768]{1,0:T(8,128)S(1)} collective-permute-done((f32[72,768]{1,0:T(8,128)S(1)}, f32[72,768]{1,0:T(8,128)S(1)}, u32[]{:S(2)}, u32[]{:S(2)}) %collective-permute-start.22) | collective-permute-done | bytes 221216 | tf_op jit(solution)/shard_map/ppermute | solution.py:386
  182.1 6.0 %assemble.4.w_ref.wu_ref = bf16[4,768,768]{2,1,0:T(8,128)(2,1)} custom-call(s32[16]{0:T(128)S(1)} %stack.336.refs_0_, bf16[768,768]{1,0:T(8,128)(2,1)} %refs_1_.3, f32[2,3,48,768]{3,2,1,0:T(8,128)S(1)} %copy-done.7, f32[2,3,48,768]{3,2,1,0:T(8,128)S(1)} %copy-done.6, f32[2,3,48,768]{3,2,1,0:T(8,128)} %collective-permute-done.17.refs_4_, ...), custom_call_target="tpu_custom_call" | custom-call | bytes 10616832 | tf_op jit(solution)/shard_map/assemble/pallas_call | solution.py:481
  188.1 10.0 %outer_forward.1 = (f32[512,768]{1,0:T(8,128)}, f32[512,768]{1,0:T(8,128)}, bf16[512,768]{1,0:T(8,128)(2,1)}, f32[1,8,768]{2,1,0:T(8,128)}) custom-call(bf16[4,512,768]{2,1,0:T(8,128)(2,1)} %get-tuple-element.134.act_ref.right_ref, bf16[4,768,768]{2,1,0:T(8,128)(2,1)} %assemble.4.w_ref.wu_ref, f32[512,768]{1,0:T(8,128)} %get-tuple-element.139.hid_ref, ...), custom_call_target="tpu_custom_call" | custom-call | flops 2415919104 | bytes 14204928 | tf_op jit(solution)/shard_map/outer_forward/pallas_call | solution.py:53
  199.3 7.9 %grad_full.2 = f32[768,3072]{1,0:T(8,128)} custom-call(bf16[512,768]{1,0:T(8,128)(2,1)} %get-tuple-element.147.left_ref.go_ref, bf16[4,512,768]{2,1,0:T(8,128)(2,1)} %get-tuple-element.134.act_ref.right_ref), custom_call_target="tpu_custom_call" | custom-call | tf_op jit(solution)/shard_map/grad_full/pallas_call | solution.py:53
  211.4 16.7 %inner_backward.1 = (bf16[4,512,768]{2,1,0:T(8,128)(2,1)}, f32[512,768]{1,0:T(8,128)}, bf16[512,768]{1,0:T(8,128)(2,1)}, f32[1,4,1,768]{3,2,1,0:T(1,128)}, f32[1,8,768]{2,1,0:T(8,128)}) custom-call(bf16[512,768]{1,0:T(8,128)(2,1)} %get-tuple-element.147.left_ref.go_ref, bf16[4,768,768]{2,1,0:T(8,128)(2,1)} %assemble.4.w_ref.wu_ref, ...), custom_call_target="tpu_custom_call" | custom-call | tf_op jit(solution)/shard_map/inner_backward/pallas_call | solution.py:53
  228.7 7.6 %grad_full.3 = f32[768,3072]{1,0:T(8,128)} custom-call(bf16[512,768]{1,0:T(8,128)(2,1)} %get-tuple-element.130.h_ref.left_ref, bf16[4,512,768]{2,1,0:T(8,128)(2,1)} %get-tuple-element.156.right_ref), custom_call_target="tpu_custom_call" | custom-call | tf_op jit(solution)/shard_map/grad_full/pallas_call | solution.py:53
  244.1 4.7 assemble.5.w_ref
  248.9 25.2 %attend_backward.1 = (bf16[4,512,576]{2,1,0:T(8,128)(2,1)}, f32[512,768]{1,0:T(8,128)}, f32[1,4,1,576]{3,2,1,0:T(1,128)}) custom-call(bf16[512,768]{1,0:T(8,128)(2,1)} %constant_dynamic-slice_fusion.1.x_ref.refs_1_, bf16[512,768]{1,0:T(8,128)(2,1)} %get-tuple-element.158.ga_ref.refs_2_, f32[512,768]{1,0:T(8,128)} %get-tuple-element.159.gr_ref, ...), custom_call_target="tpu_custom_call" | custom-call | tf_op jit(solution)/shard_map/attend_backward/pallas_call | solution.py:53
  275.6 10.1 %grad_rows.1 = (f32[384,3072]{1,0:T(8,128)}, f32[384,3072]{1,0:T(8,128)}) custom-call(bf16[768,768]{1,0:T(8,128)(2,1)} %fusion.refs_0_, bf16[512,768]{1,0:T(8,128)(2,1)} %constant_dynamic-slice_fusion.1.x_ref.refs_1_, bf16[512,768]{1,0:T(8,128)(2,1)} %get-tuple-element.158.ga_ref.refs_2_, bf16[4,512,576]{2,1,0:T(8,128)(2,1)} %get-tuple-element.164.refs_3_, ...), custom_call_target="tpu_custom_call" | custom-call | tf_op jit(solution)/shard_map/grad_rows/pallas_call | solution.py:53
  286.2 4.5 collective-permute-done.37
  293.9 5.9 %add.241 = f32[384,3072]{1,0:T(8,128)S(1)} add(f32[384,3072]{1,0:T(8,128)} %get-tuple-element.166, f32[384,3072]{1,0:T(8,128)} %collective-permute-done.36) | non-fusion elementwise | flops 1179648 | bytes 14155776 | tf_op jit(solution)/shard_map/add | solution.py:785
  304.6 5.4 %all-gather.3.cloned.1.call-done.x_ref = f32[2048,768]{1,0:T(8,128)} async-done(((f32[512,768]{1,0:T(8,128)}), f32[2048,768]{1,0:T(8,128)}) %all-gather.3.cloned.1.call-update) | async-done | bytes 6291472 | tf_op jit(solution)/shard_map/all_gather | solution.py:755
  313.5 52.2 %collective-permute-done.40 = f32[16,768]{1,0:T(8,128)S(1)} collective-permute-done((f32[16,768]{1,0:T(8,128)S(1)}, f32[16,768]{1,0:T(8,128)S(1)}, u32[]{:S(2)}, u32[]{:S(2)}) %collective-permute-start.40) | collective-permute-done | bytes 49184 | tf_op jit(solution)/shard_map/ppermute | solution.py:390
  371.0 24.1 %collective-permute-done.43 = f32[16,768]{1,0:T(8,128)S(1)} collective-permute-done((f32[16,768]{1,0:T(8,128)S(1)}, f32[16,768]{1,0:T(8,128)S(1)}, u32[]{:S(2)}, u32[]{:S(2)}) %collective-permute-start.43) | collective-permute-done | bytes 49184 | tf_op jit(solution)/shard_map/ppermute | solution.py:390
  400.6 40.0 %collective-permute-done.46 = f32[16,768]{1,0:T(8,128)S(1)} collective-permute-done((f32[16,768]{1,0:T(8,128)S(1)}, f32[16,768]{1,0:T(8,128)S(1)}, u32[]{:S(2)}, u32[]{:S(2)}) %collective-permute-start.46) | collective-permute-done | bytes 49184 | tf_op jit(solution)/shard_map/ppermute | solution.py:633
  440.8 4.4 collective-permute-start.47
  446.0 17.9 %collective-permute-done.47 = f32[288,768]{1,0:T(8,128)S(1)} collective-permute-done((f32[288,768]{1,0:T(8,128)S(1)}, f32[288,768]{1,0:T(8,128)S(1)}, u32[]{:S(2)}, u32[]{:S(2)}) %collective-permute-start.47) | collective-permute-done | bytes 884768 | tf_op jit(solution)/shard_map/ppermute | solution.py:625
  465.2 6.4 %collective-permute-start.49 = (f32[288,768]{1,0:T(8,128)}, f32[288,768]{1,0:T(8,128)S(1)}, u32[]{:S(2)}, u32[]{:S(2)}) collective-permute-start(f32[288,768]{1,0:T(8,128)} %get-tuple-element.190), channel_id=1, source_target_pairs={{0,1},{1,2},{2,3},{4,5},{5,6},{6,7},{8,9},{9,10},{10,11},{12,13},{... | collective-permute-start | bytes 2654216 | tf_op jit(solution)/shard_map/ppermute | solution.py:625
  474.9 5.0 narrow.1
  479.9 15.3 %collective-permute-done.51 = f32[16,768]{1,0:T(8,128)S(1)} collective-permute-done((f32[16,768]{1,0:T(8,128)S(1)}, f32[16,768]{1,0:T(8,128)S(1)}, u32[]{:S(2)}, u32[]{:S(2)}) %collective-permute-start.51) | collective-permute-done | bytes 49184 | tf_op jit(solution)/shard_map/ppermute | solution.py:633
  500.8 6.0 %copy.41 = f32[2048,768]{1,0:T(8,128)} copy(f32[2048,768]{1,0:T(8,128)} %all-gather.5.cloned.1.call-done) | data formatting | bytes 12582912
  (279 shorter events, 107.3 us)
Async XLA Ops:
  10.7 30.9 %collective-permute-start.2 = (f32[120,768]{1,0:T(8,128)}, f32[120,768]{1,0:T(8,128)S(1)}, u32[]{:S(2)}, u32[]{:S(2)}) collective-permute-start(f32[120,768]{1,0:T(8,128)} %maximum_convert_fusion), channel_id=1, source_target_pairs={{0,3},{1,0},{2,1},{3,2},{4,7},{5,4},{6,5},{7,6},{8,11},{9,8},{10,9... | collective-permute-start | bytes 1105928 | tf_op jit(solution)/shard_map/ppermute | solution.py:386
  15.7 25.9 %collective-permute-start.1 = (f32[120,768]{1,0:T(8,128)}, f32[120,768]{1,0:T(8,128)}, u32[]{:S(2)}, u32[]{:S(2)}) collective-permute-start(f32[120,768]{1,0:T(8,128)} %maximum_convert_fusion), channel_id=1, source_target_pairs={{0,2},{1,3},{2,0},{3,1},{4,6},{5,7},{6,4},{7,5},{8,10},{9,11},{10,... | collective-permute-start | bytes 1105928 | tf_op jit(solution)/shard_map/ppermute | solution.py:386
  17.8 22.1 %collective-permute-start.3 = (f32[1,1344]{1,0:T(1,128)S(1)}, f32[1,1344]{1,0:T(1,128)}, u32[]{:S(2)}, u32[]{:S(2)}) collective-permute-start(f32[1,1344]{1,0:T(1,128)S(1)} %convert_element_type.38), channel_id=1, source_target_pairs={{0,1},{1,2},{2,3},{3,0},{4,5},{5,6},{6,7},{7,4},{8,9},{9,10},{10,1... | collective-permute-start | bytes 16136 | tf_op jit(solution)/shard_map/ppermute | solution.py:386
  18.9 21.9 %collective-permute-start.4 = (f32[1,1344]{1,0:T(1,128)S(1)}, f32[1,1344]{1,0:T(1,128)}, u32[]{:S(2)}, u32[]{:S(2)}) collective-permute-start(f32[1,1344]{1,0:T(1,128)S(1)} %convert_element_type.38), channel_id=1, source_target_pairs={{0,2},{1,3},{2,0},{3,1},{4,6},{5,7},{6,4},{7,5},{8,10},{9,11},{10,... | collective-permute-start | bytes 16136 | tf_op jit(solution)/shard_map/ppermute | solution.py:386
  20.9 19.9 %collective-permute-start.5 = (f32[1,1344]{1,0:T(1,128)S(1)}, f32[1,1344]{1,0:T(1,128)}, u32[]{:S(2)}, u32[]{:S(2)}) collective-permute-start(f32[1,1344]{1,0:T(1,128)S(1)} %convert_element_type.38), channel_id=1, source_target_pairs={{0,3},{1,0},{2,1},{3,2},{4,7},{5,4},{6,5},{7,6},{8,11},{9,8},{10,9... | collective-permute-start | bytes 16136 | tf_op jit(solution)/shard_map/ppermute | solution.py:386
  80.1 49.9 %all-to-all-start = ((f32[4,256,384]{2,1,0:T(8,128)}), f32[4,256,384]{2,1,0:T(8,128)}, u32[]{:S(2)}, u32[]{:S(2)}) async-start(f32[4,256,384]{2,1,0:T(8,128)} %bitcast.119), calls=%async_computation | async-start | bytes 3145728 | tf_op jit(solution)/shard_map/all_to_all | solution.py:737
  88.3 221.7 %all-gather.3.cloned.1.call-start = ((), (), s32[]{:S(2)}) async-start(), calls=%async_computation.3 | async-start | bytes 7864320 | tf_op jit(solution)/shard_map/all_gather | solution.py:755
  88.3 41.7 %collective-permute-start.11 = (f32[2,3,64,768]{3,2,1,0:T(8,128)}, f32[2,3,64,768]{3,2,1,0:T(8,128)}, u32[]{:S(2)}, u32[]{:S(2)}) collective-permute-start(f32[2,3,64,768]{3,2,1,0:T(8,128)} %copy-done.19), channel_id=1, source_target_pairs={{0,16},{4,20},{8,24},{12,28},{16,0},{20,4},{24,8},{28,12},{1,17},{... | collective-permute-start | bytes 3538952 | tf_op jit(solution)/shard_map/ppermute | solution.py:390
  89.8 40.2 %collective-permute-start.12 = (f32[2,3,56,768]{3,2,1,0:T(8,128)}, f32[2,3,56,768]{3,2,1,0:T(8,128)}, u32[]{:S(2)}, u32[]{:S(2)}) collective-permute-start(f32[2,3,56,768]{3,2,1,0:T(8,128)} %copy-done.3), channel_id=1, source_target_pairs={{0,8},{4,12},{8,0},{12,4},{16,24},{20,28},{24,16},{28,20},{1,9},{5... | collective-permute-start | bytes 3096584 | tf_op jit(solution)/shard_map/ppermute | solution.py:390
  91.3 34.5 %collective-permute-start.14 = (f32[1,3,48,768]{3,2,1,0:T(8,128)}, f32[1,3,48,768]{3,2,1,0:T(8,128)}, u32[]{:S(2)}, u32[]{:S(2)}) collective-permute-start(f32[1,3,48,768]{3,2,1,0:T(8,128)} %get-tuple-element.114), channel_id=1, source_target_pairs={{0,16},{4,20},{8,24},{12,28},{16,0},{20,4},{24,8},{28,12},{1,17},{... | collective-permute-start | bytes 1327112 | tf_op jit(solution)/shard_map/ppermute | solution.py:390
  91.8 36.2 %collective-permute-start.13 = (f32[1,3,48,768]{3,2,1,0:T(8,128)}, f32[1,3,48,768]{3,2,1,0:T(8,128)}, u32[]{:S(2)}, u32[]{:S(2)}) collective-permute-start(f32[1,3,48,768]{3,2,1,0:T(8,128)} %get-tuple-element.113), channel_id=1, source_target_pairs={{0,8},{4,12},{8,0},{12,4},{16,24},{20,28},{24,16},{28,20},{1,9},{5... | collective-permute-start | bytes 1327112 | tf_op jit(solution)/shard_map/ppermute | solution.py:390
  130.6 23.8 %collective-permute-start.17 = (f32[2,3,48,768]{3,2,1,0:T(8,128)}, f32[2,3,48,768]{3,2,1,0:T(8,128)}, u32[]{:S(2)}, u32[]{:S(2)}) collective-permute-start(f32[2,3,48,768]{3,2,1,0:T(8,128)} %pad_maximum_fusion.4.refs_2_), channel_id=1, source_target_pairs={{0,16},{4,20},{8,24},{12,28},{16,0},{20,4},{24,8},{28,12},{1,17},{... | collective-permute-start | bytes 2654216 | tf_op jit(solution)/shard_map/ppermute | solution.py:390
  132.2 22.3 %collective-permute-start.18 = (f32[2,3,48,768]{3,2,1,0:T(8,128)}, f32[2,3,48,768]{3,2,1,0:T(8,128)}, u32[]{:S(2)}, u32[]{:S(2)}) collective-permute-start(f32[2,3,48,768]{3,2,1,0:T(8,128)} %pad_maximum_fusion.5.refs_3_), channel_id=1, source_target_pairs={{0,8},{4,12},{8,0},{12,4},{16,24},{20,28},{24,16},{28,20},{1,9},{5... | collective-permute-start | bytes 2654216 | tf_op jit(solution)/shard_map/ppermute | solution.py:390
  136.8 41.9 %collective-permute-start.24 = (f32[2,3,48,768]{3,2,1,0:T(8,128)}, f32[2,3,48,768]{3,2,1,0:T(8,128)S(1)}, u32[]{:S(2)}, u32[]{:S(2)}) collective-permute-start(f32[2,3,48,768]{3,2,1,0:T(8,128)} %pad_maximum_fusion.4.refs_2_), channel_id=1, source_target_pairs={{0,4},{4,0},{8,12},{12,8},{16,20},{20,16},{24,28},{28,24},{1,5},{5... | collective-permute-start | bytes 2654216 | tf_op jit(solution)/shard_map/ppermute | solution.py:390
  136.8 41.9 %collective-permute-start.25 = (f32[2,3,48,768]{3,2,1,0:T(8,128)}, f32[2,3,48,768]{3,2,1,0:T(8,128)S(1)}, u32[]{:S(2)}, u32[]{:S(2)}) collective-permute-start(f32[2,3,48,768]{3,2,1,0:T(8,128)} %pad_maximum_fusion.5.refs_3_), channel_id=1, source_target_pairs={{0,4},{4,0},{8,12},{12,8},{16,20},{20,16},{24,28},{28,24},{1,5},{5... | collective-permute-start | bytes 2654216 | tf_op jit(solution)/shard_map/ppermute | solution.py:390
  158.0 20.5 %collective-permute-start.22 = (f32[72,768]{1,0:T(8,128)S(1)}, f32[72,768]{1,0:T(8,128)S(1)}, u32[]{:S(2)}, u32[]{:S(2)}) collective-permute-start(f32[72,768]{1,0:T(8,128)S(1)} %copy-done.24), channel_id=1, source_target_pairs={{0,2},{1,3},{2,0},{3,1},{4,6},{5,7},{6,4},{7,5},{8,10},{9,11},{10,... | collective-permute-start | bytes 663560 | tf_op jit(solution)/shard_map/ppermute | solution.py:386
  198.2 197.1 %reduce-scatter.3.cloned.1.call-start = ((), (), s32[]{:S(2)}) async-start(), calls=%async_computation.5 | async-start | bytes 10616832 | tf_op jit(solution)/shard_map/reduce_scatter | solution.py:761
  209.2 187.2 %reduce-scatter.5.cloned.1.call-start = ((), (), s32[]{:S(2)}) async-start(), calls=%async_computation.6 | async-start | bytes 10616832 | tf_op jit(solution)/shard_map/reduce_scatter | solution.py:772
  236.4 243.5 %all-gather.5.cloned.1.call-start = ((), (), s32[]{:S(2)}) async-start(), calls=%async_computation.4 | async-start | bytes 7864320 | tf_op jit(solution)/shard_map/all_gather | solution.py:777
  310.0 55.7 %collective-permute-start.39 = (f32[192,1536]{1,0:T(8,128)}, f32[192,1536]{1,0:T(8,128)S(1)}, u32[]{:S(2)}, u32[]{:S(2)}) collective-permute-start(f32[192,1536]{1,0:T(8,128)} %concatenate.107), channel_id=1, source_target_pairs={{0,16},{4,20},{8,24},{12,28},{16,0},{20,4},{24,8},{28,12},{1,17},{... | collective-permute-start | bytes 3538952 | tf_op jit(solution)/shard_map/ppermute | solution.py:390
  311.4 55.8 %collective-permute-start.38 = (f32[192,1536]{1,0:T(8,128)}, f32[192,1536]{1,0:T(8,128)S(1)}, u32[]{:S(2)}, u32[]{:S(2)}) collective-permute-start(f32[192,1536]{1,0:T(8,128)} %pad_maximum_fusion.1), channel_id=1, source_target_pairs={{0,8},{4,12},{8,0},{12,4},{16,24},{20,28},{24,16},{28,20},{1,9},{5... | collective-permute-start | bytes 3538952 | tf_op jit(solution)/shard_map/ppermute | solution.py:390
  312.9 52.7 %collective-permute-start.40 = (f32[16,768]{1,0:T(8,128)S(1)}, f32[16,768]{1,0:T(8,128)S(1)}, u32[]{:S(2)}, u32[]{:S(2)}) collective-permute-start(f32[16,768]{1,0:T(8,128)S(1)} %add.242), channel_id=1, source_target_pairs={{0,8},{4,12},{8,0},{12,4},{16,24},{20,28},{24,16},{28,20},{1,9},{5... | collective-permute-start | bytes 147464 | tf_op jit(solution)/shard_map/ppermute | solution.py:390
  367.4 27.6 %collective-permute-start.41 = (f32[96,1536]{1,0:T(8,128)S(1)}, f32[96,1536]{1,0:T(8,128)S(1)}, u32[]{:S(2)}, u32[]{:S(2)}) collective-permute-start(f32[96,1536]{1,0:T(8,128)S(1)} %slice.268), channel_id=1, source_target_pairs={{0,16},{4,20},{8,24},{12,28},{16,0},{20,4},{24,8},{28,12},{1,17},{... | collective-permute-start | bytes 1769480 | tf_op jit(solution)/shard_map/ppermute | solution.py:390
  367.8 27.3 %collective-permute-start.42 = (f32[96,1536]{1,0:T(8,128)S(1)}, f32[96,1536]{1,0:T(8,128)S(1)}, u32[]{:S(2)}, u32[]{:S(2)}) collective-permute-start(f32[96,1536]{1,0:T(8,128)S(1)} %slice.269), channel_id=1, source_target_pairs={{0,8},{4,12},{8,0},{12,4},{16,24},{20,28},{24,16},{28,20},{1,9},{5... | collective-permute-start | bytes 1769480 | tf_op jit(solution)/shard_map/ppermute | solution.py:390
  369.5 25.5 %collective-permute-start.43 = (f32[16,768]{1,0:T(8,128)S(1)}, f32[16,768]{1,0:T(8,128)S(1)}, u32[]{:S(2)}, u32[]{:S(2)}) collective-permute-start(f32[16,768]{1,0:T(8,128)S(1)} %add.245), channel_id=1, source_target_pairs={{0,16},{4,20},{8,24},{12,28},{16,0},{20,4},{24,8},{28,12},{1,17},{... | collective-permute-start | bytes 147464 | tf_op jit(solution)/shard_map/ppermute | solution.py:390
  398.4 42.1 %collective-permute-start.44 = (f32[288,768]{1,0:T(8,128)S(1)}, f32[288,768]{1,0:T(8,128)S(1)}, u32[]{:S(2)}, u32[]{:S(2)}) collective-permute-start(f32[288,768]{1,0:T(8,128)S(1)} %get-tuple-element.185), channel_id=1, source_target_pairs={{0,1},{4,5},{8,9},{12,13},{16,17},{20,21},{24,25},{28,29}} | collective-permute-start | bytes 2654216 | tf_op jit(solution)/shard_map/ppermute | solution.py:625
  399.8 40.8 %collective-permute-start.45 = (f32[288,768]{1,0:T(8,128)S(1)}, f32[288,768]{1,0:T(8,128)S(1)}, u32[]{:S(2)}, u32[]{:S(2)}) collective-permute-start(f32[288,768]{1,0:T(8,128)S(1)} %get-tuple-element.186), channel_id=1, source_target_pairs={{3,2},{7,6},{11,10},{15,14},{19,18},{23,22},{27,26},{31,30}} | collective-permute-start | bytes 2654216 | tf_op jit(solution)/shard_map/ppermute | solution.py:629
  400.5 40.1 %collective-permute-start.46 = (f32[16,768]{1,0:T(8,128)S(1)}, f32[16,768]{1,0:T(8,128)S(1)}, u32[]{:S(2)}, u32[]{:S(2)}) collective-permute-start(f32[16,768]{1,0:T(8,128)S(1)} %add.248), channel_id=1, source_target_pairs={{0,1},{1,0},{2,3},{3,2},{4,5},{5,4},{6,7},{7,6},{8,9},{9,8},{10,11... | collective-permute-start | bytes 147464 | tf_op jit(solution)/shard_map/ppermute | solution.py:633
  440.8 23.0 %collective-permute-start.47 = (f32[288,768]{1,0:T(8,128)S(1)}, f32[288,768]{1,0:T(8,128)S(1)}, u32[]{:S(2)}, u32[]{:S(2)}) collective-permute-start(f32[288,768]{1,0:T(8,128)S(1)} %get-tuple-element.188), channel_id=1, source_target_pairs={{0,1},{1,2},{4,5},{5,6},{8,9},{9,10},{12,13},{13,14},{16,17},{17,1... | collective-permute-start | bytes 2654216 | tf_op jit(solution)/shard_map/ppermute | solution.py:625
  465.2 32.0 %collective-permute-start.49 = (f32[288,768]{1,0:T(8,128)}, f32[288,768]{1,0:T(8,128)S(1)}, u32[]{:S(2)}, u32[]{:S(2)}) collective-permute-start(f32[288,768]{1,0:T(8,128)} %get-tuple-element.190), channel_id=1, source_target_pairs={{0,1},{1,2},{2,3},{4,5},{5,6},{6,7},{8,9},{9,10},{10,11},{12,13},{... | collective-permute-start | bytes 2654216 | tf_op jit(solution)/shard_map/ppermute | solution.py:625
  471.5 25.6 %collective-permute-start.50 = (f32[288,768]{1,0:T(8,128)S(1)}, f32[288,768]{1,0:T(8,128)S(1)}, u32[]{:S(2)}, u32[]{:S(2)}) collective-permute-start(f32[288,768]{1,0:T(8,128)S(1)} %get-tuple-element.191), channel_id=1, source_target_pairs={{1,0},{2,1},{3,2},{5,4},{6,5},{7,6},{9,8},{10,9},{11,10},{13,12},{... | collective-permute-start | bytes 2654216 | tf_op jit(solution)/shard_map/ppermute | solution.py:629
  472.8 22.3 %collective-permute-start.51 = (f32[16,768]{1,0:T(8,128)S(1)}, f32[16,768]{1,0:T(8,128)S(1)}, u32[]{:S(2)}, u32[]{:S(2)}) collective-permute-start(f32[16,768]{1,0:T(8,128)S(1)} %add.251), channel_id=1, source_target_pairs={{0,2},{1,3},{2,0},{3,1},{4,6},{5,7},{6,4},{7,5},{8,10},{9,11},{10,... | collective-permute-start | bytes 147464 | tf_op jit(solution)/shard_map/ppermute | solution.py:633
  (62 other events, 909.7 us)
Sparse Core Ops, SparseCore 0:
  198.3 111.6 all-gather.2
  311.5 129.3 all-gather.4
Sparse Core Ops, SparseCore 1:
  209.3 74.9 reduce-scatter.2
  287.6 108.8 reduce-scatter.4

commit v4 on v3

--- a/solution.py
+++ b/solution.py
@@ -36,6 +36,10 @@
     first_mean = jnp.mean(scaled, axis=-1, keepdims=True)
     cross_mean = jnp.mean(scaled * normed, axis=-1, keepdims=True)
     return inverse * (scaled - first_mean - normed * cross_mean)
+
+
+def by_rows(rows, step, body, carry=()):
+    return lax.fori_loop(0, rows // step, lambda i, c: body(pl.ds(pl.multiple_of(i * step, step), step), c), carry)
 
 
 def row_sums(values):
@@ -126,12 +130,18 @@
 
     @pl.when(slot == pl.num_programs(1) - 1)
     def _():
-        values = x_ref[...].astype(F32) + hid_ref[...] + vec_ref[0:1]
-        hidden, normed, inverse = norm_forward(values, vec_ref[1:2], vec_ref[2:3])
-        hid_ref[...] = hidden
-        hbf_ref[...] = hidden.astype(BF16)
-        nrm_ref[...] = normed
-        inv_ref[...] = inverse
+        bias, gain, shift = vec_ref[0:1], vec_ref[1:2], vec_ref[2:3]
+
+        def block(at, carry):
+            values = x_ref[at].astype(F32) + hid_ref[at] + bias
+            hidden, normed, inverse = norm_forward(values, gain, shift)
+            hid_ref[at] = hidden
+            hbf_ref[at] = hidden.astype(BF16)
+            nrm_ref[at] = normed
+            inv_ref[at] = inverse
+            return carry
+
+        by_rows(LENGTH, 256, block)
 
 
 def output_forward(slots_at, x, context, weights, vectors):
@@ -163,7 +173,7 @@
     )
 
 
-def attend_back_kernel(x_ref, ga_ref, gr_ref, w_ref, wo_ref, bias_ref, gqkv_ref, gx_ref, sum_ref):
+def attend_back_kernel(x_ref, ga_ref, gr_ref, w_ref, wo_ref, bias_ref, ctx_ref, gw_ref, gx_ref, sum_ref, gqkv_ref):
     slot = pl.program_id(1)
     cols = wo_ref.shape[0]
     gctx = dot(ga_ref[...], wo_ref[...], COLS).astype(BF16)
@@ -184,6 +194,8 @@
     grads = gqkv_ref[...]
     sum_ref[...] = row_sums(grads.astype(F32))
     back = dot(grads, w_ref[...], PLAIN)
+    gw_ref[:, : 3 * cols] = dot(x_ref[...], grads, ROWS)
+    gw_ref[:, 3 * cols :] = dot(ga_ref[...], ctx_ref[...], ROWS)
 
     @pl.when(slot == 0)
     def _():
@@ -194,12 +206,11 @@
         gx_ref[...] += back
 
 
-def attend_backward(x, grad_attn, grad_resid, weights, w_output, bias):
+def attend_backward(x, grad_attn, grad_resid, weights, w_output, bias, context):
     rows, width = grad_attn.shape
     slots, cols, _ = w_output.shape
     mine = lambda i, j: (i, 0)
     token = (LENGTH, width)
-    heads = (None, LENGTH, 3 * cols)
     weight = lambda i, j: (j, 0, 0)
     return call(
         attend_back_kernel,
@@ -212,14 +223,16 @@
             (weights, (None, 3 * cols, width), weight),
             (w_output, (None, cols, width), weight),
             (bias, (None, 1, 3 * cols), weight),
-        ],
-        [
-            ((slots, rows, 3 * cols), BF16, heads, lambda i, j: (j, i, 0)),
+            (context, (None, LENGTH, cols), lambda i, j: (j, i, 0)),
+        ],
+        [
+            ((width, slots * 4 * cols), F32, (width, 4 * cols), lambda i, j: (0, j)),
             ((rows, width), F32, token, mine),
             ((rows // LENGTH, slots, 1, 3 * cols), F32, (None, None, 1, 3 * cols), lambda i, j: (i, j, 0, 0)),
         ],
         flops=0,
         moved=0,
+        scratch=[pltpu.VMEM((LENGTH, 3 * cols), BF16)],
     )
 
 
@@ -268,18 +281,22 @@
 
     @pl.when(slot == pl.num_programs(1) - 1)
     def _():
-        gain = vec_ref[4:5]
-        values = hid_ref[...] + (out_ref[...] + vec_ref[3:4])
-        layer_out, normed, inverse = norm_forward(values, gain, vec_ref[5:6])
-        out_ref[...] = layer_out
-        upstream = cot_ref[...].astype(F32)
-        grad = norm_backward(upstream, gain, normed, inverse)
-        rounded = grad.astype(BF16)
-        gr_ref[...] = grad
-        go_ref[...] = rounded
-        sum_ref[0:1] = row_sums(upstream * normed)
-        sum_ref[1:2] = row_sums(upstream)
-        sum_ref[2:3] = row_sums(rounded.astype(F32))
+        bias, gain, shift = vec_ref[3:4], vec_ref[4:5], vec_ref[5:6]
+
+        def block(at, sums):
+            values = hid_ref[at] + (out_ref[at] + bias)
+            layer_out, normed, inverse = norm_forward(values, gain, shift)
+            out_ref[at] = layer_out
+            upstream = cot_ref[at].astype(F32)
+            grad = norm_backward(upstream, gain, normed, inverse)
+            rounded = grad.astype(BF16)
+            gr_ref[at] = grad
+            go_ref[at] = rounded
+            found = (upstream * normed, upstream, rounded.astype(F32))
+            return tuple(s + row_sums(f) for s, f in zip(sums, found))
+
+        for i, total in enumerate(by_rows(LENGTH, 256, block, (jnp.zeros_like(gain),) * 3)):
+            sum_ref[i : i + 1] = total
 
 
 def outer_forward(active, weights, hidden, cotangent, vectors):
@@ -327,14 +344,19 @@
 
     @pl.when(slot == pl.num_programs(1) - 1)
     def _():
-        upstream, normed = g1_ref[...], nrm_ref[...]
-        grad = norm_backward(upstream, vec_ref[1:2], normed, inv_ref[...])
-        rounded = grad.astype(BF16)
-        g1_ref[...] = grad
-        ga_ref[...] = rounded
-        sum_ref[0:1] = row_sums(upstream * normed)
-        sum_ref[1:2] = row_sums(upstream)
-        sum_ref[2:3] = row_sums(rounded.astype(F32))
+        gain = vec_ref[1:2]
+
+        def block(at, sums):
+            upstream, normed = g1_ref[at], nrm_ref[at]
+            grad = norm_backward(upstream, gain, normed, inv_ref[at])
+            rounded = grad.astype(BF16)
+            g1_ref[at] = grad
+            ga_ref[at] = rounded
+            found = (upstream * normed, upstream, rounded.astype(F32))
+            return tuple(s + row_sums(f) for s, f in zip(sums, found))
+
+        for i, total in enumerate(by_rows(LENGTH, 256, block, (jnp.zeros_like(gain),) * 3)):
+            sum_ref[i : i + 1] = total
 
 
 def inner_backward(grad_outer, w_outer, slope, w_inner, grad_resid2, normed, inverse, vectors):
@@ -463,7 +485,12 @@
         copy.wait()
     for hold, out in zip(holds, outs):
         for k in range(hold.shape[0]):
-            out[k + 1] = hold[k].astype(BF16)
+
+            def block(at, carry, k=k, hold=hold, out=out):
+                out[k + 1, at] = hold[k, at].astype(BF16)
+                return carry
+
+            by_rows(hold.shape[1], 96, block)
 
 
 def assemble(locals_, pieces):
@@ -511,8 +538,43 @@
     return tuple(flip(v, 1) for v in values)
 
 
-def halves(arrived, rows):
-    return jnp.stack([v[:rows] for v in arrived])[None], jnp.stack([v[rows:] for v in arrived])[None]
+def copy_kernel(plan, count, *refs):
+    ins, outs = refs[:count], refs[count:]
+    for source, source_at, target, target_at in plan:
+        outs[target][target_at] = ins[source][source_at]
+
+
+def copies(ins, shapes, plan):
+    space = pl.BlockSpec(memory_space=pltpu.VMEM)
+    return pl.pallas_call(
+        partial(copy_kernel, plan, len(ins)),
+        in_specs=[space] * len(ins),
+        out_specs=[space] * len(shapes),
+        out_shape=[jax.ShapeDtypeStruct(shape, F32) for shape in shapes],
+        cost_estimate=pl.CostEstimate(flops=0, bytes_accessed=0, transcendentals=0),
+        compiler_params=pltpu.CompilerParams(vmem_limit_bytes=32 << 20),
+        name="copies",
+    )(*ins)
+
+
+def halves(arrived, upper):
+    rows, width = arrived[0].shape
+    n = len(arrived)
+    plan = [(k, (slice(0, upper),), 0, (0, k)) for k in range(n)]
+    plan += [(k, (slice(upper, rows),), 1, (0, k)) for k in range(n)]
+    return copies(arrived, [(1, n, upper, width), (1, n, rows - upper, width)], plan)
+
+
+def join(a, ax, b, by):
+    _, n, upper, width = a.shape
+    lower = b.shape[2]
+    plan = []
+    for i, (v, w) in enumerate(((a, b), (ax, by))):
+        every = slice(None)
+        plan += [(2 * i, (0,), 0, (i,)), (2 * i + 1, (0,), 1, (i,))]
+        plan += [(2 * i, (0,), 2, (i, every, slice(0, upper))), (2 * i + 1, (0,), 2, (i, every, slice(upper, upper + lower)))]
+    shapes = [(2, n, upper, width), (2, n, lower, width), (2, n, upper + lower, width)]
+    return copies([a, b, ax, by], shapes, plan)
 
 
 def full_weights(locals_, a, b, ay, bx, c, d):
@@ -531,14 +593,13 @@
         return found
 
     upper = lambda rels: [(i, me ^ r, 0, spans(0, cut_at)) for i, r in enumerate(rels)]
-    lower = lambda rels: [(i, me ^ r, 0, spans(cut_at, end)) for i, r in enumerate(rels)]
+    lower = lambda rels, base=0: [(i, me ^ r, base, spans(cut_at, end)) for i, r in enumerate(rels)]
     pieces = [
         (a, upper((0, 2))),
         (b, lower((0, 4))),
         (ay, upper((4, 6))),
         (bx, lower((2, 6))),
-        (c[0], upper((1, 3))),
-        (c[1], lower((1, 5))),
+        (c, upper((1, 3)) + lower((1, 5), cut_at)),
         (d[0], upper((5, 7))),
         (d[1], lower((3, 7))),
     ]
@@ -589,18 +650,26 @@
     )
 
 
-def full_kernel(left_ref, right_ref, out_ref):
-    out_ref[...] = dot(left_ref[...], right_ref[...], ROWS)
-
-
-def grad_full(left, right):
-    rows, width = left.shape
-    slots, _, cols = right.shape
+def full_kernel(count, *refs):
+    lefts, rights, out_ref = refs[:count], refs[count:-1], refs[-1]
+    start = 0
+    for left, right in zip(lefts, rights):
+        span = slice(start, start + right.shape[-1])
+        out_ref[:, span] = dot(left[...], right[...], ROWS)
+        start = span.stop
+
+
+def grad_full(*pairs):
+    rows, width = pairs[0][0].shape
+    slots = pairs[0][1].shape[0]
+    cols = sum(r.shape[-1] for _, r in pairs)
+    ins = [(left, left.shape, lambda j: (0, 0)) for left, _ in pairs]
+    ins += [(right, (None,) + right.shape[1:], lambda j: (j, 0, 0)) for _, right in pairs]
     return call(
-        full_kernel,
+        partial(full_kernel, len(pairs)),
         "grad_full",
         (slots,),
-        [(left, left.shape, lambda j: (0, 0)), (right, (None, rows, cols), lambda j: (j, 0, 0))],
+        ins,
         [((width, slots * cols), F32, (width, cols), lambda j: (0, j))],
         flops=0,
         moved=0,
@@ -615,8 +684,13 @@
     return (join(0, 2, a), join(1, 3, a)), (join(0, 1, b), join(2, 3, b))
 
 
-def columns_by_slot(left, right, tensor):
-    part = jnp.concatenate([left, right], axis=1)
+def scatter_plain(grad, tensor):
+    part = lax.psum_scatter(grad, "dp", scatter_dimension=0, tiled=True)
+    part = columns(part, tensor)
+    return sum((shift_to(part[k], tensor, tensor - k) for k in range(1, tensor)), part[0])
+
+
+def columns(part, tensor):
     cols = part.shape[1] // tensor
     return [part[:, k * cols : (k + 1) * cols] for k in range(tensor)]
 
@@ -629,16 +703,52 @@
     return lax.ppermute(values, "tensor", [(i, i - 1) for i in range(tensor - step, tensor)])
 
 
+def place_kernel(z_ref, own_ref, *refs):
+    *others, out_ref = refs
+    count = len(others) // 2
+    below, above = others[:count], others[count:]
+    away = pl.program_id(0) - z_ref[0]
+
+    @pl.when(away == 0)
+    def _():
+        out_ref[...] = own_ref[...]
+
+    for k in range(count):
+
+        @pl.when(away == -(k + 1))
+        def _(k=k):
+            out_ref[...] = below[k][...]
+
+        @pl.when(away == k + 1)
+        def _(k=k):
+            out_ref[...] = above[k][...]
+
+
+def place(own, below, above):
+    rows, width = own.shape
+    count = len(below) + 1
+    whole = (rows, width)
+    return call(
+        place_kernel,
+        "place",
+        (count,),
+        [(v, whole, lambda i, z: (0, 0)) for v in (own, *below, *above)],
+        [((count * rows, width), F32, whole, lambda i, z: (i, 0))],
+        flops=0,
+        moved=0,
+        prefetch=lax.axis_index("tensor").astype(jnp.int32).reshape(1),
+    )[0]
+
+
+def onward(values, tensor, step):
+    u, d = values
+    u = lax.ppermute(u, "tensor", [(i, i + 1) for i in range(step - 1, tensor - 1)])
+    d = lax.ppermute(d, "tensor", [(i, i - 1) for i in range(1, tensor - step + 1)])
+    return u, d
+
+
 def swap(values, tensor, bit):
     return lax.ppermute(values, "tensor", [(i, i ^ bit) for i in range(tensor)])
-
-
-def scatter_plain(left, right, dp, tensor):
-    grad = jnp.concatenate([dot(left, right[k], ROWS) for k in range(tensor)], axis=1)
-    part = lax.psum_scatter(grad, "dp", scatter_dimension=0, tiled=True)
-    cols = part.shape[1] // tensor
-    part = [part[:, k * cols : (k + 1) * cols] for k in range(tensor)]
-    return sum((shift_to(part[k], tensor, tensor - k) for k in range(1, tensor)), part[0])
 
 
 def shards(
@@ -705,16 +815,16 @@
         context, hidden, hidden_bf, normed, inverse = rest_of_attention(context, output_full)
         active, slope = inner_forward(hidden_bf, inner_full, inner_bias)
         layer_out, grad_resid2, grad_outer, sums_two = outer_half(active, outer_full, hidden)
-        layer_out = lax.all_gather(layer_out, "tensor", axis=0, tiled=True)
+        layer_out = narrow(lax.all_gather(layer_out, "tensor", axis=0, tiled=True), own_rows)
         grad_inner, grad_resid1, grad_attn, inner_sums, sums_one = inner_backward(
             grad_outer, outer_full, slope, inner_full, grad_resid2, normed, inverse, wide_vectors
         )
-        grad_qkv, grad_x, qkv_sums = attend_backward(x, grad_attn, grad_resid1, qkv_full, output_full, qkv_bias)
+        part3, grad_x, qkv_sums = attend_backward(x, grad_attn, grad_resid1, qkv_full, output_full, qkv_bias, context)
         grad_inputs = lax.all_gather(grad_x, "tensor", axis=0, tiled=True)
-        gu = scatter_plain(grad_outer, active, dp, tensor)
-        gi = scatter_plain(hidden_bf, grad_inner, dp, tensor)
-        go = scatter_plain(grad_attn, context, dp, tensor)
-        gqkv = scatter_plain(x, grad_qkv, dp, tensor)
+        gu = scatter_plain(grad_full((grad_outer, active)), tensor)
+        gi = scatter_plain(grad_full((hidden_bf, grad_inner)), tensor)
+        gqkv = scatter_plain(part3, tensor)
+        gqkv, go = gqkv[:, : 3 * cols], gqkv[:, 3 * cols :]
         sums = lax.psum(small_sums(qkv_sums, inner_sums, sums_one, sums_two), ("dp", "tensor"))
     else:
         order = block_order(width)
@@ -729,88 +839,96 @@
         qkv_bias, inner_bias = vectors[..., : 3 * cols], vectors[..., 3 * cols :]
 
         ax, by, z2 = flip(a1, 2), flip(b1, 4), across(p2, tensor)
-        a1, b1, (a2, b2) = wide(a1, ax), wide(b1, by), halves(z2, n2)
-        a1, b1, a2, b2, context, x, order = stage(a1, b1, a2, b2, context, x, order)
-
-        c1 = other_core(a1, b1)
-        context, *c1 = stage(context, *c1)
+        a1, b1, ab1 = join(a1, ax, b1, by)
+        a2, b2 = halves(z2, n2)
+        a1, b1, ab1, a2, b2, context, x, order = stage(a1, b1, ab1, a2, b2, context, x, order)
+
+        c1 = flip(ab1, 1)
+        context, c1 = stage(context, c1)
         context = lax.all_to_all(context, "tensor", 0, 0, tiled=True)
         ay1, bx1, ax, by = flip(a1, 4), flip(b1, 2), flip(a2, 2), flip(b2, 4)
-        a2, b2 = wide(a2, ax), wide(b2, by)
-        ay1, bx1, a2, b2, context, p3 = stage(ay1, bx1, a2, b2, context, p3)
-
-        d1, ay2, bx2 = other_core(ay1, bx1), flip(a2, 4), flip(b2, 2)
+        a2, b2, ab2 = join(a2, ax, b2, by)
+        d1 = other_core(ay1, bx1)
+        ay1, bx1, a2, b2, ab2, p3 = stage(ay1, bx1, a2, b2, ab2, p3)
+
+        c2, ay2, bx2 = flip(ab2, 1), flip(a2, 4), flip(b2, 2)
         inner_full, output_full = full_weights([w_inner, w_output], a1, b1, ay1, bx1, c1, d1)
         context, hidden, hidden_bf, normed, inverse = rest_of_attention(context, output_full)
-        ay2, bx2, p3, hidden_bf = stage(ay2, bx2, p3, hidden_bf)
-
-        c2, d2, z3 = other_core(a2, b2), other_core(ay2, bx2), across(p3, tensor)
+        c2, ay2, bx2, p3, hidden_bf = stage(c2, ay2, bx2, p3, hidden_bf)
+
+        d2, z3 = other_core(ay2, bx2), across(p3, tensor)
         active, slope = inner_forward(hidden_bf, inner_full, inner_bias)
-        *c2, dx, dy, active = stage(*c2, *d2, active)
-        (outer_full,) = full_weights([w_outer], a2, b2, ay2, bx2, c2, (dx, dy))
+        *d2, active = stage(*d2, active)
+
+        (outer_full,) = full_weights([w_outer], a2, b2, ay2, bx2, c2, d2)
         layer_out, grad_resid2, grad_outer, sums_two = outer_half(active, outer_full, hidden)
         a3, b3 = halves(z3, n3)
         a3, b3, layer_out, grad_outer = stage(a3, b3, layer_out, grad_outer)
 
         layer_out = lax.all_gather(layer_out, "tensor", axis=0, tiled=True)
         ax, by = flip(a3, 2), flip(b3, 4)
-        part1 = grad_full(grad_outer, active)
-        a3, b3 = wide(a3, ax), wide(b3, by)
-        a3, b3, part1, grad_outer = stage(a3, b3, part1, grad_outer)
+        part1 = grad_full((grad_outer, active))
+        a3, b3, ab3 = join(a3, ax, b3, by)
+        a3, b3, ab3, part1, grad_outer = stage(a3, b3, ab3, part1, grad_outer)
 
         part1 = lax.psum_scatter(part1, "dp", scatter_dimension=0, tiled=True)
-        ay3, bx3, c3 = flip(a3, 4), flip(b3, 2), other_core(a3, b3)
+        ay3, bx3, c3 = flip(a3, 4), flip(b3, 2), flip(ab3, 1)
         grad_inner, grad_resid1, grad_attn, inner_sums, sums_one = inner_backward(
             grad_outer, outer_full, slope, inner_full, grad_resid2, normed, inverse, wide_vectors
         )
         ay3, bx3, grad_inner, grad_attn = stage(ay3, bx3, grad_inner, grad_attn)
 
         d3 = other_core(ay3, bx3)
-        part2 = grad_full(hidden_bf, grad_inner)
-        *d3, part2, grad_attn = stage(*d3, part2, grad_attn)
-
-        part2 = lax.psum_scatter(part2, "dp", scatter_dimension=0, tiled=True)
+        send, keep = grad_rows(order, [(hidden_bf, grad_inner)])
+        *d3, send, grad_attn = stage(*d3, send, grad_attn)
+
+        got = flip(send, 1)
         (qkv_full,) = full_weights([qkv_local], a3, b3, ay3, bx3, c3, d3)
-        grad_qkv, grad_x, qkv_sums = attend_backward(x, grad_attn, grad_resid1, qkv_full, output_full, qkv_bias)
-        grad_qkv, grad_x = stage(grad_qkv, grad_x)
-
-        grad_inputs = lax.all_gather(grad_x, "tensor", axis=0, tiled=True)
-        send, keep = grad_rows(order, [(x, grad_qkv), (grad_attn, context)])
+        (a, ak), (b, bk) = split_paths(keep + got, share)
+        a, b, qkv_full, grad_attn = stage(a, b, qkv_full, grad_attn)
+
+        ax, by = flip(a, 2), flip(b, 4)
+        part3, grad_x, qkv_sums = attend_backward(
+            x, grad_attn, grad_resid1, qkv_full, output_full, qkv_bias, context
+        )
+        a, b = ak + ax, bk + by
+        a_send, b_send, part3, grad_x = stage(a[:share], b[:share], part3, grad_x)
+
+        part3 = lax.psum_scatter(part3, "dp", scatter_dimension=0, tiled=True)
+        g1 = onward((grad_x, grad_x), tensor, 1)
+        ay, bx = flip(a_send, 4), flip(b_send, 2)
+        part2 = jnp.concatenate([a[share:] + ay, b[share:] + bx], axis=1)
         extra = small_sums(qkv_sums, inner_sums, sums_one, sums_two)
         extra = jnp.pad(extra, (0, -extra.shape[0] % (8 * width))).reshape(-1, width)
-        send, extra = stage(send, extra)
-
-        got = flip(send, 1)
         extra = extra + flip(extra, 1)
-        (a, ak), (b, bk) = split_paths(keep + got, share)
-        a, b, extra, layer_out = stage(a, b, extra, layer_out)
-
-        ax, by = flip(a, 2), flip(b, 4)
+        layer_out = narrow(layer_out, own_rows)
+        first = columns(wide(part1, part2), tensor)
+        g2 = onward(g1, tensor, 2)
+        _, _, extra, first[0], first[1], first[2], first[3], layer_out = stage(*g1, extra, *first, layer_out)
+
+        u, d = up(first[1], tensor, 1), down(first[3], tensor, 1)
         extra = extra + flip(extra, 2)
-        a, b = ak + ax, bk + by
-        a_send, b_send, extra = stage(a[:share], b[:share], extra)
-
-        ay, bx = flip(a_send, 4), flip(b_send, 2)
+        g3 = onward(g2, tensor, 3)
+        _, _, u, d, part3, extra = stage(*g2, first[2] + u, first[2] + d, part3, extra)
+
+        u, d = up(u, tensor, 2), down(d, tensor, 2)
+        last = columns(part3, tensor)
+        v, w = up(last[1], tensor, 1), down(last[3], tensor, 1)
         extra = extra + flip(extra, 4)
-        part3 = jnp.concatenate([a[share:] + ay, b[share:] + bx], axis=1)
-        parts = wide(wide(part1, part2), part3)
-        parts = [parts[:, k * width : (k + 1) * width] for k in range(tensor)]
-        u, d, extra = stage(parts[1], parts[3], extra)
-
-        u, d = up(u, tensor, 1), down(d, tensor, 1)
+        _, _, u, d, v, w, extra = stage(*g3, first[3] + u, first[1] + d, last[2] + v, last[2] + w, extra)
+
+        u, d, v, w = up(u, tensor, 3), down(d, tensor, 3), up(v, tensor, 2), down(w, tensor, 2)
         extra = extra + swap(extra, tensor, 1)
-        u, d, extra = stage(parts[2] + u, parts[2] + d, extra)
-
-        u, d = up(u, tensor, 2), down(d, tensor, 2)
+        grad_inputs = place(grad_x, [g1[0], g2[0], g3[0]], [g1[1], g2[1], g3[1]])
+        gu = first[0] + u + d
+        v, w, extra, gu, grad_inputs = stage(last[3] + v, last[1] + w, extra, gu, grad_inputs)
+
+        gqkv = last[0] + up(v, tensor, 3) + down(w, tensor, 3)
         extra = extra + swap(extra, tensor, 2)
-        u, d = stage(parts[3] + u, parts[1] + d)
-
-        parts = parts[0] + up(u, tensor, 3) + down(d, tensor, 3)
-        gu, gi, gqkv = parts[:share], parts[share : 2 * share], parts[2 * share :]
+        gu, gi = gu[:share], gu[share:]
         gqkv, go = gqkv[:, : 3 * cols], gqkv[:, 3 * cols :]
         sums = extra.reshape(-1)
 
-    layer_out = narrow(layer_out, own_rows)
     span = 3 * cols + w_inner.shape[1]
     mine = lax.dynamic_slice_in_dim(sums, z * span, span, 0)
     rest = sums[span * tensor :][: 6 * width].reshape(6, width)

time: 516 us -> 477 us (0.924)
  waiting for transfers between devices: 231 us -> 161 us
  starting transfers between devices: 69.8 us -> 88.5 us
  Pallas kernels: 132 us -> 139 us
    ppermute x2, waiting for transfers between devices: 55.2 us -> 2.07 us  [swap(): return lax.ppermute(values, 'tensor', [(i, i ^ bit) for i in range(tensor)])]
    ppermute x32 -> x29, waiting for transfers between devices: 125 us -> 74.2 us  [flip(): return lax.ppermute(values, 'dp', [(i, i ^ bit) for i in range(8)])]
    ppermute x0 -> x6, waiting for transfers between devices: none -> 43.2 us  [the longest x3 28 us: onward(): lax.ppermute(d, 'tensor', [(i, i - 1) for i in range(1, tensor - step + 1)])]
    ppermute x0 -> x6, starting transfers between devices: none -> 17.1 us  [the longest x3 13 us: onward(): lax.ppermute(u, 'tensor', [(i, i + 1) for i in range(step - 1, tensor - 1)])]
    ppermute x3 -> x6, starting transfers between devices: 12.1 us -> 24.3 us  [up(): return lax.ppermute(values, 'tensor', [(i, i + 1) for i in range(step)])]
    ppermute x3 -> x6, waiting for transfers between devices: 17.9 us -> 5.9 us  [up(): return lax.ppermute(values, 'tensor', [(i, i + 1) for i in range(step)])]
    ppermute x32 -> x29, starting transfers between devices: 23.3 us -> 14.5 us  [flip(): return lax.ppermute(values, 'dp', [(i, i ^ bit) for i in range(8)])]
    add x5 -> x10, other arithmetic: 3 us -> 11 us  [the longest x2 3.08 us: shards(): part2 = jnp.concatenate([a[share:] + ay, b[share:] + bx], axis=1)]
  transfers between devices with their start and end apart: 57 -> 65, of which waited for: 20 -> 25; matrix products, arithmetic and copies ran while one was open for 8% -> 9% of each run, Pallas kernels for 23% -> 25%
where the time goes in v4:
time: 477 us; the launch traced here: 475 us
  waiting for transfers between devices  161 us (34%)
  Pallas kernels  139 us (29%)
  starting transfers between devices  88.5 us (19%)
  local copies, waits for them, and re-layouts  39.3 us (8%)
  other arithmetic  29.8 us (6%)
  between operations  16.5 us (3%)
    pallas_call x10, Pallas kernels, call(): pl.pallas_call(kernel, grid_spec=pltpu.PrefetchScalarGridSpec(num_scalar_...  114 us
    ppermute x29, waiting for transfers between devices, flip(): return lax.ppermute(values, 'dp', [(i, i ^ bit) for i in range(8)])  74.2 us
    ppermute x12, waiting for transfers between devices, shift_to(): lax.ppermute(values, 'tensor', [(i, (i + k) % tensor) for i in range(tens...  31.4 us
    ppermute x3, waiting for transfers between devices, onward(): lax.ppermute(d, 'tensor', [(i, i - 1) for i in range(1, tensor - step + 1)])  28 us
    ppermute x6, starting transfers between devices, up(): return lax.ppermute(values, 'tensor', [(i, i + 1) for i in range(step)])  24.3 us
    unnamed x100, local copies, waits for them, and re-layouts  19.3 us
    ppermute x12, starting transfers between devices, shift_to(): lax.ppermute(values, 'tensor', [(i, (i + k) % tensor) for i in range(tens...  17.8 us
    pallas_call x3, Pallas kernels, assemble(): pl.pallas_call(partial(assemble_kernel, plan), in_specs=[pl.BlockSpec(mem...  17.7 us
  transfers between devices with their start and end apart: 65, of which 25 were waited for; matrix products, arithmetic and copies ran while one was open for 9% of the time, Pallas kernels for 25%

profile of v4, /device:TPU:0, one launch (start us, length us, event | category | flops | bytes accessed | tf_op | source)
XLA Modules:
  0.0 474.8 jit_solution(2844138566143823241)
XLA Ops:
  23.6 11.6 %attend_forward.1 = f32[1024,384]{1,0:T(8,128)} custom-call(bf16[2048,768]{1,0:T(8,128)(2,1)} %x_ref.1, bf16[576,768]{1,0:T(8,128)(2,1)} %pad_maximum_fusion.1.w_ref.refs_1_, f32[1,576]{1,0:T(1,128)} %slice.185.bias_ref), custom_call_target="tpu_custom_call" | custom-call | flops 2617245696 | bytes 5605632 | tf_op jit(solution)/shard_map/attend_forward/pallas_call | solution.py:57
  42.2 6.5 %collective-permute-done.4 = f32[1,1344]{1,0:T(1,128)} collective-permute-done((f32[1,1344]{1,0:T(1,128)S(1)}, f32[1,1344]{1,0:T(1,128)}, u32[]{:S(2)}, u32[]{:S(2)}) %collective-permute-start.4) | collective-permute-done | bytes 5408 | tf_op jit(solution)/shard_map/ppermute | solution.py:408
  63.7 4.1 collective-permute-done.10.refs_2_
  67.7 5.4 %collective-permute-done.8.refs_0_ = f32[96,768]{1,0:T(8,128)S(1)} collective-permute-done((f32[96,768]{1,0:T(8,128)}, f32[96,768]{1,0:T(8,128)S(1)}, u32[]{:S(2)}, u32[]{:S(2)}) %collective-permute-start.8) | collective-permute-done | bytes 294944 | tf_op jit(solution)/shard_map/ppermute | solution.py:408
  73.1 8.3 %collective-permute-done.9.refs_1_ = f32[96,768]{1,0:T(8,128)S(1)} collective-permute-done((f32[96,768]{1,0:T(8,128)}, f32[96,768]{1,0:T(8,128)S(1)}, u32[]{:S(2)}, u32[]{:S(2)}) %collective-permute-start.9) | collective-permute-done | bytes 294944 | tf_op jit(solution)/shard_map/ppermute | solution.py:408
  89.1 4.4 all-to-all-start
  96.3 23.6 %collective-permute-done.13.refs_2_ = f32[1,3,48,768]{3,2,1,0:T(8,128)} collective-permute-done((f32[1,3,48,768]{3,2,1,0:T(8,128)}, f32[1,3,48,768]{3,2,1,0:T(8,128)}, u32[]{:S(2)}, u32[]{:S(2)}) %collective-permute-start.13) | collective-permute-done | bytes 442400 | tf_op jit(solution)/shard_map/ppermute | solution.py:412
  131.0 4.2 collective-permute-done.20.refs_9_
  136.4 7.0 %assemble.3 = (bf16[4,768,768]{2,1,0:T(8,128)(2,1)}, bf16[4,192,768]{2,1,0:T(8,128)(2,1)S(1)}) custom-call(s32[24]{0:T(128)S(1)} %stack.224.refs_0_, bf16[768,768]{1,0:T(8,128)(2,1)S(1)} %copy-done.4, bf16[192,768]{1,0:T(8,128)(2,1)S(1)} %copy-done.21, f32[2,3,64,768]{3,2,1,0:T(8,128)} %get-tuple-element.141.refs_3_, ...), custom_call_target="tpu_custom_call" | custom-call | bytes 13271040 | tf_op jit(solution)/shard_map/assemble/pallas_call | solution.py:508
  144.5 7.7 %output_forward.1 = (bf16[4,512,192]{2,1,0:T(8,128)(2,1)}, f32[512,768]{1,0:T(8,128)}, bf16[512,768]{1,0:T(8,128)(2,1)}, f32[512,768]{1,0:T(8,128)}, f32[512,1]{1,0:T(8,128)}) custom-call(s32[4]{0:T(128)} %and_select_fusion.2.slot_ref, bf16[512,768]{1,0:T(8,128)(2,1)} %constant_dynamic-slice_fusion.1.x_ref, f32[4,256,384]{2,1,0:T(8,128)} %all-to-all-done.ctx_ref, ...), custom_call_target="tpu_custom_call" | custom-call | flops 603979776 | bytes 8284160 | tf_op jit(solution)/shard_map/output_forward/pallas_call | solution.py:57
  158.4 12.2 %inner_forward.1 = (bf16[4,512,768]{2,1,0:T(8,128)(2,1)}, f32[4,512,768]{2,1,0:T(8,128)}) custom-call(bf16[512,768]{1,0:T(8,128)(2,1)} %get-tuple-element.161.h_ref.refs_1_, bf16[4,768,768]{2,1,0:T(8,128)(2,1)} %get-tuple-element.167.w_ref.wi_ref, f32[4,1,768]{2,1,0:T(1,128)} %slice.137.b_ref), custom_call_target="tpu_custom_call" | custom-call | flops 2415919104 | bytes 14954496 | tf_op jit(solution)/shard_map/inner_forward/pallas_call | solution.py:57
  174.2 7.0 %assemble.4.w_ref.wu_ref = bf16[4,768,768]{2,1,0:T(8,128)(2,1)} custom-call(s32[16]{0:T(128)S(1)} %stack.240.refs_0_, bf16[768,768]{1,0:T(8,128)(2,1)} %refs_1_.3, f32[2,3,48,768]{3,2,1,0:T(8,128)} %get-tuple-element.149.refs_2_, f32[2,3,48,768]{3,2,1,0:T(8,128)} %get-tuple-element.150.refs_3_, f32[2,3,48,768]{3,2,1,0:T(8,128)} %collective-permute-done.16.refs_4_, ...), custom_call_target="tpu_custom_call" | custom-call | bytes 10616832 | tf_op jit(solution)/shard_map/assemble/pallas_call | solution.py:508
  181.2 10.1 %outer_forward.1 = (f32[512,768]{1,0:T(8,128)}, f32[512,768]{1,0:T(8,128)}, bf16[512,768]{1,0:T(8,128)(2,1)}, f32[1,8,768]{2,1,0:T(8,128)}) custom-call(bf16[4,512,768]{2,1,0:T(8,128)(2,1)} %get-tuple-element.170.act_ref.refs_1_, bf16[4,768,768]{2,1,0:T(8,128)(2,1)} %assemble.4.w_ref.wu_ref, f32[512,768]{1,0:T(8,128)} %get-tuple-element.174.hid_ref, ...), custom_call_target="tpu_custom_call" | custom-call | flops 2415919104 | bytes 14204928 | tf_op jit(solution)/shard_map/outer_forward/pallas_call | solution.py:57
  192.7 7.6 %grad_full.1 = f32[768,3072]{1,0:T(8,128)} custom-call(bf16[512,768]{1,0:T(8,128)(2,1)} %get-tuple-element.185.refs_0_.go_ref, bf16[4,512,768]{2,1,0:T(8,128)(2,1)} %get-tuple-element.170.act_ref.refs_1_), custom_call_target="tpu_custom_call" | custom-call | tf_op jit(solution)/shard_map/grad_full/pallas_call | solution.py:57
  207.9 15.8 %inner_backward.1 = (bf16[4,512,768]{2,1,0:T(8,128)(2,1)}, f32[512,768]{1,0:T(8,128)}, bf16[512,768]{1,0:T(8,128)(2,1)}, f32[1,4,1,768]{3,2,1,0:T(1,128)}, f32[1,8,768]{2,1,0:T(8,128)}) custom-call(bf16[512,768]{1,0:T(8,128)(2,1)} %get-tuple-element.185.refs_0_.go_ref, bf16[4,768,768]{2,1,0:T(8,128)(2,1)} %assemble.4.w_ref.wu_ref, ...), custom_call_target="tpu_custom_call" | custom-call | tf_op jit(solution)/shard_map/inner_backward/pallas_call | solution.py:57
  224.3 9.1 %grad_rows.1 = (f32[384,3072]{1,0:T(8,128)}, f32[384,3072]{1,0:T(8,128)}) custom-call(bf16[768,768]{1,0:T(8,128)(2,1)} %fusion.refs_0_, bf16[512,768]{1,0:T(8,128)(2,1)} %get-tuple-element.161.h_ref.refs_1_, bf16[4,512,768]{2,1,0:T(8,128)(2,1)} %get-tuple-element.192.refs_2_), custom_call_target="tpu_custom_call" | custom-call | tf_op jit(solution)/shard_map/grad_rows/pallas_call | solution.py:57
  235.8 9.0 %collective-permute-done.33.refs_6_ = f32[2,3,72,768]{3,2,1,0:T(8,128)S(1)} collective-permute-done((f32[2,3,72,768]{3,2,1,0:T(8,128)}, f32[2,3,72,768]{3,2,1,0:T(8,128)S(1)}, u32[]{:S(2)}, u32[]{:S(2)}) %collective-permute-start.33) | collective-permute-done | bytes 1327136 | tf_op jit(solution)/shard_map/ppermute | solution.py:412
  262.4 28.1 %attend_backward.1 = (f32[768,3072]{1,0:T(8,128)}, f32[512,768]{1,0:T(8,128)}, f32[1,4,1,576]{3,2,1,0:T(1,128)}) custom-call(bf16[512,768]{1,0:T(8,128)(2,1)} %constant_dynamic-slice_fusion.1.x_ref, bf16[512,768]{1,0:T(8,128)(2,1)} %get-tuple-element.205.ga_ref, f32[512,768]{1,0:T(8,128)} %get-tuple-element.206.gr_ref, bf16[4,576,768]{2,1,0:T(8,128)(2,1)} %assemble.5.w_ref, ...), custom_call_target="tpu_custom_call" | custom-call | tf_op jit(solution)/shard_map/attend_backward/pallas_call | solution.py:57
  290.5 11.4 %collective-permute-done.35 = f32[192,1536]{1,0:T(8,128)} collective-permute-done((f32[192,1536]{1,0:T(8,128)}, f32[192,1536]{1,0:T(8,128)}, u32[]{:S(2)}, u32[]{:S(2)}) %collective-permute-start.35) | collective-permute-done | bytes 1179680 | tf_op jit(solution)/shard_map/ppermute | solution.py:412
  306.8 9.3 %collective-permute-start.36 = (f32[512,768]{1,0:T(8,128)}, f32[512,768]{1,0:T(8,128)}, u32[]{:S(2)}, u32[]{:S(2)}) collective-permute-start(f32[512,768]{1,0:T(8,128)} %get-tuple-element.211.own_ref), channel_id=1, source_target_pairs={{0,1},{1,2},{2,3},{4,5},{5,6},{6,7},{8,9},{9,10},{10,11},{12,13},{... | collective-permute-start | bytes 4718600 | tf_op jit(solution)/shard_map/ppermute | solution.py:745
  320.7 12.0 %collective-permute-done.39 = f32[96,1536]{1,0:T(8,128)} collective-permute-done((f32[96,1536]{1,0:T(8,128)S(1)}, f32[96,1536]{1,0:T(8,128)}, u32[]{:S(2)}, u32[]{:S(2)}) %collective-permute-start.39) | collective-permute-done | bytes 589856 | tf_op jit(solution)/shard_map/ppermute | solution.py:412
  333.9 15.1 %collective-permute-done.36.refs_0_ = f32[512,768]{1,0:T(8,128)} collective-permute-done((f32[512,768]{1,0:T(8,128)}, f32[512,768]{1,0:T(8,128)}, u32[]{:S(2)}, u32[]{:S(2)}) %collective-permute-start.36) | collective-permute-done | bytes 1572896 | tf_op jit(solution)/shard_map/ppermute | solution.py:745
  357.5 5.0 %narrow.1 = bf16[2048,768]{1,0:T(8,128)(2,1)} custom-call(f32[2048,768]{1,0:T(8,128)} %all-gather.2.cloned.1.call-done.x_ref), custom_call_target="tpu_custom_call" | custom-call | bytes 9437184 | tf_op jit(solution)/shard_map/narrow/pallas_call | solution.py:57
  365.3 4.5 collective-permute-start.43
  372.2 19.2 %collective-permute-done.42.refs_4_ = f32[512,768]{1,0:T(8,128)} collective-permute-done((f32[512,768]{1,0:T(8,128)}, f32[512,768]{1,0:T(8,128)}, u32[]{:S(2)}, u32[]{:S(2)}) %collective-permute-start.42) | collective-permute-done | bytes 1572896 | tf_op jit(solution)/shard_map/ppermute | solution.py:746
  400.3 6.3 %collective-permute-start.48 = (f32[192,768]{1,0:T(8,128)}, f32[192,768]{1,0:T(8,128)S(1)}, u32[]{:S(2)}, u32[]{:S(2)}) collective-permute-start(f32[192,768]{1,0:T(8,128)} %get-tuple-element.227), channel_id=1, source_target_pairs={{0,1},{1,2},{4,5},{5,6},{8,9},{9,10},{12,13},{13,14},{16,17},{17,1... | collective-permute-start | bytes 1769480 | tf_op jit(solution)/shard_map/ppermute | solution.py:699
  410.8 4.5 collective-permute-start.50
  422.2 5.5 %collective-permute-done.47.refs_5_ = f32[512,768]{1,0:T(8,128)} collective-permute-done((f32[512,768]{1,0:T(8,128)}, f32[512,768]{1,0:T(8,128)}, u32[]{:S(2)}, u32[]{:S(2)}) %collective-permute-start.47) | collective-permute-done | bytes 1572896 | tf_op jit(solution)/shard_map/ppermute | solution.py:746
  430.5 5.3 %collective-permute-start.53 = (f32[96,768]{1,0:T(8,128)S(1)}, f32[96,768]{1,0:T(8,128)}, u32[]{:S(2)}, u32[]{:S(2)}) collective-permute-start(f32[96,768]{1,0:T(8,128)S(1)} %slice_add_fusion.4), channel_id=1, source_target_pairs={{0,1},{1,2},{4,5},{5,6},{8,9},{9,10},{12,13},{13,14},{16,17},{17,1... | collective-permute-start | bytes 884744 | tf_op jit(solution)/shard_map/ppermute | solution.py:699
  437.2 7.2 %place.1 = f32[2048,768]{1,0:T(8,128)} custom-call(s32[1]{0:T(128)} %bitcast.60.z_ref, f32[512,768]{1,0:T(8,128)} %get-tuple-element.211.own_ref, f32[512,768]{1,0:T(8,128)} %collective-permute-done.36.refs_0_, f32[512,768]{1,0:T(8,128)} %collective-permute-done.41.refs_1_, f32[512,768]{1,0:T(8,128)} %collective-permute-done.46.refs_2_, ...), custom_call_target="tpu_custom_call" | custom-call | tf_op jit(solution)/shard_map/place/pallas_call | solution.py:57
  449.5 4.1 collective-permute-start.60
  460.1 4.6 collective-permute-done.59
  (302 shorter events, 162.7 us)
Async XLA Ops:
  10.7 39.3 %collective-permute-start = (f32[120,768]{1,0:T(8,128)}, f32[120,768]{1,0:T(8,128)S(1)}, u32[]{:S(2)}, u32[]{:S(2)}) collective-permute-start(f32[120,768]{1,0:T(8,128)} %maximum_convert_fusion), channel_id=1, source_target_pairs={{0,1},{1,2},{2,3},{3,0},{4,5},{5,6},{6,7},{7,4},{8,9},{9,10},{10,1... | collective-permute-start | bytes 1105928 | tf_op jit(solution)/shard_map/ppermute | solution.py:408
  13.7 36.3 %collective-permute-start.1 = (f32[120,768]{1,0:T(8,128)}, f32[120,768]{1,0:T(8,128)}, u32[]{:S(2)}, u32[]{:S(2)}) collective-permute-start(f32[120,768]{1,0:T(8,128)} %maximum_convert_fusion), channel_id=1, source_target_pairs={{0,2},{1,3},{2,0},{3,1},{4,6},{5,7},{6,4},{7,5},{8,10},{9,11},{10,... | collective-permute-start | bytes 1105928 | tf_op jit(solution)/shard_map/ppermute | solution.py:408
  16.3 33.7 %collective-permute-start.2 = (f32[120,768]{1,0:T(8,128)}, f32[120,768]{1,0:T(8,128)}, u32[]{:S(2)}, u32[]{:S(2)}) collective-permute-start(f32[120,768]{1,0:T(8,128)} %maximum_convert_fusion), channel_id=1, source_target_pairs={{0,3},{1,0},{2,1},{3,2},{4,7},{5,4},{6,5},{7,6},{8,11},{9,8},{10,9... | collective-permute-start | bytes 1105928 | tf_op jit(solution)/shard_map/ppermute | solution.py:408
  19.8 20.9 %collective-permute-start.3 = (f32[1,1344]{1,0:T(1,128)S(1)}, f32[1,1344]{1,0:T(1,128)S(1)}, u32[]{:S(2)}, u32[]{:S(2)}) collective-permute-start(f32[1,1344]{1,0:T(1,128)S(1)} %convert_element_type.38), channel_id=1, source_target_pairs={{0,1},{1,2},{2,3},{3,0},{4,5},{5,6},{6,7},{7,4},{8,9},{9,10},{10,1... | collective-permute-start | bytes 16136 | tf_op jit(solution)/shard_map/ppermute | solution.py:408
  20.5 28.2 %collective-permute-start.4 = (f32[1,1344]{1,0:T(1,128)S(1)}, f32[1,1344]{1,0:T(1,128)}, u32[]{:S(2)}, u32[]{:S(2)}) collective-permute-start(f32[1,1344]{1,0:T(1,128)S(1)} %convert_element_type.38), channel_id=1, source_target_pairs={{0,2},{1,3},{2,0},{3,1},{4,6},{5,7},{6,4},{7,5},{8,10},{9,11},{10,... | collective-permute-start | bytes 16136 | tf_op jit(solution)/shard_map/ppermute | solution.py:408
  51.2 31.8 %collective-permute-start.6 = (f32[1,3,64,768]{3,2,1,0:T(8,128)S(1)}, f32[1,3,64,768]{3,2,1,0:T(8,128)S(1)}, u32[]{:S(2)}, u32[]{:S(2)}) collective-permute-start(f32[1,3,64,768]{3,2,1,0:T(8,128)S(1)} %get-tuple-element.131.refs_0_), channel_id=1, source_target_pairs={{0,8},{4,12},{8,0},{12,4},{16,24},{20,28},{24,16},{28,20},{1,9},{5... | collective-permute-start | bytes 1769480 | tf_op jit(solution)/shard_map/ppermute | solution.py:412
  52.7 30.3 %collective-permute-start.7 = (f32[1,3,56,768]{3,2,1,0:T(8,128)S(1)}, f32[1,3,56,768]{3,2,1,0:T(8,128)S(1)}, u32[]{:S(2)}, u32[]{:S(2)}) collective-permute-start(f32[1,3,56,768]{3,2,1,0:T(8,128)S(1)} %get-tuple-element.132.refs_1_), channel_id=1, source_target_pairs={{0,16},{4,20},{8,24},{12,28},{16,0},{20,4},{24,8},{28,12},{1,17},{... | collective-permute-start | bytes 1548296 | tf_op jit(solution)/shard_map/ppermute | solution.py:412
  57.4 24.0 %collective-permute-start.9 = (f32[96,768]{1,0:T(8,128)}, f32[96,768]{1,0:T(8,128)S(1)}, u32[]{:S(2)}, u32[]{:S(2)}) collective-permute-start(f32[96,768]{1,0:T(8,128)} %dynamic-slice_convert_fusion), channel_id=1, source_target_pairs={{0,2},{1,3},{2,0},{3,1},{4,6},{5,7},{6,4},{7,5},{8,10},{9,11},{10,... | collective-permute-start | bytes 884744 | tf_op jit(solution)/shard_map/ppermute | solution.py:408
  84.6 43.2 %collective-permute-start.11 = (f32[2,3,64,768]{3,2,1,0:T(8,128)}, f32[2,3,64,768]{3,2,1,0:T(8,128)}, u32[]{:S(2)}, u32[]{:S(2)}) collective-permute-start(f32[2,3,64,768]{3,2,1,0:T(8,128)} %get-tuple-element.141.refs_3_), channel_id=1, source_target_pairs={{0,16},{4,20},{8,24},{12,28},{16,0},{20,4},{24,8},{28,12},{1,17},{... | collective-permute-start | bytes 3538952 | tf_op jit(solution)/shard_map/ppermute | solution.py:412
  85.1 42.7 %collective-permute-start.12 = (f32[2,3,56,768]{3,2,1,0:T(8,128)}, f32[2,3,56,768]{3,2,1,0:T(8,128)}, u32[]{:S(2)}, u32[]{:S(2)}) collective-permute-start(f32[2,3,56,768]{3,2,1,0:T(8,128)} %get-tuple-element.142.refs_4_), channel_id=1, source_target_pairs={{0,8},{4,12},{8,0},{12,4},{16,24},{20,28},{24,16},{28,20},{1,9},{5... | collective-permute-start | bytes 3096584 | tf_op jit(solution)/shard_map/ppermute | solution.py:412
  89.1 55.4 %all-to-all-start = ((f32[4,256,384]{2,1,0:T(8,128)}), f32[4,256,384]{2,1,0:T(8,128)}, u32[]{:S(2)}, u32[]{:S(2)}) async-start(f32[4,256,384]{2,1,0:T(8,128)} %bitcast.72), calls=%async_computation | async-start | bytes 3145728 | tf_op jit(solution)/shard_map/all_to_all | solution.py:848
  93.5 264.0 %all-gather.2.cloned.1.call-start = ((), (), s32[]{:S(2)}) async-start(), calls=%async_computation.4 | async-start | bytes 7864320 | tf_op jit(solution)/shard_map/all_gather | solution.py:868
  93.6 26.3 %collective-permute-start.13 = (f32[1,3,48,768]{3,2,1,0:T(8,128)}, f32[1,3,48,768]{3,2,1,0:T(8,128)}, u32[]{:S(2)}, u32[]{:S(2)}) collective-permute-start(f32[1,3,48,768]{3,2,1,0:T(8,128)} %copy-done.17), channel_id=1, source_target_pairs={{0,8},{4,12},{8,0},{12,4},{16,24},{20,28},{24,16},{28,20},{1,9},{5... | collective-permute-start | bytes 1327112 | tf_op jit(solution)/shard_map/ppermute | solution.py:412
  94.2 28.6 %collective-permute-start.14 = (f32[1,3,48,768]{3,2,1,0:T(8,128)}, f32[1,3,48,768]{3,2,1,0:T(8,128)}, u32[]{:S(2)}, u32[]{:S(2)}) collective-permute-start(f32[1,3,48,768]{3,2,1,0:T(8,128)} %copy-done.19), channel_id=1, source_target_pairs={{0,16},{4,20},{8,24},{12,28},{16,0},{20,4},{24,8},{28,12},{1,17},{... | collective-permute-start | bytes 1327112 | tf_op jit(solution)/shard_map/ppermute | solution.py:412
  127.9 24.3 %collective-permute-start.15 = (f32[2,3,96,768]{3,2,1,0:T(8,128)}, f32[2,3,96,768]{3,2,1,0:T(8,128)}, u32[]{:S(2)}, u32[]{:S(2)}) collective-permute-start(f32[2,3,96,768]{3,2,1,0:T(8,128)} %get-tuple-element.148), channel_id=1, source_target_pairs={{0,4},{4,0},{8,12},{12,8},{16,20},{20,16},{24,28},{28,24},{1,5},{5... | collective-permute-start | bytes 5308424 | tf_op jit(solution)/shard_map/ppermute | solution.py:412
  128.5 23.7 %collective-permute-start.16 = (f32[2,3,48,768]{3,2,1,0:T(8,128)}, f32[2,3,48,768]{3,2,1,0:T(8,128)}, u32[]{:S(2)}, u32[]{:S(2)}) collective-permute-start(f32[2,3,48,768]{3,2,1,0:T(8,128)} %get-tuple-element.149.refs_2_), channel_id=1, source_target_pairs={{0,16},{4,20},{8,24},{12,28},{16,0},{20,4},{24,8},{28,12},{1,17},{... | collective-permute-start | bytes 2654216 | tf_op jit(solution)/shard_map/ppermute | solution.py:412
  129.0 23.2 %collective-permute-start.17 = (f32[2,3,48,768]{3,2,1,0:T(8,128)}, f32[2,3,48,768]{3,2,1,0:T(8,128)}, u32[]{:S(2)}, u32[]{:S(2)}) collective-permute-start(f32[2,3,48,768]{3,2,1,0:T(8,128)} %get-tuple-element.150.refs_3_), channel_id=1, source_target_pairs={{0,8},{4,12},{8,0},{12,4},{16,24},{20,28},{24,16},{28,20},{1,9},{5... | collective-permute-start | bytes 2654216 | tf_op jit(solution)/shard_map/ppermute | solution.py:412
  152.2 22.0 %collective-permute-start.24 = (f32[2,3,48,768]{3,2,1,0:T(8,128)}, f32[2,3,48,768]{3,2,1,0:T(8,128)}, u32[]{:S(2)}, u32[]{:S(2)}) collective-permute-start(f32[2,3,48,768]{3,2,1,0:T(8,128)} %collective-permute-done.16.refs_4_), channel_id=1, source_target_pairs={{0,4},{4,0},{8,12},{12,8},{16,20},{20,16},{24,28},{28,24},{1,5},{5... | collective-permute-start | bytes 2654216 | tf_op jit(solution)/shard_map/ppermute | solution.py:412
  152.4 21.8 %collective-permute-start.25 = (f32[2,3,48,768]{3,2,1,0:T(8,128)}, f32[2,3,48,768]{3,2,1,0:T(8,128)}, u32[]{:S(2)}, u32[]{:S(2)}) collective-permute-start(f32[2,3,48,768]{3,2,1,0:T(8,128)} %collective-permute-done.17.refs_5_), channel_id=1, source_target_pairs={{0,4},{4,0},{8,12},{12,8},{16,20},{20,16},{24,28},{28,24},{1,5},{5... | collective-permute-start | bytes 2654216 | tf_op jit(solution)/shard_map/ppermute | solution.py:412
  191.3 171.2 %reduce-scatter.3.cloned.1.call-start = ((), (), s32[]{:S(2)}) async-start(), calls=%async_computation.3 | async-start | bytes 10616832 | tf_op jit(solution)/shard_map/reduce_scatter | solution.py:874
  204.4 193.5 %reduce-scatter.5.cloned.1.call-start = ((), (), s32[]{:S(2)}) async-start(), calls=%async_computation.5 | async-start | bytes 10616832 | tf_op jit(solution)/shard_map/reduce_scatter | solution.py:897
  260.7 41.2 %collective-permute-start.35 = (f32[192,1536]{1,0:T(8,128)}, f32[192,1536]{1,0:T(8,128)}, u32[]{:S(2)}, u32[]{:S(2)}) collective-permute-start(f32[192,1536]{1,0:T(8,128)} %concatenate.83), channel_id=1, source_target_pairs={{0,16},{4,20},{8,24},{12,28},{16,0},{20,4},{24,8},{28,12},{1,17},{... | collective-permute-start | bytes 3538952 | tf_op jit(solution)/shard_map/ppermute | solution.py:412
  260.9 43.3 %collective-permute-start.34 = (f32[192,1536]{1,0:T(8,128)}, f32[192,1536]{1,0:T(8,128)S(1)}, u32[]{:S(2)}, u32[]{:S(2)}) collective-permute-start(f32[192,1536]{1,0:T(8,128)} %pad_maximum_fusion), channel_id=1, source_target_pairs={{0,8},{4,12},{8,0},{12,4},{16,24},{20,28},{24,16},{28,20},{1,9},{5... | collective-permute-start | bytes 3538952 | tf_op jit(solution)/shard_map/ppermute | solution.py:412
  306.8 42.2 %collective-permute-start.36 = (f32[512,768]{1,0:T(8,128)}, f32[512,768]{1,0:T(8,128)}, u32[]{:S(2)}, u32[]{:S(2)}) collective-permute-start(f32[512,768]{1,0:T(8,128)} %get-tuple-element.211.own_ref), channel_id=1, source_target_pairs={{0,1},{1,2},{2,3},{4,5},{5,6},{6,7},{8,9},{9,10},{10,11},{12,13},{... | collective-permute-start | bytes 4718600 | tf_op jit(solution)/shard_map/ppermute | solution.py:745
  316.1 38.1 %collective-permute-start.37 = (f32[512,768]{1,0:T(8,128)}, f32[512,768]{1,0:T(8,128)}, u32[]{:S(2)}, u32[]{:S(2)}) collective-permute-start(f32[512,768]{1,0:T(8,128)} %get-tuple-element.211.own_ref), channel_id=1, source_target_pairs={{1,0},{2,1},{3,2},{5,4},{6,5},{7,6},{9,8},{10,9},{11,10},{13,12},{... | collective-permute-start | bytes 4718600 | tf_op jit(solution)/shard_map/ppermute | solution.py:746
  318.9 36.7 %collective-permute-start.40 = (f32[96,1536]{1,0:T(8,128)}, f32[96,1536]{1,0:T(8,128)}, u32[]{:S(2)}, u32[]{:S(2)}) collective-permute-start(f32[96,1536]{1,0:T(8,128)} %slice.191), channel_id=1, source_target_pairs={{0,8},{4,12},{8,0},{12,4},{16,24},{20,28},{24,16},{28,20},{1,9},{5... | collective-permute-start | bytes 1769480 | tf_op jit(solution)/shard_map/ppermute | solution.py:412
  349.0 21.4 %collective-permute-start.41 = (f32[512,768]{1,0:T(8,128)}, f32[512,768]{1,0:T(8,128)}, u32[]{:S(2)}, u32[]{:S(2)}) collective-permute-start(f32[512,768]{1,0:T(8,128)} %collective-permute-done.36.refs_0_), channel_id=1, source_target_pairs={{1,2},{2,3},{5,6},{6,7},{9,10},{10,11},{13,14},{14,15},{17,18},{18... | collective-permute-start | bytes 4718600 | tf_op jit(solution)/shard_map/ppermute | solution.py:745
  354.2 37.2 %collective-permute-start.42 = (f32[512,768]{1,0:T(8,128)}, f32[512,768]{1,0:T(8,128)}, u32[]{:S(2)}, u32[]{:S(2)}) collective-permute-start(f32[512,768]{1,0:T(8,128)} %collective-permute-done.37.refs_3_), channel_id=1, source_target_pairs={{1,0},{2,1},{5,4},{6,5},{9,8},{10,9},{13,12},{14,13},{17,16},{18,1... | collective-permute-start | bytes 4718600 | tf_op jit(solution)/shard_map/ppermute | solution.py:746
  365.3 31.6 %collective-permute-start.43 = (f32[192,768]{1,0:T(8,128)S(1)}, f32[192,768]{1,0:T(8,128)S(1)}, u32[]{:S(2)}, u32[]{:S(2)}) collective-permute-start(f32[192,768]{1,0:T(8,128)S(1)} %get-tuple-element.222), channel_id=1, source_target_pairs={{0,1},{4,5},{8,9},{12,13},{16,17},{20,21},{24,25},{28,29}} | collective-permute-start | bytes 1769480 | tf_op jit(solution)/shard_map/ppermute | solution.py:699
  369.7 27.2 %collective-permute-start.44 = (f32[192,768]{1,0:T(8,128)S(1)}, f32[192,768]{1,0:T(8,128)S(1)}, u32[]{:S(2)}, u32[]{:S(2)}) collective-permute-start(f32[192,768]{1,0:T(8,128)S(1)} %get-tuple-element.223), channel_id=1, source_target_pairs={{3,2},{7,6},{11,10},{15,14},{19,18},{23,22},{27,26},{31,30}} | collective-permute-start | bytes 1769480 | tf_op jit(solution)/shard_map/ppermute | solution.py:703
  370.4 51.8 %collective-permute-start.46 = (f32[512,768]{1,0:T(8,128)}, f32[512,768]{1,0:T(8,128)}, u32[]{:S(2)}, u32[]{:S(2)}) collective-permute-start(f32[512,768]{1,0:T(8,128)} %collective-permute-done.41.refs_1_), channel_id=1, source_target_pairs={{2,3},{6,7},{10,11},{14,15},{18,19},{22,23},{26,27},{30,31}} | collective-permute-start | bytes 4718600 | tf_op jit(solution)/shard_map/ppermute | solution.py:745
  391.4 36.3 %collective-permute-start.47 = (f32[512,768]{1,0:T(8,128)}, f32[512,768]{1,0:T(8,128)}, u32[]{:S(2)}, u32[]{:S(2)}) collective-permute-start(f32[512,768]{1,0:T(8,128)} %collective-permute-done.42.refs_4_), channel_id=1, source_target_pairs={{1,0},{5,4},{9,8},{13,12},{17,16},{21,20},{25,24},{29,28}} | collective-permute-start | bytes 4718600 | tf_op jit(solution)/shard_map/ppermute | solution.py:746
  (82 other events, 1075.9 us)
Sparse Core Ops, SparseCore 0:
  191.4 115.7 all-gather.1
Sparse Core Ops, SparseCore 1:
  204.4 91.4 reduce-scatter.2
  306.9 78.3 reduce-scatter.4

commit v5 on v4

--- a/solution.py
+++ b/solution.py
@@ -1,5 +1,6 @@
 import math
 from functools import partial
+from typing import NamedTuple
 
 import jax
 import jax.numpy as jnp
@@ -59,7 +60,7 @@
         grid_spec=pltpu.PrefetchScalarGridSpec(
             num_scalar_prefetch=len(lead),
             grid=grid,
-            in_specs=[pl.BlockSpec(b, m) for _, b, m in ins],
+            in_specs=[pl.BlockSpec(memory_space=m) if b is None else pl.BlockSpec(b, m) for _, b, m in ins],
             out_specs=[pl.BlockSpec(b, m) for _, _, b, m in outs],
             scratch_shapes=list(scratch),
         ),
@@ -68,6 +69,87 @@
         compiler_params=pltpu.CompilerParams(vmem_limit_bytes=56 << 20),
         name=name,
     )(*lead, *(a for a, _, _ in ins))
+
+
+class Stream(NamedTuple):
+    local: jax.Array
+    target: int
+    pieces: list
+
+
+def plan_of(locals_, pieces, wanted):
+    plan, where = [], []
+    for _, parts in pieces:
+        plan.append([])
+        for entry, sender, base, spans in parts:
+            for row, rows, target, offset in spans:
+                if target in wanted:
+                    plan[-1].append((entry, base + row, rows, wanted.index(target)))
+                    where.append(sender * (locals_[wanted.index(target)].shape[0] // 8) + offset)
+    return plan, jnp.stack(where)
+
+
+def piece_copies(plan, where_ref, pieces, holds, sems):
+    found = []
+    for piece, spans in zip(pieces, plan):
+        for i, source, rows, target in spans:
+            start = pl.multiple_of(where_ref[len(found)], 8)
+            found.append(
+                pltpu.make_async_copy(
+                    piece.at[i, :, pl.ds(source, rows)], holds[target].at[:, pl.ds(start, rows)], sems.at[len(found)]
+                )
+            )
+    return found
+
+
+def call_with(body, name, grid, slot_of, weights, ins, outs, flops, exps=0, prefetch=None):
+    axes = len(grid)
+    at = lambda *ids: (slot_of(*ids[:axes]), 0, 0)
+    if not isinstance(weights, Stream):
+        ins = [(weights, (None,) + weights.shape[1:], at)] + ins
+        if prefetch is not None:
+            return *call(lambda _, *refs: body(*refs), name, grid, ins, outs, flops, exps, prefetch=prefetch), weights
+        return *call(body, name, grid, ins, outs, flops, exps), weights
+    local, target, pieces = weights
+    others = pieces[0][0].shape[1]
+    plan, where = plan_of([local], pieces, [target])
+    used = [n for n, spans in enumerate(plan) if spans]
+    plan, arrays = [plan[n] for n in used], [pieces[n][0] for n in used]
+    lead, count, inner = int(prefetch is not None), len(arrays), len(ins)
+
+    def kernel(*refs):
+        refs = refs[lead:]
+        where_ref, local_ref, refs = refs[0], refs[1], refs[2:]
+        piece_refs, refs = refs[:count], refs[count:]
+        full_ref, hold, sems = refs[-3:]
+        ids = [pl.program_id(n) for n in range(axes)]
+        slot = slot_of(*ids)
+        first = sum(ids) == slot
+        moves = piece_copies(plan, where_ref, piece_refs, [hold], sems)
+
+        @pl.when(jnp.logical_and(first, slot == 0))
+        def _():
+            for move in moves:
+                move.start()
+            full_ref[...] = local_ref[...]
+
+        @pl.when(jnp.logical_and(first, slot == 1))
+        def _():
+            for move in moves:
+                move.wait()
+
+        @pl.when(jnp.logical_and(first, slot > 0))
+        def _():
+            full_ref[...] = hold[jnp.maximum(slot - 1, 0)].astype(BF16)
+
+        body(full_ref, *refs[:-3])
+
+    rows, width = local.shape
+    flat = lambda *ids: (0, 0)
+    more = [(where, None, pltpu.SMEM), (local, local.shape, flat)] + [(a, None, pl.ANY) for a in arrays]
+    full = ((others + 1, rows, width), BF16, (None, rows, width), at)
+    scratch = [pltpu.VMEM((others, rows, width), F32), pltpu.SemaphoreType.DMA((where.shape[0],))]
+    return call(kernel, name, grid, more + ins, outs + [full], flops, exps, scratch, prefetch)
 
 
 def attend_kernel(x_ref, w_ref, bias_ref, ctx_ref):
@@ -111,8 +193,7 @@
     )[0]
 
 
-def output_kernel(slot_ref, x_ref, ctx_ref, w_ref, vec_ref, low_ref, hid_ref, hbf_ref, nrm_ref, inv_ref):
-    del slot_ref
+def output_kernel(w_ref, x_ref, ctx_ref, vec_ref, low_ref, hid_ref, hbf_ref, nrm_ref, inv_ref):
     slot = pl.program_id(1)
     cols = low_ref.shape[-1]
     folds = [ctx_ref[:, i : i + cols] for i in range(0, ctx_ref.shape[-1], cols)]
@@ -146,19 +227,21 @@
 
 def output_forward(slots_at, x, context, weights, vectors):
     rows, width = x.shape
-    slots, cols, _ = weights.shape
+    slots = slots_at.shape[0]
+    cols = width // slots
     mine = lambda i, j, at: (i, 0)
     flat = lambda i, j, at: (0, 0)
     token = (LENGTH, width)
     heads = (None, LENGTH, cols)
-    return call(
+    return call_with(
         output_kernel,
         "output_forward",
         (rows // LENGTH, slots),
+        lambda i, j: j,
+        weights,
         [
             (x, token, mine),
             (context, (None, LENGTH // fold_of(cols), fold_of(cols) * cols), lambda i, j, at: (at[j], i, 0)),
-            (weights, (None, cols, width), lambda i, j, at: (j, 0, 0)),
             (vectors, vectors.shape, flat),
         ],
         [
@@ -236,7 +319,7 @@
     )
 
 
-def inner_kernel(h_ref, w_ref, b_ref, act_ref, slope_ref):
+def inner_kernel(w_ref, h_ref, b_ref, act_ref, slope_ref):
     inner = dot(h_ref[...], w_ref[...], PLAIN) + b_ref[...]
     phi = 0.5 + 0.5 * lax.erf(inner * (0.5**0.5))
     bell = jnp.exp2(inner * inner * (-0.5 * 1.4426950408889634)) * 0.3989422804014327
@@ -246,16 +329,17 @@
 
 def inner_forward(hidden, weights, bias):
     rows, width = hidden.shape
-    slots, _, units = weights.shape
+    slots, _, units = bias.shape
     slot = lambda i, j: (i, j, 0)
     block = LENGTH // 2
-    return call(
+    return call_with(
         inner_kernel,
         "inner_forward",
         (slots, rows // block),
+        lambda i, j: i,
+        weights,
         [
             (hidden, (block, width), lambda i, j: (j, 0)),
-            (weights, (None, width, units), lambda i, j: (i, 0, 0)),
             (bias, (None, 1, units), lambda i, j: (i, 0, 0)),
         ],
         [
@@ -267,7 +351,7 @@
     )
 
 
-def outer_kernel(act_ref, w_ref, hid_ref, cot_ref, vec_ref, out_ref, gr_ref, go_ref, sum_ref):
+def outer_kernel(w_ref, act_ref, hid_ref, vec_ref, out_ref, nrm_ref, inv_ref):
     slot = pl.program_id(1)
     outer = dot(act_ref[...], w_ref[...], PLAIN)
 
@@ -283,46 +367,81 @@
     def _():
         bias, gain, shift = vec_ref[3:4], vec_ref[4:5], vec_ref[5:6]
 
-        def block(at, sums):
+        def block(at, carry):
             values = hid_ref[at] + (out_ref[at] + bias)
             layer_out, normed, inverse = norm_forward(values, gain, shift)
             out_ref[at] = layer_out
-            upstream = cot_ref[at].astype(F32)
-            grad = norm_backward(upstream, gain, normed, inverse)
-            rounded = grad.astype(BF16)
-            gr_ref[at] = grad
-            go_ref[at] = rounded
-            found = (upstream * normed, upstream, rounded.astype(F32))
-            return tuple(s + row_sums(f) for s, f in zip(sums, found))
-
-        for i, total in enumerate(by_rows(LENGTH, 256, block, (jnp.zeros_like(gain),) * 3)):
-            sum_ref[i : i + 1] = total
-
-
-def outer_forward(active, weights, hidden, cotangent, vectors):
+            nrm_ref[at] = normed
+            inv_ref[at] = inverse
+            return carry
+
+        by_rows(LENGTH, 256, block)
+
+
+def outer_forward(active, weights, hidden, vectors):
     rows, width = hidden.shape
-    slots, units, _ = weights.shape
+    slots, _, units = active.shape
     mine = lambda i, j: (i, 0)
-    flat = lambda i, j: (0, 0)
     token = (LENGTH, width)
-    return call(
+    return call_with(
         outer_kernel,
         "outer_forward",
         (rows // LENGTH, slots),
+        lambda i, j: j,
+        weights,
         [
             (active, (None, LENGTH, units), lambda i, j: (j, i, 0)),
-            (weights, (None, units, width), lambda i, j: (j, 0, 0)),
             (hidden, token, mine),
-            (cotangent, token, mine),
-            (vectors, vectors.shape, flat),
+            (vectors, vectors.shape, lambda i, j: (0, 0)),
         ],
         [
             ((rows, width), F32, token, mine),
             ((rows, width), F32, token, mine),
+            ((rows, 1), F32, (LENGTH, 1), mine),
+        ],
+        flops=2 * rows * width * slots * units,
+    )
+
+
+def last_norm_kernel(cot_ref, nrm_ref, inv_ref, vec_ref, gr_ref, go_ref, sum_ref):
+    upstream, normed = cot_ref[...].astype(F32), nrm_ref[...]
+    grad = norm_backward(upstream, vec_ref[4:5], normed, inv_ref[...])
+    rounded = grad.astype(BF16)
+    gr_ref[...] = grad
+    go_ref[...] = rounded
+    found = (upstream * normed, upstream, rounded.astype(F32))
+
+    @pl.when(pl.program_id(0) == 0)
+    def _():
+        sum_ref[...] = jnp.zeros_like(sum_ref)
+
+    for i, value in enumerate(found):
+        sum_ref[i : i + 1] += row_sums(value)
+
+
+def last_norm_backward(cotangent, normed, inverse, vectors):
+    rows, width = normed.shape
+    block = 128
+    mine = lambda i: (i, 0)
+    flat = lambda i: (0, 0)
+    token = (block, width)
+    return call(
+        last_norm_kernel,
+        "last_norm_backward",
+        (rows // block,),
+        [
+            (cotangent, token, mine),
+            (normed, token, mine),
+            (inverse, (block, 1), mine),
+            (vectors, vectors.shape, flat),
+        ],
+        [
+            ((rows, width), F32, token, mine),
             ((rows, width), BF16, token, mine),
-            ((rows // LENGTH, 8, width), F32, (None, 8, width), lambda i, j: (i, 0, 0)),
-        ],
-        flops=2 * rows * width * slots * units,
+            ((8, width), F32, (8, width), flat),
+        ],
+        flops=0,
+        moved=0,
     )
 
 
@@ -456,68 +575,39 @@
     )(order, local, full)
 
 
-def assemble_kernel(plan, *refs):
-    where_ref, refs = refs[0], refs[1:]
-    count = len(plan)
-    targets = (len(refs) - count - 1) // 3
-    locals_, pieces, outs, holds, sems = (
-        refs[:targets],
-        refs[targets : targets + count],
-        refs[targets + count : 2 * targets + count],
-        refs[2 * targets + count : -1],
-        refs[-1],
-    )
-    copies = []
-    for piece, spans in zip(pieces, plan):
-        for i, source, rows, target in spans:
-            start = pl.multiple_of(where_ref[len(copies)], 8)
-            copies.append(
-                pltpu.make_async_copy(
-                    piece.at[i, :, pl.ds(source, rows)],
-                    holds[target].at[:, pl.ds(start, rows)],
-                    sems.at[len(copies)],
-                )
-            )
-            copies[-1].start()
-    for local, out in zip(locals_, outs):
-        out[0] = local[...]
-    for copy in copies:
-        copy.wait()
-    for hold, out in zip(holds, outs):
-        for k in range(hold.shape[0]):
-
-            def block(at, carry, k=k, hold=hold, out=out):
-                out[k + 1, at] = hold[k, at].astype(BF16)
-                return carry
-
-            by_rows(hold.shape[1], 96, block)
-
-
-def assemble(locals_, pieces):
-    width = locals_[0].shape[1]
+def assemble_kernel(plan, where_ref, local_ref, *refs):
+    *pieces, out_ref, hold, sems = refs
+    moves = piece_copies(plan, where_ref, pieces, [hold], sems)
+    for move in moves:
+        move.start()
+    out_ref[0] = local_ref[...]
+    for move in moves:
+        move.wait()
+    for k in range(hold.shape[0]):
+
+        def block(at, carry, k=k):
+            out_ref[k + 1, at] = hold[k, at].astype(BF16)
+            return carry
+
+        by_rows(hold.shape[1], 96, block)
+
+
+def assemble(stream):
+    local, target, pieces = stream
+    rows, width = local.shape
     others = pieces[0][0].shape[1]
-    where, plan = [], []
-    for _, parts in pieces:
-        plan.append([])
-        for entry, sender, base, spans in parts:
-            for row, rows, target, offset in spans:
-                plan[-1].append((entry, base + row, rows, target))
-                where.append(sender * (locals_[target].shape[0] // 8) + offset)
-    total = sum(w.shape[0] for w in locals_)
+    plan, where = plan_of([local], pieces, [target])
     space = pl.BlockSpec(memory_space=pltpu.VMEM)
     return pl.pallas_call(
         partial(assemble_kernel, plan),
-        in_specs=[pl.BlockSpec(memory_space=pltpu.SMEM)]
-        + [space] * len(locals_)
-        + [pl.BlockSpec(memory_space=pl.ANY)] * len(pieces),
-        out_specs=[space] * len(locals_),
-        out_shape=[jax.ShapeDtypeStruct((others + 1,) + w.shape, BF16) for w in locals_],
-        scratch_shapes=[pltpu.VMEM((others,) + w.shape, F32) for w in locals_]
-        + [pltpu.SemaphoreType.DMA((len(where),))],
-        cost_estimate=pl.CostEstimate(flops=0, bytes_accessed=others * total * width * 6, transcendentals=0),
+        in_specs=[pl.BlockSpec(memory_space=pltpu.SMEM), space] + [pl.BlockSpec(memory_space=pl.ANY)] * len(pieces),
+        out_specs=space,
+        out_shape=jax.ShapeDtypeStruct((others + 1, rows, width), BF16),
+        scratch_shapes=[pltpu.VMEM((others, rows, width), F32), pltpu.SemaphoreType.DMA((where.shape[0],))],
+        cost_estimate=pl.CostEstimate(flops=0, bytes_accessed=others * rows * width * 6, transcendentals=0),
         compiler_params=pltpu.CompilerParams(vmem_limit_bytes=48 << 20),
         name="assemble",
-    )(jnp.stack(where), *locals_, *(array for array, _ in pieces))
+    )(where, local, *(array for array, _ in pieces))
 
 
 def shares(weights, dp=8):
@@ -577,7 +667,7 @@
     return copies([a, b, ax, by], shapes, plan)
 
 
-def full_weights(locals_, a, b, ay, bx, c, d):
+def pieces_of(locals_, a, b, ay, bx, c, d):
     me = lax.axis_index("dp")
     cut_at, end = a.shape[2], a.shape[2] + b.shape[2]
     ends = [0]
@@ -594,7 +684,7 @@
 
     upper = lambda rels: [(i, me ^ r, 0, spans(0, cut_at)) for i, r in enumerate(rels)]
     lower = lambda rels, base=0: [(i, me ^ r, base, spans(cut_at, end)) for i, r in enumerate(rels)]
-    pieces = [
+    return [
         (a, upper((0, 2))),
         (b, lower((0, 4))),
         (ay, upper((4, 6))),
@@ -603,7 +693,6 @@
         (d[0], upper((5, 7))),
         (d[1], lower((3, 7))),
     ]
-    return assemble(locals_, pieces)
 
 
 def block_order(width):
@@ -793,13 +882,11 @@
     def rest_of_attention(context, weights):
         return output_forward(slots_at, x, context, weights, wide_vectors)
 
-    def outer_half(active, weights, hidden):
-        return outer_forward(active, weights, hidden, cot, wide_vectors)
 
     def small_sums(qkv_sums, inner_sums, sums_one, sums_two):
         by_slot = jnp.concatenate([jnp.sum(qkv_sums, axis=0), jnp.sum(inner_sums, axis=0)], axis=-1)
         by_place = by_slot[slots_at].reshape(-1)
-        rest = jnp.concatenate([jnp.sum(sums_one, axis=0)[:3], jnp.sum(sums_two, axis=0)[:3]]).reshape(-1)
+        rest = jnp.concatenate([jnp.sum(sums_one, axis=0)[:3], sums_two[:3]]).reshape(-1)
         return jnp.concatenate([by_place, rest])
 
     local_bias = vectors[:, : 3 * cols]
@@ -812,9 +899,10 @@
             gather_plain(w, dp, tensor) for w in (w_inner, w_output, w_outer, qkv_local)
         )
         context = lax.all_to_all(context, "tensor", 0, 0, tiled=True)
-        context, hidden, hidden_bf, normed, inverse = rest_of_attention(context, output_full)
-        active, slope = inner_forward(hidden_bf, inner_full, inner_bias)
-        layer_out, grad_resid2, grad_outer, sums_two = outer_half(active, outer_full, hidden)
+        context, hidden, hidden_bf, normed, inverse, output_full = rest_of_attention(context, output_full)
+        active, slope, inner_full = inner_forward(hidden_bf, inner_full, inner_bias)
+        layer_out, normed_two, inverse_two, outer_full = outer_forward(active, outer_full, hidden, wide_vectors)
+        grad_resid2, grad_outer, sums_two = last_norm_backward(cot, normed_two, inverse_two, wide_vectors)
         layer_out = narrow(lax.all_gather(layer_out, "tensor", axis=0, tiled=True), own_rows)
         grad_inner, grad_resid1, grad_attn, inner_sums, sums_one = inner_backward(
             grad_outer, outer_full, slope, inner_full, grad_resid2, normed, inverse, wide_vectors
@@ -852,21 +940,22 @@
         ay1, bx1, a2, b2, ab2, p3 = stage(ay1, bx1, a2, b2, ab2, p3)
 
         c2, ay2, bx2 = flip(ab2, 1), flip(a2, 4), flip(b2, 2)
-        inner_full, output_full = full_weights([w_inner, w_output], a1, b1, ay1, bx1, c1, d1)
-        context, hidden, hidden_bf, normed, inverse = rest_of_attention(context, output_full)
-        c2, ay2, bx2, p3, hidden_bf = stage(c2, ay2, bx2, p3, hidden_bf)
+        pieces = pieces_of([w_inner, w_output], a1, b1, ay1, bx1, c1, d1)
+        context, hidden, hidden_bf, normed, inverse, output_full = rest_of_attention(context, Stream(w_output, 1, pieces))
+        active, slope, inner_full = inner_forward(hidden_bf, Stream(w_inner, 0, pieces), inner_bias)
+        c2, ay2, bx2, p3, active = stage(c2, ay2, bx2, p3, active)
 
         d2, z3 = other_core(ay2, bx2), across(p3, tensor)
-        active, slope = inner_forward(hidden_bf, inner_full, inner_bias)
-        *d2, active = stage(*d2, active)
-
-        (outer_full,) = full_weights([w_outer], a2, b2, ay2, bx2, c2, d2)
-        layer_out, grad_resid2, grad_outer, sums_two = outer_half(active, outer_full, hidden)
+        pieces = pieces_of([w_outer], a2, b2, ay2, bx2, c2, d2)
+        layer_out, normed_two, inverse_two, outer_full = outer_forward(
+            active, Stream(w_outer, 0, pieces), hidden, wide_vectors
+        )
+        *z3, layer_out, normed_two = stage(*z3, layer_out, normed_two)
+
+        layer_out = lax.all_gather(layer_out, "tensor", axis=0, tiled=True)
         a3, b3 = halves(z3, n3)
-        a3, b3, layer_out, grad_outer = stage(a3, b3, layer_out, grad_outer)
-
-        layer_out = lax.all_gather(layer_out, "tensor", axis=0, tiled=True)
         ax, by = flip(a3, 2), flip(b3, 4)
+        grad_resid2, grad_outer, sums_two = last_norm_backward(cot, normed_two, inverse_two, wide_vectors)
         part1 = grad_full((grad_outer, active))
         a3, b3, ab3 = join(a3, ax, b3, by)
         a3, b3, ab3, part1, grad_outer = stage(a3, b3, ab3, part1, grad_outer)
@@ -883,7 +972,7 @@
         *d3, send, grad_attn = stage(*d3, send, grad_attn)
 
         got = flip(send, 1)
-        (qkv_full,) = full_weights([qkv_local], a3, b3, ay3, bx3, c3, d3)
+        qkv_full = assemble(Stream(qkv_local, 0, pieces_of([qkv_local], a3, b3, ay3, bx3, c3, d3)))
         (a, ak), (b, bk) = split_paths(keep + got, share)
         a, b, qkv_full, grad_attn = stage(a, b, qkv_full, grad_attn)
 
@@ -892,7 +981,7 @@
             x, grad_attn, grad_resid1, qkv_full, output_full, qkv_bias, context
         )
         a, b = ak + ax, bk + by
-        a_send, b_send, part3, grad_x = stage(a[:share], b[:share], part3, grad_x)
+        a_send, b_send = stage(a[:share], b[:share])
 
         part3 = lax.psum_scatter(part3, "dp", scatter_dimension=0, tiled=True)
         g1 = onward((grad_x, grad_x), tensor, 1)

time: 477 us -> 458 us (0.960)
  waiting for transfers between devices: 161 us -> 140 us
  starting transfers between devices: 88.5 us -> 95.1 us
    ppermute x3, waiting for transfers between devices: 28 us -> 8.18 us  [onward(): lax.ppermute(d, 'tensor', [(i, i - 1) for i in range(1, tensor - step + 1)])]
    pallas_call x3 -> x1, Pallas kernels: 17.7 us -> 3.61 us  [assemble(): pl.pallas_call(partial(assemble_kernel, plan), in_specs=[pl.BlockSpec(mem...]
    pallas_call x10 -> x11, Pallas kernels: 114 us -> 124 us  [call(): pl.pallas_call(kernel, grid_spec=pltpu.PrefetchScalarGridSpec(num_scalar_...]
    ppermute x3, waiting for transfers between devices: 15.1 us -> 7.88 us  [onward(): lax.ppermute(u, 'tensor', [(i, i + 1) for i in range(step - 1, tensor - 1)])]
    ppermute x6, starting transfers between devices: 24.3 us -> 29.9 us  [up(): return lax.ppermute(values, 'tensor', [(i, i + 1) for i in range(step)])]
    unnamed x100 -> x96, local copies, waits for them, and re-layouts: 19.3 us -> 18.9 us
  transfers between devices with their start and end apart: 65 -> 65, of which waited for: 25 -> 27; matrix products, arithmetic and copies ran while one was open for 9% -> 9% of each run, Pallas kernels for 25% -> 29%
where the time goes in v5:
time: 458 us; the launch traced here: 456 us
  waiting for transfers between devices  140 us (31%)
  Pallas kernels  137 us (30%)
  starting transfers between devices  95.1 us (21%)
  local copies, waits for them, and re-layouts  39.9 us (9%)
  other arithmetic  27.5 us (6%)
  between operations  16.4 us (4%)
    pallas_call x11, Pallas kernels, call(): pl.pallas_call(kernel, grid_spec=pltpu.PrefetchScalarGridSpec(num_scalar_...  124 us
    ppermute x29, waiting for transfers between devices, flip(): return lax.ppermute(values, 'dp', [(i, i ^ bit) for i in range(8)])  77.2 us
    ppermute x12, waiting for transfers between devices, shift_to(): lax.ppermute(values, 'tensor', [(i, (i + k) % tensor) for i in range(tens...  31.6 us
    ppermute x6, starting transfers between devices, up(): return lax.ppermute(values, 'tensor', [(i, i + 1) for i in range(step)])  29.9 us
    unnamed x96, local copies, waits for them, and re-layouts  18.9 us
    ppermute x12, starting transfers between devices, shift_to(): lax.ppermute(values, 'tensor', [(i, (i + k) % tensor) for i in range(tens...  17.8 us
    ppermute x29, starting transfers between devices, flip(): return lax.ppermute(values, 'dp', [(i, i ^ bit) for i in range(8)])  16.7 us
    ppermute x3, starting transfers between devices, onward(): lax.ppermute(u, 'tensor', [(i, i + 1) for i in range(step - 1, tensor - 1)])  11.8 us
  transfers between devices with their start and end apart: 65, of which 27 were waited for; matrix products, arithmetic and copies ran while one was open for 9% of the time, Pallas kernels for 29%

profile of v5, /device:TPU:0, one launch (start us, length us, event | category | flops | bytes accessed | tf_op | source)
XLA Modules:
  0.0 456.2 jit_solution(10190203571530506998)
XLA Ops:
  23.5 11.6 %attend_forward.1 = f32[1024,384]{1,0:T(8,128)} custom-call(bf16[2048,768]{1,0:T(8,128)(2,1)} %x_ref.1, bf16[576,768]{1,0:T(8,128)(2,1)} %pad_maximum_fusion.1.w_ref.local_ref, f32[1,576]{1,0:T(1,128)} %slice.181.bias_ref), custom_call_target="tpu_custom_call" | custom-call | flops 2617245696 | bytes 5605632 | tf_op jit(solution)/shard_map/attend_forward/pallas_call | solution.py:58
  36.8 3.9 collective-permute-done.3
  41.4 7.3 %collective-permute-done.4 = f32[1,1344]{1,0:T(1,128)} collective-permute-done((f32[1,1344]{1,0:T(1,128)S(1)}, f32[1,1344]{1,0:T(1,128)}, u32[]{:S(2)}, u32[]{:S(2)}) %collective-permute-start.4) | collective-permute-done | bytes 5408 | tf_op jit(solution)/shard_map/ppermute | solution.py:527
  63.7 4.1 collective-permute-done.10.refs_2_
  67.7 5.4 %collective-permute-done.8.refs_0_ = f32[96,768]{1,0:T(8,128)S(1)} collective-permute-done((f32[96,768]{1,0:T(8,128)}, f32[96,768]{1,0:T(8,128)S(1)}, u32[]{:S(2)}, u32[]{:S(2)}) %collective-permute-start.8) | collective-permute-done | bytes 294944 | tf_op jit(solution)/shard_map/ppermute | solution.py:527
  73.1 8.3 %collective-permute-done.9.refs_1_ = f32[96,768]{1,0:T(8,128)S(1)} collective-permute-done((f32[96,768]{1,0:T(8,128)}, f32[96,768]{1,0:T(8,128)S(1)}, u32[]{:S(2)}, u32[]{:S(2)}) %collective-permute-start.9) | collective-permute-done | bytes 294944 | tf_op jit(solution)/shard_map/ppermute | solution.py:527
  89.1 4.3 all-to-all-start
  95.6 24.3 %collective-permute-done.13.refs_2_ = f32[1,3,48,768]{3,2,1,0:T(8,128)} collective-permute-done((f32[1,3,48,768]{3,2,1,0:T(8,128)}, f32[1,3,48,768]{3,2,1,0:T(8,128)}, u32[]{:S(2)}, u32[]{:S(2)}) %collective-permute-start.13) | collective-permute-done | bytes 442400 | tf_op jit(solution)/shard_map/ppermute | solution.py:531
  135.2 9.0 %output_forward.1 = (bf16[4,512,192]{2,1,0:T(8,128)(2,1)}, f32[512,768]{1,0:T(8,128)}, bf16[512,768]{1,0:T(8,128)(2,1)}, f32[512,768]{1,0:T(8,128)}, f32[512,1]{1,0:T(8,128)}, /*index=5*/bf16[4,192,768]{2,1,0:T(8,128)(2,1)}) custom-call(s32[4]{0:T(128)} %and_select_fusion.2.refs_0_, s32[8]{0:T(128)} %stack.211.refs_1_, bf16[192,768]{1,0:T(8,128)(2,1)} %refs_2_.1, ...), custom_call_target="tpu_custom_call" | custom-call | flops 603979776 | bytes 13887520 | tf_op jit(solution)/shard_map/output_forward/pallas_call | solution.py:58
  144.2 13.5 %inner_forward.1 = (bf16[4,512,768]{2,1,0:T(8,128)(2,1)}, f32[4,512,768]{2,1,0:T(8,128)}, bf16[4,768,768]{2,1,0:T(8,128)(2,1)}) custom-call(s32[16]{0:T(128)} %stack.235.refs_0_, bf16[768,768]{1,0:T(8,128)(2,1)} %refs_1_.2, f32[2,3,64,768]{3,2,1,0:T(8,128)} %get-tuple-element.142.refs_2_, f32[2,3,56,768]{3,2,1,0:T(8,128)} %get-tuple-element.141.refs_3_, ...), custom_call_target="tpu_custom_call" | custom-call | flops 2415919104 | bytes 24981568 | tf_op jit(solution)/shard_map/inner_forward/pallas_call | solution.py:58
  162.8 12.1 %outer_forward.1 = (f32[512,768]{1,0:T(8,128)}, f32[512,768]{1,0:T(8,128)}, f32[512,1]{1,0:T(8,128)}, bf16[4,768,768]{2,1,0:T(8,128)(2,1)}) custom-call(s32[16]{0:T(128)} %stack.244.refs_0_, bf16[768,768]{1,0:T(8,128)(2,1)} %refs_1_.3, f32[2,3,48,768]{3,2,1,0:T(8,128)} %get-tuple-element.155.refs_2_, f32[2,3,48,768]{3,2,1,0:T(8,128)} %get-tuple-element.156.refs_3_, ...), custom_call_target="tpu_custom_call" | custom-call | flops 2415919104 | bytes 20867136 | tf_op jit(solution)/shard_map/outer_forward/pallas_call | solution.py:58
  184.8 4.7 %last_norm_backward.1 = (f32[512,768]{1,0:T(8,128)}, bf16[512,768]{1,0:T(8,128)(2,1)}, f32[8,768]{1,0:T(8,128)}) custom-call(bf16[512,768]{1,0:T(8,128)(2,1)} %constant_dynamic-slice_fusion.cot_ref, f32[512,768]{1,0:T(8,128)} %get-tuple-element.177.nrm_ref, f32[512,1]{1,0:T(8,128)} %get-tuple-element.178.inv_ref, ...), custom_call_target="tpu_custom_call" | custom-call | tf_op jit(solution)/shard_map/last_norm_backward/pallas_call | solution.py:58
  189.5 7.7 %grad_full.1 = f32[768,3072]{1,0:T(8,128)} custom-call(bf16[512,768]{1,0:T(8,128)(2,1)} %get-tuple-element.182.refs_0_.go_ref, bf16[4,512,768]{2,1,0:T(8,128)(2,1)} %get-tuple-element.165.refs_9_.refs_1_), custom_call_target="tpu_custom_call" | custom-call | tf_op jit(solution)/shard_map/grad_full/pallas_call | solution.py:58
  203.4 16.5 %inner_backward.1 = (bf16[4,512,768]{2,1,0:T(8,128)(2,1)}, f32[512,768]{1,0:T(8,128)}, bf16[512,768]{1,0:T(8,128)(2,1)}, f32[1,4,1,768]{3,2,1,0:T(1,128)}, f32[1,8,768]{2,1,0:T(8,128)}) custom-call(bf16[512,768]{1,0:T(8,128)(2,1)} %get-tuple-element.182.refs_0_.go_ref, bf16[4,768,768]{2,1,0:T(8,128)(2,1)} %get-tuple-element.183.wu_ref, ...), custom_call_target="tpu_custom_call" | custom-call | tf_op jit(solution)/shard_map/inner_backward/pallas_call | solution.py:58
  220.6 8.9 %grad_rows.1 = (f32[384,3072]{1,0:T(8,128)}, f32[384,3072]{1,0:T(8,128)}) custom-call(bf16[768,768]{1,0:T(8,128)(2,1)} %fusion.refs_0_, bf16[512,768]{1,0:T(8,128)(2,1)} %get-tuple-element.153.refs_9_.refs_1_, bf16[4,512,768]{2,1,0:T(8,128)(2,1)} %get-tuple-element.191.refs_2_), custom_call_target="tpu_custom_call" | custom-call | tf_op jit(solution)/shard_map/grad_rows/pallas_call | solution.py:58
  232.4 8.4 %collective-permute-done.33.refs_4_ = f32[2,3,72,768]{3,2,1,0:T(8,128)S(1)} collective-permute-done((f32[2,3,72,768]{3,2,1,0:T(8,128)}, f32[2,3,72,768]{3,2,1,0:T(8,128)S(1)}, u32[]{:S(2)}, u32[]{:S(2)}) %collective-permute-start.33) | collective-permute-done | bytes 1327136 | tf_op jit(solution)/shard_map/ppermute | solution.py:531
  246.4 3.6 assemble.1.w_ref
  257.0 28.0 %attend_backward.1 = (f32[768,3072]{1,0:T(8,128)}, f32[512,768]{1,0:T(8,128)}, f32[1,4,1,576]{3,2,1,0:T(1,128)}) custom-call(bf16[512,768]{1,0:T(8,128)(2,1)} %constant_dynamic-slice_fusion.1.refs_7_.x_ref, bf16[512,768]{1,0:T(8,128)(2,1)} %get-tuple-element.202.ga_ref, f32[512,768]{1,0:T(8,128)} %get-tuple-element.203.gr_ref, ...), custom_call_target="tpu_custom_call" | custom-call | tf_op jit(solution)/shard_map/attend_backward/pallas_call | solution.py:58
  286.9 8.1 %collective-permute-start.34 = (f32[512,768]{1,0:T(8,128)}, f32[512,768]{1,0:T(8,128)}, u32[]{:S(2)}, u32[]{:S(2)}) collective-permute-start(f32[512,768]{1,0:T(8,128)} %get-tuple-element.207.own_ref), channel_id=1, source_target_pairs={{0,1},{1,2},{2,3},{4,5},{5,6},{6,7},{8,9},{9,10},{10,11},{12,13},{... | collective-permute-start | bytes 4718600 | tf_op jit(solution)/shard_map/ppermute | solution.py:834
  296.5 18.7 %collective-permute-done.38 = f32[192,1536]{1,0:T(8,128)S(1)} collective-permute-done((f32[192,1536]{1,0:T(8,128)S(1)}, f32[192,1536]{1,0:T(8,128)S(1)}, u32[]{:S(2)}, u32[]{:S(2)}) %collective-permute-start.38) | collective-permute-done | bytes 1179680 | tf_op jit(solution)/shard_map/ppermute | solution.py:531
  320.5 7.9 %collective-permute-done.34.refs_0_ = f32[512,768]{1,0:T(8,128)} collective-permute-done((f32[512,768]{1,0:T(8,128)}, f32[512,768]{1,0:T(8,128)}, u32[]{:S(2)}, u32[]{:S(2)}) %collective-permute-start.34) | collective-permute-done | bytes 1572896 | tf_op jit(solution)/shard_map/ppermute | solution.py:834
  334.9 11.2 %collective-permute-done.39 = f32[96,1536]{1,0:T(8,128)} collective-permute-done((f32[96,1536]{1,0:T(8,128)S(1)}, f32[96,1536]{1,0:T(8,128)}, u32[]{:S(2)}, u32[]{:S(2)}) %collective-permute-start.39) | collective-permute-done | bytes 589856 | tf_op jit(solution)/shard_map/ppermute | solution.py:531
  349.6 4.9 %narrow.1 = bf16[2048,768]{1,0:T(8,128)(2,1)} custom-call(f32[2048,768]{1,0:T(8,128)} %all-gather.2.cloned.1.call-done.x_ref), custom_call_target="tpu_custom_call" | custom-call | bytes 9437184 | tf_op jit(solution)/shard_map/narrow/pallas_call | solution.py:58
  357.2 11.3 %collective-permute-start.43 = (f32[192,768]{1,0:T(8,128)S(1)}, f32[192,768]{1,0:T(8,128)S(1)}, u32[]{:S(2)}, u32[]{:S(2)}) collective-permute-start(f32[192,768]{1,0:T(8,128)S(1)} %get-tuple-element.220), channel_id=1, source_target_pairs={{0,1},{4,5},{8,9},{12,13},{16,17},{20,21},{24,25},{28,29}} | collective-permute-start | bytes 1769480 | tf_op jit(solution)/shard_map/ppermute | solution.py:788
  382.5 5.0 %collective-permute-start.48 = (f32[192,768]{1,0:T(8,128)}, f32[192,768]{1,0:T(8,128)S(1)}, u32[]{:S(2)}, u32[]{:S(2)}) collective-permute-start(f32[192,768]{1,0:T(8,128)} %get-tuple-element.225), channel_id=1, source_target_pairs={{0,1},{1,2},{4,5},{5,6},{8,9},{9,10},{12,13},{13,14},{16,17},{17,1... | collective-permute-start | bytes 1769480 | tf_op jit(solution)/shard_map/ppermute | solution.py:788
  391.7 4.5 collective-permute-start.50
  396.4 4.5 collective-permute-done.48
  404.0 4.4 collective-permute-done.47.refs_5_
  411.2 5.3 %collective-permute-start.53 = (f32[96,768]{1,0:T(8,128)S(1)}, f32[96,768]{1,0:T(8,128)}, u32[]{:S(2)}, u32[]{:S(2)}) collective-permute-start(f32[96,768]{1,0:T(8,128)S(1)} %slice_add_fusion.4), channel_id=1, source_target_pairs={{0,1},{1,2},{4,5},{5,6},{8,9},{9,10},{12,13},{13,14},{16,17},{17,1... | collective-permute-start | bytes 884744 | tf_op jit(solution)/shard_map/ppermute | solution.py:788
  417.9 7.2 %place.1 = f32[2048,768]{1,0:T(8,128)} custom-call(s32[1]{0:T(128)} %bitcast.59.z_ref, f32[512,768]{1,0:T(8,128)} %get-tuple-element.207.own_ref, f32[512,768]{1,0:T(8,128)} %collective-permute-done.34.refs_0_, f32[512,768]{1,0:T(8,128)} %collective-permute-done.41.refs_1_, f32[512,768]{1,0:T(8,128)} %collective-permute-done.46.refs_2_, ...), custom_call_target="tpu_custom_call" | custom-call | tf_op jit(solution)/shard_map/place/pallas_call | solution.py:58
  430.9 4.2 collective-permute-start.60
  441.5 4.6 %collective-permute-done.59 = f32[96,768]{1,0:T(8,128)} collective-permute-done((f32[96,768]{1,0:T(8,128)S(1)}, f32[96,768]{1,0:T(8,128)}, u32[]{:S(2)}, u32[]{:S(2)}) %collective-permute-start.59) | collective-permute-done | bytes 294944 | tf_op jit(solution)/shard_map/ppermute | solution.py:792
  (299 shorter events, 156.4 us)
Async XLA Ops:
  10.7 39.3 %collective-permute-start = (f32[120,768]{1,0:T(8,128)}, f32[120,768]{1,0:T(8,128)S(1)}, u32[]{:S(2)}, u32[]{:S(2)}) collective-permute-start(f32[120,768]{1,0:T(8,128)} %maximum_convert_fusion), channel_id=1, source_target_pairs={{0,1},{1,2},{2,3},{3,0},{4,5},{5,6},{6,7},{7,4},{8,9},{9,10},{10,1... | collective-permute-start | bytes 1105928 | tf_op jit(solution)/shard_map/ppermute | solution.py:527
  13.7 36.3 %collective-permute-start.1 = (f32[120,768]{1,0:T(8,128)}, f32[120,768]{1,0:T(8,128)}, u32[]{:S(2)}, u32[]{:S(2)}) collective-permute-start(f32[120,768]{1,0:T(8,128)} %maximum_convert_fusion), channel_id=1, source_target_pairs={{0,2},{1,3},{2,0},{3,1},{4,6},{5,7},{6,4},{7,5},{8,10},{9,11},{10,... | collective-permute-start | bytes 1105928 | tf_op jit(solution)/shard_map/ppermute | solution.py:527
  16.3 33.7 %collective-permute-start.2 = (f32[120,768]{1,0:T(8,128)}, f32[120,768]{1,0:T(8,128)}, u32[]{:S(2)}, u32[]{:S(2)}) collective-permute-start(f32[120,768]{1,0:T(8,128)} %maximum_convert_fusion), channel_id=1, source_target_pairs={{0,3},{1,0},{2,1},{3,2},{4,7},{5,4},{6,5},{7,6},{8,11},{9,8},{10,9... | collective-permute-start | bytes 1105928 | tf_op jit(solution)/shard_map/ppermute | solution.py:527
  19.8 20.9 %collective-permute-start.3 = (f32[1,1344]{1,0:T(1,128)S(1)}, f32[1,1344]{1,0:T(1,128)S(1)}, u32[]{:S(2)}, u32[]{:S(2)}) collective-permute-start(f32[1,1344]{1,0:T(1,128)S(1)} %convert_element_type.38), channel_id=1, source_target_pairs={{0,1},{1,2},{2,3},{3,0},{4,5},{5,6},{6,7},{7,4},{8,9},{9,10},{10,1... | collective-permute-start | bytes 16136 | tf_op jit(solution)/shard_map/ppermute | solution.py:527
  20.5 28.2 %collective-permute-start.4 = (f32[1,1344]{1,0:T(1,128)S(1)}, f32[1,1344]{1,0:T(1,128)}, u32[]{:S(2)}, u32[]{:S(2)}) collective-permute-start(f32[1,1344]{1,0:T(1,128)S(1)} %convert_element_type.38), channel_id=1, source_target_pairs={{0,2},{1,3},{2,0},{3,1},{4,6},{5,7},{6,4},{7,5},{8,10},{9,11},{10,... | collective-permute-start | bytes 16136 | tf_op jit(solution)/shard_map/ppermute | solution.py:527
  51.2 31.8 %collective-permute-start.6 = (f32[1,3,64,768]{3,2,1,0:T(8,128)S(1)}, f32[1,3,64,768]{3,2,1,0:T(8,128)S(1)}, u32[]{:S(2)}, u32[]{:S(2)}) collective-permute-start(f32[1,3,64,768]{3,2,1,0:T(8,128)S(1)} %get-tuple-element.130.refs_0_), channel_id=1, source_target_pairs={{0,8},{4,12},{8,0},{12,4},{16,24},{20,28},{24,16},{28,20},{1,9},{5... | collective-permute-start | bytes 1769480 | tf_op jit(solution)/shard_map/ppermute | solution.py:531
  52.7 30.3 %collective-permute-start.7 = (f32[1,3,56,768]{3,2,1,0:T(8,128)S(1)}, f32[1,3,56,768]{3,2,1,0:T(8,128)S(1)}, u32[]{:S(2)}, u32[]{:S(2)}) collective-permute-start(f32[1,3,56,768]{3,2,1,0:T(8,128)S(1)} %get-tuple-element.131.refs_1_), channel_id=1, source_target_pairs={{0,16},{4,20},{8,24},{12,28},{16,0},{20,4},{24,8},{28,12},{1,17},{... | collective-permute-start | bytes 1548296 | tf_op jit(solution)/shard_map/ppermute | solution.py:531
  57.2 24.2 %collective-permute-start.9 = (f32[96,768]{1,0:T(8,128)}, f32[96,768]{1,0:T(8,128)S(1)}, u32[]{:S(2)}, u32[]{:S(2)}) collective-permute-start(f32[96,768]{1,0:T(8,128)} %dynamic-slice_convert_fusion), channel_id=1, source_target_pairs={{0,2},{1,3},{2,0},{3,1},{4,6},{5,7},{6,4},{7,5},{8,10},{9,11},{10,... | collective-permute-start | bytes 884744 | tf_op jit(solution)/shard_map/ppermute | solution.py:527
  84.7 43.3 %collective-permute-start.11 = (f32[2,3,64,768]{3,2,1,0:T(8,128)}, f32[2,3,64,768]{3,2,1,0:T(8,128)}, u32[]{:S(2)}, u32[]{:S(2)}) collective-permute-start(f32[2,3,64,768]{3,2,1,0:T(8,128)} %get-tuple-element.142.refs_2_), channel_id=1, source_target_pairs={{0,16},{4,20},{8,24},{12,28},{16,0},{20,4},{24,8},{28,12},{1,17},{... | collective-permute-start | bytes 3538952 | tf_op jit(solution)/shard_map/ppermute | solution.py:531
  85.2 42.8 %collective-permute-start.12 = (f32[2,3,56,768]{3,2,1,0:T(8,128)}, f32[2,3,56,768]{3,2,1,0:T(8,128)}, u32[]{:S(2)}, u32[]{:S(2)}) collective-permute-start(f32[2,3,56,768]{3,2,1,0:T(8,128)} %get-tuple-element.141.refs_3_), channel_id=1, source_target_pairs={{0,8},{4,12},{8,0},{12,4},{16,24},{20,28},{24,16},{28,20},{1,9},{5... | collective-permute-start | bytes 3096584 | tf_op jit(solution)/shard_map/ppermute | solution.py:531
  89.1 46.1 %all-to-all-start = ((f32[4,256,384]{2,1,0:T(8,128)}), f32[4,256,384]{2,1,0:T(8,128)}, u32[]{:S(2)}, u32[]{:S(2)}) async-start(f32[4,256,384]{2,1,0:T(8,128)} %bitcast.70), calls=%async_computation | async-start | bytes 3145728 | tf_op jit(solution)/shard_map/all_to_all | solution.py:936
  93.5 256.1 %all-gather.2.cloned.1.call-start = ((), (), s32[]{:S(2)}) async-start(), calls=%async_computation.4 | async-start | bytes 7864320 | tf_op jit(solution)/shard_map/all_gather | solution.py:955
  93.6 26.3 %collective-permute-start.13 = (f32[1,3,48,768]{3,2,1,0:T(8,128)}, f32[1,3,48,768]{3,2,1,0:T(8,128)}, u32[]{:S(2)}, u32[]{:S(2)}) collective-permute-start(f32[1,3,48,768]{3,2,1,0:T(8,128)} %copy-done.15), channel_id=1, source_target_pairs={{0,8},{4,12},{8,0},{12,4},{16,24},{20,28},{24,16},{28,20},{1,9},{5... | collective-permute-start | bytes 1327112 | tf_op jit(solution)/shard_map/ppermute | solution.py:531
  94.2 28.7 %collective-permute-start.14 = (f32[1,3,48,768]{3,2,1,0:T(8,128)}, f32[1,3,48,768]{3,2,1,0:T(8,128)}, u32[]{:S(2)}, u32[]{:S(2)}) collective-permute-start(f32[1,3,48,768]{3,2,1,0:T(8,128)} %copy-done.17), channel_id=1, source_target_pairs={{0,16},{4,20},{8,24},{12,28},{16,0},{20,4},{24,8},{28,12},{1,17},{... | collective-permute-start | bytes 1327112 | tf_op jit(solution)/shard_map/ppermute | solution.py:531
  127.9 29.8 %collective-permute-start.17 = (f32[2,3,96,768]{3,2,1,0:T(8,128)}, f32[2,3,96,768]{3,2,1,0:T(8,128)}, u32[]{:S(2)}, u32[]{:S(2)}) collective-permute-start(f32[2,3,96,768]{3,2,1,0:T(8,128)} %get-tuple-element.154), channel_id=1, source_target_pairs={{0,4},{4,0},{8,12},{12,8},{16,20},{20,16},{24,28},{28,24},{1,5},{5... | collective-permute-start | bytes 5308424 | tf_op jit(solution)/shard_map/ppermute | solution.py:531
  128.6 29.1 %collective-permute-start.18 = (f32[2,3,48,768]{3,2,1,0:T(8,128)}, f32[2,3,48,768]{3,2,1,0:T(8,128)}, u32[]{:S(2)}, u32[]{:S(2)}) collective-permute-start(f32[2,3,48,768]{3,2,1,0:T(8,128)} %get-tuple-element.155.refs_2_), channel_id=1, source_target_pairs={{0,16},{4,20},{8,24},{12,28},{16,0},{20,4},{24,8},{28,12},{1,17},{... | collective-permute-start | bytes 2654216 | tf_op jit(solution)/shard_map/ppermute | solution.py:531
  129.1 28.6 %collective-permute-start.19 = (f32[2,3,48,768]{3,2,1,0:T(8,128)}, f32[2,3,48,768]{3,2,1,0:T(8,128)}, u32[]{:S(2)}, u32[]{:S(2)}) collective-permute-start(f32[2,3,48,768]{3,2,1,0:T(8,128)} %get-tuple-element.156.refs_3_), channel_id=1, source_target_pairs={{0,8},{4,12},{8,0},{12,4},{16,24},{20,28},{24,16},{28,20},{1,9},{5... | collective-permute-start | bytes 2654216 | tf_op jit(solution)/shard_map/ppermute | solution.py:531
  179.2 175.3 %reduce-scatter.3.cloned.1.call-start = ((), (), s32[]{:S(2)}) async-start(), calls=%async_computation.3 | async-start | bytes 10616832 | tf_op jit(solution)/shard_map/reduce_scatter | solution.py:963
  199.6 180.5 %reduce-scatter.5.cloned.1.call-start = ((), (), s32[]{:S(2)}) async-start(), calls=%async_computation.5 | async-start | bytes 10616832 | tf_op jit(solution)/shard_map/reduce_scatter | solution.py:986
  286.3 28.9 %collective-permute-start.38 = (f32[192,1536]{1,0:T(8,128)S(1)}, f32[192,1536]{1,0:T(8,128)S(1)}, u32[]{:S(2)}, u32[]{:S(2)}) collective-permute-start(f32[192,1536]{1,0:T(8,128)S(1)} %copy-done.32), channel_id=1, source_target_pairs={{0,16},{4,20},{8,24},{12,28},{16,0},{20,4},{24,8},{28,12},{1,17},{... | collective-permute-start | bytes 3538952 | tf_op jit(solution)/shard_map/ppermute | solution.py:531
  286.3 31.1 %collective-permute-start.37 = (f32[192,1536]{1,0:T(8,128)}, f32[192,1536]{1,0:T(8,128)S(1)}, u32[]{:S(2)}, u32[]{:S(2)}) collective-permute-start(f32[192,1536]{1,0:T(8,128)} %pad_maximum_fusion), channel_id=1, source_target_pairs={{0,8},{4,12},{8,0},{12,4},{16,24},{20,28},{24,16},{28,20},{1,9},{5... | collective-permute-start | bytes 3538952 | tf_op jit(solution)/shard_map/ppermute | solution.py:531
  286.9 41.5 %collective-permute-start.34 = (f32[512,768]{1,0:T(8,128)}, f32[512,768]{1,0:T(8,128)}, u32[]{:S(2)}, u32[]{:S(2)}) collective-permute-start(f32[512,768]{1,0:T(8,128)} %get-tuple-element.207.own_ref), channel_id=1, source_target_pairs={{0,1},{1,2},{2,3},{4,5},{5,6},{6,7},{8,9},{9,10},{10,11},{12,13},{... | collective-permute-start | bytes 4718600 | tf_op jit(solution)/shard_map/ppermute | solution.py:834
  295.0 38.7 %collective-permute-start.35 = (f32[512,768]{1,0:T(8,128)}, f32[512,768]{1,0:T(8,128)}, u32[]{:S(2)}, u32[]{:S(2)}) collective-permute-start(f32[512,768]{1,0:T(8,128)} %get-tuple-element.207.own_ref), channel_id=1, source_target_pairs={{1,0},{2,1},{3,2},{5,4},{6,5},{7,6},{9,8},{10,9},{11,10},{13,12},{... | collective-permute-start | bytes 4718600 | tf_op jit(solution)/shard_map/ppermute | solution.py:835
  317.7 28.4 %collective-permute-start.39 = (f32[96,1536]{1,0:T(8,128)S(1)}, f32[96,1536]{1,0:T(8,128)}, u32[]{:S(2)}, u32[]{:S(2)}) collective-permute-start(f32[96,1536]{1,0:T(8,128)S(1)} %slice.187), channel_id=1, source_target_pairs={{0,16},{4,20},{8,24},{12,28},{16,0},{20,4},{24,8},{28,12},{1,17},{... | collective-permute-start | bytes 1769480 | tf_op jit(solution)/shard_map/ppermute | solution.py:531
  319.2 28.5 %collective-permute-start.40 = (f32[96,1536]{1,0:T(8,128)}, f32[96,1536]{1,0:T(8,128)}, u32[]{:S(2)}, u32[]{:S(2)}) collective-permute-start(f32[96,1536]{1,0:T(8,128)} %slice.188), channel_id=1, source_target_pairs={{0,8},{4,12},{8,0},{12,4},{16,24},{20,28},{24,16},{28,20},{1,9},{5... | collective-permute-start | bytes 1769480 | tf_op jit(solution)/shard_map/ppermute | solution.py:531
  328.4 40.8 %collective-permute-start.41 = (f32[512,768]{1,0:T(8,128)}, f32[512,768]{1,0:T(8,128)}, u32[]{:S(2)}, u32[]{:S(2)}) collective-permute-start(f32[512,768]{1,0:T(8,128)} %collective-permute-done.34.refs_0_), channel_id=1, source_target_pairs={{1,2},{2,3},{5,6},{6,7},{9,10},{10,11},{13,14},{14,15},{17,18},{18... | collective-permute-start | bytes 4718600 | tf_op jit(solution)/shard_map/ppermute | solution.py:834
  333.6 37.8 %collective-permute-start.42 = (f32[512,768]{1,0:T(8,128)}, f32[512,768]{1,0:T(8,128)}, u32[]{:S(2)}, u32[]{:S(2)}) collective-permute-start(f32[512,768]{1,0:T(8,128)} %collective-permute-done.35.refs_3_), channel_id=1, source_target_pairs={{1,0},{2,1},{5,4},{6,5},{9,8},{10,9},{13,12},{14,13},{17,16},{18,1... | collective-permute-start | bytes 4718600 | tf_op jit(solution)/shard_map/ppermute | solution.py:835
  357.2 21.9 %collective-permute-start.43 = (f32[192,768]{1,0:T(8,128)S(1)}, f32[192,768]{1,0:T(8,128)S(1)}, u32[]{:S(2)}, u32[]{:S(2)}) collective-permute-start(f32[192,768]{1,0:T(8,128)S(1)} %get-tuple-element.220), channel_id=1, source_target_pairs={{0,1},{4,5},{8,9},{12,13},{16,17},{20,21},{24,25},{28,29}} | collective-permute-start | bytes 1769480 | tf_op jit(solution)/shard_map/ppermute | solution.py:788
  369.2 34.8 %collective-permute-start.46 = (f32[512,768]{1,0:T(8,128)}, f32[512,768]{1,0:T(8,128)}, u32[]{:S(2)}, u32[]{:S(2)}) collective-permute-start(f32[512,768]{1,0:T(8,128)} %collective-permute-done.41.refs_1_), channel_id=1, source_target_pairs={{2,3},{6,7},{10,11},{14,15},{18,19},{22,23},{26,27},{30,31}} | collective-permute-start | bytes 4718600 | tf_op jit(solution)/shard_map/ppermute | solution.py:834
  371.5 36.9 %collective-permute-start.47 = (f32[512,768]{1,0:T(8,128)}, f32[512,768]{1,0:T(8,128)}, u32[]{:S(2)}, u32[]{:S(2)}) collective-permute-start(f32[512,768]{1,0:T(8,128)} %collective-permute-done.42.refs_4_), channel_id=1, source_target_pairs={{1,0},{5,4},{9,8},{13,12},{17,16},{21,20},{25,24},{29,28}} | collective-permute-start | bytes 4718600 | tf_op jit(solution)/shard_map/ppermute | solution.py:835
  408.4 21.3 %collective-permute-start.56 = (f32[192,768]{1,0:T(8,128)}, f32[192,768]{1,0:T(8,128)S(1)}, u32[]{:S(2)}, u32[]{:S(2)}) collective-permute-start(f32[192,768]{1,0:T(8,128)} %add.268), channel_id=1, source_target_pairs={{0,1},{1,2},{2,3},{4,5},{5,6},{6,7},{8,9},{9,10},{10,11},{12,13},{... | collective-permute-start | bytes 1769480 | tf_op jit(solution)/shard_map/ppermute | solution.py:788
  409.9 19.8 %collective-permute-start.57 = (f32[192,768]{1,0:T(8,128)S(1)}, f32[192,768]{1,0:T(8,128)}, u32[]{:S(2)}, u32[]{:S(2)}) collective-permute-start(f32[192,768]{1,0:T(8,128)S(1)} %add.269), channel_id=1, source_target_pairs={{1,0},{2,1},{3,2},{5,4},{6,5},{7,6},{9,8},{10,9},{11,10},{13,12},{... | collective-permute-start | bytes 1769480 | tf_op jit(solution)/shard_map/ppermute | solution.py:792
  (80 other events, 1010.9 us)
Sparse Core Ops, SparseCore 0:
  179.3 115.1 all-gather.1
Sparse Core Ops, SparseCore 1:
  199.7 77.8 reduce-scatter.2
  285.2 93.7 reduce-scatter.4

commit v6 on v5

--- a/solution.py
+++ b/solution.py
@@ -956,16 +956,17 @@
         a3, b3 = halves(z3, n3)
         ax, by = flip(a3, 2), flip(b3, 4)
         grad_resid2, grad_outer, sums_two = last_norm_backward(cot, normed_two, inverse_two, wide_vectors)
+        a3, b3, ab3 = join(a3, ax, b3, by)
+        a3, b3, ab3, grad_outer = stage(a3, b3, ab3, grad_outer)
+
+        ay3, bx3, c3 = flip(a3, 4), flip(b3, 2), flip(ab3, 1)
         part1 = grad_full((grad_outer, active))
-        a3, b3, ab3 = join(a3, ax, b3, by)
-        a3, b3, ab3, part1, grad_outer = stage(a3, b3, ab3, part1, grad_outer)
-
+        part1, grad_outer = stage(part1, grad_outer)
         part1 = lax.psum_scatter(part1, "dp", scatter_dimension=0, tiled=True)
-        ay3, bx3, c3 = flip(a3, 4), flip(b3, 2), flip(ab3, 1)
         grad_inner, grad_resid1, grad_attn, inner_sums, sums_one = inner_backward(
             grad_outer, outer_full, slope, inner_full, grad_resid2, normed, inverse, wide_vectors
         )
-        ay3, bx3, grad_inner, grad_attn = stage(ay3, bx3, grad_inner, grad_attn)
+        ay3, bx3, c3, grad_inner, grad_attn = stage(ay3, bx3, c3, grad_inner, grad_attn)
 
         d3 = other_core(ay3, bx3)
         send, keep = grad_rows(order, [(hidden_bf, grad_inner)])

time: 458 us -> 456 us (level)
  waiting for transfers between devices: 140 us -> 145 us
    ppermute x29, waiting for transfers between devices: 77.2 us -> 64.9 us  [flip(): return lax.ppermute(values, 'dp', [(i, i ^ bit) for i in range(8)])]
    ppermute x3, waiting for transfers between devices: 8.18 us -> 18 us  [onward(): lax.ppermute(d, 'tensor', [(i, i - 1) for i in range(1, tensor - step + 1)])]
    ppermute x3, waiting for transfers between devices: 7.88 us -> 13.6 us  [onward(): lax.ppermute(u, 'tensor', [(i, i + 1) for i in range(step - 1, tensor - 1)])]
    unnamed x96 -> x94, local copies, waits for them, and re-layouts: 18.9 us -> 17 us
  transfers between devices with their start and end apart: 65 -> 65, of which waited for: 27 -> 28; matrix products, arithmetic and copies ran while one was open for 9% -> 10% of each run, Pallas kernels for 29% -> 29%
where the time goes in v6:
time: 456 us; the launch traced here: 454 us
  waiting for transfers between devices  145 us (32%)
  Pallas kernels  134 us (29%)
  starting transfers between devices  92.7 us (20%)
  local copies, waits for them, and re-layouts  37.9 us (8%)
  other arithmetic  28.4 us (6%)
  between operations  16.4 us (4%)
    pallas_call x11, Pallas kernels, call(): pl.pallas_call(kernel, grid_spec=pltpu.PrefetchScalarGridSpec(num_scalar_...  124 us
    ppermute x29, waiting for transfers between devices, flip(): return lax.ppermute(values, 'dp', [(i, i ^ bit) for i in range(8)])  64.9 us
    ppermute x12, waiting for transfers between devices, shift_to(): lax.ppermute(values, 'tensor', [(i, (i + k) % tensor) for i in range(tens...  32.5 us
    ppermute x6, starting transfers between devices, up(): return lax.ppermute(values, 'tensor', [(i, i + 1) for i in range(step)])  28 us
    ppermute x3, waiting for transfers between devices, onward(): lax.ppermute(d, 'tensor', [(i, i - 1) for i in range(1, tensor - step + 1)])  18 us
    ppermute x12, starting transfers between devices, shift_to(): lax.ppermute(values, 'tensor', [(i, (i + k) % tensor) for i in range(tens...  17.8 us
    unnamed x94, local copies, waits for them, and re-layouts  17 us
    ppermute x29, starting transfers between devices, flip(): return lax.ppermute(values, 'dp', [(i, i ^ bit) for i in range(8)])  15.8 us
  transfers between devices with their start and end apart: 65, of which 28 were waited for; matrix products, arithmetic and copies ran while one was open for 10% of the time, Pallas kernels for 29%

profile of v6, /device:TPU:0, one launch (start us, length us, event | category | flops | bytes accessed | tf_op | source)
XLA Modules:
  0.0 453.8 jit_solution(8716361565976782604)
XLA Ops:
  23.5 11.6 %attend_forward.1 = f32[1024,384]{1,0:T(8,128)} custom-call(bf16[2048,768]{1,0:T(8,128)(2,1)} %x_ref.1, bf16[576,768]{1,0:T(8,128)(2,1)} %pad_maximum_fusion.1.w_ref.local_ref, f32[1,576]{1,0:T(1,128)} %slice.181.bias_ref), custom_call_target="tpu_custom_call" | custom-call | flops 2617245696 | bytes 5605632 | tf_op jit(solution)/shard_map/attend_forward/pallas_call | solution.py:58
  36.8 3.9 collective-permute-done.3
  41.4 7.3 %collective-permute-done.4 = f32[1,1344]{1,0:T(1,128)} collective-permute-done((f32[1,1344]{1,0:T(1,128)S(1)}, f32[1,1344]{1,0:T(1,128)}, u32[]{:S(2)}, u32[]{:S(2)}) %collective-permute-start.4) | collective-permute-done | bytes 5408 | tf_op jit(solution)/shard_map/ppermute | solution.py:527
  63.7 4.1 collective-permute-done.10.refs_2_
  67.7 5.4 %collective-permute-done.8.refs_0_ = f32[96,768]{1,0:T(8,128)S(1)} collective-permute-done((f32[96,768]{1,0:T(8,128)}, f32[96,768]{1,0:T(8,128)S(1)}, u32[]{:S(2)}, u32[]{:S(2)}) %collective-permute-start.8) | collective-permute-done | bytes 294944 | tf_op jit(solution)/shard_map/ppermute | solution.py:527
  73.1 8.3 %collective-permute-done.9.refs_1_ = f32[96,768]{1,0:T(8,128)S(1)} collective-permute-done((f32[96,768]{1,0:T(8,128)}, f32[96,768]{1,0:T(8,128)S(1)}, u32[]{:S(2)}, u32[]{:S(2)}) %collective-permute-start.9) | collective-permute-done | bytes 294944 | tf_op jit(solution)/shard_map/ppermute | solution.py:527
  89.1 4.3 all-to-all-start
  96.3 23.6 %collective-permute-done.13.refs_2_ = f32[1,3,48,768]{3,2,1,0:T(8,128)} collective-permute-done((f32[1,3,48,768]{3,2,1,0:T(8,128)}, f32[1,3,48,768]{3,2,1,0:T(8,128)}, u32[]{:S(2)}, u32[]{:S(2)}) %collective-permute-start.13) | collective-permute-done | bytes 442400 | tf_op jit(solution)/shard_map/ppermute | solution.py:531
  135.2 9.0 %output_forward.1 = (bf16[4,512,192]{2,1,0:T(8,128)(2,1)}, f32[512,768]{1,0:T(8,128)}, bf16[512,768]{1,0:T(8,128)(2,1)}, f32[512,768]{1,0:T(8,128)}, f32[512,1]{1,0:T(8,128)}, /*index=5*/bf16[4,192,768]{2,1,0:T(8,128)(2,1)}) custom-call(s32[4]{0:T(128)} %and_select_fusion.2.refs_0_, s32[8]{0:T(128)} %stack.211.refs_1_, bf16[192,768]{1,0:T(8,128)(2,1)} %refs_2_.1, ...), custom_call_target="tpu_custom_call" | custom-call | flops 603979776 | bytes 13887520 | tf_op jit(solution)/shard_map/output_forward/pallas_call | solution.py:58
  144.2 13.5 %inner_forward.1 = (bf16[4,512,768]{2,1,0:T(8,128)(2,1)}, f32[4,512,768]{2,1,0:T(8,128)}, bf16[4,768,768]{2,1,0:T(8,128)(2,1)}) custom-call(s32[16]{0:T(128)} %stack.235.refs_0_, bf16[768,768]{1,0:T(8,128)(2,1)} %refs_1_.2, f32[2,3,64,768]{3,2,1,0:T(8,128)} %get-tuple-element.144.refs_2_, f32[2,3,56,768]{3,2,1,0:T(8,128)} %get-tuple-element.143.refs_3_, ...), custom_call_target="tpu_custom_call" | custom-call | flops 2415919104 | bytes 24981568 | tf_op jit(solution)/shard_map/inner_forward/pallas_call | solution.py:58
  162.7 12.2 %outer_forward.1 = (f32[512,768]{1,0:T(8,128)}, f32[512,768]{1,0:T(8,128)}, f32[512,1]{1,0:T(8,128)}, bf16[4,768,768]{2,1,0:T(8,128)(2,1)}) custom-call(s32[16]{0:T(128)} %stack.244.refs_0_, bf16[768,768]{1,0:T(8,128)(2,1)} %refs_1_.3, f32[2,3,48,768]{3,2,1,0:T(8,128)} %get-tuple-element.157.refs_2_, f32[2,3,48,768]{3,2,1,0:T(8,128)} %get-tuple-element.158.refs_3_, ...), custom_call_target="tpu_custom_call" | custom-call | flops 2415919104 | bytes 20867136 | tf_op jit(solution)/shard_map/outer_forward/pallas_call | solution.py:58
  183.4 4.5 last_norm_backward.1
  191.0 8.6 %grad_full.1 = f32[768,3072]{1,0:T(8,128)} custom-call(bf16[512,768]{1,0:T(8,128)(2,1)} %get-tuple-element.186.refs_0_.go_ref, bf16[4,512,768]{2,1,0:T(8,128)(2,1)} %get-tuple-element.167.refs_9_.refs_1_), custom_call_target="tpu_custom_call" | custom-call | tf_op jit(solution)/shard_map/grad_full/pallas_call | solution.py:58
  201.1 15.7 %inner_backward.1 = (bf16[4,512,768]{2,1,0:T(8,128)(2,1)}, f32[512,768]{1,0:T(8,128)}, bf16[512,768]{1,0:T(8,128)(2,1)}, f32[1,4,1,768]{3,2,1,0:T(1,128)}, f32[1,8,768]{2,1,0:T(8,128)}) custom-call(bf16[512,768]{1,0:T(8,128)(2,1)} %get-tuple-element.186.refs_0_.go_ref, bf16[4,768,768]{2,1,0:T(8,128)(2,1)} %get-tuple-element.187.wu_ref, ...), custom_call_target="tpu_custom_call" | custom-call | tf_op jit(solution)/shard_map/inner_backward/pallas_call | solution.py:58
  219.4 8.7 %grad_rows.1 = (f32[384,3072]{1,0:T(8,128)}, f32[384,3072]{1,0:T(8,128)}) custom-call(bf16[768,768]{1,0:T(8,128)(2,1)} %fusion.refs_0_, bf16[512,768]{1,0:T(8,128)(2,1)} %get-tuple-element.155.refs_9_.refs_1_, bf16[4,512,768]{2,1,0:T(8,128)(2,1)} %get-tuple-element.195.refs_2_), custom_call_target="tpu_custom_call" | custom-call | tf_op jit(solution)/shard_map/grad_rows/pallas_call | solution.py:58
  236.1 3.6 assemble.1.w_ref
  246.7 28.1 %attend_backward.1 = (f32[768,3072]{1,0:T(8,128)}, f32[512,768]{1,0:T(8,128)}, f32[1,4,1,576]{3,2,1,0:T(1,128)}) custom-call(bf16[512,768]{1,0:T(8,128)(2,1)} %constant_dynamic-slice_fusion.1.refs_7_.x_ref, bf16[512,768]{1,0:T(8,128)(2,1)} %get-tuple-element.206.ga_ref, f32[512,768]{1,0:T(8,128)} %get-tuple-element.207.gr_ref, ...), custom_call_target="tpu_custom_call" | custom-call | tf_op jit(solution)/shard_map/attend_backward/pallas_call | solution.py:58
  277.6 9.5 %collective-permute-start.34 = (f32[512,768]{1,0:T(8,128)}, f32[512,768]{1,0:T(8,128)}, u32[]{:S(2)}, u32[]{:S(2)}) collective-permute-start(f32[512,768]{1,0:T(8,128)} %get-tuple-element.211.own_ref), channel_id=1, source_target_pairs={{0,1},{1,2},{2,3},{4,5},{5,6},{6,7},{8,9},{9,10},{10,11},{12,13},{... | collective-permute-start | bytes 4718600 | tf_op jit(solution)/shard_map/ppermute | solution.py:834
  288.6 16.3 %collective-permute-done.38 = f32[192,1536]{1,0:T(8,128)S(1)} collective-permute-done((f32[192,1536]{1,0:T(8,128)S(1)}, f32[192,1536]{1,0:T(8,128)S(1)}, u32[]{:S(2)}, u32[]{:S(2)}) %collective-permute-start.38) | collective-permute-done | bytes 1179680 | tf_op jit(solution)/shard_map/ppermute | solution.py:531
  310.5 13.6 %collective-permute-done.34.refs_0_ = f32[512,768]{1,0:T(8,128)} collective-permute-done((f32[512,768]{1,0:T(8,128)}, f32[512,768]{1,0:T(8,128)}, u32[]{:S(2)}, u32[]{:S(2)}) %collective-permute-start.34) | collective-permute-done | bytes 1572896 | tf_op jit(solution)/shard_map/ppermute | solution.py:834
  329.4 6.9 %collective-permute-done.39 = f32[96,1536]{1,0:T(8,128)} collective-permute-done((f32[96,1536]{1,0:T(8,128)S(1)}, f32[96,1536]{1,0:T(8,128)}, u32[]{:S(2)}, u32[]{:S(2)}) %collective-permute-start.39) | collective-permute-done | bytes 589856 | tf_op jit(solution)/shard_map/ppermute | solution.py:531
  339.7 4.9 %narrow.1 = bf16[2048,768]{1,0:T(8,128)(2,1)} custom-call(f32[2048,768]{1,0:T(8,128)} %all-gather.2.cloned.1.call-done.x_ref), custom_call_target="tpu_custom_call" | custom-call | bytes 9437184 | tf_op jit(solution)/shard_map/narrow/pallas_call | solution.py:58
  347.3 7.6 %collective-permute-start.43 = (f32[192,768]{1,0:T(8,128)S(1)}, f32[192,768]{1,0:T(8,128)S(1)}, u32[]{:S(2)}, u32[]{:S(2)}) collective-permute-start(f32[192,768]{1,0:T(8,128)S(1)} %get-tuple-element.224), channel_id=1, source_target_pairs={{0,1},{4,5},{8,9},{12,13},{16,17},{20,21},{24,25},{28,29}} | collective-permute-start | bytes 1769480 | tf_op jit(solution)/shard_map/ppermute | solution.py:788
  357.4 10.4 %collective-permute-done.42.refs_4_ = f32[512,768]{1,0:T(8,128)} collective-permute-done((f32[512,768]{1,0:T(8,128)}, f32[512,768]{1,0:T(8,128)}, u32[]{:S(2)}, u32[]{:S(2)}) %collective-permute-start.42) | collective-permute-done | bytes 1572896 | tf_op jit(solution)/shard_map/ppermute | solution.py:835
  376.6 6.3 %collective-permute-start.48 = (f32[192,768]{1,0:T(8,128)}, f32[192,768]{1,0:T(8,128)S(1)}, u32[]{:S(2)}, u32[]{:S(2)}) collective-permute-start(f32[192,768]{1,0:T(8,128)} %get-tuple-element.229), channel_id=1, source_target_pairs={{0,1},{1,2},{4,5},{5,6},{8,9},{9,10},{12,13},{13,14},{16,17},{17,1... | collective-permute-start | bytes 1769480 | tf_op jit(solution)/shard_map/ppermute | solution.py:788
  387.1 4.5 collective-permute-start.50
  391.7 5.2 %collective-permute-done.48 = f32[192,768]{1,0:T(8,128)S(1)} collective-permute-done((f32[192,768]{1,0:T(8,128)}, f32[192,768]{1,0:T(8,128)S(1)}, u32[]{:S(2)}, u32[]{:S(2)}) %collective-permute-start.48) | collective-permute-done | bytes 589856 | tf_op jit(solution)/shard_map/ppermute | solution.py:788
  400.1 5.5 %collective-permute-done.47.refs_5_ = f32[512,768]{1,0:T(8,128)} collective-permute-done((f32[512,768]{1,0:T(8,128)}, f32[512,768]{1,0:T(8,128)}, u32[]{:S(2)}, u32[]{:S(2)}) %collective-permute-start.47) | collective-permute-done | bytes 1572896 | tf_op jit(solution)/shard_map/ppermute | solution.py:835
  408.4 5.3 %collective-permute-start.53 = (f32[96,768]{1,0:T(8,128)S(1)}, f32[96,768]{1,0:T(8,128)}, u32[]{:S(2)}, u32[]{:S(2)}) collective-permute-start(f32[96,768]{1,0:T(8,128)S(1)} %slice_add_fusion.4), channel_id=1, source_target_pairs={{0,1},{1,2},{4,5},{5,6},{8,9},{9,10},{12,13},{13,14},{16,17},{17,1... | collective-permute-start | bytes 884744 | tf_op jit(solution)/shard_map/ppermute | solution.py:788
  415.0 7.2 %place.1 = f32[2048,768]{1,0:T(8,128)} custom-call(s32[1]{0:T(128)} %bitcast.59.z_ref, f32[512,768]{1,0:T(8,128)} %get-tuple-element.211.own_ref, f32[512,768]{1,0:T(8,128)} %collective-permute-done.34.refs_0_, f32[512,768]{1,0:T(8,128)} %collective-permute-done.41.refs_1_, f32[512,768]{1,0:T(8,128)} %collective-permute-done.46.refs_2_, ...), custom_call_target="tpu_custom_call" | custom-call | tf_op jit(solution)/shard_map/place/pallas_call | solution.py:58
  422.3 3.6 collective-permute-done.55
  439.1 4.6 %collective-permute-done.59 = f32[96,768]{1,0:T(8,128)} collective-permute-done((f32[96,768]{1,0:T(8,128)S(1)}, f32[96,768]{1,0:T(8,128)}, u32[]{:S(2)}, u32[]{:S(2)}) %collective-permute-start.59) | collective-permute-done | bytes 294944 | tf_op jit(solution)/shard_map/ppermute | solution.py:792
  (297 shorter events, 153.8 us)
Async XLA Ops:
  10.7 39.3 %collective-permute-start = (f32[120,768]{1,0:T(8,128)}, f32[120,768]{1,0:T(8,128)S(1)}, u32[]{:S(2)}, u32[]{:S(2)}) collective-permute-start(f32[120,768]{1,0:T(8,128)} %maximum_convert_fusion), channel_id=1, source_target_pairs={{0,1},{1,2},{2,3},{3,0},{4,5},{5,6},{6,7},{7,4},{8,9},{9,10},{10,1... | collective-permute-start | bytes 1105928 | tf_op jit(solution)/shard_map/ppermute | solution.py:527
  13.7 36.3 %collective-permute-start.1 = (f32[120,768]{1,0:T(8,128)}, f32[120,768]{1,0:T(8,128)}, u32[]{:S(2)}, u32[]{:S(2)}) collective-permute-start(f32[120,768]{1,0:T(8,128)} %maximum_convert_fusion), channel_id=1, source_target_pairs={{0,2},{1,3},{2,0},{3,1},{4,6},{5,7},{6,4},{7,5},{8,10},{9,11},{10,... | collective-permute-start | bytes 1105928 | tf_op jit(solution)/shard_map/ppermute | solution.py:527
  16.3 33.7 %collective-permute-start.2 = (f32[120,768]{1,0:T(8,128)}, f32[120,768]{1,0:T(8,128)}, u32[]{:S(2)}, u32[]{:S(2)}) collective-permute-start(f32[120,768]{1,0:T(8,128)} %maximum_convert_fusion), channel_id=1, source_target_pairs={{0,3},{1,0},{2,1},{3,2},{4,7},{5,4},{6,5},{7,6},{8,11},{9,8},{10,9... | collective-permute-start | bytes 1105928 | tf_op jit(solution)/shard_map/ppermute | solution.py:527
  19.8 20.9 %collective-permute-start.3 = (f32[1,1344]{1,0:T(1,128)S(1)}, f32[1,1344]{1,0:T(1,128)S(1)}, u32[]{:S(2)}, u32[]{:S(2)}) collective-permute-start(f32[1,1344]{1,0:T(1,128)S(1)} %convert_element_type.38), channel_id=1, source_target_pairs={{0,1},{1,2},{2,3},{3,0},{4,5},{5,6},{6,7},{7,4},{8,9},{9,10},{10,1... | collective-permute-start | bytes 16136 | tf_op jit(solution)/shard_map/ppermute | solution.py:527
  20.5 28.2 %collective-permute-start.4 = (f32[1,1344]{1,0:T(1,128)S(1)}, f32[1,1344]{1,0:T(1,128)}, u32[]{:S(2)}, u32[]{:S(2)}) collective-permute-start(f32[1,1344]{1,0:T(1,128)S(1)} %convert_element_type.38), channel_id=1, source_target_pairs={{0,2},{1,3},{2,0},{3,1},{4,6},{5,7},{6,4},{7,5},{8,10},{9,11},{10,... | collective-permute-start | bytes 16136 | tf_op jit(solution)/shard_map/ppermute | solution.py:527
  51.2 31.8 %collective-permute-start.6 = (f32[1,3,64,768]{3,2,1,0:T(8,128)S(1)}, f32[1,3,64,768]{3,2,1,0:T(8,128)S(1)}, u32[]{:S(2)}, u32[]{:S(2)}) collective-permute-start(f32[1,3,64,768]{3,2,1,0:T(8,128)S(1)} %get-tuple-element.132.refs_0_), channel_id=1, source_target_pairs={{0,8},{4,12},{8,0},{12,4},{16,24},{20,28},{24,16},{28,20},{1,9},{5... | collective-permute-start | bytes 1769480 | tf_op jit(solution)/shard_map/ppermute | solution.py:531
  52.7 30.3 %collective-permute-start.7 = (f32[1,3,56,768]{3,2,1,0:T(8,128)S(1)}, f32[1,3,56,768]{3,2,1,0:T(8,128)S(1)}, u32[]{:S(2)}, u32[]{:S(2)}) collective-permute-start(f32[1,3,56,768]{3,2,1,0:T(8,128)S(1)} %get-tuple-element.133.refs_1_), channel_id=1, source_target_pairs={{0,16},{4,20},{8,24},{12,28},{16,0},{20,4},{24,8},{28,12},{1,17},{... | collective-permute-start | bytes 1548296 | tf_op jit(solution)/shard_map/ppermute | solution.py:531
  57.2 24.2 %collective-permute-start.9 = (f32[96,768]{1,0:T(8,128)}, f32[96,768]{1,0:T(8,128)S(1)}, u32[]{:S(2)}, u32[]{:S(2)}) collective-permute-start(f32[96,768]{1,0:T(8,128)} %dynamic-slice_convert_fusion), channel_id=1, source_target_pairs={{0,2},{1,3},{2,0},{3,1},{4,6},{5,7},{6,4},{7,5},{8,10},{9,11},{10,... | collective-permute-start | bytes 884744 | tf_op jit(solution)/shard_map/ppermute | solution.py:527
  84.7 43.2 %collective-permute-start.11 = (f32[2,3,64,768]{3,2,1,0:T(8,128)}, f32[2,3,64,768]{3,2,1,0:T(8,128)}, u32[]{:S(2)}, u32[]{:S(2)}) collective-permute-start(f32[2,3,64,768]{3,2,1,0:T(8,128)} %get-tuple-element.144.refs_2_), channel_id=1, source_target_pairs={{0,16},{4,20},{8,24},{12,28},{16,0},{20,4},{24,8},{28,12},{1,17},{... | collective-permute-start | bytes 3538952 | tf_op jit(solution)/shard_map/ppermute | solution.py:531
  85.2 42.7 %collective-permute-start.12 = (f32[2,3,56,768]{3,2,1,0:T(8,128)}, f32[2,3,56,768]{3,2,1,0:T(8,128)}, u32[]{:S(2)}, u32[]{:S(2)}) collective-permute-start(f32[2,3,56,768]{3,2,1,0:T(8,128)} %get-tuple-element.143.refs_3_), channel_id=1, source_target_pairs={{0,8},{4,12},{8,0},{12,4},{16,24},{20,28},{24,16},{28,20},{1,9},{5... | collective-permute-start | bytes 3096584 | tf_op jit(solution)/shard_map/ppermute | solution.py:531
  89.1 46.0 %all-to-all-start = ((f32[4,256,384]{2,1,0:T(8,128)}), f32[4,256,384]{2,1,0:T(8,128)}, u32[]{:S(2)}, u32[]{:S(2)}) async-start(f32[4,256,384]{2,1,0:T(8,128)} %bitcast.70), calls=%async_computation | async-start | bytes 3145728 | tf_op jit(solution)/shard_map/all_to_all | solution.py:936
  93.5 246.2 %all-gather.2.cloned.1.call-start = ((), (), s32[]{:S(2)}) async-start(), calls=%async_computation.4 | async-start | bytes 7864320 | tf_op jit(solution)/shard_map/all_gather | solution.py:955
  93.6 26.3 %collective-permute-start.13 = (f32[1,3,48,768]{3,2,1,0:T(8,128)}, f32[1,3,48,768]{3,2,1,0:T(8,128)}, u32[]{:S(2)}, u32[]{:S(2)}) collective-permute-start(f32[1,3,48,768]{3,2,1,0:T(8,128)} %copy-done.15), channel_id=1, source_target_pairs={{0,8},{4,12},{8,0},{12,4},{16,24},{20,28},{24,16},{28,20},{1,9},{5... | collective-permute-start | bytes 1327112 | tf_op jit(solution)/shard_map/ppermute | solution.py:531
  94.2 28.7 %collective-permute-start.14 = (f32[1,3,48,768]{3,2,1,0:T(8,128)}, f32[1,3,48,768]{3,2,1,0:T(8,128)}, u32[]{:S(2)}, u32[]{:S(2)}) collective-permute-start(f32[1,3,48,768]{3,2,1,0:T(8,128)} %copy-done.17), channel_id=1, source_target_pairs={{0,16},{4,20},{8,24},{12,28},{16,0},{20,4},{24,8},{28,12},{1,17},{... | collective-permute-start | bytes 1327112 | tf_op jit(solution)/shard_map/ppermute | solution.py:531
  127.9 29.8 %collective-permute-start.17 = (f32[2,3,96,768]{3,2,1,0:T(8,128)}, f32[2,3,96,768]{3,2,1,0:T(8,128)}, u32[]{:S(2)}, u32[]{:S(2)}) collective-permute-start(f32[2,3,96,768]{3,2,1,0:T(8,128)} %get-tuple-element.156), channel_id=1, source_target_pairs={{0,4},{4,0},{8,12},{12,8},{16,20},{20,16},{24,28},{28,24},{1,5},{5... | collective-permute-start | bytes 5308424 | tf_op jit(solution)/shard_map/ppermute | solution.py:531
  128.5 29.1 %collective-permute-start.18 = (f32[2,3,48,768]{3,2,1,0:T(8,128)}, f32[2,3,48,768]{3,2,1,0:T(8,128)}, u32[]{:S(2)}, u32[]{:S(2)}) collective-permute-start(f32[2,3,48,768]{3,2,1,0:T(8,128)} %get-tuple-element.157.refs_2_), channel_id=1, source_target_pairs={{0,16},{4,20},{8,24},{12,28},{16,0},{20,4},{24,8},{28,12},{1,17},{... | collective-permute-start | bytes 2654216 | tf_op jit(solution)/shard_map/ppermute | solution.py:531
  129.1 28.6 %collective-permute-start.19 = (f32[2,3,48,768]{3,2,1,0:T(8,128)}, f32[2,3,48,768]{3,2,1,0:T(8,128)}, u32[]{:S(2)}, u32[]{:S(2)}) collective-permute-start(f32[2,3,48,768]{3,2,1,0:T(8,128)} %get-tuple-element.158.refs_3_), channel_id=1, source_target_pairs={{0,8},{4,12},{8,0},{12,4},{16,24},{20,28},{24,16},{28,20},{1,9},{5... | collective-permute-start | bytes 2654216 | tf_op jit(solution)/shard_map/ppermute | solution.py:531
  179.4 165.3 %reduce-scatter.3.cloned.1.call-start = ((), (), s32[]{:S(2)}) async-start(), calls=%async_computation.3 | async-start | bytes 10616832 | tf_op jit(solution)/shard_map/reduce_scatter | solution.py:965
  199.6 174.6 %reduce-scatter.5.cloned.1.call-start = ((), (), s32[]{:S(2)}) async-start(), calls=%async_computation.5 | async-start | bytes 10616832 | tf_op jit(solution)/shard_map/reduce_scatter | solution.py:987
  276.1 28.8 %collective-permute-start.38 = (f32[192,1536]{1,0:T(8,128)S(1)}, f32[192,1536]{1,0:T(8,128)S(1)}, u32[]{:S(2)}, u32[]{:S(2)}) collective-permute-start(f32[192,1536]{1,0:T(8,128)S(1)} %copy-done.31), channel_id=1, source_target_pairs={{0,16},{4,20},{8,24},{12,28},{16,0},{20,4},{24,8},{28,12},{1,17},{... | collective-permute-start | bytes 3538952 | tf_op jit(solution)/shard_map/ppermute | solution.py:531
  276.8 30.6 %collective-permute-start.37 = (f32[192,1536]{1,0:T(8,128)}, f32[192,1536]{1,0:T(8,128)S(1)}, u32[]{:S(2)}, u32[]{:S(2)}) collective-permute-start(f32[192,1536]{1,0:T(8,128)} %pad_maximum_fusion), channel_id=1, source_target_pairs={{0,8},{4,12},{8,0},{12,4},{16,24},{20,28},{24,16},{28,20},{1,9},{5... | collective-permute-start | bytes 3538952 | tf_op jit(solution)/shard_map/ppermute | solution.py:531
  277.6 46.6 %collective-permute-start.34 = (f32[512,768]{1,0:T(8,128)}, f32[512,768]{1,0:T(8,128)}, u32[]{:S(2)}, u32[]{:S(2)}) collective-permute-start(f32[512,768]{1,0:T(8,128)} %get-tuple-element.211.own_ref), channel_id=1, source_target_pairs={{0,1},{1,2},{2,3},{4,5},{5,6},{6,7},{8,9},{9,10},{10,11},{12,13},{... | collective-permute-start | bytes 4718600 | tf_op jit(solution)/shard_map/ppermute | solution.py:834
  287.0 41.1 %collective-permute-start.35 = (f32[512,768]{1,0:T(8,128)}, f32[512,768]{1,0:T(8,128)}, u32[]{:S(2)}, u32[]{:S(2)}) collective-permute-start(f32[512,768]{1,0:T(8,128)} %get-tuple-element.211.own_ref), channel_id=1, source_target_pairs={{1,0},{2,1},{3,2},{5,4},{6,5},{7,6},{9,8},{10,9},{11,10},{13,12},{... | collective-permute-start | bytes 4718600 | tf_op jit(solution)/shard_map/ppermute | solution.py:835
  307.6 28.7 %collective-permute-start.39 = (f32[96,1536]{1,0:T(8,128)S(1)}, f32[96,1536]{1,0:T(8,128)}, u32[]{:S(2)}, u32[]{:S(2)}) collective-permute-start(f32[96,1536]{1,0:T(8,128)S(1)} %slice.187), channel_id=1, source_target_pairs={{0,16},{4,20},{8,24},{12,28},{16,0},{20,4},{24,8},{28,12},{1,17},{... | collective-permute-start | bytes 1769480 | tf_op jit(solution)/shard_map/ppermute | solution.py:531
  308.9 28.8 %collective-permute-start.40 = (f32[96,1536]{1,0:T(8,128)}, f32[96,1536]{1,0:T(8,128)}, u32[]{:S(2)}, u32[]{:S(2)}) collective-permute-start(f32[96,1536]{1,0:T(8,128)} %slice.188), channel_id=1, source_target_pairs={{0,8},{4,12},{8,0},{12,4},{16,24},{20,28},{24,16},{28,20},{1,9},{5... | collective-permute-start | bytes 1769480 | tf_op jit(solution)/shard_map/ppermute | solution.py:531
  324.1 31.4 %collective-permute-start.41 = (f32[512,768]{1,0:T(8,128)}, f32[512,768]{1,0:T(8,128)}, u32[]{:S(2)}, u32[]{:S(2)}) collective-permute-start(f32[512,768]{1,0:T(8,128)} %collective-permute-done.34.refs_0_), channel_id=1, source_target_pairs={{1,2},{2,3},{5,6},{6,7},{9,10},{10,11},{13,14},{14,15},{17,18},{18... | collective-permute-start | bytes 4718600 | tf_op jit(solution)/shard_map/ppermute | solution.py:834
  328.1 39.7 %collective-permute-start.42 = (f32[512,768]{1,0:T(8,128)}, f32[512,768]{1,0:T(8,128)}, u32[]{:S(2)}, u32[]{:S(2)}) collective-permute-start(f32[512,768]{1,0:T(8,128)} %collective-permute-done.35.refs_3_), channel_id=1, source_target_pairs={{1,0},{2,1},{5,4},{6,5},{9,8},{10,9},{13,12},{14,13},{17,16},{18,1... | collective-permute-start | bytes 4718600 | tf_op jit(solution)/shard_map/ppermute | solution.py:835
  347.3 26.0 %collective-permute-start.43 = (f32[192,768]{1,0:T(8,128)S(1)}, f32[192,768]{1,0:T(8,128)S(1)}, u32[]{:S(2)}, u32[]{:S(2)}) collective-permute-start(f32[192,768]{1,0:T(8,128)S(1)} %get-tuple-element.224), channel_id=1, source_target_pairs={{0,1},{4,5},{8,9},{12,13},{16,17},{20,21},{24,25},{28,29}} | collective-permute-start | bytes 1769480 | tf_op jit(solution)/shard_map/ppermute | solution.py:788
  355.6 44.5 %collective-permute-start.46 = (f32[512,768]{1,0:T(8,128)}, f32[512,768]{1,0:T(8,128)}, u32[]{:S(2)}, u32[]{:S(2)}) collective-permute-start(f32[512,768]{1,0:T(8,128)} %collective-permute-done.41.refs_1_), channel_id=1, source_target_pairs={{2,3},{6,7},{10,11},{14,15},{18,19},{22,23},{26,27},{30,31}} | collective-permute-start | bytes 4718600 | tf_op jit(solution)/shard_map/ppermute | solution.py:834
  367.8 37.8 %collective-permute-start.47 = (f32[512,768]{1,0:T(8,128)}, f32[512,768]{1,0:T(8,128)}, u32[]{:S(2)}, u32[]{:S(2)}) collective-permute-start(f32[512,768]{1,0:T(8,128)} %collective-permute-done.42.refs_4_), channel_id=1, source_target_pairs={{1,0},{5,4},{9,8},{13,12},{17,16},{21,20},{25,24},{29,28}} | collective-permute-start | bytes 4718600 | tf_op jit(solution)/shard_map/ppermute | solution.py:835
  405.6 22.1 %collective-permute-start.56 = (f32[192,768]{1,0:T(8,128)}, f32[192,768]{1,0:T(8,128)S(1)}, u32[]{:S(2)}, u32[]{:S(2)}) collective-permute-start(f32[192,768]{1,0:T(8,128)} %add.268), channel_id=1, source_target_pairs={{0,1},{1,2},{2,3},{4,5},{5,6},{6,7},{8,9},{9,10},{10,11},{12,13},{... | collective-permute-start | bytes 1769480 | tf_op jit(solution)/shard_map/ppermute | solution.py:788
  407.1 20.6 %collective-permute-start.57 = (f32[192,768]{1,0:T(8,128)S(1)}, f32[192,768]{1,0:T(8,128)}, u32[]{:S(2)}, u32[]{:S(2)}) collective-permute-start(f32[192,768]{1,0:T(8,128)S(1)} %add.269), channel_id=1, source_target_pairs={{1,0},{2,1},{3,2},{5,4},{6,5},{7,6},{9,8},{10,9},{11,10},{13,12},{... | collective-permute-start | bytes 1769480 | tf_op jit(solution)/shard_map/ppermute | solution.py:792
  (79 other events, 1024.0 us)
Sparse Core Ops, SparseCore 0:
  179.5 118.3 all-gather.1
Sparse Core Ops, SparseCore 1:
  199.7 76.7 reduce-scatter.2
  279.8 88.9 reduce-scatter.4

commit v7 on v6

--- a/solution.py
+++ b/solution.py
@@ -1005,16 +1005,17 @@
         last = columns(part3, tensor)
         v, w = up(last[1], tensor, 1), down(last[3], tensor, 1)
         extra = extra + flip(extra, 4)
-        _, _, u, d, v, w, extra = stage(*g3, first[3] + u, first[1] + d, last[2] + v, last[2] + w, extra)
-
-        u, d, v, w = up(u, tensor, 3), down(d, tensor, 3), up(v, tensor, 2), down(w, tensor, 2)
+        v, w, extra = stage(last[2] + v, last[2] + w, extra)
+
+        v, w = up(v, tensor, 2), down(w, tensor, 2)
         extra = extra + swap(extra, tensor, 1)
+        _, _, u, d, v, w, extra = stage(*g3, first[3] + u, first[1] + d, last[3] + v, last[1] + w, extra)
+
+        u, d, v, w = up(u, tensor, 3), down(d, tensor, 3), up(v, tensor, 3), down(w, tensor, 3)
+        extra = extra + swap(extra, tensor, 2)
+        v, w, grad_x = stage(v, w, grad_x)
         grad_inputs = place(grad_x, [g1[0], g2[0], g3[0]], [g1[1], g2[1], g3[1]])
-        gu = first[0] + u + d
-        v, w, extra, gu, grad_inputs = stage(last[3] + v, last[1] + w, extra, gu, grad_inputs)
-
-        gqkv = last[0] + up(v, tensor, 3) + down(w, tensor, 3)
-        extra = extra + swap(extra, tensor, 2)
+        gu, gqkv = first[0] + u + d, last[0] + v + w
         gu, gi = gu[:share], gu[share:]
         gqkv, go = gqkv[:, : 3 * cols], gqkv[:, 3 * cols :]
         sums = extra.reshape(-1)

time: 456 us -> 451 us (0.989)
    ppermute x3, waiting for transfers between devices: 18 us -> 2.71 us  [onward(): lax.ppermute(d, 'tensor', [(i, i - 1) for i in range(1, tensor - step + 1)])]
    ppermute x6, waiting for transfers between devices: 7.36 us -> 14.6 us  [up(): return lax.ppermute(values, 'tensor', [(i, i + 1) for i in range(step)])]
  transfers between devices with their start and end apart: 65 -> 65, of which waited for: 28 -> 30; matrix products, arithmetic and copies ran while one was open for 10% -> 9% of each run, Pallas kernels for 29% -> 29%
where the time goes in v7:
time: 451 us; the launch traced here: 449 us
  waiting for transfers between devices  142 us (31%)
  Pallas kernels  134 us (30%)
  starting transfers between devices  92.8 us (21%)
  local copies, waits for them, and re-layouts  38 us (8%)
  other arithmetic  26 us (6%)
  between operations  16.4 us (4%)
    pallas_call x11, Pallas kernels, call(): pl.pallas_call(kernel, grid_spec=pltpu.PrefetchScalarGridSpec(num_scalar_...  124 us
    ppermute x29, waiting for transfers between devices, flip(): return lax.ppermute(values, 'dp', [(i, i ^ bit) for i in range(8)])  68.2 us
    ppermute x12, waiting for transfers between devices, shift_to(): lax.ppermute(values, 'tensor', [(i, (i + k) % tensor) for i in range(tens...  32.5 us
    ppermute x6, starting transfers between devices, up(): return lax.ppermute(values, 'tensor', [(i, i + 1) for i in range(step)])  25.8 us
    ppermute x12, starting transfers between devices, shift_to(): lax.ppermute(values, 'tensor', [(i, (i + k) % tensor) for i in range(tens...  17.8 us
    unnamed x94, local copies, waits for them, and re-layouts  17 us
    ppermute x29, starting transfers between devices, flip(): return lax.ppermute(values, 'dp', [(i, i ^ bit) for i in range(8)])  15.3 us
    ppermute x6, waiting for transfers between devices, up(): return lax.ppermute(values, 'tensor', [(i, i + 1) for i in range(step)])  14.6 us
  transfers between devices with their start and end apart: 65, of which 30 were waited for; matrix products, arithmetic and copies ran while one was open for 9% of the time, Pallas kernels for 29%

profile of v7, /device:TPU:0, one launch (start us, length us, event | category | flops | bytes accessed | tf_op | source)
XLA Modules:
  0.0 449.0 jit_solution(7046782486388914806)
XLA Ops:
  23.5 11.6 %attend_forward.1 = f32[1024,384]{1,0:T(8,128)} custom-call(bf16[2048,768]{1,0:T(8,128)(2,1)} %x_ref.1, bf16[576,768]{1,0:T(8,128)(2,1)} %pad_maximum_fusion.1.w_ref.local_ref, f32[1,576]{1,0:T(1,128)} %slice.181.bias_ref), custom_call_target="tpu_custom_call" | custom-call | flops 2617245696 | bytes 5605632 | tf_op jit(solution)/shard_map/attend_forward/pallas_call | solution.py:58
  36.8 3.9 collective-permute-done.3
  41.4 7.3 %collective-permute-done.4 = f32[1,1344]{1,0:T(1,128)} collective-permute-done((f32[1,1344]{1,0:T(1,128)S(1)}, f32[1,1344]{1,0:T(1,128)}, u32[]{:S(2)}, u32[]{:S(2)}) %collective-permute-start.4) | collective-permute-done | bytes 5408 | tf_op jit(solution)/shard_map/ppermute | solution.py:527
  63.7 4.1 collective-permute-done.10.refs_2_
  67.7 5.4 %collective-permute-done.8.refs_0_ = f32[96,768]{1,0:T(8,128)S(1)} collective-permute-done((f32[96,768]{1,0:T(8,128)}, f32[96,768]{1,0:T(8,128)S(1)}, u32[]{:S(2)}, u32[]{:S(2)}) %collective-permute-start.8) | collective-permute-done | bytes 294944 | tf_op jit(solution)/shard_map/ppermute | solution.py:527
  73.1 8.3 %collective-permute-done.9.refs_1_ = f32[96,768]{1,0:T(8,128)S(1)} collective-permute-done((f32[96,768]{1,0:T(8,128)}, f32[96,768]{1,0:T(8,128)S(1)}, u32[]{:S(2)}, u32[]{:S(2)}) %collective-permute-start.9) | collective-permute-done | bytes 294944 | tf_op jit(solution)/shard_map/ppermute | solution.py:527
  89.1 4.3 all-to-all-start
  96.3 23.6 %collective-permute-done.13.refs_2_ = f32[1,3,48,768]{3,2,1,0:T(8,128)} collective-permute-done((f32[1,3,48,768]{3,2,1,0:T(8,128)}, f32[1,3,48,768]{3,2,1,0:T(8,128)}, u32[]{:S(2)}, u32[]{:S(2)}) %collective-permute-start.13) | collective-permute-done | bytes 442400 | tf_op jit(solution)/shard_map/ppermute | solution.py:531
  135.2 9.0 %output_forward.1 = (bf16[4,512,192]{2,1,0:T(8,128)(2,1)}, f32[512,768]{1,0:T(8,128)}, bf16[512,768]{1,0:T(8,128)(2,1)}, f32[512,768]{1,0:T(8,128)}, f32[512,1]{1,0:T(8,128)}, /*index=5*/bf16[4,192,768]{2,1,0:T(8,128)(2,1)}) custom-call(s32[4]{0:T(128)} %and_select_fusion.2.refs_0_, s32[8]{0:T(128)} %stack.211.refs_1_, bf16[192,768]{1,0:T(8,128)(2,1)} %refs_2_.1, ...), custom_call_target="tpu_custom_call" | custom-call | flops 603979776 | bytes 13887520 | tf_op jit(solution)/shard_map/output_forward/pallas_call | solution.py:58
  144.2 13.5 %inner_forward.1 = (bf16[4,512,768]{2,1,0:T(8,128)(2,1)}, f32[4,512,768]{2,1,0:T(8,128)}, bf16[4,768,768]{2,1,0:T(8,128)(2,1)}) custom-call(s32[16]{0:T(128)} %stack.235.refs_0_, bf16[768,768]{1,0:T(8,128)(2,1)} %refs_1_.2, f32[2,3,64,768]{3,2,1,0:T(8,128)} %get-tuple-element.145.refs_2_, f32[2,3,56,768]{3,2,1,0:T(8,128)} %get-tuple-element.144.refs_3_, ...), custom_call_target="tpu_custom_call" | custom-call | flops 2415919104 | bytes 24981568 | tf_op jit(solution)/shard_map/inner_forward/pallas_call | solution.py:58
  162.7 12.2 %outer_forward.1 = (f32[512,768]{1,0:T(8,128)}, f32[512,768]{1,0:T(8,128)}, f32[512,1]{1,0:T(8,128)}, bf16[4,768,768]{2,1,0:T(8,128)(2,1)}) custom-call(s32[16]{0:T(128)} %stack.244.refs_0_, bf16[768,768]{1,0:T(8,128)(2,1)} %refs_1_.3, f32[2,3,48,768]{3,2,1,0:T(8,128)} %get-tuple-element.158.refs_2_, f32[2,3,48,768]{3,2,1,0:T(8,128)} %get-tuple-element.159.refs_3_, ...), custom_call_target="tpu_custom_call" | custom-call | flops 2415919104 | bytes 20867136 | tf_op jit(solution)/shard_map/outer_forward/pallas_call | solution.py:58
  183.4 4.5 last_norm_backward.1
  191.0 8.6 %grad_full.1 = f32[768,3072]{1,0:T(8,128)} custom-call(bf16[512,768]{1,0:T(8,128)(2,1)} %get-tuple-element.187.refs_0_.go_ref, bf16[4,512,768]{2,1,0:T(8,128)(2,1)} %get-tuple-element.168.refs_9_.refs_1_), custom_call_target="tpu_custom_call" | custom-call | tf_op jit(solution)/shard_map/grad_full/pallas_call | solution.py:58
  201.1 15.7 %inner_backward.1 = (bf16[4,512,768]{2,1,0:T(8,128)(2,1)}, f32[512,768]{1,0:T(8,128)}, bf16[512,768]{1,0:T(8,128)(2,1)}, f32[1,4,1,768]{3,2,1,0:T(1,128)}, f32[1,8,768]{2,1,0:T(8,128)}) custom-call(bf16[512,768]{1,0:T(8,128)(2,1)} %get-tuple-element.187.refs_0_.go_ref, bf16[4,768,768]{2,1,0:T(8,128)(2,1)} %get-tuple-element.188.wu_ref, ...), custom_call_target="tpu_custom_call" | custom-call | tf_op jit(solution)/shard_map/inner_backward/pallas_call | solution.py:58
  219.4 8.7 %grad_rows.1 = (f32[384,3072]{1,0:T(8,128)}, f32[384,3072]{1,0:T(8,128)}) custom-call(bf16[768,768]{1,0:T(8,128)(2,1)} %fusion.refs_0_, bf16[512,768]{1,0:T(8,128)(2,1)} %get-tuple-element.156.refs_9_.refs_1_, bf16[4,512,768]{2,1,0:T(8,128)(2,1)} %get-tuple-element.196.refs_2_), custom_call_target="tpu_custom_call" | custom-call | tf_op jit(solution)/shard_map/grad_rows/pallas_call | solution.py:58
  236.1 3.6 assemble.1.w_ref
  246.7 28.1 %attend_backward.1 = (f32[768,3072]{1,0:T(8,128)}, f32[512,768]{1,0:T(8,128)}, f32[1,4,1,576]{3,2,1,0:T(1,128)}) custom-call(bf16[512,768]{1,0:T(8,128)(2,1)} %constant_dynamic-slice_fusion.1.refs_7_.x_ref, bf16[512,768]{1,0:T(8,128)(2,1)} %get-tuple-element.207.ga_ref, f32[512,768]{1,0:T(8,128)} %get-tuple-element.208.gr_ref, ...), custom_call_target="tpu_custom_call" | custom-call | tf_op jit(solution)/shard_map/attend_backward/pallas_call | solution.py:58
  277.6 9.5 %collective-permute-start.34 = (f32[512,768]{1,0:T(8,128)}, f32[512,768]{1,0:T(8,128)}, u32[]{:S(2)}, u32[]{:S(2)}) collective-permute-start(f32[512,768]{1,0:T(8,128)} %get-tuple-element.238.own_ref), channel_id=1, source_target_pairs={{0,1},{1,2},{2,3},{4,5},{5,6},{6,7},{8,9},{9,10},{10,11},{12,13},{... | collective-permute-start | bytes 4718600 | tf_op jit(solution)/shard_map/ppermute | solution.py:834
  288.6 16.3 %collective-permute-done.38 = f32[192,1536]{1,0:T(8,128)S(1)} collective-permute-done((f32[192,1536]{1,0:T(8,128)S(1)}, f32[192,1536]{1,0:T(8,128)S(1)}, u32[]{:S(2)}, u32[]{:S(2)}) %collective-permute-start.38) | collective-permute-done | bytes 1179680 | tf_op jit(solution)/shard_map/ppermute | solution.py:531
  310.5 13.6 %collective-permute-done.34.refs_0_ = f32[512,768]{1,0:T(8,128)} collective-permute-done((f32[512,768]{1,0:T(8,128)}, f32[512,768]{1,0:T(8,128)}, u32[]{:S(2)}, u32[]{:S(2)}) %collective-permute-start.34) | collective-permute-done | bytes 1572896 | tf_op jit(solution)/shard_map/ppermute | solution.py:834
  329.4 6.9 %collective-permute-done.39 = f32[96,1536]{1,0:T(8,128)} collective-permute-done((f32[96,1536]{1,0:T(8,128)S(1)}, f32[96,1536]{1,0:T(8,128)}, u32[]{:S(2)}, u32[]{:S(2)}) %collective-permute-start.39) | collective-permute-done | bytes 589856 | tf_op jit(solution)/shard_map/ppermute | solution.py:531
  339.7 4.9 %narrow.1 = bf16[2048,768]{1,0:T(8,128)(2,1)} custom-call(f32[2048,768]{1,0:T(8,128)} %all-gather.2.cloned.1.call-done.x_ref), custom_call_target="tpu_custom_call" | custom-call | bytes 9437184 | tf_op jit(solution)/shard_map/narrow/pallas_call | solution.py:58
  347.3 7.6 %collective-permute-start.45 = (f32[192,768]{1,0:T(8,128)S(1)}, f32[192,768]{1,0:T(8,128)S(1)}, u32[]{:S(2)}, u32[]{:S(2)}) collective-permute-start(f32[192,768]{1,0:T(8,128)S(1)} %get-tuple-element.226), channel_id=1, source_target_pairs={{0,1},{4,5},{8,9},{12,13},{16,17},{20,21},{24,25},{28,29}} | collective-permute-start | bytes 1769480 | tf_op jit(solution)/shard_map/ppermute | solution.py:788
  357.1 3.6 collective-permute-done.47
  360.8 5.3 %collective-permute-done.45 = f32[192,768]{1,0:T(8,128)S(1)} collective-permute-done((f32[192,768]{1,0:T(8,128)S(1)}, f32[192,768]{1,0:T(8,128)S(1)}, u32[]{:S(2)}, u32[]{:S(2)}) %collective-permute-start.45) | collective-permute-done | bytes 589856 | tf_op jit(solution)/shard_map/ppermute | solution.py:788
  376.4 6.3 %collective-permute-start.50 = (f32[96,768]{1,0:T(8,128)S(1)}, f32[96,768]{1,0:T(8,128)S(1)}, u32[]{:S(2)}, u32[]{:S(2)}) collective-permute-start(f32[96,768]{1,0:T(8,128)S(1)} %get-tuple-element.296), channel_id=1, source_target_pairs={{0,1},{4,5},{8,9},{12,13},{16,17},{20,21},{24,25},{28,29}} | collective-permute-start | bytes 884744 | tf_op jit(solution)/shard_map/ppermute | solution.py:788
  389.9 4.4 collective-permute-start.53
  395.0 7.6 %collective-permute-done.48 = f32[192,768]{1,0:T(8,128)S(1)} collective-permute-done((f32[192,768]{1,0:T(8,128)}, f32[192,768]{1,0:T(8,128)S(1)}, u32[]{:S(2)}, u32[]{:S(2)}) %collective-permute-start.48) | collective-permute-done | bytes 589856 | tf_op jit(solution)/shard_map/ppermute | solution.py:788
  407.3 5.2 %collective-permute-done.55 = f32[16,768]{1,0:T(8,128)S(1)} collective-permute-done((f32[16,768]{1,0:T(8,128)S(1)}, f32[16,768]{1,0:T(8,128)S(1)}, u32[]{:S(2)}, u32[]{:S(2)}) %collective-permute-start.55) | collective-permute-done | bytes 49184 | tf_op jit(solution)/shard_map/ppermute | solution.py:840
  415.3 3.8 collective-permute-start.58
  419.1 4.7 %collective-permute-start.59 = (f32[192,768]{1,0:T(8,128)}, f32[192,768]{1,0:T(8,128)}, u32[]{:S(2)}, u32[]{:S(2)}) collective-permute-start(f32[192,768]{1,0:T(8,128)} %add.268), channel_id=1, source_target_pairs={{0,1},{1,2},{2,3},{4,5},{5,6},{6,7},{8,9},{9,10},{10,11},{12,13},{... | collective-permute-start | bytes 1769480 | tf_op jit(solution)/shard_map/ppermute | solution.py:788
  430.8 7.4 %place.1 = f32[2048,768]{1,0:T(8,128)} custom-call(s32[1]{0:T(128)} %bitcast.59.z_ref, f32[512,768]{1,0:T(8,128)} %get-tuple-element.238.own_ref, f32[512,768]{1,0:T(8,128)} %collective-permute-done.34.refs_0_, f32[512,768]{1,0:T(8,128)} %collective-permute-done.41.refs_1_, f32[512,768]{1,0:T(8,128)} %collective-permute-done.42.refs_2_, ...), custom_call_target="tpu_custom_call" | custom-call | tf_op jit(solution)/shard_map/place/pallas_call | solution.py:58
  (297 shorter events, 153.3 us)
Async XLA Ops:
  10.7 39.3 %collective-permute-start = (f32[120,768]{1,0:T(8,128)}, f32[120,768]{1,0:T(8,128)S(1)}, u32[]{:S(2)}, u32[]{:S(2)}) collective-permute-start(f32[120,768]{1,0:T(8,128)} %maximum_convert_fusion), channel_id=1, source_target_pairs={{0,1},{1,2},{2,3},{3,0},{4,5},{5,6},{6,7},{7,4},{8,9},{9,10},{10,1... | collective-permute-start | bytes 1105928 | tf_op jit(solution)/shard_map/ppermute | solution.py:527
  13.7 36.3 %collective-permute-start.1 = (f32[120,768]{1,0:T(8,128)}, f32[120,768]{1,0:T(8,128)}, u32[]{:S(2)}, u32[]{:S(2)}) collective-permute-start(f32[120,768]{1,0:T(8,128)} %maximum_convert_fusion), channel_id=1, source_target_pairs={{0,2},{1,3},{2,0},{3,1},{4,6},{5,7},{6,4},{7,5},{8,10},{9,11},{10,... | collective-permute-start | bytes 1105928 | tf_op jit(solution)/shard_map/ppermute | solution.py:527
  16.3 33.7 %collective-permute-start.2 = (f32[120,768]{1,0:T(8,128)}, f32[120,768]{1,0:T(8,128)}, u32[]{:S(2)}, u32[]{:S(2)}) collective-permute-start(f32[120,768]{1,0:T(8,128)} %maximum_convert_fusion), channel_id=1, source_target_pairs={{0,3},{1,0},{2,1},{3,2},{4,7},{5,4},{6,5},{7,6},{8,11},{9,8},{10,9... | collective-permute-start | bytes 1105928 | tf_op jit(solution)/shard_map/ppermute | solution.py:527
  19.8 20.9 %collective-permute-start.3 = (f32[1,1344]{1,0:T(1,128)S(1)}, f32[1,1344]{1,0:T(1,128)S(1)}, u32[]{:S(2)}, u32[]{:S(2)}) collective-permute-start(f32[1,1344]{1,0:T(1,128)S(1)} %convert_element_type.38), channel_id=1, source_target_pairs={{0,1},{1,2},{2,3},{3,0},{4,5},{5,6},{6,7},{7,4},{8,9},{9,10},{10,1... | collective-permute-start | bytes 16136 | tf_op jit(solution)/shard_map/ppermute | solution.py:527
  20.5 28.2 %collective-permute-start.4 = (f32[1,1344]{1,0:T(1,128)S(1)}, f32[1,1344]{1,0:T(1,128)}, u32[]{:S(2)}, u32[]{:S(2)}) collective-permute-start(f32[1,1344]{1,0:T(1,128)S(1)} %convert_element_type.38), channel_id=1, source_target_pairs={{0,2},{1,3},{2,0},{3,1},{4,6},{5,7},{6,4},{7,5},{8,10},{9,11},{10,... | collective-permute-start | bytes 16136 | tf_op jit(solution)/shard_map/ppermute | solution.py:527
  51.2 31.8 %collective-permute-start.6 = (f32[1,3,64,768]{3,2,1,0:T(8,128)S(1)}, f32[1,3,64,768]{3,2,1,0:T(8,128)S(1)}, u32[]{:S(2)}, u32[]{:S(2)}) collective-permute-start(f32[1,3,64,768]{3,2,1,0:T(8,128)S(1)} %get-tuple-element.133.refs_0_), channel_id=1, source_target_pairs={{0,8},{4,12},{8,0},{12,4},{16,24},{20,28},{24,16},{28,20},{1,9},{5... | collective-permute-start | bytes 1769480 | tf_op jit(solution)/shard_map/ppermute | solution.py:531
  52.7 30.3 %collective-permute-start.7 = (f32[1,3,56,768]{3,2,1,0:T(8,128)S(1)}, f32[1,3,56,768]{3,2,1,0:T(8,128)S(1)}, u32[]{:S(2)}, u32[]{:S(2)}) collective-permute-start(f32[1,3,56,768]{3,2,1,0:T(8,128)S(1)} %get-tuple-element.134.refs_1_), channel_id=1, source_target_pairs={{0,16},{4,20},{8,24},{12,28},{16,0},{20,4},{24,8},{28,12},{1,17},{... | collective-permute-start | bytes 1548296 | tf_op jit(solution)/shard_map/ppermute | solution.py:531
  57.2 24.2 %collective-permute-start.9 = (f32[96,768]{1,0:T(8,128)}, f32[96,768]{1,0:T(8,128)S(1)}, u32[]{:S(2)}, u32[]{:S(2)}) collective-permute-start(f32[96,768]{1,0:T(8,128)} %dynamic-slice_convert_fusion), channel_id=1, source_target_pairs={{0,2},{1,3},{2,0},{3,1},{4,6},{5,7},{6,4},{7,5},{8,10},{9,11},{10,... | collective-permute-start | bytes 884744 | tf_op jit(solution)/shard_map/ppermute | solution.py:527
  84.7 43.2 %collective-permute-start.11 = (f32[2,3,64,768]{3,2,1,0:T(8,128)}, f32[2,3,64,768]{3,2,1,0:T(8,128)}, u32[]{:S(2)}, u32[]{:S(2)}) collective-permute-start(f32[2,3,64,768]{3,2,1,0:T(8,128)} %get-tuple-element.145.refs_2_), channel_id=1, source_target_pairs={{0,16},{4,20},{8,24},{12,28},{16,0},{20,4},{24,8},{28,12},{1,17},{... | collective-permute-start | bytes 3538952 | tf_op jit(solution)/shard_map/ppermute | solution.py:531
  85.2 42.7 %collective-permute-start.12 = (f32[2,3,56,768]{3,2,1,0:T(8,128)}, f32[2,3,56,768]{3,2,1,0:T(8,128)}, u32[]{:S(2)}, u32[]{:S(2)}) collective-permute-start(f32[2,3,56,768]{3,2,1,0:T(8,128)} %get-tuple-element.144.refs_3_), channel_id=1, source_target_pairs={{0,8},{4,12},{8,0},{12,4},{16,24},{20,28},{24,16},{28,20},{1,9},{5... | collective-permute-start | bytes 3096584 | tf_op jit(solution)/shard_map/ppermute | solution.py:531
  89.1 46.0 %all-to-all-start = ((f32[4,256,384]{2,1,0:T(8,128)}), f32[4,256,384]{2,1,0:T(8,128)}, u32[]{:S(2)}, u32[]{:S(2)}) async-start(f32[4,256,384]{2,1,0:T(8,128)} %bitcast.70), calls=%async_computation | async-start | bytes 3145728 | tf_op jit(solution)/shard_map/all_to_all | solution.py:936
  93.5 246.2 %all-gather.2.cloned.1.call-start = ((), (), s32[]{:S(2)}) async-start(), calls=%async_computation.4 | async-start | bytes 7864320 | tf_op jit(solution)/shard_map/all_gather | solution.py:955
  93.6 26.3 %collective-permute-start.13 = (f32[1,3,48,768]{3,2,1,0:T(8,128)}, f32[1,3,48,768]{3,2,1,0:T(8,128)}, u32[]{:S(2)}, u32[]{:S(2)}) collective-permute-start(f32[1,3,48,768]{3,2,1,0:T(8,128)} %copy-done.15), channel_id=1, source_target_pairs={{0,8},{4,12},{8,0},{12,4},{16,24},{20,28},{24,16},{28,20},{1,9},{5... | collective-permute-start | bytes 1327112 | tf_op jit(solution)/shard_map/ppermute | solution.py:531
  94.2 28.7 %collective-permute-start.14 = (f32[1,3,48,768]{3,2,1,0:T(8,128)}, f32[1,3,48,768]{3,2,1,0:T(8,128)}, u32[]{:S(2)}, u32[]{:S(2)}) collective-permute-start(f32[1,3,48,768]{3,2,1,0:T(8,128)} %copy-done.17), channel_id=1, source_target_pairs={{0,16},{4,20},{8,24},{12,28},{16,0},{20,4},{24,8},{28,12},{1,17},{... | collective-permute-start | bytes 1327112 | tf_op jit(solution)/shard_map/ppermute | solution.py:531
  127.9 29.8 %collective-permute-start.17 = (f32[2,3,96,768]{3,2,1,0:T(8,128)}, f32[2,3,96,768]{3,2,1,0:T(8,128)}, u32[]{:S(2)}, u32[]{:S(2)}) collective-permute-start(f32[2,3,96,768]{3,2,1,0:T(8,128)} %get-tuple-element.157), channel_id=1, source_target_pairs={{0,4},{4,0},{8,12},{12,8},{16,20},{20,16},{24,28},{28,24},{1,5},{5... | collective-permute-start | bytes 5308424 | tf_op jit(solution)/shard_map/ppermute | solution.py:531
  128.5 29.1 %collective-permute-start.18 = (f32[2,3,48,768]{3,2,1,0:T(8,128)}, f32[2,3,48,768]{3,2,1,0:T(8,128)}, u32[]{:S(2)}, u32[]{:S(2)}) collective-permute-start(f32[2,3,48,768]{3,2,1,0:T(8,128)} %get-tuple-element.158.refs_2_), channel_id=1, source_target_pairs={{0,16},{4,20},{8,24},{12,28},{16,0},{20,4},{24,8},{28,12},{1,17},{... | collective-permute-start | bytes 2654216 | tf_op jit(solution)/shard_map/ppermute | solution.py:531
  129.1 28.6 %collective-permute-start.19 = (f32[2,3,48,768]{3,2,1,0:T(8,128)}, f32[2,3,48,768]{3,2,1,0:T(8,128)}, u32[]{:S(2)}, u32[]{:S(2)}) collective-permute-start(f32[2,3,48,768]{3,2,1,0:T(8,128)} %get-tuple-element.159.refs_3_), channel_id=1, source_target_pairs={{0,8},{4,12},{8,0},{12,4},{16,24},{20,28},{24,16},{28,20},{1,9},{5... | collective-permute-start | bytes 2654216 | tf_op jit(solution)/shard_map/ppermute | solution.py:531
  158.9 19.1 %collective-permute-start.22 = (f32[72,768]{1,0:T(8,128)}, f32[72,768]{1,0:T(8,128)S(1)}, u32[]{:S(2)}, u32[]{:S(2)}) collective-permute-start(f32[72,768]{1,0:T(8,128)} %dynamic-slice_convert_fusion.1), channel_id=1, source_target_pairs={{0,2},{1,3},{2,0},{3,1},{4,6},{5,7},{6,4},{7,5},{8,10},{9,11},{10,... | collective-permute-start | bytes 663560 | tf_op jit(solution)/shard_map/ppermute | solution.py:527
  179.4 165.3 %reduce-scatter.3.cloned.1.call-start = ((), (), s32[]{:S(2)}) async-start(), calls=%async_computation.3 | async-start | bytes 10616832 | tf_op jit(solution)/shard_map/reduce_scatter | solution.py:965
  199.6 170.0 %reduce-scatter.5.cloned.1.call-start = ((), (), s32[]{:S(2)}) async-start(), calls=%async_computation.5 | async-start | bytes 10616832 | tf_op jit(solution)/shard_map/reduce_scatter | solution.py:987
  276.1 28.8 %collective-permute-start.38 = (f32[192,1536]{1,0:T(8,128)S(1)}, f32[192,1536]{1,0:T(8,128)S(1)}, u32[]{:S(2)}, u32[]{:S(2)}) collective-permute-start(f32[192,1536]{1,0:T(8,128)S(1)} %copy-done.31), channel_id=1, source_target_pairs={{0,16},{4,20},{8,24},{12,28},{16,0},{20,4},{24,8},{28,12},{1,17},{... | collective-permute-start | bytes 3538952 | tf_op jit(solution)/shard_map/ppermute | solution.py:531
  276.8 30.6 %collective-permute-start.37 = (f32[192,1536]{1,0:T(8,128)}, f32[192,1536]{1,0:T(8,128)S(1)}, u32[]{:S(2)}, u32[]{:S(2)}) collective-permute-start(f32[192,1536]{1,0:T(8,128)} %pad_maximum_fusion), channel_id=1, source_target_pairs={{0,8},{4,12},{8,0},{12,4},{16,24},{20,28},{24,16},{28,20},{1,9},{5... | collective-permute-start | bytes 3538952 | tf_op jit(solution)/shard_map/ppermute | solution.py:531
  277.6 46.6 %collective-permute-start.34 = (f32[512,768]{1,0:T(8,128)}, f32[512,768]{1,0:T(8,128)}, u32[]{:S(2)}, u32[]{:S(2)}) collective-permute-start(f32[512,768]{1,0:T(8,128)} %get-tuple-element.238.own_ref), channel_id=1, source_target_pairs={{0,1},{1,2},{2,3},{4,5},{5,6},{6,7},{8,9},{9,10},{10,11},{12,13},{... | collective-permute-start | bytes 4718600 | tf_op jit(solution)/shard_map/ppermute | solution.py:834
  287.0 41.1 %collective-permute-start.35 = (f32[512,768]{1,0:T(8,128)}, f32[512,768]{1,0:T(8,128)}, u32[]{:S(2)}, u32[]{:S(2)}) collective-permute-start(f32[512,768]{1,0:T(8,128)} %get-tuple-element.238.own_ref), channel_id=1, source_target_pairs={{1,0},{2,1},{3,2},{5,4},{6,5},{7,6},{9,8},{10,9},{11,10},{13,12},{... | collective-permute-start | bytes 4718600 | tf_op jit(solution)/shard_map/ppermute | solution.py:835
  307.6 28.7 %collective-permute-start.39 = (f32[96,1536]{1,0:T(8,128)S(1)}, f32[96,1536]{1,0:T(8,128)}, u32[]{:S(2)}, u32[]{:S(2)}) collective-permute-start(f32[96,1536]{1,0:T(8,128)S(1)} %slice.187), channel_id=1, source_target_pairs={{0,16},{4,20},{8,24},{12,28},{16,0},{20,4},{24,8},{28,12},{1,17},{... | collective-permute-start | bytes 1769480 | tf_op jit(solution)/shard_map/ppermute | solution.py:531
  308.9 28.8 %collective-permute-start.40 = (f32[96,1536]{1,0:T(8,128)}, f32[96,1536]{1,0:T(8,128)}, u32[]{:S(2)}, u32[]{:S(2)}) collective-permute-start(f32[96,1536]{1,0:T(8,128)} %slice.188), channel_id=1, source_target_pairs={{0,8},{4,12},{8,0},{12,4},{16,24},{20,28},{24,16},{28,20},{1,9},{5... | collective-permute-start | bytes 1769480 | tf_op jit(solution)/shard_map/ppermute | solution.py:531
  324.1 43.0 %collective-permute-start.41 = (f32[512,768]{1,0:T(8,128)}, f32[512,768]{1,0:T(8,128)}, u32[]{:S(2)}, u32[]{:S(2)}) collective-permute-start(f32[512,768]{1,0:T(8,128)} %collective-permute-done.34.refs_0_), channel_id=1, source_target_pairs={{1,2},{2,3},{5,6},{6,7},{9,10},{10,11},{13,14},{14,15},{17,18},{18... | collective-permute-start | bytes 4718600 | tf_op jit(solution)/shard_map/ppermute | solution.py:834
  328.1 39.7 %collective-permute-start.43 = (f32[512,768]{1,0:T(8,128)}, f32[512,768]{1,0:T(8,128)}, u32[]{:S(2)}, u32[]{:S(2)}) collective-permute-start(f32[512,768]{1,0:T(8,128)} %collective-permute-done.35.refs_3_), channel_id=1, source_target_pairs={{1,0},{2,1},{5,4},{6,5},{9,8},{10,9},{13,12},{14,13},{17,16},{18,1... | collective-permute-start | bytes 4718600 | tf_op jit(solution)/shard_map/ppermute | solution.py:835
  371.4 41.1 %collective-permute-start.42 = (f32[512,768]{1,0:T(8,128)}, f32[512,768]{1,0:T(8,128)}, u32[]{:S(2)}, u32[]{:S(2)}) collective-permute-start(f32[512,768]{1,0:T(8,128)} %collective-permute-done.41.refs_1_), channel_id=1, source_target_pairs={{2,3},{6,7},{10,11},{14,15},{18,19},{22,23},{26,27},{30,31}} | collective-permute-start | bytes 4718600 | tf_op jit(solution)/shard_map/ppermute | solution.py:834
  373.2 39.3 %collective-permute-start.44 = (f32[512,768]{1,0:T(8,128)}, f32[512,768]{1,0:T(8,128)}, u32[]{:S(2)}, u32[]{:S(2)}) collective-permute-start(f32[512,768]{1,0:T(8,128)} %collective-permute-done.43.refs_4_), channel_id=1, source_target_pairs={{1,0},{5,4},{9,8},{13,12},{17,16},{21,20},{25,24},{29,28}} | collective-permute-start | bytes 4718600 | tf_op jit(solution)/shard_map/ppermute | solution.py:835
  374.5 19.8 %collective-permute-start.49 = (f32[192,768]{1,0:T(8,128)}, f32[192,768]{1,0:T(8,128)S(1)}, u32[]{:S(2)}, u32[]{:S(2)}) collective-permute-start(f32[192,768]{1,0:T(8,128)} %get-tuple-element.230), channel_id=1, source_target_pairs={{2,1},{3,2},{6,5},{7,6},{10,9},{11,10},{14,13},{15,14},{18,17},{19... | collective-permute-start | bytes 1769480 | tf_op jit(solution)/shard_map/ppermute | solution.py:792
  389.9 22.6 %collective-permute-start.53 = (f32[96,768]{1,0:T(8,128)S(1)}, f32[96,768]{1,0:T(8,128)S(1)}, u32[]{:S(2)}, u32[]{:S(2)}) collective-permute-start(f32[96,768]{1,0:T(8,128)S(1)} %slice_add_fusion.4), channel_id=1, source_target_pairs={{0,1},{1,2},{4,5},{5,6},{8,9},{9,10},{12,13},{13,14},{16,17},{17,1... | collective-permute-start | bytes 884744 | tf_op jit(solution)/shard_map/ppermute | solution.py:788
  (79 other events, 1058.4 us)
Sparse Core Ops, SparseCore 0:
  179.5 118.3 all-gather.1
Sparse Core Ops, SparseCore 1:
  199.7 76.7 reduce-scatter.2
  279.8 89.8 reduce-scatter.4

commit v8 on v7

--- a/solution.py
+++ b/solution.py
@@ -942,19 +942,21 @@
         c2, ay2, bx2 = flip(ab2, 1), flip(a2, 4), flip(b2, 2)
         pieces = pieces_of([w_inner, w_output], a1, b1, ay1, bx1, c1, d1)
         context, hidden, hidden_bf, normed, inverse, output_full = rest_of_attention(context, Stream(w_output, 1, pieces))
+        hidden_bf, c2, p3 = stage(hidden_bf, c2, p3)
+        z3 = across(p3, tensor)
         active, slope, inner_full = inner_forward(hidden_bf, Stream(w_inner, 0, pieces), inner_bias)
-        c2, ay2, bx2, p3, active = stage(c2, ay2, bx2, p3, active)
-
-        d2, z3 = other_core(ay2, bx2), across(p3, tensor)
+        ay2, bx2, *z3, active = stage(ay2, bx2, *z3, active)
+
+        d2 = other_core(ay2, bx2)
+        a3, b3 = halves(z3, n3)
+        ax, by = flip(a3, 2), flip(b3, 4)
         pieces = pieces_of([w_outer], a2, b2, ay2, bx2, c2, d2)
         layer_out, normed_two, inverse_two, outer_full = outer_forward(
             active, Stream(w_outer, 0, pieces), hidden, wide_vectors
         )
-        *z3, layer_out, normed_two = stage(*z3, layer_out, normed_two)
+        ax, by, layer_out, normed_two = stage(ax, by, layer_out, normed_two)
 
         layer_out = lax.all_gather(layer_out, "tensor", axis=0, tiled=True)
-        a3, b3 = halves(z3, n3)
-        ax, by = flip(a3, 2), flip(b3, 4)
         grad_resid2, grad_outer, sums_two = last_norm_backward(cot, normed_two, inverse_two, wide_vectors)
         a3, b3, ab3 = join(a3, ax, b3, by)
         a3, b3, ab3, grad_outer = stage(a3, b3, ab3, grad_outer)

time: 451 us -> 447 us (level)
    ppermute x29, waiting for transfers between devices: 68.2 us -> 62.5 us  [flip(): return lax.ppermute(values, 'dp', [(i, i ^ bit) for i in range(8)])]
    ppermute x3, waiting for transfers between devices: 13.6 us -> 18.8 us  [onward(): lax.ppermute(u, 'tensor', [(i, i + 1) for i in range(step - 1, tensor - 1)])]
    unnamed x94 -> x86, local copies, waits for them, and re-layouts: 17 us -> 13.3 us
  transfers between devices with their start and end apart: 65 -> 65, of which waited for: 30 -> 27; matrix products, arithmetic and copies ran while one was open for 9% -> 9% of each run, Pallas kernels for 29% -> 30%
where the time goes in v8:
time: 447 us; the launch traced here: 445 us
  waiting for transfers between devices  141 us (32%)
  Pallas kernels  136 us (30%)
  starting transfers between devices  92.2 us (21%)
  local copies, waits for them, and re-layouts  34.4 us (8%)
  other arithmetic  25.3 us (6%)
  between operations  16.4 us (4%)
    pallas_call x11, Pallas kernels, call(): pl.pallas_call(kernel, grid_spec=pltpu.PrefetchScalarGridSpec(num_scalar_...  125 us
    ppermute x29, waiting for transfers between devices, flip(): return lax.ppermute(values, 'dp', [(i, i ^ bit) for i in range(8)])  62.5 us
    ppermute x12, waiting for transfers between devices, shift_to(): lax.ppermute(values, 'tensor', [(i, (i + k) % tensor) for i in range(tens...  31 us
    ppermute x6, starting transfers between devices, up(): return lax.ppermute(values, 'tensor', [(i, i + 1) for i in range(step)])  25.6 us
    ppermute x3, waiting for transfers between devices, onward(): lax.ppermute(u, 'tensor', [(i, i + 1) for i in range(step - 1, tensor - 1)])  18.8 us
    ppermute x29, starting transfers between devices, flip(): return lax.ppermute(values, 'dp', [(i, i ^ bit) for i in range(8)])  18 us
    ppermute x12, starting transfers between devices, shift_to(): lax.ppermute(values, 'tensor', [(i, (i + k) % tensor) for i in range(tens...  17.8 us
    ppermute x6, waiting for transfers between devices, up(): return lax.ppermute(values, 'tensor', [(i, i + 1) for i in range(step)])  14.9 us
  transfers between devices with their start and end apart: 65, of which 27 were waited for; matrix products, arithmetic and copies ran while one was open for 9% of the time, Pallas kernels for 30%

profile of v8, /device:TPU:0, one launch (start us, length us, event | category | flops | bytes accessed | tf_op | source)
XLA Modules:
  0.0 445.3 jit_solution(11008677696768197810)
XLA Ops:
  23.5 11.6 %attend_forward.1 = f32[1024,384]{1,0:T(8,128)} custom-call(bf16[2048,768]{1,0:T(8,128)(2,1)} %x_ref.1, bf16[576,768]{1,0:T(8,128)(2,1)} %pad_maximum_fusion.1.w_ref.local_ref, f32[1,576]{1,0:T(1,128)} %slice.181.bias_ref), custom_call_target="tpu_custom_call" | custom-call | flops 2617245696 | bytes 5605632 | tf_op jit(solution)/shard_map/attend_forward/pallas_call | solution.py:58
  36.8 3.9 collective-permute-done.3
  41.4 7.3 %collective-permute-done.4 = f32[1,1344]{1,0:T(1,128)} collective-permute-done((f32[1,1344]{1,0:T(1,128)S(1)}, f32[1,1344]{1,0:T(1,128)}, u32[]{:S(2)}, u32[]{:S(2)}) %collective-permute-start.4) | collective-permute-done | bytes 5408 | tf_op jit(solution)/shard_map/ppermute | solution.py:527
  63.7 4.1 collective-permute-done.10.refs_2_
  67.7 5.4 %collective-permute-done.8.refs_0_ = f32[96,768]{1,0:T(8,128)S(1)} collective-permute-done((f32[96,768]{1,0:T(8,128)}, f32[96,768]{1,0:T(8,128)S(1)}, u32[]{:S(2)}, u32[]{:S(2)}) %collective-permute-start.8) | collective-permute-done | bytes 294944 | tf_op jit(solution)/shard_map/ppermute | solution.py:527
  73.1 8.3 %collective-permute-done.9.refs_1_ = f32[96,768]{1,0:T(8,128)S(1)} collective-permute-done((f32[96,768]{1,0:T(8,128)}, f32[96,768]{1,0:T(8,128)S(1)}, u32[]{:S(2)}, u32[]{:S(2)}) %collective-permute-start.9) | collective-permute-done | bytes 294944 | tf_op jit(solution)/shard_map/ppermute | solution.py:527
  85.7 3.4 collective-permute-done.15.refs_5_.refs_6_
  89.1 4.3 all-to-all-start
  95.6 24.3 %collective-permute-done.13.refs_2_ = f32[1,3,48,768]{3,2,1,0:T(8,128)} collective-permute-done((f32[1,3,48,768]{3,2,1,0:T(8,128)}, f32[1,3,48,768]{3,2,1,0:T(8,128)}, u32[]{:S(2)}, u32[]{:S(2)}) %collective-permute-start.13) | collective-permute-done | bytes 442400 | tf_op jit(solution)/shard_map/ppermute | solution.py:531
  135.2 9.0 %output_forward.1 = (bf16[4,512,192]{2,1,0:T(8,128)(2,1)}, f32[512,768]{1,0:T(8,128)}, bf16[512,768]{1,0:T(8,128)(2,1)}, f32[512,768]{1,0:T(8,128)}, f32[512,1]{1,0:T(8,128)}, /*index=5*/bf16[4,192,768]{2,1,0:T(8,128)(2,1)}) custom-call(s32[4]{0:T(128)} %and_select_fusion.2.refs_0_, s32[8]{0:T(128)} %stack.211.refs_1_, bf16[192,768]{1,0:T(8,128)(2,1)} %refs_2_.1, ...), custom_call_target="tpu_custom_call" | custom-call | flops 603979776 | bytes 13887520 | tf_op jit(solution)/shard_map/output_forward/pallas_call | solution.py:58
  148.1 13.4 %inner_forward.1 = (bf16[4,512,768]{2,1,0:T(8,128)(2,1)}, f32[4,512,768]{2,1,0:T(8,128)}, bf16[4,768,768]{2,1,0:T(8,128)(2,1)}) custom-call(s32[16]{0:T(128)} %stack.235.refs_0_, bf16[768,768]{1,0:T(8,128)(2,1)} %refs_1_.2, f32[2,3,64,768]{3,2,1,0:T(8,128)} %get-tuple-element.148.refs_2_, f32[2,3,56,768]{3,2,1,0:T(8,128)} %get-tuple-element.147.refs_3_, ...), custom_call_target="tpu_custom_call" | custom-call | flops 2415919104 | bytes 24981568 | tf_op jit(solution)/shard_map/inner_forward/pallas_call | solution.py:58
  167.2 12.1 %outer_forward.1 = (f32[512,768]{1,0:T(8,128)}, f32[512,768]{1,0:T(8,128)}, f32[512,1]{1,0:T(8,128)}, bf16[4,768,768]{2,1,0:T(8,128)(2,1)}) custom-call(s32[16]{0:T(128)} %stack.244.refs_0_, bf16[768,768]{1,0:T(8,128)(2,1)} %refs_1_.3, f32[2,3,48,768]{3,2,1,0:T(8,128)} %get-tuple-element.163.refs_2_, f32[2,3,48,768]{3,2,1,0:T(8,128)} %get-tuple-element.164.refs_3_, ...), custom_call_target="tpu_custom_call" | custom-call | flops 2415919104 | bytes 20867136 | tf_op jit(solution)/shard_map/outer_forward/pallas_call | solution.py:58
  181.7 5.3 %last_norm_backward.1 = (f32[512,768]{1,0:T(8,128)}, bf16[512,768]{1,0:T(8,128)(2,1)}, f32[8,768]{1,0:T(8,128)}) custom-call(bf16[512,768]{1,0:T(8,128)(2,1)} %constant_dynamic-slice_fusion.cot_ref, f32[512,768]{1,0:T(8,128)} %get-tuple-element.186.nrm_ref, f32[512,1]{1,0:T(8,128)} %get-tuple-element.187.inv_ref, ...), custom_call_target="tpu_custom_call" | custom-call | tf_op jit(solution)/shard_map/last_norm_backward/pallas_call | solution.py:58
  187.0 8.0 %grad_full.1 = f32[768,3072]{1,0:T(8,128)} custom-call(bf16[512,768]{1,0:T(8,128)(2,1)} %get-tuple-element.193.refs_0_.go_ref, bf16[4,512,768]{2,1,0:T(8,128)(2,1)} %get-tuple-element.177.refs_9_.refs_1_), custom_call_target="tpu_custom_call" | custom-call | tf_op jit(solution)/shard_map/grad_full/pallas_call | solution.py:58
  197.3 15.8 %inner_backward.1 = (bf16[4,512,768]{2,1,0:T(8,128)(2,1)}, f32[512,768]{1,0:T(8,128)}, bf16[512,768]{1,0:T(8,128)(2,1)}, f32[1,4,1,768]{3,2,1,0:T(1,128)}, f32[1,8,768]{2,1,0:T(8,128)}) custom-call(bf16[512,768]{1,0:T(8,128)(2,1)} %get-tuple-element.193.refs_0_.go_ref, bf16[4,768,768]{2,1,0:T(8,128)(2,1)} %get-tuple-element.194.wu_ref, ...), custom_call_target="tpu_custom_call" | custom-call | tf_op jit(solution)/shard_map/inner_backward/pallas_call | solution.py:58
  214.9 8.7 %grad_rows.1 = (f32[384,3072]{1,0:T(8,128)}, f32[384,3072]{1,0:T(8,128)}) custom-call(bf16[768,768]{1,0:T(8,128)(2,1)} %fusion.refs_0_, bf16[512,768]{1,0:T(8,128)(2,1)} %get-tuple-element.162.refs_9_.refs_1_, bf16[4,512,768]{2,1,0:T(8,128)(2,1)} %get-tuple-element.202.refs_2_), custom_call_target="tpu_custom_call" | custom-call | tf_op jit(solution)/shard_map/grad_rows/pallas_call | solution.py:58
  231.5 3.6 assemble.1.w_ref
  242.3 28.1 %attend_backward.1 = (f32[768,3072]{1,0:T(8,128)}, f32[512,768]{1,0:T(8,128)}, f32[1,4,1,576]{3,2,1,0:T(1,128)}) custom-call(bf16[512,768]{1,0:T(8,128)(2,1)} %constant_dynamic-slice_fusion.1.refs_7_.x_ref, bf16[512,768]{1,0:T(8,128)(2,1)} %get-tuple-element.213.ga_ref, f32[512,768]{1,0:T(8,128)} %get-tuple-element.214.gr_ref, ...), custom_call_target="tpu_custom_call" | custom-call | tf_op jit(solution)/shard_map/attend_backward/pallas_call | solution.py:58
  273.8 8.0 %collective-permute-start.34 = (f32[512,768]{1,0:T(8,128)}, f32[512,768]{1,0:T(8,128)}, u32[]{:S(2)}, u32[]{:S(2)}) collective-permute-start(f32[512,768]{1,0:T(8,128)} %get-tuple-element.244.own_ref), channel_id=1, source_target_pairs={{0,1},{1,2},{2,3},{4,5},{5,6},{6,7},{8,9},{9,10},{10,11},{12,13},{... | collective-permute-start | bytes 4718600 | tf_op jit(solution)/shard_map/ppermute | solution.py:834
  283.3 16.8 %collective-permute-done.38 = f32[192,1536]{1,0:T(8,128)S(1)} collective-permute-done((f32[192,1536]{1,0:T(8,128)S(1)}, f32[192,1536]{1,0:T(8,128)S(1)}, u32[]{:S(2)}, u32[]{:S(2)}) %collective-permute-start.38) | collective-permute-done | bytes 1179680 | tf_op jit(solution)/shard_map/ppermute | solution.py:531
  306.7 18.8 %collective-permute-done.34.refs_0_ = f32[512,768]{1,0:T(8,128)} collective-permute-done((f32[512,768]{1,0:T(8,128)}, f32[512,768]{1,0:T(8,128)}, u32[]{:S(2)}, u32[]{:S(2)}) %collective-permute-start.34) | collective-permute-done | bytes 1572896 | tf_op jit(solution)/shard_map/ppermute | solution.py:834
  334.6 5.0 %narrow.1 = bf16[2048,768]{1,0:T(8,128)(2,1)} custom-call(f32[2048,768]{1,0:T(8,128)} %all-gather.2.cloned.1.call-done.x_ref), custom_call_target="tpu_custom_call" | custom-call | bytes 9437184 | tf_op jit(solution)/shard_map/narrow/pallas_call | solution.py:58
  342.3 7.4 %collective-permute-start.45 = (f32[192,768]{1,0:T(8,128)S(1)}, f32[192,768]{1,0:T(8,128)S(1)}, u32[]{:S(2)}, u32[]{:S(2)}) collective-permute-start(f32[192,768]{1,0:T(8,128)S(1)} %get-tuple-element.232), channel_id=1, source_target_pairs={{0,1},{4,5},{8,9},{12,13},{16,17},{20,21},{24,25},{28,29}} | collective-permute-start | bytes 1769480 | tf_op jit(solution)/shard_map/ppermute | solution.py:788
  351.3 4.3 collective-permute-done.47
  355.6 6.0 %collective-permute-done.45 = f32[192,768]{1,0:T(8,128)S(1)} collective-permute-done((f32[192,768]{1,0:T(8,128)S(1)}, f32[192,768]{1,0:T(8,128)S(1)}, u32[]{:S(2)}, u32[]{:S(2)}) %collective-permute-start.45) | collective-permute-done | bytes 589856 | tf_op jit(solution)/shard_map/ppermute | solution.py:788
  362.8 6.1 %collective-permute-done.43.refs_4_ = f32[512,768]{1,0:T(8,128)} collective-permute-done((f32[512,768]{1,0:T(8,128)}, f32[512,768]{1,0:T(8,128)}, u32[]{:S(2)}, u32[]{:S(2)}) %collective-permute-start.43) | collective-permute-done | bytes 1572896 | tf_op jit(solution)/shard_map/ppermute | solution.py:835
  375.6 6.3 %collective-permute-start.50 = (f32[96,768]{1,0:T(8,128)S(1)}, f32[96,768]{1,0:T(8,128)S(1)}, u32[]{:S(2)}, u32[]{:S(2)}) collective-permute-start(f32[96,768]{1,0:T(8,128)S(1)} %get-tuple-element.302), channel_id=1, source_target_pairs={{0,1},{4,5},{8,9},{12,13},{16,17},{20,21},{24,25},{28,29}} | collective-permute-start | bytes 884744 | tf_op jit(solution)/shard_map/ppermute | solution.py:788
  388.3 4.4 collective-permute-start.53
  393.4 8.1 %collective-permute-done.48 = f32[192,768]{1,0:T(8,128)S(1)} collective-permute-done((f32[192,768]{1,0:T(8,128)}, f32[192,768]{1,0:T(8,128)S(1)}, u32[]{:S(2)}, u32[]{:S(2)}) %collective-permute-start.48) | collective-permute-done | bytes 589856 | tf_op jit(solution)/shard_map/ppermute | solution.py:788
  405.6 5.3 %collective-permute-done.55 = f32[16,768]{1,0:T(8,128)S(1)} collective-permute-done((f32[16,768]{1,0:T(8,128)S(1)}, f32[16,768]{1,0:T(8,128)S(1)}, u32[]{:S(2)}, u32[]{:S(2)}) %collective-permute-start.55) | collective-permute-done | bytes 49184 | tf_op jit(solution)/shard_map/ppermute | solution.py:840
  416.5 4.8 %collective-permute-start.59 = (f32[192,768]{1,0:T(8,128)}, f32[192,768]{1,0:T(8,128)}, u32[]{:S(2)}, u32[]{:S(2)}) collective-permute-start(f32[192,768]{1,0:T(8,128)} %add.268), channel_id=1, source_target_pairs={{0,1},{1,2},{2,3},{4,5},{5,6},{6,7},{8,9},{9,10},{10,11},{12,13},{... | collective-permute-start | bytes 1769480 | tf_op jit(solution)/shard_map/ppermute | solution.py:788
  427.5 7.4 %place.1 = f32[2048,768]{1,0:T(8,128)} custom-call(s32[1]{0:T(128)} %bitcast.59.z_ref, f32[512,768]{1,0:T(8,128)} %get-tuple-element.244.own_ref, f32[512,768]{1,0:T(8,128)} %collective-permute-done.34.refs_0_, f32[512,768]{1,0:T(8,128)} %collective-permute-done.41.refs_1_, f32[512,768]{1,0:T(8,128)} %collective-permute-done.42.refs_2_, ...), custom_call_target="tpu_custom_call" | custom-call | tf_op jit(solution)/shard_map/place/pallas_call | solution.py:58
  (289 shorter events, 143.6 us)
Async XLA Ops:
  10.7 39.3 %collective-permute-start = (f32[120,768]{1,0:T(8,128)}, f32[120,768]{1,0:T(8,128)S(1)}, u32[]{:S(2)}, u32[]{:S(2)}) collective-permute-start(f32[120,768]{1,0:T(8,128)} %maximum_convert_fusion), channel_id=1, source_target_pairs={{0,1},{1,2},{2,3},{3,0},{4,5},{5,6},{6,7},{7,4},{8,9},{9,10},{10,1... | collective-permute-start | bytes 1105928 | tf_op jit(solution)/shard_map/ppermute | solution.py:527
  13.7 36.3 %collective-permute-start.1 = (f32[120,768]{1,0:T(8,128)}, f32[120,768]{1,0:T(8,128)}, u32[]{:S(2)}, u32[]{:S(2)}) collective-permute-start(f32[120,768]{1,0:T(8,128)} %maximum_convert_fusion), channel_id=1, source_target_pairs={{0,2},{1,3},{2,0},{3,1},{4,6},{5,7},{6,4},{7,5},{8,10},{9,11},{10,... | collective-permute-start | bytes 1105928 | tf_op jit(solution)/shard_map/ppermute | solution.py:527
  16.3 33.7 %collective-permute-start.2 = (f32[120,768]{1,0:T(8,128)}, f32[120,768]{1,0:T(8,128)}, u32[]{:S(2)}, u32[]{:S(2)}) collective-permute-start(f32[120,768]{1,0:T(8,128)} %maximum_convert_fusion), channel_id=1, source_target_pairs={{0,3},{1,0},{2,1},{3,2},{4,7},{5,4},{6,5},{7,6},{8,11},{9,8},{10,9... | collective-permute-start | bytes 1105928 | tf_op jit(solution)/shard_map/ppermute | solution.py:527
  19.8 20.9 %collective-permute-start.3 = (f32[1,1344]{1,0:T(1,128)S(1)}, f32[1,1344]{1,0:T(1,128)S(1)}, u32[]{:S(2)}, u32[]{:S(2)}) collective-permute-start(f32[1,1344]{1,0:T(1,128)S(1)} %convert_element_type.38), channel_id=1, source_target_pairs={{0,1},{1,2},{2,3},{3,0},{4,5},{5,6},{6,7},{7,4},{8,9},{9,10},{10,1... | collective-permute-start | bytes 16136 | tf_op jit(solution)/shard_map/ppermute | solution.py:527
  20.5 28.2 %collective-permute-start.4 = (f32[1,1344]{1,0:T(1,128)S(1)}, f32[1,1344]{1,0:T(1,128)}, u32[]{:S(2)}, u32[]{:S(2)}) collective-permute-start(f32[1,1344]{1,0:T(1,128)S(1)} %convert_element_type.38), channel_id=1, source_target_pairs={{0,2},{1,3},{2,0},{3,1},{4,6},{5,7},{6,4},{7,5},{8,10},{9,11},{10,... | collective-permute-start | bytes 16136 | tf_op jit(solution)/shard_map/ppermute | solution.py:527
  51.2 31.8 %collective-permute-start.6 = (f32[1,3,64,768]{3,2,1,0:T(8,128)S(1)}, f32[1,3,64,768]{3,2,1,0:T(8,128)S(1)}, u32[]{:S(2)}, u32[]{:S(2)}) collective-permute-start(f32[1,3,64,768]{3,2,1,0:T(8,128)S(1)} %get-tuple-element.136.refs_0_), channel_id=1, source_target_pairs={{0,8},{4,12},{8,0},{12,4},{16,24},{20,28},{24,16},{28,20},{1,9},{5... | collective-permute-start | bytes 1769480 | tf_op jit(solution)/shard_map/ppermute | solution.py:531
  52.7 30.3 %collective-permute-start.7 = (f32[1,3,56,768]{3,2,1,0:T(8,128)S(1)}, f32[1,3,56,768]{3,2,1,0:T(8,128)S(1)}, u32[]{:S(2)}, u32[]{:S(2)}) collective-permute-start(f32[1,3,56,768]{3,2,1,0:T(8,128)S(1)} %get-tuple-element.137.refs_1_), channel_id=1, source_target_pairs={{0,16},{4,20},{8,24},{12,28},{16,0},{20,4},{24,8},{28,12},{1,17},{... | collective-permute-start | bytes 1548296 | tf_op jit(solution)/shard_map/ppermute | solution.py:531
  57.2 24.2 %collective-permute-start.9 = (f32[96,768]{1,0:T(8,128)}, f32[96,768]{1,0:T(8,128)S(1)}, u32[]{:S(2)}, u32[]{:S(2)}) collective-permute-start(f32[96,768]{1,0:T(8,128)} %dynamic-slice_convert_fusion), channel_id=1, source_target_pairs={{0,2},{1,3},{2,0},{3,1},{4,6},{5,7},{6,4},{7,5},{8,10},{9,11},{10,... | collective-permute-start | bytes 884744 | tf_op jit(solution)/shard_map/ppermute | solution.py:527
  84.7 43.2 %collective-permute-start.11 = (f32[2,3,64,768]{3,2,1,0:T(8,128)}, f32[2,3,64,768]{3,2,1,0:T(8,128)}, u32[]{:S(2)}, u32[]{:S(2)}) collective-permute-start(f32[2,3,64,768]{3,2,1,0:T(8,128)} %get-tuple-element.148.refs_2_), channel_id=1, source_target_pairs={{0,16},{4,20},{8,24},{12,28},{16,0},{20,4},{24,8},{28,12},{1,17},{... | collective-permute-start | bytes 3538952 | tf_op jit(solution)/shard_map/ppermute | solution.py:531
  85.2 42.7 %collective-permute-start.12 = (f32[2,3,56,768]{3,2,1,0:T(8,128)}, f32[2,3,56,768]{3,2,1,0:T(8,128)}, u32[]{:S(2)}, u32[]{:S(2)}) collective-permute-start(f32[2,3,56,768]{3,2,1,0:T(8,128)} %get-tuple-element.147.refs_3_), channel_id=1, source_target_pairs={{0,8},{4,12},{8,0},{12,4},{16,24},{20,28},{24,16},{28,20},{1,9},{5... | collective-permute-start | bytes 3096584 | tf_op jit(solution)/shard_map/ppermute | solution.py:531
  89.1 46.0 %all-to-all-start = ((f32[4,256,384]{2,1,0:T(8,128)}), f32[4,256,384]{2,1,0:T(8,128)}, u32[]{:S(2)}, u32[]{:S(2)}) async-start(f32[4,256,384]{2,1,0:T(8,128)} %bitcast.70), calls=%async_computation | async-start | bytes 3145728 | tf_op jit(solution)/shard_map/all_to_all | solution.py:936
  93.6 241.0 %all-gather.2.cloned.1.call-start = ((), (), s32[]{:S(2)}) async-start(), calls=%async_computation.4 | async-start | bytes 7864320 | tf_op jit(solution)/shard_map/all_gather | solution.py:959
  93.6 26.3 %collective-permute-start.13 = (f32[1,3,48,768]{3,2,1,0:T(8,128)}, f32[1,3,48,768]{3,2,1,0:T(8,128)}, u32[]{:S(2)}, u32[]{:S(2)}) collective-permute-start(f32[1,3,48,768]{3,2,1,0:T(8,128)} %copy-done.15), channel_id=1, source_target_pairs={{0,8},{4,12},{8,0},{12,4},{16,24},{20,28},{24,16},{28,20},{1,9},{5... | collective-permute-start | bytes 1327112 | tf_op jit(solution)/shard_map/ppermute | solution.py:531
  94.2 28.6 %collective-permute-start.14 = (f32[1,3,48,768]{3,2,1,0:T(8,128)}, f32[1,3,48,768]{3,2,1,0:T(8,128)}, u32[]{:S(2)}, u32[]{:S(2)}) collective-permute-start(f32[1,3,48,768]{3,2,1,0:T(8,128)} %copy-done.17), channel_id=1, source_target_pairs={{0,16},{4,20},{8,24},{12,28},{16,0},{20,4},{24,8},{28,12},{1,17},{... | collective-permute-start | bytes 1327112 | tf_op jit(solution)/shard_map/ppermute | solution.py:531
  128.0 19.5 %collective-permute-start.23 = (f32[2,3,64,768]{3,2,1,0:T(8,128)}, f32[2,3,64,768]{3,2,1,0:T(8,128)}, u32[]{:S(2)}, u32[]{:S(2)}) collective-permute-start(f32[2,3,64,768]{3,2,1,0:T(8,128)} %collective-permute-done.11.refs_4_), channel_id=1, source_target_pairs={{0,4},{4,0},{8,12},{12,8},{16,20},{20,16},{24,28},{28,24},{1,5},{5... | collective-permute-start | bytes 3538952 | tf_op jit(solution)/shard_map/ppermute | solution.py:531
  128.6 33.0 %collective-permute-start.18 = (f32[2,3,48,768]{3,2,1,0:T(8,128)}, f32[2,3,48,768]{3,2,1,0:T(8,128)}, u32[]{:S(2)}, u32[]{:S(2)}) collective-permute-start(f32[2,3,48,768]{3,2,1,0:T(8,128)} %get-tuple-element.163.refs_2_), channel_id=1, source_target_pairs={{0,16},{4,20},{8,24},{12,28},{16,0},{20,4},{24,8},{28,12},{1,17},{... | collective-permute-start | bytes 2654216 | tf_op jit(solution)/shard_map/ppermute | solution.py:531
  129.1 32.5 %collective-permute-start.19 = (f32[2,3,48,768]{3,2,1,0:T(8,128)}, f32[2,3,48,768]{3,2,1,0:T(8,128)}, u32[]{:S(2)}, u32[]{:S(2)}) collective-permute-start(f32[2,3,48,768]{3,2,1,0:T(8,128)} %get-tuple-element.164.refs_3_), channel_id=1, source_target_pairs={{0,8},{4,12},{8,0},{12,4},{16,24},{20,28},{24,16},{28,20},{1,9},{5... | collective-permute-start | bytes 2654216 | tf_op jit(solution)/shard_map/ppermute | solution.py:531
  179.3 160.3 %reduce-scatter.3.cloned.1.call-start = ((), (), s32[]{:S(2)}) async-start(), calls=%async_computation.3 | async-start | bytes 10616832 | tf_op jit(solution)/shard_map/reduce_scatter | solution.py:967
  195.1 173.8 %reduce-scatter.5.cloned.1.call-start = ((), (), s32[]{:S(2)}) async-start(), calls=%async_computation.5 | async-start | bytes 10616832 | tf_op jit(solution)/shard_map/reduce_scatter | solution.py:989
  195.3 19.0 %collective-permute-start.30 = (f32[2,3,72,768]{3,2,1,0:T(8,128)}, f32[2,3,72,768]{3,2,1,0:T(8,128)S(1)}, u32[]{:S(2)}, u32[]{:S(2)}) collective-permute-start(f32[2,3,72,768]{3,2,1,0:T(8,128)} %copy-done.19), channel_id=1, source_target_pairs={{0,4},{4,0},{8,12},{12,8},{16,20},{20,16},{24,28},{28,24},{1,5},{5... | collective-permute-start | bytes 3981320 | tf_op jit(solution)/shard_map/ppermute | solution.py:531
  271.7 28.3 %collective-permute-start.38 = (f32[192,1536]{1,0:T(8,128)S(1)}, f32[192,1536]{1,0:T(8,128)S(1)}, u32[]{:S(2)}, u32[]{:S(2)}) collective-permute-start(f32[192,1536]{1,0:T(8,128)S(1)} %copy-done.27), channel_id=1, source_target_pairs={{0,16},{4,20},{8,24},{12,28},{16,0},{20,4},{24,8},{28,12},{1,17},{... | collective-permute-start | bytes 3538952 | tf_op jit(solution)/shard_map/ppermute | solution.py:531
  272.5 29.9 %collective-permute-start.37 = (f32[192,1536]{1,0:T(8,128)}, f32[192,1536]{1,0:T(8,128)S(1)}, u32[]{:S(2)}, u32[]{:S(2)}) collective-permute-start(f32[192,1536]{1,0:T(8,128)} %pad_maximum_fusion), channel_id=1, source_target_pairs={{0,8},{4,12},{8,0},{12,4},{16,24},{20,28},{24,16},{28,20},{1,9},{5... | collective-permute-start | bytes 3538952 | tf_op jit(solution)/shard_map/ppermute | solution.py:531
  273.8 51.7 %collective-permute-start.34 = (f32[512,768]{1,0:T(8,128)}, f32[512,768]{1,0:T(8,128)}, u32[]{:S(2)}, u32[]{:S(2)}) collective-permute-start(f32[512,768]{1,0:T(8,128)} %get-tuple-element.244.own_ref), channel_id=1, source_target_pairs={{0,1},{1,2},{2,3},{4,5},{5,6},{6,7},{8,9},{9,10},{10,11},{12,13},{... | collective-permute-start | bytes 4718600 | tf_op jit(solution)/shard_map/ppermute | solution.py:834
  281.8 45.7 %collective-permute-start.35 = (f32[512,768]{1,0:T(8,128)}, f32[512,768]{1,0:T(8,128)}, u32[]{:S(2)}, u32[]{:S(2)}) collective-permute-start(f32[512,768]{1,0:T(8,128)} %get-tuple-element.244.own_ref), channel_id=1, source_target_pairs={{1,0},{2,1},{3,2},{5,4},{6,5},{7,6},{9,8},{10,9},{11,10},{13,12},{... | collective-permute-start | bytes 4718600 | tf_op jit(solution)/shard_map/ppermute | solution.py:835
  302.5 28.5 %collective-permute-start.39 = (f32[96,1536]{1,0:T(8,128)S(1)}, f32[96,1536]{1,0:T(8,128)}, u32[]{:S(2)}, u32[]{:S(2)}) collective-permute-start(f32[96,1536]{1,0:T(8,128)S(1)} %slice.187), channel_id=1, source_target_pairs={{0,16},{4,20},{8,24},{12,28},{16,0},{20,4},{24,8},{28,12},{1,17},{... | collective-permute-start | bytes 1769480 | tf_op jit(solution)/shard_map/ppermute | solution.py:531
  303.9 28.7 %collective-permute-start.40 = (f32[96,1536]{1,0:T(8,128)}, f32[96,1536]{1,0:T(8,128)}, u32[]{:S(2)}, u32[]{:S(2)}) collective-permute-start(f32[96,1536]{1,0:T(8,128)} %slice.188), channel_id=1, source_target_pairs={{0,8},{4,12},{8,0},{12,4},{16,24},{20,28},{24,16},{28,20},{1,9},{5... | collective-permute-start | bytes 1769480 | tf_op jit(solution)/shard_map/ppermute | solution.py:531
  325.5 37.2 %collective-permute-start.41 = (f32[512,768]{1,0:T(8,128)}, f32[512,768]{1,0:T(8,128)}, u32[]{:S(2)}, u32[]{:S(2)}) collective-permute-start(f32[512,768]{1,0:T(8,128)} %collective-permute-done.34.refs_0_), channel_id=1, source_target_pairs={{1,2},{2,3},{5,6},{6,7},{9,10},{10,11},{13,14},{14,15},{17,18},{18... | collective-permute-start | bytes 4718600 | tf_op jit(solution)/shard_map/ppermute | solution.py:834
  327.4 41.5 %collective-permute-start.43 = (f32[512,768]{1,0:T(8,128)}, f32[512,768]{1,0:T(8,128)}, u32[]{:S(2)}, u32[]{:S(2)}) collective-permute-start(f32[512,768]{1,0:T(8,128)} %collective-permute-done.35.refs_3_), channel_id=1, source_target_pairs={{1,0},{2,1},{5,4},{6,5},{9,8},{10,9},{13,12},{14,13},{17,16},{18,1... | collective-permute-start | bytes 4718600 | tf_op jit(solution)/shard_map/ppermute | solution.py:835
  342.3 19.3 %collective-permute-start.45 = (f32[192,768]{1,0:T(8,128)S(1)}, f32[192,768]{1,0:T(8,128)S(1)}, u32[]{:S(2)}, u32[]{:S(2)}) collective-permute-start(f32[192,768]{1,0:T(8,128)S(1)} %get-tuple-element.232), channel_id=1, source_target_pairs={{0,1},{4,5},{8,9},{12,13},{16,17},{20,21},{24,25},{28,29}} | collective-permute-start | bytes 1769480 | tf_op jit(solution)/shard_map/ppermute | solution.py:788
  370.7 40.4 %collective-permute-start.42 = (f32[512,768]{1,0:T(8,128)}, f32[512,768]{1,0:T(8,128)}, u32[]{:S(2)}, u32[]{:S(2)}) collective-permute-start(f32[512,768]{1,0:T(8,128)} %collective-permute-done.41.refs_1_), channel_id=1, source_target_pairs={{2,3},{6,7},{10,11},{14,15},{18,19},{22,23},{26,27},{30,31}} | collective-permute-start | bytes 4718600 | tf_op jit(solution)/shard_map/ppermute | solution.py:834
  372.5 38.6 %collective-permute-start.44 = (f32[512,768]{1,0:T(8,128)}, f32[512,768]{1,0:T(8,128)}, u32[]{:S(2)}, u32[]{:S(2)}) collective-permute-start(f32[512,768]{1,0:T(8,128)} %collective-permute-done.43.refs_4_), channel_id=1, source_target_pairs={{1,0},{5,4},{9,8},{13,12},{17,16},{21,20},{25,24},{29,28}} | collective-permute-start | bytes 4718600 | tf_op jit(solution)/shard_map/ppermute | solution.py:835
  388.3 22.7 %collective-permute-start.53 = (f32[96,768]{1,0:T(8,128)S(1)}, f32[96,768]{1,0:T(8,128)S(1)}, u32[]{:S(2)}, u32[]{:S(2)}) collective-permute-start(f32[96,768]{1,0:T(8,128)S(1)} %slice_add_fusion.4), channel_id=1, source_target_pairs={{0,1},{1,2},{4,5},{5,6},{8,9},{9,10},{12,13},{13,14},{16,17},{17,1... | collective-permute-start | bytes 884744 | tf_op jit(solution)/shard_map/ppermute | solution.py:788
  (75 other events, 1069.9 us)
Sparse Core Ops, SparseCore 0:
  179.4 123.1 all-gather.1
Sparse Core Ops, SparseCore 1:
  195.2 77.5 reduce-scatter.2
  276.1 89.8 reduce-scatter.4
